TPU v7x, 512 devices: a whole 4x8x8 slice. The times are simulated.
512 devices in a mesh: lon: 32 (over y_lo, z), sec: 4 (over y_hi, core), rad: 4 (over x).
Axes of the slice: x: 4, y: 8 (y_hi: 2, y_lo: 4; y = y_hi * 4 + y_lo), z: 8, core: 2. Of those that a mesh axis runs over, the one named last changes fastest.
Arguments:
- plasma_fields: float32 [8, 64, 128, 512], P(None, 'sec', 'lon', 'rad'), may hold values from -6 to 6
- velocity: bfloat16 [3, 64, 128, 512], P(None, 'sec', 'lon', 'rad'), may hold values from -1 to 1
- resistivity: bfloat16 [64, 128, 512], P('sec', 'lon', 'rad'), may hold values from 0.0049743652 to 0.039794922
- conductance: float32 [128, 512], P('lon', 'rad'), may hold values from 0.5 to 5
- foot_map: int32 [65536, 256], P(('lon', 'sec', 'rad')), may hold values from 0 to 511
- foot_owner: int32 [65536, 1], P(('lon', 'sec', 'rad')), may hold values from 0 to 127; in each aligned block of 128 rows (0 to 127, 128 to 255, ...) at most 2 rows name the same one
- foot_row: int32 [65536], P(('lon', 'sec', 'rad')), may hold values from 0 to 31
Outputs:
- advanced_fields: float32 [8, 64, 128, 512], P(None, 'sec', 'lon', 'rad')
- potential: float32 [128, 512], P('lon', 'rad')
- foot_table: float32 [16384, 256], P(('lon', 'sec', 'rad'))
Inputs may be any that keep to these rules, and one draw needn't show every extreme that they name: `foot_owner`: in each aligned block of 128 rows (the records of one device) no owner index appears more than 2 times.
All inputs are finite; a program needn't handle non-finite values.
Results may differ from a plain program's by a relative error of at most 0.0003.
Values sent between devices are 32-bit elements; how exact they have to be, the bound alone decides.
No kernel may reach another device: no remote copies, remote signals or barrier semaphores. Data moves between devices by JAX's collectives and lax.ppermute only.
A program may use at most 128 MiB of HBM per device.

v0:
```python
import jax
import jax.numpy as jnp
from jax import lax
from jax.sharding import PartitionSpec as P

PHASES = 4
SWEEPS = 8
ROWS_OWN = 32


COURANT = 0.25
DAMPING = 0.05
RELAX = 0.8


def with_halo(cells, sides, width, closed):
    for axis, dim in sides:
        count = lax.axis_size(axis)
        ends = count if closed else count - 1
        head = lax.slice_in_dim(cells, 0, width, axis=dim)
        tail = lax.slice_in_dim(cells, cells.shape[dim] - width, cells.shape[dim], axis=dim)
        cells = jnp.concatenate(
            [
                lax.ppermute(tail, axis, [(i, (i + 1) % count) for i in range(ends)]),
                cells,
                lax.ppermute(head, axis, [((i + 1) % count, i) for i in range(ends)]),
            ],
            axis=dim,
        )
    return cells


def broadcast(value, axis, source):
    kept = jnp.where(lax.axis_index(axis) == source, value, 0).astype(value.dtype)
    return lax.psum(kept, axis)


def advance(padded, velocity_f, resist_f):
    centre = padded[:, 1:-1, 1:-1, 1:-1]
    shell_lo = padded[:, :-2, 1:-1, 1:-1]
    shell_hi = padded[:, 2:, 1:-1, 1:-1]
    lon_lo = padded[:, 1:-1, :-2, 1:-1]
    lon_hi = padded[:, 1:-1, 2:, 1:-1]
    lat_lo = padded[:, 1:-1, 1:-1, :-2]
    lat_hi = padded[:, 1:-1, 1:-1, 2:]

    def upwind(component, lower_side, upper_side):
        return jnp.maximum(component, 0.0) * (centre - lower_side) + jnp.minimum(component, 0.0) * (
            upper_side - centre
        )

    transport = (
        upwind(velocity_f[0], shell_lo, shell_hi)
        + upwind(velocity_f[1], lon_lo, lon_hi)
        + upwind(velocity_f[2], lat_lo, lat_hi)
    )
    spread = shell_lo + shell_hi + lon_lo + lon_hi + lat_lo + lat_hi - 6.0 * centre
    return centre - COURANT * transport + resist_f * spread


def lon_faces(block):
    return with_halo(block, (("lon", 2),), 1, True)


def band_faces(block):
    return with_halo(block, (("rad", 3),), 1, False)


def relax_plane(framed, framer):
    field_lon = framed[0]
    field_lat = framed[1]
    cond_all = framed[2]
    source = (
        field_lat[2:, 1:-1] - field_lat[:-2, 1:-1] - (field_lon[1:-1, 2:] - field_lon[1:-1, :-2])
    )
    middle = cond_all[1:-1, 1:-1]
    east = 0.5 * (middle + cond_all[2:, 1:-1])
    west = 0.5 * (middle + cond_all[:-2, 1:-1])
    north = 0.5 * (middle + cond_all[1:-1, 2:])
    south = 0.5 * (middle + cond_all[1:-1, :-2])
    diagonal = DAMPING * middle + east + west + north + south
    potential = RELAX * source / diagonal
    for sweep_index in range(SWEEPS - 1):
        framed_phi = framer(potential)
        centre = framed_phi[1:-1, 1:-1]
        image = diagonal * centre - (
            east * framed_phi[2:, 1:-1]
            + west * framed_phi[:-2, 1:-1]
            + north * framed_phi[1:-1, 2:]
            + south * framed_phi[1:-1, :-2]
        )
        potential = centre + RELAX * (source - image) / diagonal
    return potential


def shards(plasma_fields, velocity, resistivity, conductance, foot_map, foot_owner, foot_row):
    velocity_f = velocity.astype(jnp.float32)
    resist_f = resistivity.astype(jnp.float32)
    current = plasma_fields
    for step_index in range(PHASES):
        padded = with_halo(lon_faces(current), (("sec", 1), ("rad", 3)), 1, False)
        current = advance(padded, velocity_f, resist_f)
    magnetic_rows = broadcast(current[5:7, 0], "sec", 0)
    base = jnp.concatenate([magnetic_rows, conductance[None]], axis=0)
    lon_count = lax.axis_size("lon")
    rad_count = lax.axis_size("rad")
    patch_lons = conductance.shape[0]
    patch_lats = conductance.shape[1]
    framed = band_faces(lon_faces(base[:, None]))[:, 0]

    def patch_framer(values):
        return band_faces(lon_faces(values[None, None]))[0, 0]

    potential = relax_plane(framed, patch_framer)
    points = foot_map.shape[1]
    record_count = foot_map.shape[0]
    owner_count = lon_count * rad_count
    capacity = 2 * record_count // owner_count
    patch_cells = patch_lons * patch_lats
    flat_patch = potential.reshape(patch_cells)
    cell_ids = jnp.arange(patch_cells, dtype=jnp.int32)

    def lookup_block(map_block):
        onehot = (map_block[:, None, :] == cell_ids[None, :, None]).astype(jnp.float32)
        return jnp.einsum(
            "c,rcp->rp",
            flat_patch,
            onehot,
            precision=lax.Precision.HIGHEST,
            preferred_element_type=jnp.float32,
        )

    records = lax.map(lookup_block, foot_map.reshape(record_count // 8, 8, points)).reshape(
        record_count, points
    )
    owners = foot_owner[:, 0]
    order_ids = jnp.arange(record_count, dtype=jnp.int32)
    before = (owners[:, None] == owners[None, :]) & (order_ids[:, None] > order_ids[None, :])
    ranks = jnp.sum(before.astype(jnp.int32), axis=1)
    slots = owners * capacity + ranks
    slot_ids = jnp.arange(owner_count * capacity, dtype=jnp.int32)
    placement = slot_ids[:, None] == slots[None, :]
    send_rows = jnp.dot(
        placement.astype(jnp.float32),
        records,
        precision=lax.Precision.HIGHEST,
        preferred_element_type=jnp.float32,
    )
    placement_int = placement.astype(jnp.int32)
    filled = jnp.sum(placement_int, axis=1)
    send_targets = jnp.dot(placement_int, foot_row) + filled - 1
    received, received_rows = (
        lax.all_to_all(
            send_rows.reshape(owner_count, capacity, points),
            ("lon", "rad"),
            split_axis=0,
            concat_axis=0,
            tiled=True,
        ),
        lax.all_to_all(
            send_targets.reshape(owner_count, capacity),
            ("lon", "rad"),
            split_axis=0,
            concat_axis=0,
            tiled=True,
        ),
    )
    received = received.reshape(-1, points)
    received_rows = received_rows.reshape(-1)
    selector = (jnp.arange(ROWS_OWN, dtype=jnp.int32)[:, None] == received_rows[None, :]).astype(
        jnp.float32
    )
    foot_table = jnp.dot(
        selector, received, precision=lax.Precision.HIGHEST, preferred_element_type=jnp.float32
    )
    return (current, potential, foot_table)


def solution(mesh):
    in_specs = (
        P(None, "sec", "lon", "rad"),
        P(None, "sec", "lon", "rad"),
        P("sec", "lon", "rad"),
        P("lon", "rad"),
        P(("lon", "sec", "rad"), None),
        P(("lon", "sec", "rad"), None),
        P(("lon", "sec", "rad")),
    )
    out_specs = (P(None, "sec", "lon", "rad"), P("lon", "rad"), P(("lon", "sec", "rad"), None))
    return jax.shard_map(shards, mesh=mesh, in_specs=in_specs, out_specs=out_specs, check_vma=False)
```

profile of v0, /device:TPU:32, one launch (start us, length us, event | category | flops | bytes accessed | tf_op | source)
XLA Modules:
  0.0 373.3 jit_solution(9063135048425477298)
XLA Ops:
  1.8 4.3 %collective-permute-start = (f32[8,16,1,128]{3,0,2,1:T(8,128)S(1)}, f32[8,16,1,128]{3,0,2,1:T(8,128)S(1)}, u32[]{:S(2)}, u32[]{:S(2)}) collective-permute-start(f32[8,16,1,128]{3,0,2,1:T(8,128)S(1)} %get-tuple-element.89), channel_id=1, source_target_pairs={{0,16},{16,32},{32,48},{48,64},{64,80},{80,96},{96,112},{112,128},... | collective-permute-start | bytes 196616 | tf_op jit(solution)/shard_map/ppermute | solution.py:24
  6.1 9.1 %collective-permute-start.1 = (f32[8,16,1,128]{3,0,2,1:T(8,128)S(1)}, f32[8,16,1,128]{3,0,2,1:T(8,128)S(1)}, u32[]{:S(2)}, u32[]{:S(2)}) collective-permute-start(f32[8,16,1,128]{3,0,2,1:T(8,128)S(1)} %get-tuple-element.90), channel_id=1, source_target_pairs={{16,0},{32,16},{48,32},{64,48},{80,64},{96,80},{112,96},{128,112},... | collective-permute-start | bytes 196616 | tf_op jit(solution)/shard_map/ppermute | solution.py:26
  17.1 1.9 collective-permute-start.2
  19.0 7.5 %collective-permute-start.3 = (f32[8,1,6,128]{3,0,2,1:T(8,128)S(1)}, f32[8,1,6,128]{3,0,2,1:T(8,128)S(1)}, u32[]{:S(2)}, u32[]{:S(2)}) collective-permute-start(f32[8,1,6,128]{3,0,2,1:T(8,128)S(1)} %get-tuple-element.82), channel_id=1, source_target_pairs={{4,0},{8,4},{12,8},{5,1},{9,5},{13,9},{6,2},{10,6},{14,10},{7,3},{... | collective-permute-start | bytes 73736 | tf_op jit(solution)/shard_map/ppermute | solution.py:26
  28.7 3.5 collective-permute-start.4
  34.4 3.9 %collective-permute-done.5 = f32[8,18,6,1]{1,0,3,2:T(8,128)S(1)} collective-permute-done((f32[8,18,6,1]{1,0,3,2:T(8,128)S(1)}, f32[8,18,6,1]{1,0,3,2:T(8,128)S(1)}, u32[]{:S(2)}, u32[]{:S(2)}) %collective-permute-start.5) | collective-permute-done | bytes 3488 | tf_op jit(solution)/shard_map/ppermute | solution.py:26
  39.1 1.9 collective-permute-start.6
  41.1 8.2 %collective-permute-start.7 = (f32[8,16,1,128]{3,0,2,1:T(8,128)S(1)}, f32[8,16,1,128]{3,0,2,1:T(8,128)S(1)}, u32[]{:S(2)}, u32[]{:S(2)}) collective-permute-start(f32[8,16,1,128]{3,0,2,1:T(8,128)S(1)} %get-tuple-element.88), channel_id=1, source_target_pairs={{16,0},{32,16},{48,32},{64,48},{80,64},{96,80},{112,96},{128,112},... | collective-permute-start | bytes 196616 | tf_op jit(solution)/shard_map/ppermute | solution.py:26
  53.1 7.5 %collective-permute-start.9 = (f32[8,1,6,128]{3,0,2,1:T(8,128)S(1)}, f32[8,1,6,128]{3,0,2,1:T(8,128)S(1)}, u32[]{:S(2)}, u32[]{:S(2)}) collective-permute-start(f32[8,1,6,128]{3,0,2,1:T(8,128)S(1)} %get-tuple-element.80), channel_id=1, source_target_pairs={{4,0},{8,4},{12,8},{5,1},{9,5},{13,9},{6,2},{10,6},{14,10},{7,3},{... | collective-permute-start | bytes 73736 | tf_op jit(solution)/shard_map/ppermute | solution.py:26
  62.7 3.4 collective-permute-start.10
  68.2 4.0 %collective-permute-done.11 = f32[8,18,6,1]{1,0,3,2:T(8,128)S(1)} collective-permute-done((f32[8,18,6,1]{1,0,3,2:T(8,128)S(1)}, f32[8,18,6,1]{1,0,3,2:T(8,128)S(1)}, u32[]{:S(2)}, u32[]{:S(2)}) %collective-permute-start.11) | collective-permute-done | bytes 3488 | tf_op jit(solution)/shard_map/ppermute | solution.py:26
  73.0 1.9 collective-permute-start.12
  75.0 8.2 %collective-permute-start.13 = (f32[8,16,1,128]{3,0,2,1:T(8,128)S(1)}, f32[8,16,1,128]{3,0,2,1:T(8,128)S(1)}, u32[]{:S(2)}, u32[]{:S(2)}) collective-permute-start(f32[8,16,1,128]{3,0,2,1:T(8,128)S(1)} %get-tuple-element.86), channel_id=1, source_target_pairs={{16,0},{32,16},{48,32},{64,48},{80,64},{96,80},{112,96},{128,112},... | collective-permute-start | bytes 196616 | tf_op jit(solution)/shard_map/ppermute | solution.py:26
  86.9 7.5 %collective-permute-start.15 = (f32[8,1,6,128]{3,0,2,1:T(8,128)S(1)}, f32[8,1,6,128]{3,0,2,1:T(8,128)S(1)}, u32[]{:S(2)}, u32[]{:S(2)}) collective-permute-start(f32[8,1,6,128]{3,0,2,1:T(8,128)S(1)} %get-tuple-element.78), channel_id=1, source_target_pairs={{4,0},{8,4},{12,8},{5,1},{9,5},{13,9},{6,2},{10,6},{14,10},{7,3},{... | collective-permute-start | bytes 73736 | tf_op jit(solution)/shard_map/ppermute | solution.py:26
  96.6 3.1 collective-permute-start.16
  101.8 4.0 %collective-permute-done.17 = f32[8,18,6,1]{1,0,3,2:T(8,128)S(1)} collective-permute-done((f32[8,18,6,1]{1,0,3,2:T(8,128)S(1)}, f32[8,18,6,1]{1,0,3,2:T(8,128)S(1)}, u32[]{:S(2)}, u32[]{:S(2)}) %collective-permute-start.17) | collective-permute-done | bytes 3488 | tf_op jit(solution)/shard_map/ppermute | solution.py:26
  106.6 1.9 collective-permute-start.18
  108.5 8.2 %collective-permute-start.19 = (f32[8,16,1,128]{3,0,2,1:T(8,128)S(1)}, f32[8,16,1,128]{3,0,2,1:T(8,128)S(1)}, u32[]{:S(2)}, u32[]{:S(2)}) collective-permute-start(f32[8,16,1,128]{3,0,2,1:T(8,128)S(1)} %get-tuple-element.84), channel_id=1, source_target_pairs={{16,0},{32,16},{48,32},{64,48},{80,64},{96,80},{112,96},{128,112},... | collective-permute-start | bytes 196616 | tf_op jit(solution)/shard_map/ppermute | solution.py:26
  120.5 7.5 %collective-permute-start.21 = (f32[8,1,6,128]{3,0,2,1:T(8,128)S(1)}, f32[8,1,6,128]{3,0,2,1:T(8,128)S(1)}, u32[]{:S(2)}, u32[]{:S(2)}) collective-permute-start(f32[8,1,6,128]{3,0,2,1:T(8,128)S(1)} %get-tuple-element.76), channel_id=1, source_target_pairs={{4,0},{8,4},{12,8},{5,1},{9,5},{13,9},{6,2},{10,6},{14,10},{7,3},{... | collective-permute-start | bytes 73736 | tf_op jit(solution)/shard_map/ppermute | solution.py:26
  134.2 4.0 %collective-permute-done.23 = f32[8,18,6,1]{1,0,3,2:T(8,128)S(1)} collective-permute-done((f32[8,18,6,1]{1,0,3,2:T(8,128)S(1)}, f32[8,18,6,1]{1,0,3,2:T(8,128)S(1)}, u32[]{:S(2)}, u32[]{:S(2)}) %collective-permute-start.23) | collective-permute-done | bytes 3488 | tf_op jit(solution)/shard_map/ppermute | solution.py:26
  139.1 13.8 %psum.7 = f32[2,4,128]{2,1,0:T(4,128)S(1)} all-reduce(f32[2,4,128]{2,1,0:T(4,128)S(1)} %bitcast.80), channel_id=1, replica_groups=mesh['lon'=32,'sec'=4,'rad'=4] {'sec'}, use_global_device_ids=true, to_apply=%region_0.1 | all-reduce | flops 1024 | bytes 8192 | tf_op jit(solution)/shard_map/psum | solution.py:35
  152.9 1.9 collective-permute-start.24
  154.8 8.2 %collective-permute-start.25 = (f32[3,1,1,128]{3,2,0,1:T(1,128)S(1)}, f32[3,1,1,128]{3,2,0,1:T(1,128)S(1)}, u32[]{:S(2)}, u32[]{:S(2)}) collective-permute-start(f32[3,1,1,128]{3,2,0,1:T(1,128)S(1)} %get-tuple-element.102), channel_id=1, source_target_pairs={{16,0},{32,16},{48,32},{64,48},{80,64},{96,80},{112,96},{128,112},... | collective-permute-start | bytes 4616 | tf_op jit(solution)/shard_map/ppermute | solution.py:26
  164.3 2.2 collective-permute-start.26
  167.9 4.2 %collective-permute-done.27 = f32[3,1,6,1]{3,2,0,1:T(8,128)S(1)} collective-permute-done((f32[3,1,6,1]{3,2,0,1:T(8,128)S(1)}, f32[3,1,6,1]{3,2,0,1:T(8,128)S(1)}, u32[]{:S(2)}, u32[]{:S(2)}) %collective-permute-start.27) | collective-permute-done | bytes 104 | tf_op jit(solution)/shard_map/ppermute | solution.py:26
  172.4 1.9 collective-permute-start.28
  174.4 8.1 %collective-permute-start.29 = (f32[1,1,1,128]{3,2,1,0:T(1,128)S(1)}, f32[1,1,1,128]{3,2,1,0:T(1,128)S(1)}, u32[]{:S(2)}, u32[]{:S(2)}) collective-permute-start(f32[1,1,1,128]{3,2,1,0:T(1,128)S(1)} %get-tuple-element.130), channel_id=1, source_target_pairs={{16,0},{32,16},{48,32},{64,48},{80,64},{96,80},{112,96},{128,112},... | collective-permute-start | bytes 1544 | tf_op jit(solution)/shard_map/ppermute | solution.py:26
  187.0 4.2 %collective-permute-done.31 = f32[1,1,6,1]{3,2,1,0:T(8,128)S(1)} collective-permute-done((f32[1,1,6,1]{3,2,1,0:T(8,128)S(1)}, f32[1,1,6,1]{3,2,1,0:T(8,128)S(1)}, u32[]{:S(2)}, u32[]{:S(2)}) %collective-permute-start.31) | collective-permute-done | bytes 56 | tf_op jit(solution)/shard_map/ppermute | solution.py:26
  191.4 1.9 collective-permute-start.32
  193.3 8.1 %collective-permute-start.33 = (f32[1,1,1,128]{3,2,1,0:T(1,128)S(1)}, f32[1,1,1,128]{3,2,1,0:T(1,128)S(1)}, u32[]{:S(2)}, u32[]{:S(2)}) collective-permute-start(f32[1,1,1,128]{3,2,1,0:T(1,128)S(1)} %get-tuple-element.128), channel_id=1, source_target_pairs={{16,0},{32,16},{48,32},{64,48},{80,64},{96,80},{112,96},{128,112},... | collective-permute-start | bytes 1544 | tf_op jit(solution)/shard_map/ppermute | solution.py:26
  206.0 4.2 %collective-permute-done.35 = f32[1,1,6,1]{3,2,1,0:T(8,128)S(1)} collective-permute-done((f32[1,1,6,1]{3,2,1,0:T(8,128)S(1)}, f32[1,1,6,1]{3,2,1,0:T(8,128)S(1)}, u32[]{:S(2)}, u32[]{:S(2)}) %collective-permute-start.35) | collective-permute-done | bytes 56 | tf_op jit(solution)/shard_map/ppermute | solution.py:26
  212.3 8.1 %collective-permute-start.37 = (f32[1,1,1,128]{3,2,1,0:T(1,128)S(1)}, f32[1,1,1,128]{3,2,1,0:T(1,128)S(1)}, u32[]{:S(2)}, u32[]{:S(2)}) collective-permute-start(f32[1,1,1,128]{3,2,1,0:T(1,128)S(1)} %get-tuple-element.126), channel_id=1, source_target_pairs={{16,0},{32,16},{48,32},{64,48},{80,64},{96,80},{112,96},{128,112},... | collective-permute-start | bytes 1544 | tf_op jit(solution)/shard_map/ppermute | solution.py:26
  224.9 4.2 %collective-permute-done.39 = f32[1,1,6,1]{3,2,1,0:T(8,128)S(1)} collective-permute-done((f32[1,1,6,1]{3,2,1,0:T(8,128)S(1)}, f32[1,1,6,1]{3,2,1,0:T(8,128)S(1)}, u32[]{:S(2)}, u32[]{:S(2)}) %collective-permute-start.39) | collective-permute-done | bytes 56 | tf_op jit(solution)/shard_map/ppermute | solution.py:26
  231.2 8.1 %collective-permute-start.41 = (f32[1,1,1,128]{3,2,1,0:T(1,128)S(1)}, f32[1,1,1,128]{3,2,1,0:T(1,128)S(1)}, u32[]{:S(2)}, u32[]{:S(2)}) collective-permute-start(f32[1,1,1,128]{3,2,1,0:T(1,128)S(1)} %get-tuple-element.124), channel_id=1, source_target_pairs={{16,0},{32,16},{48,32},{64,48},{80,64},{96,80},{112,96},{128,112},... | collective-permute-start | bytes 1544 | tf_op jit(solution)/shard_map/ppermute | solution.py:26
  243.9 4.2 %collective-permute-done.43 = f32[1,1,6,1]{3,2,1,0:T(8,128)S(1)} collective-permute-done((f32[1,1,6,1]{3,2,1,0:T(8,128)S(1)}, f32[1,1,6,1]{3,2,1,0:T(8,128)S(1)}, u32[]{:S(2)}, u32[]{:S(2)}) %collective-permute-start.43) | collective-permute-done | bytes 56 | tf_op jit(solution)/shard_map/ppermute | solution.py:26
  250.2 8.1 %collective-permute-start.45 = (f32[1,1,1,128]{3,2,1,0:T(1,128)S(1)}, f32[1,1,1,128]{3,2,1,0:T(1,128)S(1)}, u32[]{:S(2)}, u32[]{:S(2)}) collective-permute-start(f32[1,1,1,128]{3,2,1,0:T(1,128)S(1)} %get-tuple-element.122), channel_id=1, source_target_pairs={{16,0},{32,16},{48,32},{64,48},{80,64},{96,80},{112,96},{128,112},... | collective-permute-start | bytes 1544 | tf_op jit(solution)/shard_map/ppermute | solution.py:26
  262.8 4.2 %collective-permute-done.47 = f32[1,1,6,1]{3,2,1,0:T(8,128)S(1)} collective-permute-done((f32[1,1,6,1]{3,2,1,0:T(8,128)S(1)}, f32[1,1,6,1]{3,2,1,0:T(8,128)S(1)}, u32[]{:S(2)}, u32[]{:S(2)}) %collective-permute-start.47) | collective-permute-done | bytes 56 | tf_op jit(solution)/shard_map/ppermute | solution.py:26
  269.1 8.1 %collective-permute-start.49 = (f32[1,1,1,128]{3,2,1,0:T(1,128)S(1)}, f32[1,1,1,128]{3,2,1,0:T(1,128)S(1)}, u32[]{:S(2)}, u32[]{:S(2)}) collective-permute-start(f32[1,1,1,128]{3,2,1,0:T(1,128)S(1)} %get-tuple-element.120), channel_id=1, source_target_pairs={{16,0},{32,16},{48,32},{64,48},{80,64},{96,80},{112,96},{128,112},... | collective-permute-start | bytes 1544 | tf_op jit(solution)/shard_map/ppermute | solution.py:26
  278.0 6.3 %all-to-all-start = ((s32[128,1,2]{2,1,0:T(1,128)}), s32[128,1,2]{2,1,0:T(1,128)S(1)}, u32[]{:S(2)}, u32[]{:S(2)}) async-start(s32[128,1,2]{2,1,0:T(1,128)} %bitcast.30), calls=%async_computation | async-start | bytes 131072 | tf_op jit(solution)/shard_map/all_to_all | solution.py:160
  284.4 2.9 collective-permute-start.50
  288.6 4.2 %collective-permute-done.51 = f32[1,1,6,1]{3,2,1,0:T(8,128)S(1)} collective-permute-done((f32[1,1,6,1]{3,2,1,0:T(8,128)S(1)}, f32[1,1,6,1]{3,2,1,0:T(8,128)S(1)}, u32[]{:S(2)}, u32[]{:S(2)}) %collective-permute-start.51) | collective-permute-done | bytes 56 | tf_op jit(solution)/shard_map/ppermute | solution.py:26
  293.0 3.4 collective-permute-start.52
  296.4 6.6 %collective-permute-start.53 = (f32[1,1,1,128]{3,2,1,0:T(1,128)S(1)}, f32[1,1,1,128]{3,2,1,0:T(1,128)S(1)}, u32[]{:S(2)}, u32[]{:S(2)}) collective-permute-start(f32[1,1,1,128]{3,2,1,0:T(1,128)S(1)} %get-tuple-element.118), channel_id=1, source_target_pairs={{16,0},{32,16},{48,32},{64,48},{80,64},{96,80},{112,96},{128,112},... | collective-permute-start | bytes 1544 | tf_op jit(solution)/shard_map/ppermute | solution.py:26
  304.4 3.4 collective-permute-start.54
  309.1 4.2 %collective-permute-done.55 = f32[1,1,6,1]{3,2,1,0:T(8,128)S(1)} collective-permute-done((f32[1,1,6,1]{3,2,1,0:T(8,128)S(1)}, f32[1,1,6,1]{3,2,1,0:T(8,128)S(1)}, u32[]{:S(2)}, u32[]{:S(2)}) %collective-permute-start.55) | collective-permute-done | bytes 56 | tf_op jit(solution)/shard_map/ppermute | solution.py:26
  313.5 33.5 %while.11 = (s32[]{:T(128)}, f32[16,8,256]{2,1,0:T(8,128)S(1)}, s32[16,8,256]{2,1,0:T(8,128)}, f32[512]{0:T(512)S(1)}, s32[]{:T(128)}) while((s32[]{:T(128)}, f32[16,8,256]{2,1,0:T(8,128)S(1)}, s32[16,8,256]{2,1,0:T(8,128)}, f32[512]{0:T(512)S(1)}, s32[]{:T(128)}) %tuple.72), condition=%wide.region_4.5_spmd.clone, body=%wide.region_3.4_spmd.clone.sunk | while | flops 13631490 | bytes 51269 | solution.py:133
  348.2 10.8 %all-to-all-start.1 = ((f32[128,2,256]{2,1,0:T(2,128)}), f32[128,2,256]{2,1,0:T(2,128)S(1)}, u32[]{:S(2)}, u32[]{:S(2)}) async-start(f32[128,2,256]{2,1,0:T(2,128)} %copy.180), calls=%async_computation.1 | async-start | bytes 524288 | tf_op jit(solution)/shard_map/all_to_all | solution.py:153
  361.2 11.1 %all-to-all-done.1 = f32[128,2,256]{2,1,0:T(2,128)S(1)} async-done(((f32[128,2,256]{2,1,0:T(2,128)}), f32[128,2,256]{2,1,0:T(2,128)S(1)}, u32[]{:S(2)}, u32[]{:S(2)}) %all-to-all-start.1) | async-done | bytes 262176 | tf_op jit(solution)/shard_map/all_to_all | solution.py:153
  (237 shorter events, 113.6 us)
Async XLA Ops:
  1.8 13.5 %collective-permute-start = (f32[8,16,1,128]{3,0,2,1:T(8,128)S(1)}, f32[8,16,1,128]{3,0,2,1:T(8,128)S(1)}, u32[]{:S(2)}, u32[]{:S(2)}) collective-permute-start(f32[8,16,1,128]{3,0,2,1:T(8,128)S(1)} %get-tuple-element.89), channel_id=1, source_target_pairs={{0,16},{16,32},{32,48},{48,64},{64,80},{80,96},{96,112},{112,128},... | collective-permute-start | bytes 196616 | tf_op jit(solution)/shard_map/ppermute | solution.py:24
  6.1 11.0 %collective-permute-start.1 = (f32[8,16,1,128]{3,0,2,1:T(8,128)S(1)}, f32[8,16,1,128]{3,0,2,1:T(8,128)S(1)}, u32[]{:S(2)}, u32[]{:S(2)}) collective-permute-start(f32[8,16,1,128]{3,0,2,1:T(8,128)S(1)} %get-tuple-element.90), channel_id=1, source_target_pairs={{16,0},{32,16},{48,32},{64,48},{80,64},{96,80},{112,96},{128,112},... | collective-permute-start | bytes 196616 | tf_op jit(solution)/shard_map/ppermute | solution.py:26
  17.1 9.5 %collective-permute-start.2 = (f32[8,1,6,128]{3,0,2,1:T(8,128)S(1)}, f32[8,1,6,128]{3,0,2,1:T(8,128)S(1)}, u32[]{:S(2)}, u32[]{:S(2)}) collective-permute-start(f32[8,1,6,128]{3,0,2,1:T(8,128)S(1)} %get-tuple-element.81), channel_id=1, source_target_pairs={{0,4},{4,8},{8,12},{1,5},{5,9},{9,13},{2,6},{6,10},{10,14},{3,7},{... | collective-permute-start | bytes 73736 | tf_op jit(solution)/shard_map/ppermute | solution.py:24
  19.0 9.1 %collective-permute-start.3 = (f32[8,1,6,128]{3,0,2,1:T(8,128)S(1)}, f32[8,1,6,128]{3,0,2,1:T(8,128)S(1)}, u32[]{:S(2)}, u32[]{:S(2)}) collective-permute-start(f32[8,1,6,128]{3,0,2,1:T(8,128)S(1)} %get-tuple-element.82), channel_id=1, source_target_pairs={{4,0},{8,4},{12,8},{5,1},{9,5},{13,9},{6,2},{10,6},{14,10},{7,3},{... | collective-permute-start | bytes 73736 | tf_op jit(solution)/shard_map/ppermute | solution.py:26
  28.7 5.3 %collective-permute-start.4 = (f32[8,18,6,1]{1,0,3,2:T(8,128)S(1)}, f32[8,18,6,1]{1,0,3,2:T(8,128)S(1)}, u32[]{:S(2)}, u32[]{:S(2)}) collective-permute-start(f32[8,18,6,1]{1,0,3,2:T(8,128)S(1)} %copy.157), channel_id=1, source_target_pairs={{0,1},{1,2},{2,3},{4,5},{5,6},{6,7},{8,9},{9,10},{10,11},{12,13},{... | collective-permute-start | bytes 10376 | tf_op jit(solution)/shard_map/ppermute | solution.py:24
  32.6 5.7 %collective-permute-start.5 = (f32[8,18,6,1]{1,0,3,2:T(8,128)S(1)}, f32[8,18,6,1]{1,0,3,2:T(8,128)S(1)}, u32[]{:S(2)}, u32[]{:S(2)}) collective-permute-start(f32[8,18,6,1]{1,0,3,2:T(8,128)S(1)} %copy.160), channel_id=1, source_target_pairs={{1,0},{2,1},{3,2},{5,4},{6,5},{7,6},{9,8},{10,9},{11,10},{13,12},{... | collective-permute-start | bytes 10376 | tf_op jit(solution)/shard_map/ppermute | solution.py:26
  39.1 10.4 %collective-permute-start.6 = (f32[8,16,1,128]{3,0,2,1:T(8,128)S(1)}, f32[8,16,1,128]{3,0,2,1:T(8,128)S(1)}, u32[]{:S(2)}, u32[]{:S(2)}) collective-permute-start(f32[8,16,1,128]{3,0,2,1:T(8,128)S(1)} %get-tuple-element.87), channel_id=1, source_target_pairs={{0,16},{16,32},{32,48},{48,64},{64,80},{80,96},{96,112},{112,128},... | collective-permute-start | bytes 196616 | tf_op jit(solution)/shard_map/ppermute | solution.py:24
  41.1 10.1 %collective-permute-start.7 = (f32[8,16,1,128]{3,0,2,1:T(8,128)S(1)}, f32[8,16,1,128]{3,0,2,1:T(8,128)S(1)}, u32[]{:S(2)}, u32[]{:S(2)}) collective-permute-start(f32[8,16,1,128]{3,0,2,1:T(8,128)S(1)} %get-tuple-element.88), channel_id=1, source_target_pairs={{16,0},{32,16},{48,32},{64,48},{80,64},{96,80},{112,96},{128,112},... | collective-permute-start | bytes 196616 | tf_op jit(solution)/shard_map/ppermute | solution.py:26
  51.1 9.5 %collective-permute-start.8 = (f32[8,1,6,128]{3,0,2,1:T(8,128)S(1)}, f32[8,1,6,128]{3,0,2,1:T(8,128)S(1)}, u32[]{:S(2)}, u32[]{:S(2)}) collective-permute-start(f32[8,1,6,128]{3,0,2,1:T(8,128)S(1)} %get-tuple-element.79), channel_id=1, source_target_pairs={{0,4},{4,8},{8,12},{1,5},{5,9},{9,13},{2,6},{6,10},{10,14},{3,7},{... | collective-permute-start | bytes 73736 | tf_op jit(solution)/shard_map/ppermute | solution.py:24
  53.1 9.1 %collective-permute-start.9 = (f32[8,1,6,128]{3,0,2,1:T(8,128)S(1)}, f32[8,1,6,128]{3,0,2,1:T(8,128)S(1)}, u32[]{:S(2)}, u32[]{:S(2)}) collective-permute-start(f32[8,1,6,128]{3,0,2,1:T(8,128)S(1)} %get-tuple-element.80), channel_id=1, source_target_pairs={{4,0},{8,4},{12,8},{5,1},{9,5},{13,9},{6,2},{10,6},{14,10},{7,3},{... | collective-permute-start | bytes 73736 | tf_op jit(solution)/shard_map/ppermute | solution.py:26
  62.7 5.1 %collective-permute-start.10 = (f32[8,18,6,1]{1,0,3,2:T(8,128)S(1)}, f32[8,18,6,1]{1,0,3,2:T(8,128)S(1)}, u32[]{:S(2)}, u32[]{:S(2)}) collective-permute-start(f32[8,18,6,1]{1,0,3,2:T(8,128)S(1)} %copy.165), channel_id=1, source_target_pairs={{0,1},{1,2},{2,3},{4,5},{5,6},{6,7},{8,9},{9,10},{10,11},{12,13},{... | collective-permute-start | bytes 10376 | tf_op jit(solution)/shard_map/ppermute | solution.py:24
  66.5 5.7 %collective-permute-start.11 = (f32[8,18,6,1]{1,0,3,2:T(8,128)S(1)}, f32[8,18,6,1]{1,0,3,2:T(8,128)S(1)}, u32[]{:S(2)}, u32[]{:S(2)}) collective-permute-start(f32[8,18,6,1]{1,0,3,2:T(8,128)S(1)} %copy.167), channel_id=1, source_target_pairs={{1,0},{2,1},{3,2},{5,4},{6,5},{7,6},{9,8},{10,9},{11,10},{13,12},{... | collective-permute-start | bytes 10376 | tf_op jit(solution)/shard_map/ppermute | solution.py:26
  73.0 10.4 %collective-permute-start.12 = (f32[8,16,1,128]{3,0,2,1:T(8,128)S(1)}, f32[8,16,1,128]{3,0,2,1:T(8,128)S(1)}, u32[]{:S(2)}, u32[]{:S(2)}) collective-permute-start(f32[8,16,1,128]{3,0,2,1:T(8,128)S(1)} %get-tuple-element.85), channel_id=1, source_target_pairs={{0,16},{16,32},{32,48},{48,64},{64,80},{80,96},{96,112},{112,128},... | collective-permute-start | bytes 196616 | tf_op jit(solution)/shard_map/ppermute | solution.py:24
  75.0 10.1 %collective-permute-start.13 = (f32[8,16,1,128]{3,0,2,1:T(8,128)S(1)}, f32[8,16,1,128]{3,0,2,1:T(8,128)S(1)}, u32[]{:S(2)}, u32[]{:S(2)}) collective-permute-start(f32[8,16,1,128]{3,0,2,1:T(8,128)S(1)} %get-tuple-element.86), channel_id=1, source_target_pairs={{16,0},{32,16},{48,32},{64,48},{80,64},{96,80},{112,96},{128,112},... | collective-permute-start | bytes 196616 | tf_op jit(solution)/shard_map/ppermute | solution.py:26
  85.0 9.5 %collective-permute-start.14 = (f32[8,1,6,128]{3,0,2,1:T(8,128)S(1)}, f32[8,1,6,128]{3,0,2,1:T(8,128)S(1)}, u32[]{:S(2)}, u32[]{:S(2)}) collective-permute-start(f32[8,1,6,128]{3,0,2,1:T(8,128)S(1)} %get-tuple-element.77), channel_id=1, source_target_pairs={{0,4},{4,8},{8,12},{1,5},{5,9},{9,13},{2,6},{6,10},{10,14},{3,7},{... | collective-permute-start | bytes 73736 | tf_op jit(solution)/shard_map/ppermute | solution.py:24
  86.9 9.1 %collective-permute-start.15 = (f32[8,1,6,128]{3,0,2,1:T(8,128)S(1)}, f32[8,1,6,128]{3,0,2,1:T(8,128)S(1)}, u32[]{:S(2)}, u32[]{:S(2)}) collective-permute-start(f32[8,1,6,128]{3,0,2,1:T(8,128)S(1)} %get-tuple-element.78), channel_id=1, source_target_pairs={{4,0},{8,4},{12,8},{5,1},{9,5},{13,9},{6,2},{10,6},{14,10},{7,3},{... | collective-permute-start | bytes 73736 | tf_op jit(solution)/shard_map/ppermute | solution.py:26
  100.1 5.7 %collective-permute-start.17 = (f32[8,18,6,1]{1,0,3,2:T(8,128)S(1)}, f32[8,18,6,1]{1,0,3,2:T(8,128)S(1)}, u32[]{:S(2)}, u32[]{:S(2)}) collective-permute-start(f32[8,18,6,1]{1,0,3,2:T(8,128)S(1)} %copy.171), channel_id=1, source_target_pairs={{1,0},{2,1},{3,2},{5,4},{6,5},{7,6},{9,8},{10,9},{11,10},{13,12},{... | collective-permute-start | bytes 10376 | tf_op jit(solution)/shard_map/ppermute | solution.py:26
  106.6 10.4 %collective-permute-start.18 = (f32[8,16,1,128]{3,0,2,1:T(8,128)S(1)}, f32[8,16,1,128]{3,0,2,1:T(8,128)S(1)}, u32[]{:S(2)}, u32[]{:S(2)}) collective-permute-start(f32[8,16,1,128]{3,0,2,1:T(8,128)S(1)} %get-tuple-element.83), channel_id=1, source_target_pairs={{0,16},{16,32},{32,48},{48,64},{64,80},{80,96},{96,112},{112,128},... | collective-permute-start | bytes 196616 | tf_op jit(solution)/shard_map/ppermute | solution.py:24
  108.5 10.1 %collective-permute-start.19 = (f32[8,16,1,128]{3,0,2,1:T(8,128)S(1)}, f32[8,16,1,128]{3,0,2,1:T(8,128)S(1)}, u32[]{:S(2)}, u32[]{:S(2)}) collective-permute-start(f32[8,16,1,128]{3,0,2,1:T(8,128)S(1)} %get-tuple-element.84), channel_id=1, source_target_pairs={{16,0},{32,16},{48,32},{64,48},{80,64},{96,80},{112,96},{128,112},... | collective-permute-start | bytes 196616 | tf_op jit(solution)/shard_map/ppermute | solution.py:26
  118.6 9.5 %collective-permute-start.20 = (f32[8,1,6,128]{3,0,2,1:T(8,128)S(1)}, f32[8,1,6,128]{3,0,2,1:T(8,128)S(1)}, u32[]{:S(2)}, u32[]{:S(2)}) collective-permute-start(f32[8,1,6,128]{3,0,2,1:T(8,128)S(1)} %get-tuple-element.75), channel_id=1, source_target_pairs={{0,4},{4,8},{8,12},{1,5},{5,9},{9,13},{2,6},{6,10},{10,14},{3,7},{... | collective-permute-start | bytes 73736 | tf_op jit(solution)/shard_map/ppermute | solution.py:24
  120.5 9.1 %collective-permute-start.21 = (f32[8,1,6,128]{3,0,2,1:T(8,128)S(1)}, f32[8,1,6,128]{3,0,2,1:T(8,128)S(1)}, u32[]{:S(2)}, u32[]{:S(2)}) collective-permute-start(f32[8,1,6,128]{3,0,2,1:T(8,128)S(1)} %get-tuple-element.76), channel_id=1, source_target_pairs={{4,0},{8,4},{12,8},{5,1},{9,5},{13,9},{6,2},{10,6},{14,10},{7,3},{... | collective-permute-start | bytes 73736 | tf_op jit(solution)/shard_map/ppermute | solution.py:26
  132.5 5.7 %collective-permute-start.23 = (f32[8,18,6,1]{1,0,3,2:T(8,128)S(1)}, f32[8,18,6,1]{1,0,3,2:T(8,128)S(1)}, u32[]{:S(2)}, u32[]{:S(2)}) collective-permute-start(f32[8,18,6,1]{1,0,3,2:T(8,128)S(1)} %copy.175), channel_id=1, source_target_pairs={{1,0},{2,1},{3,2},{5,4},{6,5},{7,6},{9,8},{10,9},{11,10},{13,12},{... | collective-permute-start | bytes 10376 | tf_op jit(solution)/shard_map/ppermute | solution.py:26
  152.9 10.1 %collective-permute-start.24 = (f32[3,1,1,128]{3,2,0,1:T(1,128)S(1)}, f32[3,1,1,128]{3,2,0,1:T(1,128)S(1)}, u32[]{:S(2)}, u32[]{:S(2)}) collective-permute-start(f32[3,1,1,128]{3,2,0,1:T(1,128)S(1)} %get-tuple-element.101), channel_id=1, source_target_pairs={{0,16},{16,32},{32,48},{48,64},{64,80},{80,96},{96,112},{112,128},... | collective-permute-start | bytes 4616 | tf_op jit(solution)/shard_map/ppermute | solution.py:24
  154.8 9.5 %collective-permute-start.25 = (f32[3,1,1,128]{3,2,0,1:T(1,128)S(1)}, f32[3,1,1,128]{3,2,0,1:T(1,128)S(1)}, u32[]{:S(2)}, u32[]{:S(2)}) collective-permute-start(f32[3,1,1,128]{3,2,0,1:T(1,128)S(1)} %get-tuple-element.102), channel_id=1, source_target_pairs={{16,0},{32,16},{48,32},{64,48},{80,64},{96,80},{112,96},{128,112},... | collective-permute-start | bytes 4616 | tf_op jit(solution)/shard_map/ppermute | solution.py:26
  166.5 5.6 %collective-permute-start.27 = (f32[3,1,6,1]{3,2,0,1:T(8,128)S(1)}, f32[3,1,6,1]{3,2,0,1:T(8,128)S(1)}, u32[]{:S(2)}, u32[]{:S(2)}) collective-permute-start(f32[3,1,6,1]{3,2,0,1:T(8,128)S(1)} %get-tuple-element.100), channel_id=1, source_target_pairs={{1,0},{2,1},{3,2},{5,4},{6,5},{7,6},{9,8},{10,9},{11,10},{13,12},{... | collective-permute-start | bytes 224 | tf_op jit(solution)/shard_map/ppermute | solution.py:26
  172.4 10.0 %collective-permute-start.28 = (f32[1,1,1,128]{3,2,1,0:T(1,128)S(1)}, f32[1,1,1,128]{3,2,1,0:T(1,128)S(1)}, u32[]{:S(2)}, u32[]{:S(2)}) collective-permute-start(f32[1,1,1,128]{3,2,1,0:T(1,128)S(1)} %get-tuple-element.129), channel_id=1, source_target_pairs={{0,16},{16,32},{32,48},{48,64},{64,80},{80,96},{96,112},{112,128},... | collective-permute-start | bytes 1544 | tf_op jit(solution)/shard_map/ppermute | solution.py:24
  174.4 9.4 %collective-permute-start.29 = (f32[1,1,1,128]{3,2,1,0:T(1,128)S(1)}, f32[1,1,1,128]{3,2,1,0:T(1,128)S(1)}, u32[]{:S(2)}, u32[]{:S(2)}) collective-permute-start(f32[1,1,1,128]{3,2,1,0:T(1,128)S(1)} %get-tuple-element.130), channel_id=1, source_target_pairs={{16,0},{32,16},{48,32},{64,48},{80,64},{96,80},{112,96},{128,112},... | collective-permute-start | bytes 1544 | tf_op jit(solution)/shard_map/ppermute | solution.py:26
  185.7 5.5 %collective-permute-start.31 = (f32[1,1,6,1]{3,2,1,0:T(8,128)S(1)}, f32[1,1,6,1]{3,2,1,0:T(8,128)S(1)}, u32[]{:S(2)}, u32[]{:S(2)}) collective-permute-start(f32[1,1,6,1]{3,2,1,0:T(8,128)S(1)} %get-tuple-element.116), channel_id=1, source_target_pairs={{1,0},{2,1},{3,2},{5,4},{6,5},{7,6},{9,8},{10,9},{11,10},{13,12},{... | collective-permute-start | bytes 80 | tf_op jit(solution)/shard_map/ppermute | solution.py:26
  191.4 10.2 %collective-permute-start.32 = (f32[1,1,1,128]{3,2,1,0:T(1,128)S(1)}, f32[1,1,1,128]{3,2,1,0:T(1,128)S(1)}, u32[]{:S(2)}, u32[]{:S(2)}) collective-permute-start(f32[1,1,1,128]{3,2,1,0:T(1,128)S(1)} %get-tuple-element.127), channel_id=1, source_target_pairs={{0,16},{16,32},{32,48},{48,64},{64,80},{80,96},{96,112},{112,128},... | collective-permute-start | bytes 1544 | tf_op jit(solution)/shard_map/ppermute | solution.py:24
  193.3 9.3 %collective-permute-start.33 = (f32[1,1,1,128]{3,2,1,0:T(1,128)S(1)}, f32[1,1,1,128]{3,2,1,0:T(1,128)S(1)}, u32[]{:S(2)}, u32[]{:S(2)}) collective-permute-start(f32[1,1,1,128]{3,2,1,0:T(1,128)S(1)} %get-tuple-element.128), channel_id=1, source_target_pairs={{16,0},{32,16},{48,32},{64,48},{80,64},{96,80},{112,96},{128,112},... | collective-permute-start | bytes 1544 | tf_op jit(solution)/shard_map/ppermute | solution.py:26
  204.7 5.5 %collective-permute-start.35 = (f32[1,1,6,1]{3,2,1,0:T(8,128)S(1)}, f32[1,1,6,1]{3,2,1,0:T(8,128)S(1)}, u32[]{:S(2)}, u32[]{:S(2)}) collective-permute-start(f32[1,1,6,1]{3,2,1,0:T(8,128)S(1)} %get-tuple-element.114), channel_id=1, source_target_pairs={{1,0},{2,1},{3,2},{5,4},{6,5},{7,6},{9,8},{10,9},{11,10},{13,12},{... | collective-permute-start | bytes 80 | tf_op jit(solution)/shard_map/ppermute | solution.py:26
  210.3 10.0 %collective-permute-start.36 = (f32[1,1,1,128]{3,2,1,0:T(1,128)S(1)}, f32[1,1,1,128]{3,2,1,0:T(1,128)S(1)}, u32[]{:S(2)}, u32[]{:S(2)}) collective-permute-start(f32[1,1,1,128]{3,2,1,0:T(1,128)S(1)} %get-tuple-element.125), channel_id=1, source_target_pairs={{0,16},{16,32},{32,48},{48,64},{64,80},{80,96},{96,112},{112,128},... | collective-permute-start | bytes 1544 | tf_op jit(solution)/shard_map/ppermute | solution.py:24
  212.3 9.3 %collective-permute-start.37 = (f32[1,1,1,128]{3,2,1,0:T(1,128)S(1)}, f32[1,1,1,128]{3,2,1,0:T(1,128)S(1)}, u32[]{:S(2)}, u32[]{:S(2)}) collective-permute-start(f32[1,1,1,128]{3,2,1,0:T(1,128)S(1)} %get-tuple-element.126), channel_id=1, source_target_pairs={{16,0},{32,16},{48,32},{64,48},{80,64},{96,80},{112,96},{128,112},... | collective-permute-start | bytes 1544 | tf_op jit(solution)/shard_map/ppermute | solution.py:26
  223.6 5.5 %collective-permute-start.39 = (f32[1,1,6,1]{3,2,1,0:T(8,128)S(1)}, f32[1,1,6,1]{3,2,1,0:T(8,128)S(1)}, u32[]{:S(2)}, u32[]{:S(2)}) collective-permute-start(f32[1,1,6,1]{3,2,1,0:T(8,128)S(1)} %get-tuple-element.112), channel_id=1, source_target_pairs={{1,0},{2,1},{3,2},{5,4},{6,5},{7,6},{9,8},{10,9},{11,10},{13,12},{... | collective-permute-start | bytes 80 | tf_op jit(solution)/shard_map/ppermute | solution.py:26
  229.3 10.2 %collective-permute-start.40 = (f32[1,1,1,128]{3,2,1,0:T(1,128)S(1)}, f32[1,1,1,128]{3,2,1,0:T(1,128)S(1)}, u32[]{:S(2)}, u32[]{:S(2)}) collective-permute-start(f32[1,1,1,128]{3,2,1,0:T(1,128)S(1)} %get-tuple-element.123), channel_id=1, source_target_pairs={{0,16},{16,32},{32,48},{48,64},{64,80},{80,96},{96,112},{112,128},... | collective-permute-start | bytes 1544 | tf_op jit(solution)/shard_map/ppermute | solution.py:24
  231.2 9.3 %collective-permute-start.41 = (f32[1,1,1,128]{3,2,1,0:T(1,128)S(1)}, f32[1,1,1,128]{3,2,1,0:T(1,128)S(1)}, u32[]{:S(2)}, u32[]{:S(2)}) collective-permute-start(f32[1,1,1,128]{3,2,1,0:T(1,128)S(1)} %get-tuple-element.124), channel_id=1, source_target_pairs={{16,0},{32,16},{48,32},{64,48},{80,64},{96,80},{112,96},{128,112},... | collective-permute-start | bytes 1544 | tf_op jit(solution)/shard_map/ppermute | solution.py:26
  242.6 5.5 %collective-permute-start.43 = (f32[1,1,6,1]{3,2,1,0:T(8,128)S(1)}, f32[1,1,6,1]{3,2,1,0:T(8,128)S(1)}, u32[]{:S(2)}, u32[]{:S(2)}) collective-permute-start(f32[1,1,6,1]{3,2,1,0:T(8,128)S(1)} %get-tuple-element.110), channel_id=1, source_target_pairs={{1,0},{2,1},{3,2},{5,4},{6,5},{7,6},{9,8},{10,9},{11,10},{13,12},{... | collective-permute-start | bytes 80 | tf_op jit(solution)/shard_map/ppermute | solution.py:26
  248.2 10.1 %collective-permute-start.44 = (f32[1,1,1,128]{3,2,1,0:T(1,128)S(1)}, f32[1,1,1,128]{3,2,1,0:T(1,128)S(1)}, u32[]{:S(2)}, u32[]{:S(2)}) collective-permute-start(f32[1,1,1,128]{3,2,1,0:T(1,128)S(1)} %get-tuple-element.121), channel_id=1, source_target_pairs={{0,16},{16,32},{32,48},{48,64},{64,80},{80,96},{96,112},{112,128},... | collective-permute-start | bytes 1544 | tf_op jit(solution)/shard_map/ppermute | solution.py:24
  250.2 9.3 %collective-permute-start.45 = (f32[1,1,1,128]{3,2,1,0:T(1,128)S(1)}, f32[1,1,1,128]{3,2,1,0:T(1,128)S(1)}, u32[]{:S(2)}, u32[]{:S(2)}) collective-permute-start(f32[1,1,1,128]{3,2,1,0:T(1,128)S(1)} %get-tuple-element.122), channel_id=1, source_target_pairs={{16,0},{32,16},{48,32},{64,48},{80,64},{96,80},{112,96},{128,112},... | collective-permute-start | bytes 1544 | tf_op jit(solution)/shard_map/ppermute | solution.py:26
  261.5 5.5 %collective-permute-start.47 = (f32[1,1,6,1]{3,2,1,0:T(8,128)S(1)}, f32[1,1,6,1]{3,2,1,0:T(8,128)S(1)}, u32[]{:S(2)}, u32[]{:S(2)}) collective-permute-start(f32[1,1,6,1]{3,2,1,0:T(8,128)S(1)} %get-tuple-element.108), channel_id=1, source_target_pairs={{1,0},{2,1},{3,2},{5,4},{6,5},{7,6},{9,8},{10,9},{11,10},{13,12},{... | collective-permute-start | bytes 80 | tf_op jit(solution)/shard_map/ppermute | solution.py:26
  267.2 17.1 %collective-permute-start.48 = (f32[1,1,1,128]{3,2,1,0:T(1,128)S(1)}, f32[1,1,1,128]{3,2,1,0:T(1,128)S(1)}, u32[]{:S(2)}, u32[]{:S(2)}) collective-permute-start(f32[1,1,1,128]{3,2,1,0:T(1,128)S(1)} %get-tuple-element.119), channel_id=1, source_target_pairs={{0,16},{16,32},{32,48},{48,64},{64,80},{80,96},{96,112},{112,128},... | collective-permute-start | bytes 1544 | tf_op jit(solution)/shard_map/ppermute | solution.py:24
  269.1 15.2 %collective-permute-start.49 = (f32[1,1,1,128]{3,2,1,0:T(1,128)S(1)}, f32[1,1,1,128]{3,2,1,0:T(1,128)S(1)}, u32[]{:S(2)}, u32[]{:S(2)}) collective-permute-start(f32[1,1,1,128]{3,2,1,0:T(1,128)S(1)} %get-tuple-element.120), channel_id=1, source_target_pairs={{16,0},{32,16},{48,32},{64,48},{80,64},{96,80},{112,96},{128,112},... | collective-permute-start | bytes 1544 | tf_op jit(solution)/shard_map/ppermute | solution.py:26
  278.0 70.2 %all-to-all-start = ((s32[128,1,2]{2,1,0:T(1,128)}), s32[128,1,2]{2,1,0:T(1,128)S(1)}, u32[]{:S(2)}, u32[]{:S(2)}) async-start(s32[128,1,2]{2,1,0:T(1,128)} %bitcast.30), calls=%async_computation | async-start | bytes 131072 | tf_op jit(solution)/shard_map/all_to_all | solution.py:160
  287.3 5.5 %collective-permute-start.51 = (f32[1,1,6,1]{3,2,1,0:T(8,128)S(1)}, f32[1,1,6,1]{3,2,1,0:T(8,128)S(1)}, u32[]{:S(2)}, u32[]{:S(2)}) collective-permute-start(f32[1,1,6,1]{3,2,1,0:T(8,128)S(1)} %get-tuple-element.106), channel_id=1, source_target_pairs={{1,0},{2,1},{3,2},{5,4},{6,5},{7,6},{9,8},{10,9},{11,10},{13,12},{... | collective-permute-start | bytes 80 | tf_op jit(solution)/shard_map/ppermute | solution.py:26
  293.0 10.1 %collective-permute-start.52 = (f32[1,1,1,128]{3,2,1,0:T(1,128)S(1)}, f32[1,1,1,128]{3,2,1,0:T(1,128)S(1)}, u32[]{:S(2)}, u32[]{:S(2)}) collective-permute-start(f32[1,1,1,128]{3,2,1,0:T(1,128)S(1)} %get-tuple-element.117), channel_id=1, source_target_pairs={{0,16},{16,32},{32,48},{48,64},{64,80},{80,96},{96,112},{112,128},... | collective-permute-start | bytes 1544 | tf_op jit(solution)/shard_map/ppermute | solution.py:24
  296.4 7.9 %collective-permute-start.53 = (f32[1,1,1,128]{3,2,1,0:T(1,128)S(1)}, f32[1,1,1,128]{3,2,1,0:T(1,128)S(1)}, u32[]{:S(2)}, u32[]{:S(2)}) collective-permute-start(f32[1,1,1,128]{3,2,1,0:T(1,128)S(1)} %get-tuple-element.118), channel_id=1, source_target_pairs={{16,0},{32,16},{48,32},{64,48},{80,64},{96,80},{112,96},{128,112},... | collective-permute-start | bytes 1544 | tf_op jit(solution)/shard_map/ppermute | solution.py:26
  307.8 5.5 %collective-permute-start.55 = (f32[1,1,6,1]{3,2,1,0:T(8,128)S(1)}, f32[1,1,6,1]{3,2,1,0:T(8,128)S(1)}, u32[]{:S(2)}, u32[]{:S(2)}) collective-permute-start(f32[1,1,6,1]{3,2,1,0:T(8,128)S(1)} %get-tuple-element.104), channel_id=1, source_target_pairs={{1,0},{2,1},{3,2},{5,4},{6,5},{7,6},{9,8},{10,9},{11,10},{13,12},{... | collective-permute-start | bytes 80 | tf_op jit(solution)/shard_map/ppermute | solution.py:26
  348.2 24.1 %all-to-all-start.1 = ((f32[128,2,256]{2,1,0:T(2,128)}), f32[128,2,256]{2,1,0:T(2,128)S(1)}, u32[]{:S(2)}, u32[]{:S(2)}) async-start(f32[128,2,256]{2,1,0:T(2,128)} %copy.180), calls=%async_computation.1 | async-start | bytes 524288 | tf_op jit(solution)/shard_map/all_to_all | solution.py:153
  (17 other events, 394.3 us)
where the time goes:
time: 376 us; the launch traced here: 373 us
  starting transfers between devices  224 us (60%)
  waiting for transfers between devices  82.4 us (22%)
  local copies, waits for them, and re-layouts  23.9 us (6%)
  matrix products  23.4 us (6%)
  blocking collectives  13.8 us (4%)
  other arithmetic  4.18 us (1%)
    ppermute x28, starting transfers between devices, with_halo(): lax.ppermute(head, axis, [((i + 1) % count, i) for i in range(ends)])  142 us
    ppermute x28, waiting for transfers between devices, with_halo(): lax.ppermute(head, axis, [((i + 1) % count, i) for i in range(ends)])  70.1 us
    ppermute x28, starting transfers between devices, with_halo(): lax.ppermute(tail, axis, [(i, (i + 1) % count) for i in range(ends)])  64.5 us
    dot_general x16, matrix products, lookup_block(): jnp.einsum('c,rcp->rp', flat_patch, onehot, precision=lax.Precision.HIGHE...  22.1 us
    psum x1, blocking collectives, broadcast(): return lax.psum(kept, axis)  13.8 us
    eq x16, local copies, waits for them, and re-layouts, lookup_block(): map_block[:, None, :] == cell_ids[None, :, None]  11.3 us
    all_to_all x1, waiting for transfers between devices, shards(): lax.all_to_all(send_rows.reshape(owner_count, capacity, points), ('lon',...  11.1 us
    all_to_all x1, starting transfers between devices, shards(): lax.all_to_all(send_rows.reshape(owner_count, capacity, points), ('lon',...  10.8 us
  transfers between devices with their start and end apart: 58, of which 33 were waited for; matrix products, arithmetic and copies ran while one was open for 11% of the time, Pallas kernels for 0%

commit v1 on v0

v1 whole, which is shorter than its diff:
```python
import jax
import jax.numpy as jnp
from jax import lax
from jax.experimental import pallas as pl
from jax.experimental.pallas import tpu as pltpu
from jax.sharding import PartitionSpec as P

PHASES = 4
SWEEPS = 8
ROWS_OWN = 32
COURANT = 0.25
DAMPING = 0.05
RELAX = 0.8

FIELDS = 8
PLANES = FIELDS + 4
SHELLS = 16
LONS = 4
LATS = 128
WIDE = 3 * LONS
TALL = SHELLS + 2 * PHASES
F32 = jnp.float32


def call(body, out_shape, args, scratch=(), smem=(), flops=10**6, traffic=10**6):
    specs = [
        pl.BlockSpec(memory_space=pltpu.SMEM if i in smem else pltpu.VMEM)
        for i in range(len(args))
    ]
    many = isinstance(out_shape, (tuple, list))
    vmem = pl.BlockSpec(memory_space=pltpu.VMEM)
    return pl.pallas_call(
        body,
        out_shape=out_shape,
        in_specs=specs,
        out_specs=[vmem] * len(out_shape) if many else vmem,
        scratch_shapes=list(scratch),
        compiler_params=pltpu.CompilerParams(vmem_limit_bytes=40 * 2**20),
        cost_estimate=pl.CostEstimate(flops=flops, bytes_accessed=traffic, transcendentals=0),
    )(*args)


def arr(*shape):
    return jax.ShapeDtypeStruct(shape, F32)


def shift(axis, step, closed):
    count = lax.axis_size(axis)
    return [
        (i, (i + step) % count) for i in range(count) if closed or 0 <= i + step < count
    ]


def stage_body(fields, speeds, out):
    for plane in range(PLANES):
        for lon in range(LONS):
            rows = pl.ds(lon, SHELLS, stride=LONS)
            if plane < FIELDS:
                out[plane, lon] = fields[plane, rows, :]
            else:
                out[plane, lon] = speeds[plane - FIELDS, rows, :]


def edge_body(low, own, high, out):
    group = lax.broadcasted_iota(jnp.int32, (SHELLS, LATS), 1) // 8
    for plane in range(PLANES):
        packed = jnp.zeros((SHELLS, LATS), F32)
        for wide in range(1, WIDE - 1):
            ref = (low, own, high)[wide // LONS]
            turned = pltpu.roll(ref[plane, wide % LONS], 8 * wide + 4, axis=1)
            packed = jnp.where(group == wide, turned, packed)
        out[plane] = packed


def halo_lanes(edges, wide):
    lane = lax.broadcasted_iota(jnp.int32, edges.shape, 1)
    turned = pltpu.roll(edges, (LATS - 8 * wide - 4) % LATS, axis=1)
    return jnp.where((lane < 4) | (lane >= LATS - 4), turned, 0.0)


def weights(speeds, resist):
    out = []
    total = None
    for speed in speeds:
        lower = COURANT * jnp.maximum(speed, 0.0) + resist
        upper = resist - COURANT * jnp.minimum(speed, 0.0)
        out += [lower, upper]
        total = lower + upper if total is None else total + lower + upper
    return [1.0 - total] + out


def blend(w, centre, shell_lo, shell_hi, lon_lo, lon_hi, lat_lo, lat_hi):
    return (
        w[0] * centre
        + (w[1] * shell_lo + w[2] * shell_hi)
        + (w[3] * lon_lo + w[4] * lon_hi)
        + (w[5] * lat_lo + w[6] * lat_hi)
    )


def inner_body(spot, low, own, high, from_low, from_high, conductance, out, rows):
    lane = lax.broadcasted_iota(jnp.int32, (8, LATS), 1)
    bottom = lax.broadcasted_iota(jnp.int32, (8, 2 * LATS), 0) == 0

    def plane_of(plane):
        edges = jnp.where(lane % 8 < 4, from_low[plane, :8, :], from_high[plane, :8, :])
        made = []
        for wide in range(WIDE):
            ref = (low, own, high)[wide // LONS]
            if 0 < wide < WIDE - 1:
                tail = halo_lanes(edges, wide)
            else:
                tail = jnp.zeros((8, LATS), F32)
            made.append(jnp.concatenate([ref[plane, wide % LONS, :8, :], tail], axis=1))
        return made

    speeds = [plane_of(FIELDS + d) for d in range(4)]
    w = [None] + [
        weights([speeds[d][wide] for d in range(3)], speeds[3][wide])
        for wide in range(1, WIDE - 1)
    ]
    for part in range(2):
        cells = plane_of(5 + part)
        for phase in range(PHASES):
            fresh = list(cells)
            for wide in range(phase + 1, WIDE - 1 - phase):
                c = cells[wide]
                fresh[wide] = blend(
                    w[wide],
                    c,
                    jnp.where(bottom, 0.0, pltpu.roll(c, 1, axis=0)),
                    pltpu.roll(c, 7, axis=0),
                    cells[wide - 1],
                    cells[wide + 1],
                    pltpu.roll(c, 1, axis=1),
                    pltpu.roll(c, 2 * LATS - 1, axis=1),
                )
            cells = fresh
        for lon in range(LONS):
            row = part * LONS + lon
            rows[row : row + 1, :] = cells[LONS + lon][0:1, :LATS]
    rows[8:12, :] = conductance[...]
    rows[12:16, :] = jnp.zeros((4, LATS), F32)
    mine = rows[...]
    for rad in range(4):
        kept = jnp.where((spot[0] == 0) & (spot[1] == rad), mine, 0.0)
        out[rad * 12 : rad * 12 + 12, :] = kept[:12]


def chunks():
    found = []
    at = 0
    for wide in range(1, WIDE - 1):
        far = max(LONS - wide, wide - 2 * LONS + 1, 0)
        count = PHASES - far
        found.append((wide, at, count))
        at += count
    return found, at


def pack_body(low, own, high, from_low, from_high, up, down):
    found, at = chunks()
    lane = lax.broadcasted_iota(jnp.int32, (8, LATS), 1)
    for plane in range(PLANES):
        for wide, start, count in found:
            ref = (low, own, high)[wide // LONS]
            up[plane, start : start + count, :] = ref[plane, wide % LONS, SHELLS - count :, :]
            down[plane, start : start + count, :] = ref[plane, wide % LONS, :count, :]
        first = jnp.where(lane % 8 < 4, from_low[plane, :8, :], from_high[plane, :8, :])
        last = jnp.where(lane % 8 < 4, from_low[plane, 8:, :], from_high[plane, 8:, :])
        up[plane, at : at + 4, :] = last[4:]
        down[plane, at : at + 4, :] = first[:4]


def main_body(low, own, high, from_low, from_high, above, below, out, cells, w, speeds, edges):
    found, at = chunks()
    lane = lax.broadcasted_iota(jnp.int32, (SHELLS, LATS), 1)

    def fill(plane, target):
        edges[:SHELLS, :] = jnp.where(lane % 8 < 4, from_low[plane], from_high[plane])
        edges[SHELLS : SHELLS + 4, :] = above[plane, at : at + 4, :]
        edges[SHELLS + 4 :, :] = below[plane, at : at + 4, :]
        strip = edges[...]
        for wide in range(WIDE):
            ref = (low, own, high)[wide // LONS]
            target[wide, :SHELLS, :LATS] = ref[plane, wide % LONS]
            target[wide, SHELLS:, :LATS] = jnp.zeros((8, LATS), F32)
            if 0 < wide < WIDE - 1:
                target[wide, :, LATS:] = halo_lanes(strip, wide)
            else:
                target[wide, :, LATS:] = jnp.zeros((TALL, LATS), F32)
        for wide, start, count in found:
            target[wide, SHELLS : SHELLS + count, :LATS] = above[plane, start : start + count, :]
            target[wide, TALL - count :, :LATS] = below[plane, start : start + count, :]

    for d in range(4):
        fill(FIELDS + d, speeds.at[d])
    for wide in range(1, WIDE - 1):
        made = weights([speeds[d, wide] for d in range(3)], speeds[3, wide])
        for i in range(7):
            w[i, wide] = made[i]

    def one(field, carry):
        fill(field, cells.at[0])
        for phase in range(PHASES):
            old = cells.at[phase % 2]
            new = cells.at[(phase + 1) % 2]
            for wide in range(phase + 1, WIDE - 1 - phase):
                c = old[wide]
                made = blend(
                    [w[i, wide] for i in range(7)],
                    c,
                    pltpu.roll(c, 1, axis=0),
                    pltpu.roll(c, TALL - 1, axis=0),
                    old[wide - 1],
                    old[wide + 1],
                    pltpu.roll(c, 1, axis=1),
                    pltpu.roll(c, 2 * LATS - 1, axis=1),
                )
                if phase == PHASES - 1:
                    out[field, pl.ds(wide - LONS, SHELLS, stride=LONS), :] = made[:SHELLS, :LATS]
                else:
                    new[wide] = made
        return carry

    lax.fori_loop(0, FIELDS, one, 0)


def slot_body(owners, rows, maps, out):
    count = owners.shape[1]
    here = lax.broadcasted_iota(jnp.int32, (count, count), 0)
    there = lax.broadcasted_iota(jnp.int32, (count, count), 1)
    aimed = here == owners[...]
    earlier = jnp.dot(
        aimed.astype(jnp.bfloat16), (here < there).astype(jnp.bfloat16), preferred_element_type=F32
    )
    cell = maps[...]
    small = (cell & 127).astype(F32).astype(jnp.bfloat16)
    large = (cell >> 7).astype(F32).astype(jnp.bfloat16)
    row = (rows[...] + 1).astype(F32)
    marks = []
    for slot in range(2):
        chosen = jnp.where(aimed & (earlier == float(slot)), 1.0, 0.0)
        marks.append(jnp.sum(chosen * row, axis=1, keepdims=True) - 1.0)
        pick = chosen.astype(jnp.bfloat16)
        made = jnp.dot(pick, small, preferred_element_type=F32) + 128.0 * jnp.dot(
            pick, large, preferred_element_type=F32
        )
        for half in range(2):
            out[pl.ds(2 * slot + half, count, stride=8), :] = made[:, 128 * half : 128 * half + 128]
    out[pl.ds(4, count, stride=8), :] = jnp.where(there < 64, marks[0], marks[1])
    for spare in range(5, 8):
        out[pl.ds(spare, count, stride=8), :] = jnp.zeros((count, count), F32)


def final_body(spot, planes, maps, pot, foot, phi, east_w, west_w, north_w, south_w, start, picked, hot):
    devs, rads = 32, 4
    wide = rads * LATS
    lane = lax.broadcasted_iota(jnp.int32, (devs, wide), 1)

    def gather(part):
        return [
            jnp.concatenate(
                [
                    planes[pl.ds(rad * 12 + part * LONS + lon, devs, stride=48), :]
                    for rad in range(rads)
                ],
                axis=1,
            )
            for lon in range(LONS)
        ]

    def lon_up(values, lon):
        return values[lon + 1] if lon < LONS - 1 else pltpu.roll(values[0], devs - 1, axis=0)

    def lon_down(values, lon):
        return values[lon - 1] if lon > 0 else pltpu.roll(values[LONS - 1], 1, axis=0)

    def lat_up(value):
        return pltpu.roll(value, wide - 1, axis=1)

    def lat_down(value):
        return pltpu.roll(value, 1, axis=1)

    blon, blat, cond = gather(0), gather(1), gather(2)
    last, first = lane == wide - 1, lane == 0
    for lon in range(LONS):
        source = (
            lon_up(blat, lon)
            - lon_down(blat, lon)
            - (
                jnp.where(last, 0.0, lat_up(blon[lon]))
                - jnp.where(first, 0.0, lat_down(blon[lon]))
            )
        )
        c = cond[lon]
        east = 0.5 * (c + lon_up(cond, lon))
        west = 0.5 * (c + lon_down(cond, lon))
        north = 0.5 * (c + jnp.where(last, 0.0, lat_up(c)))
        south = 0.5 * (c + jnp.where(first, 0.0, lat_down(c)))
        scale = RELAX / (DAMPING * c + east + west + north + south)
        east_w[lon] = east * scale
        west_w[lon] = west * scale
        north_w[lon] = jnp.where(last, 0.0, north * scale)
        south_w[lon] = jnp.where(first, 0.0, south * scale)
        start[lon] = source * scale
        phi[0, lon] = source * scale

    def sweep(old, new):
        values = [phi[old, lon] for lon in range(LONS)]
        for lon in range(LONS):
            c = values[lon]
            phi[new, lon] = (
                (1.0 - RELAX) * c
                + start[lon]
                + (east_w[lon] * lon_up(values, lon) + west_w[lon] * lon_down(values, lon))
                + (north_w[lon] * lat_up(c) + south_w[lon] * lat_down(c))
            )

    for turn in range(SWEEPS - 1):
        sweep(turn % 2, (turn + 1) % 2)
    done = (SWEEPS - 1) % 2
    at_lon = lax.broadcasted_iota(jnp.int32, (devs, LATS), 0) == spot[2]
    for rad in range(rads):

        @pl.when(spot[1] == rad)
        def _():
            for lon in range(LONS):
                block = phi[done, lon, :, rad * LATS : (rad + 1) * LATS]
                pot[lon : lon + 1, :] = jnp.sum(
                    jnp.where(at_lon, block, 0.0), axis=0, keepdims=True
                )

    slot_lane = lax.broadcasted_iota(jnp.int32, (devs, LATS), 1).astype(F32)
    for rad in range(rads):
        table = [phi[done, lon, :, rad * LATS : (rad + 1) * LATS] for lon in range(LONS)]
        marks = maps[pl.ds(rad * 8 + 4, devs, stride=32), :]
        for slot in range(2):
            at = (slot * rads + rad) * devs
            row = marks if slot == 0 else pltpu.roll(marks, 64, axis=1)
            hot[at : at + devs, :] = jnp.where(row == slot_lane, 1.0, 0.0)
            for half in range(2):
                cell = maps[pl.ds(rad * 8 + 2 * slot + half, devs, stride=32), :].astype(jnp.int32)
                place, lon_at = cell & 127, cell >> 7
                value = jnp.zeros((devs, LATS), F32)
                for lon in range(LONS):
                    found = jnp.take_along_axis(
                        table[lon], place, axis=1, mode="promise_in_bounds"
                    )
                    value = jnp.where(lon_at == lon, found, value)
                picked[at : at + devs, 128 * half : 128 * half + 128] = value
    summed = lax.dot_general(
        hot[...],
        picked[...],
        (((0,), (0,)), ((), ())),
        precision=lax.Precision.HIGHEST,
        preferred_element_type=F32,
    )
    foot[...] = summed[:ROWS_OWN]


def shards(plasma_fields, velocity, resistivity, conductance, foot_map, foot_owner, foot_row):
    spot = jnp.stack([lax.axis_index("sec"), lax.axis_index("rad"), lax.axis_index("lon")])
    speeds = (
        jnp.concatenate([velocity, resistivity[None]], axis=0)
        .astype(F32)
        .reshape(4, SHELLS * LONS, LATS)
    )
    own = call(
        stage_body,
        arr(PLANES, LONS, SHELLS, LATS),
        (plasma_fields.reshape(FIELDS, SHELLS * LONS, LATS), speeds),
    )
    low = lax.ppermute(own, "lon", shift("lon", 1, True))
    high = lax.ppermute(own, "lon", shift("lon", -1, True))

    slots = call(
        slot_body,
        arr(128 * 8, 128),
        (foot_owner.reshape(1, -1), foot_row.reshape(1, -1), foot_map),
    )
    maps = lax.all_to_all(
        slots.reshape(128, 8, 128), ("lon", "rad"), split_axis=0, concat_axis=0, tiled=True
    )

    edges = call(edge_body, arr(PLANES, SHELLS, LATS), (low, own, high))
    from_low = lax.ppermute(edges, "rad", shift("rad", 1, False))
    from_high = lax.ppermute(edges, "rad", shift("rad", -1, False))
    blocks = (low, own, high, from_low, from_high)

    inner = call(
        inner_body,
        arr(48, LATS),
        (spot,) + blocks + (conductance,),
        scratch=(pltpu.VMEM((16, LATS), F32),),
        smem=(0,),
    )
    inner = lax.psum(inner, ("sec", "rad"))
    planes = lax.all_to_all(
        jnp.broadcast_to(inner[None], (32, 48, LATS)),
        "lon",
        split_axis=0,
        concat_axis=0,
        tiled=True,
    )

    up, down = call(pack_body, (arr(PLANES, 32, LATS), arr(PLANES, 32, LATS)), blocks)
    below = lax.ppermute(up, "sec", shift("sec", 1, False))
    above = lax.ppermute(down, "sec", shift("sec", -1, False))
    advanced = call(
        main_body,
        arr(FIELDS, SHELLS * LONS, LATS),
        blocks + (above, below),
        scratch=(
            pltpu.VMEM((2, WIDE, TALL, 2 * LATS), F32),
            pltpu.VMEM((7, WIDE, TALL, 2 * LATS), F32),
            pltpu.VMEM((4, WIDE, TALL, 2 * LATS), F32),
            pltpu.VMEM((TALL, LATS), F32),
        ),
    ).reshape(FIELDS, SHELLS, LONS, LATS)

    plane = pltpu.VMEM((LONS, 32, 4 * LATS), F32)
    potential, foot_table = call(
        final_body,
        (arr(LONS, LATS), arr(ROWS_OWN, 256)),
        (spot, planes.reshape(32 * 48, LATS), maps.reshape(128 * 8, 128)),
        scratch=(
            pltpu.VMEM((2, LONS, 32, 4 * LATS), F32),
            plane,
            plane,
            plane,
            plane,
            plane,
            pltpu.VMEM((256, 256), F32),
            pltpu.VMEM((256, 128), F32),
        ),
        smem=(0,),
    )
    return (advanced, potential, foot_table)


def solution(mesh):
    in_specs = (
        P(None, "sec", "lon", "rad"),
        P(None, "sec", "lon", "rad"),
        P("sec", "lon", "rad"),
        P("lon", "rad"),
        P(("lon", "sec", "rad"), None),
        P(("lon", "sec", "rad"), None),
        P(("lon", "sec", "rad")),
    )
    out_specs = (P(None, "sec", "lon", "rad"), P("lon", "rad"), P(("lon", "sec", "rad"), None))
    return jax.shard_map(shards, mesh=mesh, in_specs=in_specs, out_specs=out_specs, check_vma=False)
```

time: 376 us -> 174 us (0.46)
  the two profiles are of different devices: /device:TPU:32 before, /device:TPU:25 now
where the time goes in v1:
time: 174 us
  blocking collectives  78 us (45%)
  starting transfers between devices  54.3 us (31%)
  waiting for transfers between devices  26 us (15%)
  Pallas kernels  11.9 us (7%)
  local copies, waits for them, and re-layouts  2.53 us (1%)
    psum x1, blocking collectives, shards(): inner = lax.psum(inner, ('sec', 'rad'))  78 us
    all_to_all x1, starting transfers between devices, shards(): lax.all_to_all(slots.reshape(128, 8, 128), ('lon', 'rad'), split_axis=0,...  17.5 us
    ppermute x1, waiting for transfers between devices, shards(): low = lax.ppermute(own, 'lon', shift('lon', 1, True))  13.8 us
    ppermute x1, starting transfers between devices, shards(): above = lax.ppermute(down, 'sec', shift('sec', -1, False))  12.6 us
    pallas_call x7, Pallas kernels, call(): pl.pallas_call(body, out_shape=out_shape, in_specs=specs, out_specs=[vmem...  11.9 us
    ppermute x1, waiting for transfers between devices, shards(): above = lax.ppermute(down, 'sec', shift('sec', -1, False))  8.22 us
    all_to_all x1, starting transfers between devices, shards(): lax.all_to_all(jnp.broadcast_to(inner[None], (32, 48, LATS)), 'lon', spli...  8.1 us
    ppermute x1, starting transfers between devices, shards(): below = lax.ppermute(up, 'sec', shift('sec', 1, False))  4.37 us
  transfers between devices with their start and end apart: 8, of which 4 were waited for; matrix products, arithmetic and copies ran while one was open for 0% of the time, Pallas kernels for 4%

profile of v1, /device:TPU:25, one launch (start us, length us, event | category | flops | bytes accessed | tf_op | source)
XLA Modules:
  0.0 173.7 jit_solution(14605265040560941656)
XLA Ops:
  0.6 0.0 copy-start.3
  0.6 0.0 copy-start.4
  0.7 0.6 copy-done.3
  1.3 0.0 copy-done.4
  1.3 0.0 copy-start.1
  1.3 0.9 copy-done.1
  2.2 1.1 shard_map.99
  3.4 0.0 copy-start.5
  3.4 0.0 copy-start.6
  3.4 0.0 copy-start
  3.4 17.5 %all-to-all-start.1 = ((f32[128,8,128]{2,1,0:T(8,128)}), f32[128,8,128]{2,1,0:T(8,128)S(1)}, u32[]{:S(2)}, u32[]{:S(2)}) async-start(f32[128,8,128]{2,1,0:T(8,128)} %bitcast.10), calls=%async_computation.1 | async-start | bytes 1048576 | tf_op jit(solution)/shard_map/all_to_all | solution.py:382
  20.9 0.0 copy-done.5
  20.9 0.0 copy-done.6
  20.9 0.0 copy-done
  20.9 3.1 %collective-permute-start = (f32[12,4,16,128]{3,2,1,0:T(8,128)S(1)}, f32[12,4,16,128]{3,2,1,0:T(8,128)S(1)}, u32[]{:S(2)}, u32[]{:S(2)}) collective-permute-start(f32[12,4,16,128]{3,2,1,0:T(8,128)S(1)} %shard_map.94.own), channel_id=1, source_target_pairs={{0,16},{16,32},{32,48},{48,64},{64,80},{80,96},{96,112},{112,128},... | collective-permute-start | bytes 1179656 | tf_op jit(solution)/shard_map/ppermute | solution.py:374
  24.1 4.3 %collective-permute-start.1 = (f32[12,4,16,128]{3,2,1,0:T(8,128)S(1)}, f32[12,4,16,128]{3,2,1,0:T(8,128)S(1)}, u32[]{:S(2)}, u32[]{:S(2)}) collective-permute-start(f32[12,4,16,128]{3,2,1,0:T(8,128)S(1)} %shard_map.94.own), channel_id=1, source_target_pairs={{0,496},{16,0},{32,16},{48,32},{64,48},{80,64},{96,80},{112,96},{1... | collective-permute-start | bytes 1179656 | tf_op jit(solution)/shard_map/ppermute | solution.py:375
  28.4 13.8 %collective-permute-done.low = f32[12,4,16,128]{3,2,1,0:T(8,128)S(1)} collective-permute-done((f32[12,4,16,128]{3,2,1,0:T(8,128)S(1)}, f32[12,4,16,128]{3,2,1,0:T(8,128)S(1)}, u32[]{:S(2)}, u32[]{:S(2)}) %collective-permute-start) | collective-permute-done | bytes 393248 | tf_op jit(solution)/shard_map/ppermute | solution.py:374
  42.2 0.0 collective-permute-done.1.high
  42.2 0.3 shard_map.95
  42.5 3.1 %collective-permute-start.2 = (f32[12,16,128]{2,1,0:T(8,128)S(1)}, f32[12,16,128]{2,1,0:T(8,128)S(1)}, u32[]{:S(2)}, u32[]{:S(2)}) collective-permute-start(f32[12,16,128]{2,1,0:T(8,128)S(1)} %shard_map.95), channel_id=1, source_target_pairs={{0,1},{1,2},{2,3},{4,5},{5,6},{6,7},{8,9},{9,10},{10,11},{12,13},{... | collective-permute-start | bytes 294920 | tf_op jit(solution)/shard_map/ppermute | solution.py:387
  45.6 1.3 collective-permute-start.3
  46.9 0.0 copy-start.2
  46.9 0.1 pad_add_fusion.spot
  47.0 0.2 collective-permute-done.2.from_low
  47.2 3.7 %collective-permute-done.3.from_high = f32[12,16,128]{2,1,0:T(8,128)S(1)} collective-permute-done((f32[12,16,128]{2,1,0:T(8,128)S(1)}, f32[12,16,128]{2,1,0:T(8,128)S(1)}, u32[]{:S(2)}, u32[]{:S(2)}) %collective-permute-start.3) | collective-permute-done | bytes 98336 | tf_op jit(solution)/shard_map/ppermute | solution.py:388
  51.0 0.0 copy-done.2
  51.0 1.1 shard_map.98
  52.1 78.0 %psum.7 = f32[48,128]{1,0:T(8,128)S(1)} all-reduce(f32[48,128]{1,0:T(8,128)S(1)} %shard_map.98), channel_id=1, replica_groups=mesh['lon'=32,'sec'=4,'rad'=4] {'sec','rad'}, use_global_device_ids=true, to_apply=%region_0.0 | all-reduce | flops 6144 | bytes 49152 | tf_op jit(solution)/shard_map/psum | solution.py:398
  130.1 0.0 all-to-all-done.1
  130.1 1.0 broadcast_in_dim.2
  131.1 8.1 %all-to-all-start = ((f32[32,48,128]{2,1,0:T(8,128)}), f32[32,48,128]{2,1,0:T(8,128)S(1)}, u32[]{:S(2)}, u32[]{:S(2)}) async-start(f32[32,48,128]{2,1,0:T(8,128)} %broadcast_in_dim.2), calls=%async_computation | async-start | bytes 1572864 | tf_op jit(solution)/shard_map/all_to_all | solution.py:399
  139.2 0.1 shard_map.96
  139.3 12.6 %collective-permute-start.4 = (f32[12,32,128]{2,1,0:T(8,128)S(1)}, f32[12,32,128]{2,1,0:T(8,128)S(1)}, u32[]{:S(2)}, u32[]{:S(2)}) collective-permute-start(f32[12,32,128]{2,1,0:T(8,128)S(1)} %get-tuple-element.7), channel_id=1, source_target_pairs={{4,0},{8,4},{12,8},{5,1},{9,5},{13,9},{6,2},{10,6},{14,10},{7,3},{... | collective-permute-start | bytes 589832 | tf_op jit(solution)/shard_map/ppermute | solution.py:409
  151.9 4.4 %collective-permute-start.5 = (f32[12,32,128]{2,1,0:T(8,128)S(1)}, f32[12,32,128]{2,1,0:T(8,128)S(1)}, u32[]{:S(2)}, u32[]{:S(2)}) collective-permute-start(f32[12,32,128]{2,1,0:T(8,128)S(1)} %get-tuple-element.8), channel_id=1, source_target_pairs={{0,4},{4,8},{8,12},{1,5},{5,9},{9,13},{2,6},{6,10},{10,14},{3,7},{... | collective-permute-start | bytes 589832 | tf_op jit(solution)/shard_map/ppermute | solution.py:408
  156.2 8.2 %collective-permute-done.4.above = f32[12,32,128]{2,1,0:T(8,128)S(1)} collective-permute-done((f32[12,32,128]{2,1,0:T(8,128)S(1)}, f32[12,32,128]{2,1,0:T(8,128)S(1)}, u32[]{:S(2)}, u32[]{:S(2)}) %collective-permute-start.4) | collective-permute-done | bytes 196640 | tf_op jit(solution)/shard_map/ppermute | solution.py:409
  164.5 0.0 collective-permute-done.5.below
  164.5 5.5 %shard_map.97 = f32[8,64,128]{2,1,0:T(8,128)} custom-call(f32[12,4,16,128]{3,2,1,0:T(8,128)S(1)} %collective-permute-done.low, f32[12,4,16,128]{3,2,1,0:T(8,128)S(1)} %shard_map.94.own, f32[12,4,16,128]{3,2,1,0:T(8,128)S(1)} %collective-permute-done.1.high, f32[12,16,128]{2,1,0:T(8,128)S(1)} %collective-permute-done.2.from_low, ...), custom_call_target="tpu_custom_call" | custom-call | flops 1000000 | bytes 1000000 | tf_op jit(solution)/shard_map/pallas_call | solution.py:32
  169.9 0.0 all-to-all-done
  169.9 3.8 %shard_map.100 = (f32[4,128]{1,0:T(4,128)}, f32[32,256]{1,0:T(8,128)}) custom-call(s32[3]{0:T(128)S(1)} %pad_add_fusion.spot, f32[1536,128]{1,0:T(8,128)S(1)} %bitcast.12, f32[1024,128]{1,0:T(8,128)S(1)} %bitcast.13), custom_call_target="tpu_custom_call" | custom-call | flops 1000000 | bytes 1000000 | tf_op jit(solution)/shard_map/pallas_call | solution.py:32
  (2 shorter events, 0.0 us)
Async XLA Ops:
  0.6 0.7 copy-start.3
  0.6 0.7 copy-start.4
  1.3 0.9 copy-start.1
  3.4 17.5 %copy-start.5 = (bf16[3,16,4,128]{3,2,1,0:T(4,128)(2,1)S(1)}, bf16[3,16,4,128]{3,2,1,0:T(4,128)(2,1)}, u32[]{:S(2)}) copy-start(bf16[3,16,4,128]{3,2,1,0:T(4,128)(2,1)} %param.8) | copy-start | bytes 147460
  3.4 17.5 %copy-start.6 = (bf16[16,4,128]{2,1,0:T(4,128)(2,1)S(1)}, bf16[16,4,128]{2,1,0:T(4,128)(2,1)}, u32[]{:S(2)}) copy-start(bf16[16,4,128]{2,1,0:T(4,128)(2,1)} %param.9) | copy-start | bytes 49156
  3.4 17.5 %copy-start = (f32[8,16,4,128]{3,2,1,0:T(4,128)S(1)}, f32[8,16,4,128]{3,2,1,0:T(4,128)}, u32[]{:S(2)}) copy-start(f32[8,16,4,128]{3,2,1,0:T(4,128)} %param.7) | copy-start | bytes 786436
  3.4 126.8 %all-to-all-start.1 = ((f32[128,8,128]{2,1,0:T(8,128)}), f32[128,8,128]{2,1,0:T(8,128)S(1)}, u32[]{:S(2)}, u32[]{:S(2)}) async-start(f32[128,8,128]{2,1,0:T(8,128)} %bitcast.10), calls=%async_computation.1 | async-start | bytes 1048576 | tf_op jit(solution)/shard_map/all_to_all | solution.py:382
  20.9 21.3 %collective-permute-start = (f32[12,4,16,128]{3,2,1,0:T(8,128)S(1)}, f32[12,4,16,128]{3,2,1,0:T(8,128)S(1)}, u32[]{:S(2)}, u32[]{:S(2)}) collective-permute-start(f32[12,4,16,128]{3,2,1,0:T(8,128)S(1)} %shard_map.94.own), channel_id=1, source_target_pairs={{0,16},{16,32},{32,48},{48,64},{64,80},{80,96},{96,112},{112,128},... | collective-permute-start | bytes 1179656 | tf_op jit(solution)/shard_map/ppermute | solution.py:374
  24.1 18.1 %collective-permute-start.1 = (f32[12,4,16,128]{3,2,1,0:T(8,128)S(1)}, f32[12,4,16,128]{3,2,1,0:T(8,128)S(1)}, u32[]{:S(2)}, u32[]{:S(2)}) collective-permute-start(f32[12,4,16,128]{3,2,1,0:T(8,128)S(1)} %shard_map.94.own), channel_id=1, source_target_pairs={{0,496},{16,0},{32,16},{48,32},{64,48},{80,64},{96,80},{112,96},{1... | collective-permute-start | bytes 1179656 | tf_op jit(solution)/shard_map/ppermute | solution.py:375
  42.5 4.7 %collective-permute-start.2 = (f32[12,16,128]{2,1,0:T(8,128)S(1)}, f32[12,16,128]{2,1,0:T(8,128)S(1)}, u32[]{:S(2)}, u32[]{:S(2)}) collective-permute-start(f32[12,16,128]{2,1,0:T(8,128)S(1)} %shard_map.95), channel_id=1, source_target_pairs={{0,1},{1,2},{2,3},{4,5},{5,6},{6,7},{8,9},{9,10},{10,11},{12,13},{... | collective-permute-start | bytes 294920 | tf_op jit(solution)/shard_map/ppermute | solution.py:387
  45.6 5.4 %collective-permute-start.3 = (f32[12,16,128]{2,1,0:T(8,128)S(1)}, f32[12,16,128]{2,1,0:T(8,128)S(1)}, u32[]{:S(2)}, u32[]{:S(2)}) collective-permute-start(f32[12,16,128]{2,1,0:T(8,128)S(1)} %shard_map.95), channel_id=1, source_target_pairs={{1,0},{2,1},{3,2},{5,4},{6,5},{7,6},{9,8},{10,9},{11,10},{13,12},{... | collective-permute-start | bytes 294920 | tf_op jit(solution)/shard_map/ppermute | solution.py:388
  46.9 4.1 %copy-start.2 = (f32[4,128]{1,0:T(4,128)S(1)}, f32[4,128]{1,0:T(4,128)}, u32[]{:S(2)}) copy-start(f32[4,128]{1,0:T(4,128)} %conductance.1) | copy-start | bytes 6148
  131.1 38.9 %all-to-all-start = ((f32[32,48,128]{2,1,0:T(8,128)}), f32[32,48,128]{2,1,0:T(8,128)S(1)}, u32[]{:S(2)}, u32[]{:S(2)}) async-start(f32[32,48,128]{2,1,0:T(8,128)} %broadcast_in_dim.2), calls=%async_computation | async-start | bytes 1572864 | tf_op jit(solution)/shard_map/all_to_all | solution.py:399
  139.3 25.2 %collective-permute-start.4 = (f32[12,32,128]{2,1,0:T(8,128)S(1)}, f32[12,32,128]{2,1,0:T(8,128)S(1)}, u32[]{:S(2)}, u32[]{:S(2)}) collective-permute-start(f32[12,32,128]{2,1,0:T(8,128)S(1)} %get-tuple-element.7), channel_id=1, source_target_pairs={{4,0},{8,4},{12,8},{5,1},{9,5},{13,9},{6,2},{10,6},{14,10},{7,3},{... | collective-permute-start | bytes 589832 | tf_op jit(solution)/shard_map/ppermute | solution.py:409
  151.9 12.6 %collective-permute-start.5 = (f32[12,32,128]{2,1,0:T(8,128)S(1)}, f32[12,32,128]{2,1,0:T(8,128)S(1)}, u32[]{:S(2)}, u32[]{:S(2)}) collective-permute-start(f32[12,32,128]{2,1,0:T(8,128)S(1)} %get-tuple-element.8), channel_id=1, source_target_pairs={{0,4},{4,8},{8,12},{1,5},{5,9},{9,13},{2,6},{6,10},{10,14},{3,7},{... | collective-permute-start | bytes 589832 | tf_op jit(solution)/shard_map/ppermute | solution.py:408

commit v2 on v1

--- a/solution.py
+++ b/solution.py
@@ -18,6 +18,7 @@
 LONS = 4
 LATS = 128
 WIDE = 3 * LONS
+JOINED = 72
 TALL = SHELLS + 2 * PHASES
 F32 = jnp.float32
 
@@ -98,7 +99,7 @@
     )
 
 
-def inner_body(spot, low, own, high, from_low, from_high, conductance, out, rows):
+def inner_body(low, own, high, from_low, from_high, conductance, out, rows):
     lane = lax.broadcasted_iota(jnp.int32, (8, LATS), 1)
     bottom = lax.broadcasted_iota(jnp.int32, (8, 2 * LATS), 0) == 0
 
@@ -142,9 +143,20 @@
     rows[8:12, :] = conductance[...]
     rows[12:16, :] = jnp.zeros((4, LATS), F32)
     mine = rows[...]
+    for block in range(16):
+        out[block * 16 : block * 16 + 16, :] = mine
+
+
+def join_body(planes, maps, out):
     for rad in range(4):
-        kept = jnp.where((spot[0] == 0) & (spot[1] == rad), mine, 0.0)
-        out[rad * 12 : rad * 12 + 12, :] = kept[:12]
+        for row in range(12):
+            line = jnp.broadcast_to(planes[rad * 16 + row : rad * 16 + row + 1, :], (32, LATS))
+            out[pl.ds(rad * 12 + row, 32, stride=JOINED), :] = line
+        for row in range(5):
+            at = (rad * 5 + row) * 32
+            out[pl.ds(48 + rad * 5 + row, 32, stride=JOINED), :] = maps[at : at + 32, :]
+    for spare in range(68, JOINED):
+        out[pl.ds(spare, 32, stride=JOINED), :] = jnp.zeros((32, LATS), F32)
 
 
 def chunks():
@@ -230,7 +242,7 @@
     count = owners.shape[1]
     here = lax.broadcasted_iota(jnp.int32, (count, count), 0)
     there = lax.broadcasted_iota(jnp.int32, (count, count), 1)
-    aimed = here == owners[...]
+    aimed = (here % 32) * 4 + here // 32 == owners[...]
     earlier = jnp.dot(
         aimed.astype(jnp.bfloat16), (here < there).astype(jnp.bfloat16), preferred_element_type=F32
     )
@@ -239,6 +251,7 @@
     large = (cell >> 7).astype(F32).astype(jnp.bfloat16)
     row = (rows[...] + 1).astype(F32)
     marks = []
+    lines = []
     for slot in range(2):
         chosen = jnp.where(aimed & (earlier == float(slot)), 1.0, 0.0)
         marks.append(jnp.sum(chosen * row, axis=1, keepdims=True) - 1.0)
@@ -246,14 +259,14 @@
         made = jnp.dot(pick, small, preferred_element_type=F32) + 128.0 * jnp.dot(
             pick, large, preferred_element_type=F32
         )
-        for half in range(2):
-            out[pl.ds(2 * slot + half, count, stride=8), :] = made[:, 128 * half : 128 * half + 128]
-    out[pl.ds(4, count, stride=8), :] = jnp.where(there < 64, marks[0], marks[1])
-    for spare in range(5, 8):
-        out[pl.ds(spare, count, stride=8), :] = jnp.zeros((count, count), F32)
-
-
-def final_body(spot, planes, maps, pot, foot, phi, east_w, west_w, north_w, south_w, start, picked, hot):
+        lines += [made[:, :128], made[:, 128:]]
+    lines.append(jnp.where(there < 64, marks[0], marks[1]))
+    for rad in range(4):
+        for j in range(5):
+            out[(rad * 5 + j) * 32 : (rad * 5 + j) * 32 + 32, :] = lines[j][rad * 32 : rad * 32 + 32]
+
+
+def final_body(spot, planes, pot, foot, phi, east_w, west_w, north_w, south_w, start, picked, hot):
     devs, rads = 32, 4
     wide = rads * LATS
     lane = lax.broadcasted_iota(jnp.int32, (devs, wide), 1)
@@ -262,7 +275,7 @@
         return [
             jnp.concatenate(
                 [
-                    planes[pl.ds(rad * 12 + part * LONS + lon, devs, stride=48), :]
+                    planes[pl.ds(rad * 12 + part * LONS + lon, devs, stride=JOINED), :]
                     for rad in range(rads)
                 ],
                 axis=1,
@@ -334,13 +347,15 @@
     slot_lane = lax.broadcasted_iota(jnp.int32, (devs, LATS), 1).astype(F32)
     for rad in range(rads):
         table = [phi[done, lon, :, rad * LATS : (rad + 1) * LATS] for lon in range(LONS)]
-        marks = maps[pl.ds(rad * 8 + 4, devs, stride=32), :]
+        marks = planes[pl.ds(48 + rad * 5 + 4, devs, stride=JOINED), :]
         for slot in range(2):
             at = (slot * rads + rad) * devs
             row = marks if slot == 0 else pltpu.roll(marks, 64, axis=1)
             hot[at : at + devs, :] = jnp.where(row == slot_lane, 1.0, 0.0)
             for half in range(2):
-                cell = maps[pl.ds(rad * 8 + 2 * slot + half, devs, stride=32), :].astype(jnp.int32)
+                cell = planes[
+                    pl.ds(48 + rad * 5 + 2 * slot + half, devs, stride=JOINED), :
+                ].astype(jnp.int32)
                 place, lon_at = cell & 127, cell >> 7
                 value = jnp.zeros((devs, LATS), F32)
                 for lon in range(LONS):
@@ -376,11 +391,11 @@
 
     slots = call(
         slot_body,
-        arr(128 * 8, 128),
+        arr(4 * 160, LATS),
         (foot_owner.reshape(1, -1), foot_row.reshape(1, -1), foot_map),
     )
     maps = lax.all_to_all(
-        slots.reshape(128, 8, 128), ("lon", "rad"), split_axis=0, concat_axis=0, tiled=True
+        slots.reshape(4, 160, LATS), "rad", split_axis=0, concat_axis=0, tiled=True
     )
 
     edges = call(edge_body, arr(PLANES, SHELLS, LATS), (low, own, high))
@@ -390,18 +405,18 @@
 
     inner = call(
         inner_body,
-        arr(48, LATS),
-        (spot,) + blocks + (conductance,),
+        arr(256, LATS),
+        blocks + (conductance,),
         scratch=(pltpu.VMEM((16, LATS), F32),),
-        smem=(0,),
-    )
-    inner = lax.psum(inner, ("sec", "rad"))
+    )
+    inner = lax.all_to_all(
+        inner.reshape(16, 16, LATS), ("sec", "rad"), split_axis=0, concat_axis=0, tiled=True
+    )
+    joined = call(
+        join_body, arr(32 * JOINED, LATS), (inner.reshape(256, LATS), maps.reshape(640, LATS))
+    )
     planes = lax.all_to_all(
-        jnp.broadcast_to(inner[None], (32, 48, LATS)),
-        "lon",
-        split_axis=0,
-        concat_axis=0,
-        tiled=True,
+        joined.reshape(32, JOINED, LATS), "lon", split_axis=0, concat_axis=0, tiled=True
     )
 
     up, down = call(pack_body, (arr(PLANES, 32, LATS), arr(PLANES, 32, LATS)), blocks)
@@ -423,7 +438,7 @@
     potential, foot_table = call(
         final_body,
         (arr(LONS, LATS), arr(ROWS_OWN, 256)),
-        (spot, planes.reshape(32 * 48, LATS), maps.reshape(128 * 8, 128)),
+        (spot, planes.reshape(32 * JOINED, LATS)),
         scratch=(
             pltpu.VMEM((2, LONS, 32, 4 * LATS), F32),
             plane,

time: 174 us -> 104 us (0.60)
  the two profiles are of different devices: /device:TPU:25 before, /device:TPU:72 now
where the time goes in v2:
time: 104 us
  waiting for transfers between devices  35.2 us (34%)
  starting transfers between devices  28.8 us (28%)
  blocking collectives  22.3 us (21%)
  Pallas kernels  12.5 us (12%)
  local copies, waits for them, and re-layouts  3.16 us (3%)
    all_to_all x1, waiting for transfers between devices, shards(): lax.all_to_all(joined.reshape(32, JOINED, LATS), 'lon', split_axis=0, con...  24.6 us
    all_to_all x1, blocking collectives, shards(): lax.all_to_all(inner.reshape(16, 16, LATS), ('sec', 'rad'), split_axis=0,...  22.3 us
    pallas_call x8, Pallas kernels, call(): pl.pallas_call(body, out_shape=out_shape, in_specs=specs, out_specs=[vmem...  12.5 us
    all_to_all x1, starting transfers between devices, shards(): lax.all_to_all(joined.reshape(32, JOINED, LATS), 'lon', split_axis=0, con...  8.11 us
    ppermute x1, waiting for transfers between devices, shards(): low = lax.ppermute(own, 'lon', shift('lon', 1, True))  7.42 us
    ppermute x1, starting transfers between devices, shards(): from_low = lax.ppermute(edges, 'rad', shift('rad', 1, False))  4.55 us
    all_to_all x1, starting transfers between devices, shards(): lax.all_to_all(slots.reshape(4, 160, LATS), 'rad', split_axis=0, concat_a...  4.29 us
    ppermute x1, starting transfers between devices, shards(): low = lax.ppermute(own, 'lon', shift('lon', 1, True))  4.28 us
  transfers between devices with their start and end apart: 8, of which 5 were waited for; matrix products, arithmetic and copies ran while one was open for 0% of the time, Pallas kernels for 7%

profile of v2, /device:TPU:72, one launch (start us, length us, event | category | flops | bytes accessed | tf_op | source)
XLA Modules:
  0.0 103.6 jit_solution(13143393895152538256)
XLA Ops:
  0.6 0.8 maximum_convert_fusion.speeds
  1.5 0.0 copy-start
  1.5 0.9 copy-done
  2.4 1.9 %collective-permute-start.1 = (f32[12,4,16,128]{3,2,1,0:T(8,128)S(1)}, f32[12,4,16,128]{3,2,1,0:T(8,128)S(1)}, u32[]{:S(2)}, u32[]{:S(2)}) collective-permute-start(f32[12,4,16,128]{3,2,1,0:T(8,128)S(1)} %shard_map.94.own), channel_id=1, source_target_pairs={{0,496},{16,0},{32,16},{48,32},{64,48},{80,64},{96,80},{112,96},{1... | collective-permute-start | bytes 1179656 | tf_op jit(solution)/shard_map/ppermute | solution.py:390
  4.4 4.3 %collective-permute-start = (f32[12,4,16,128]{3,2,1,0:T(8,128)S(1)}, f32[12,4,16,128]{3,2,1,0:T(8,128)S(1)}, u32[]{:S(2)}, u32[]{:S(2)}) collective-permute-start(f32[12,4,16,128]{3,2,1,0:T(8,128)S(1)} %shard_map.94.own), channel_id=1, source_target_pairs={{0,16},{16,32},{32,48},{48,64},{64,80},{80,96},{96,112},{112,128},... | collective-permute-start | bytes 1179656 | tf_op jit(solution)/shard_map/ppermute | solution.py:389
  8.7 0.0 copy-start.1
  8.7 0.9 copy-done.1
  9.6 0.0 copy-start.3
  9.6 0.7 copy-done.3
  10.2 0.0 copy-start.4
  10.2 0.7 copy-done.4
  10.9 0.0 copy-start.2
  10.9 1.1 %shard_map.99 = f32[640,128]{1,0:T(8,128)} custom-call(s32[1,128]{1,0:T(1,128)S(1)} %bitcast.20, s32[1,128]{1,0:T(1,128)S(1)} %bitcast.21, s32[128,256]{1,0:T(8,128)S(1)} %copy-done.1), custom_call_target="tpu_custom_call" | custom-call | flops 1000000 | bytes 1000000 | tf_op jit(solution)/shard_map/pallas_call | solution.py:33
  12.0 4.3 %all-to-all-start.1 = ((f32[4,160,128]{2,1,0:T(8,128)}), f32[4,160,128]{2,1,0:T(8,128)S(1)}, u32[]{:S(2)}, u32[]{:S(2)}) async-start(f32[4,160,128]{2,1,0:T(8,128)} %bitcast.11), calls=%async_computation.1 | async-start | bytes 655360 | tf_op jit(solution)/shard_map/all_to_all | solution.py:397
  16.2 0.0 collective-permute-done.1.high
  16.3 7.4 %collective-permute-done.low = f32[12,4,16,128]{3,2,1,0:T(8,128)S(1)} collective-permute-done((f32[12,4,16,128]{3,2,1,0:T(8,128)S(1)}, f32[12,4,16,128]{3,2,1,0:T(8,128)S(1)}, u32[]{:S(2)}, u32[]{:S(2)}) %collective-permute-start) | collective-permute-done | bytes 393248 | tf_op jit(solution)/shard_map/ppermute | solution.py:389
  23.7 0.3 shard_map.95
  24.0 1.3 %collective-permute-start.3 = (f32[12,16,128]{2,1,0:T(8,128)S(1)}, f32[12,16,128]{2,1,0:T(8,128)S(1)}, u32[]{:S(2)}, u32[]{:S(2)}) collective-permute-start(f32[12,16,128]{2,1,0:T(8,128)S(1)} %shard_map.95), channel_id=1, source_target_pairs={{1,0},{2,1},{3,2},{5,4},{6,5},{7,6},{9,8},{10,9},{11,10},{13,12},{... | collective-permute-start | bytes 294920 | tf_op jit(solution)/shard_map/ppermute | solution.py:403
  25.3 4.6 %collective-permute-start.2 = (f32[12,16,128]{2,1,0:T(8,128)S(1)}, f32[12,16,128]{2,1,0:T(8,128)S(1)}, u32[]{:S(2)}, u32[]{:S(2)}) collective-permute-start(f32[12,16,128]{2,1,0:T(8,128)S(1)} %shard_map.95), channel_id=1, source_target_pairs={{0,1},{1,2},{2,3},{4,5},{5,6},{6,7},{8,9},{9,10},{10,11},{12,13},{... | collective-permute-start | bytes 294920 | tf_op jit(solution)/shard_map/ppermute | solution.py:402
  29.9 0.7 collective-permute-done.3.from_high
  30.5 1.5 %collective-permute-done.2.from_low = f32[12,16,128]{2,1,0:T(8,128)S(1)} collective-permute-done((f32[12,16,128]{2,1,0:T(8,128)S(1)}, f32[12,16,128]{2,1,0:T(8,128)S(1)}, u32[]{:S(2)}, u32[]{:S(2)}) %collective-permute-start.2) | collective-permute-done | bytes 98336 | tf_op jit(solution)/shard_map/ppermute | solution.py:402
  32.0 0.0 copy-done.2
  32.0 0.5 shard_map.98
  32.6 0.0 all-to-all-done.1
  32.6 22.3 %all_to_all.15 = f32[16,16,128]{2,1,0:T(8,128)S(1)} all-to-all(f32[16,16,128]{2,1,0:T(8,128)S(1)} %bitcast.17), channel_id=1, replica_groups=mesh['lon'=32,'sec'=4,'rad'=4] {'sec','rad'}, dimensions={0} | all-to-all | bytes 262144 | tf_op jit(solution)/shard_map/all_to_all | solution.py:412
  54.9 1.2 %shard_map.100 = f32[2304,128]{1,0:T(8,128)} custom-call(f32[256,128]{1,0:T(8,128)S(1)} %bitcast.18, f32[640,128]{1,0:T(8,128)S(1)} %bitcast.16), custom_call_target="tpu_custom_call" | custom-call | flops 1000000 | bytes 1000000 | tf_op jit(solution)/shard_map/pallas_call | solution.py:33
  56.2 8.1 %all-to-all-start.2 = ((f32[32,72,128]{2,1,0:T(8,128)}), f32[32,72,128]{2,1,0:T(8,128)S(1)}, u32[]{:S(2)}, u32[]{:S(2)}) async-start(f32[32,72,128]{2,1,0:T(8,128)} %bitcast.13), calls=%async_computation.2 | async-start | bytes 2359296 | tf_op jit(solution)/shard_map/all_to_all | solution.py:418
  64.3 0.1 shard_map.96
  64.4 1.3 %collective-permute-start.4 = (f32[12,32,128]{2,1,0:T(8,128)S(1)}, f32[12,32,128]{2,1,0:T(8,128)S(1)}, u32[]{:S(2)}, u32[]{:S(2)}) collective-permute-start(f32[12,32,128]{2,1,0:T(8,128)S(1)} %get-tuple-element.7), channel_id=1, source_target_pairs={{4,0},{8,4},{12,8},{5,1},{9,5},{13,9},{6,2},{10,6},{14,10},{7,3},{... | collective-permute-start | bytes 589832 | tf_op jit(solution)/shard_map/ppermute | solution.py:424
  65.7 3.0 %collective-permute-start.5 = (f32[12,32,128]{2,1,0:T(8,128)S(1)}, f32[12,32,128]{2,1,0:T(8,128)S(1)}, u32[]{:S(2)}, u32[]{:S(2)}) collective-permute-start(f32[12,32,128]{2,1,0:T(8,128)S(1)} %get-tuple-element.8), channel_id=1, source_target_pairs={{0,4},{4,8},{8,12},{1,5},{5,9},{9,13},{2,6},{6,10},{10,14},{3,7},{... | collective-permute-start | bytes 589832 | tf_op jit(solution)/shard_map/ppermute | solution.py:423
  68.7 0.1 pad_add_fusion.spot
  68.8 0.0 collective-permute-done.4.above
  68.8 1.0 collective-permute-done.5.below
  69.8 5.5 %shard_map.97 = f32[8,64,128]{2,1,0:T(8,128)} custom-call(f32[12,4,16,128]{3,2,1,0:T(8,128)S(1)} %collective-permute-done.low, f32[12,4,16,128]{3,2,1,0:T(8,128)S(1)} %shard_map.94.own, f32[12,4,16,128]{3,2,1,0:T(8,128)S(1)} %collective-permute-done.1.high, f32[12,16,128]{2,1,0:T(8,128)S(1)} %collective-permute-done.2.from_low, ...), custom_call_target="tpu_custom_call" | custom-call | flops 1000000 | bytes 1000000 | tf_op jit(solution)/shard_map/pallas_call | solution.py:33
  75.3 24.6 %all-to-all-done.2 = f32[32,72,128]{2,1,0:T(8,128)S(1)} async-done(((f32[32,72,128]{2,1,0:T(8,128)}), f32[32,72,128]{2,1,0:T(8,128)S(1)}, u32[]{:S(2)}, u32[]{:S(2)}) %all-to-all-start.2) | async-done | bytes 1179680 | tf_op jit(solution)/shard_map/all_to_all | solution.py:418
  99.9 3.7 %shard_map.101 = (f32[4,128]{1,0:T(4,128)}, f32[32,256]{1,0:T(8,128)}) custom-call(s32[3]{0:T(128)S(1)} %pad_add_fusion.spot, f32[2304,128]{1,0:T(8,128)S(1)} %bitcast.15), custom_call_target="tpu_custom_call" | custom-call | flops 1000000 | bytes 1000000 | tf_op jit(solution)/shard_map/pallas_call | solution.py:33
  (1 shorter events, 0.0 us)
Async XLA Ops:
  1.5 1.0 copy-start
  2.4 13.8 %collective-permute-start.1 = (f32[12,4,16,128]{3,2,1,0:T(8,128)S(1)}, f32[12,4,16,128]{3,2,1,0:T(8,128)S(1)}, u32[]{:S(2)}, u32[]{:S(2)}) collective-permute-start(f32[12,4,16,128]{3,2,1,0:T(8,128)S(1)} %shard_map.94.own), channel_id=1, source_target_pairs={{0,496},{16,0},{32,16},{48,32},{64,48},{80,64},{96,80},{112,96},{1... | collective-permute-start | bytes 1179656 | tf_op jit(solution)/shard_map/ppermute | solution.py:390
  4.4 19.3 %collective-permute-start = (f32[12,4,16,128]{3,2,1,0:T(8,128)S(1)}, f32[12,4,16,128]{3,2,1,0:T(8,128)S(1)}, u32[]{:S(2)}, u32[]{:S(2)}) collective-permute-start(f32[12,4,16,128]{3,2,1,0:T(8,128)S(1)} %shard_map.94.own), channel_id=1, source_target_pairs={{0,16},{16,32},{32,48},{48,64},{64,80},{80,96},{96,112},{112,128},... | collective-permute-start | bytes 1179656 | tf_op jit(solution)/shard_map/ppermute | solution.py:389
  8.7 0.9 copy-start.1
  9.6 0.7 copy-start.3
  10.2 0.7 copy-start.4
  10.9 21.2 %copy-start.2 = (f32[4,128]{1,0:T(4,128)S(1)}, f32[4,128]{1,0:T(4,128)}, u32[]{:S(2)}) copy-start(f32[4,128]{1,0:T(4,128)} %conductance.1) | copy-start | bytes 6148
  12.0 20.6 %all-to-all-start.1 = ((f32[4,160,128]{2,1,0:T(8,128)}), f32[4,160,128]{2,1,0:T(8,128)S(1)}, u32[]{:S(2)}, u32[]{:S(2)}) async-start(f32[4,160,128]{2,1,0:T(8,128)} %bitcast.11), calls=%async_computation.1 | async-start | bytes 655360 | tf_op jit(solution)/shard_map/all_to_all | solution.py:397
  24.0 6.5 %collective-permute-start.3 = (f32[12,16,128]{2,1,0:T(8,128)S(1)}, f32[12,16,128]{2,1,0:T(8,128)S(1)}, u32[]{:S(2)}, u32[]{:S(2)}) collective-permute-start(f32[12,16,128]{2,1,0:T(8,128)S(1)} %shard_map.95), channel_id=1, source_target_pairs={{1,0},{2,1},{3,2},{5,4},{6,5},{7,6},{9,8},{10,9},{11,10},{13,12},{... | collective-permute-start | bytes 294920 | tf_op jit(solution)/shard_map/ppermute | solution.py:403
  25.3 6.8 %collective-permute-start.2 = (f32[12,16,128]{2,1,0:T(8,128)S(1)}, f32[12,16,128]{2,1,0:T(8,128)S(1)}, u32[]{:S(2)}, u32[]{:S(2)}) collective-permute-start(f32[12,16,128]{2,1,0:T(8,128)S(1)} %shard_map.95), channel_id=1, source_target_pairs={{0,1},{1,2},{2,3},{4,5},{5,6},{6,7},{8,9},{9,10},{10,11},{12,13},{... | collective-permute-start | bytes 294920 | tf_op jit(solution)/shard_map/ppermute | solution.py:402
  56.2 43.7 %all-to-all-start.2 = ((f32[32,72,128]{2,1,0:T(8,128)}), f32[32,72,128]{2,1,0:T(8,128)S(1)}, u32[]{:S(2)}, u32[]{:S(2)}) async-start(f32[32,72,128]{2,1,0:T(8,128)} %bitcast.13), calls=%async_computation.2 | async-start | bytes 2359296 | tf_op jit(solution)/shard_map/all_to_all | solution.py:418
  64.4 4.4 %collective-permute-start.4 = (f32[12,32,128]{2,1,0:T(8,128)S(1)}, f32[12,32,128]{2,1,0:T(8,128)S(1)}, u32[]{:S(2)}, u32[]{:S(2)}) collective-permute-start(f32[12,32,128]{2,1,0:T(8,128)S(1)} %get-tuple-element.7), channel_id=1, source_target_pairs={{4,0},{8,4},{12,8},{5,1},{9,5},{13,9},{6,2},{10,6},{14,10},{7,3},{... | collective-permute-start | bytes 589832 | tf_op jit(solution)/shard_map/ppermute | solution.py:424
  65.7 4.1 %collective-permute-start.5 = (f32[12,32,128]{2,1,0:T(8,128)S(1)}, f32[12,32,128]{2,1,0:T(8,128)S(1)}, u32[]{:S(2)}, u32[]{:S(2)}) collective-permute-start(f32[12,32,128]{2,1,0:T(8,128)S(1)} %get-tuple-element.8), channel_id=1, source_target_pairs={{0,4},{4,8},{8,12},{1,5},{5,9},{9,13},{2,6},{6,10},{10,14},{3,7},{... | collective-permute-start | bytes 589832 | tf_op jit(solution)/shard_map/ppermute | solution.py:423

commit v3 on v2

--- a/solution.py
+++ b/solution.py
@@ -18,7 +18,9 @@
 LONS = 4
 LATS = 128
 WIDE = 3 * LONS
-JOINED = 72
+EARLY = 40
+LATE = 24
+SENT = 168
 TALL = SHELLS + 2 * PHASES
 F32 = jnp.float32
 
@@ -99,7 +101,7 @@
     )
 
 
-def inner_body(low, own, high, from_low, from_high, conductance, out, rows):
+def inner_body(low, own, high, from_low, from_high, out):
     lane = lax.broadcasted_iota(jnp.int32, (8, LATS), 1)
     bottom = lax.broadcasted_iota(jnp.int32, (8, 2 * LATS), 0) == 0
 
@@ -139,24 +141,42 @@
             cells = fresh
         for lon in range(LONS):
             row = part * LONS + lon
-            rows[row : row + 1, :] = cells[LONS + lon][0:1, :LATS]
-    rows[8:12, :] = conductance[...]
-    rows[12:16, :] = jnp.zeros((4, LATS), F32)
-    mine = rows[...]
-    for block in range(16):
-        out[block * 16 : block * 16 + 16, :] = mine
-
-
-def join_body(planes, maps, out):
+            out[row : row + 1, :] = cells[LONS + lon][0:1, :LATS]
+
+
+def early_body(sent, out):
     for rad in range(4):
-        for row in range(12):
-            line = jnp.broadcast_to(planes[rad * 16 + row : rad * 16 + row + 1, :], (32, LATS))
-            out[pl.ds(rad * 12 + row, 32, stride=JOINED), :] = line
         for row in range(5):
-            at = (rad * 5 + row) * 32
-            out[pl.ds(48 + rad * 5 + row, 32, stride=JOINED), :] = maps[at : at + 32, :]
-    for spare in range(68, JOINED):
-        out[pl.ds(spare, 32, stride=JOINED), :] = jnp.zeros((32, LATS), F32)
+            at = rad * SENT + row * 32
+            out[pl.ds(rad * 5 + row, 32, stride=EARLY), :] = sent[at : at + 32, :]
+        for lon in range(LONS):
+            line = sent[rad * SENT + 160 + lon : rad * SENT + 161 + lon, :]
+            out[pl.ds(20 + rad * 4 + lon, 32, stride=EARLY), :] = jnp.broadcast_to(line, (32, LATS))
+    for spare in range(36, EARLY):
+        out[pl.ds(spare, 32, stride=EARLY), :] = jnp.zeros((32, LATS), F32)
+
+
+def late_body(planes, out, block):
+    wide = 4 * LATS
+    lane = lax.broadcasted_iota(jnp.int32, (LONS, wide), 1)
+    lon = lax.broadcasted_iota(jnp.int32, (LONS, wide), 0)
+    blon = jnp.concatenate([planes[r * 8 : r * 8 + 4, :] for r in range(4)], axis=1)
+    blat = jnp.concatenate([planes[r * 8 + 4 : r * 8 + 8, :] for r in range(4)], axis=1)
+    upper = jnp.concatenate([blat[1:], blat[:1]], axis=0)
+    lower = jnp.concatenate([blat[3:], blat[:3]], axis=0)
+    north = jnp.where(lane == wide - 1, 0.0, pltpu.roll(blon, wide - 1, axis=1))
+    south = jnp.where(lane == 0, 0.0, pltpu.roll(blon, 1, axis=1))
+    source = (
+        jnp.where(lon == LONS - 1, 0.0, upper) - jnp.where(lon == 0, 0.0, lower) - (north - south)
+    )
+    for rad in range(4):
+        part = slice(rad * LATS, (rad + 1) * LATS)
+        block[rad * 4 : rad * 4 + 4, :] = source[:, part]
+        block[16 + rad : 17 + rad, :] = blat[0:1, part]
+        block[20 + rad : 21 + rad, :] = blat[3:4, part]
+    mine = block[...]
+    for owner in range(32):
+        out[owner * LATE : owner * LATE + LATE, :] = mine
 
 
 def chunks():
@@ -238,7 +258,7 @@
     lax.fori_loop(0, FIELDS, one, 0)
 
 
-def slot_body(owners, rows, maps, out):
+def slot_body(owners, rows, maps, conductance, out):
     count = owners.shape[1]
     here = lax.broadcasted_iota(jnp.int32, (count, count), 0)
     there = lax.broadcasted_iota(jnp.int32, (count, count), 1)
@@ -263,25 +283,22 @@
     lines.append(jnp.where(there < 64, marks[0], marks[1]))
     for rad in range(4):
         for j in range(5):
-            out[(rad * 5 + j) * 32 : (rad * 5 + j) * 32 + 32, :] = lines[j][rad * 32 : rad * 32 + 32]
-
-
-def final_body(spot, planes, pot, foot, phi, east_w, west_w, north_w, south_w, start, picked, hot):
+            at = rad * SENT + j * 32
+            out[at : at + 32, :] = lines[j][rad * 32 : rad * 32 + 32]
+        at = rad * SENT + 160
+        out[at : at + 4, :] = conductance[...]
+        out[at + 4 : at + 8, :] = jnp.zeros((4, LATS), F32)
+
+
+def final_body(spot, early, late, pot, foot, phi, east_w, west_w, north_w, south_w, start, picked, hot):
     devs, rads = 32, 4
     wide = rads * LATS
     lane = lax.broadcasted_iota(jnp.int32, (devs, wide), 1)
 
-    def gather(part):
-        return [
-            jnp.concatenate(
-                [
-                    planes[pl.ds(rad * 12 + part * LONS + lon, devs, stride=JOINED), :]
-                    for rad in range(rads)
-                ],
-                axis=1,
-            )
-            for lon in range(LONS)
-        ]
+    def gather(ref, at, step, stride):
+        return jnp.concatenate(
+            [ref[pl.ds(at + rad * step, devs, stride=stride), :] for rad in range(rads)], axis=1
+        )
 
     def lon_up(values, lon):
         return values[lon + 1] if lon < LONS - 1 else pltpu.roll(values[0], devs - 1, axis=0)
@@ -295,17 +312,13 @@
     def lat_down(value):
         return pltpu.roll(value, 1, axis=1)
 
-    blon, blat, cond = gather(0), gather(1), gather(2)
+    cond = [gather(early, 20 + lon, 4, EARLY) for lon in range(LONS)]
+    sources = [gather(late, lon, 4, LATE) for lon in range(LONS)]
+    sources[LONS - 1] += pltpu.roll(gather(late, 16, 1, LATE), devs - 1, axis=0)
+    sources[0] -= pltpu.roll(gather(late, 20, 1, LATE), 1, axis=0)
     last, first = lane == wide - 1, lane == 0
     for lon in range(LONS):
-        source = (
-            lon_up(blat, lon)
-            - lon_down(blat, lon)
-            - (
-                jnp.where(last, 0.0, lat_up(blon[lon]))
-                - jnp.where(first, 0.0, lat_down(blon[lon]))
-            )
-        )
+        source = sources[lon]
         c = cond[lon]
         east = 0.5 * (c + lon_up(cond, lon))
         west = 0.5 * (c + lon_down(cond, lon))
@@ -347,15 +360,13 @@
     slot_lane = lax.broadcasted_iota(jnp.int32, (devs, LATS), 1).astype(F32)
     for rad in range(rads):
         table = [phi[done, lon, :, rad * LATS : (rad + 1) * LATS] for lon in range(LONS)]
-        marks = planes[pl.ds(48 + rad * 5 + 4, devs, stride=JOINED), :]
+        marks = early[pl.ds(rad * 5 + 4, devs, stride=EARLY), :]
         for slot in range(2):
             at = (slot * rads + rad) * devs
             row = marks if slot == 0 else pltpu.roll(marks, 64, axis=1)
             hot[at : at + devs, :] = jnp.where(row == slot_lane, 1.0, 0.0)
             for half in range(2):
-                cell = planes[
-                    pl.ds(48 + rad * 5 + 2 * slot + half, devs, stride=JOINED), :
-                ].astype(jnp.int32)
+                cell = early[pl.ds(rad * 5 + 2 * slot + half, devs, stride=EARLY), :].astype(jnp.int32)
                 place, lon_at = cell & 127, cell >> 7
                 value = jnp.zeros((devs, LATS), F32)
                 for lon in range(LONS):
@@ -391,37 +402,43 @@
 
     slots = call(
         slot_body,
-        arr(4 * 160, LATS),
-        (foot_owner.reshape(1, -1), foot_row.reshape(1, -1), foot_map),
-    )
-    maps = lax.all_to_all(
-        slots.reshape(4, 160, LATS), "rad", split_axis=0, concat_axis=0, tiled=True
-    )
-
+        arr(4 * SENT, LATS),
+        (foot_owner.reshape(1, -1), foot_row.reshape(1, -1), foot_map, conductance),
+    )
+    sent = lax.all_to_all(
+        slots.reshape(4, SENT, LATS), "rad", split_axis=0, concat_axis=0, tiled=True
+    )
+
+    low, high, sent = lax.optimization_barrier((low, high, sent))
     edges = call(edge_body, arr(PLANES, SHELLS, LATS), (low, own, high))
+    early = call(early_body, arr(32 * EARLY, LATS), (sent.reshape(4 * SENT, LATS),))
+    edges, early = lax.optimization_barrier((edges, early))
+    early = lax.all_to_all(
+        early.reshape(32, EARLY, LATS), "lon", split_axis=0, concat_axis=0, tiled=True
+    )
     from_low = lax.ppermute(edges, "rad", shift("rad", 1, False))
     from_high = lax.ppermute(edges, "rad", shift("rad", -1, False))
     blocks = (low, own, high, from_low, from_high)
 
-    inner = call(
-        inner_body,
-        arr(256, LATS),
-        blocks + (conductance,),
-        scratch=(pltpu.VMEM((16, LATS), F32),),
-    )
-    inner = lax.all_to_all(
-        inner.reshape(16, 16, LATS), ("sec", "rad"), split_axis=0, concat_axis=0, tiled=True
-    )
-    joined = call(
-        join_body, arr(32 * JOINED, LATS), (inner.reshape(256, LATS), maps.reshape(640, LATS))
-    )
-    planes = lax.all_to_all(
-        joined.reshape(32, JOINED, LATS), "lon", split_axis=0, concat_axis=0, tiled=True
-    )
-
+    inner = call(inner_body, arr(8, LATS), blocks)
+    copies = [lax.ppermute(inner, "sec", [(0, sec)]) for sec in range(1, 4)]
+    inner = jnp.where(lax.axis_index("sec") == 0, inner, copies[0] + copies[1] + copies[2])
+    inner = lax.all_gather(inner, "rad")
     up, down = call(pack_body, (arr(PLANES, 32, LATS), arr(PLANES, 32, LATS)), blocks)
+
+    late = call(
+        late_body,
+        arr(32 * LATE, LATS),
+        (inner.reshape(32, LATS),),
+        scratch=(pltpu.VMEM((LATE, LATS), F32),),
+    )
+    late, early, up, down = lax.optimization_barrier((late, early, up, down))
     below = lax.ppermute(up, "sec", shift("sec", 1, False))
     above = lax.ppermute(down, "sec", shift("sec", -1, False))
+    late = lax.all_to_all(
+        late.reshape(32, LATE, LATS), "lon", split_axis=0, concat_axis=0, tiled=True
+    )
+
     advanced = call(
         main_body,
         arr(FIELDS, SHELLS * LONS, LATS),
@@ -438,7 +455,7 @@
     potential, foot_table = call(
         final_body,
         (arr(LONS, LATS), arr(ROWS_OWN, 256)),
-        (spot, planes.reshape(32 * JOINED, LATS)),
+        (spot, early.reshape(32 * EARLY, LATS), late.reshape(32 * LATE, LATS)),
         scratch=(
             pltpu.VMEM((2, LONS, 32, 4 * LATS), F32),
             plane,

time: 104 us -> 104 us (level)
  the two profiles are of different devices: /device:TPU:72 before, /device:TPU:48 now
where the time goes in v3:
time: 104 us; the launch traced here: 103 us
  starting transfers between devices  41 us (39%)
  waiting for transfers between devices  23.4 us (22%)
  blocking collectives  23.3 us (22%)
  Pallas kernels  12.2 us (12%)
  local copies, waits for them, and re-layouts  1.59 us (2%)
    pallas_call x9, Pallas kernels, call(): pl.pallas_call(body, out_shape=out_shape, in_specs=specs, out_specs=[vmem...  12.2 us
    all_gather x1, blocking collectives, shards(): inner = lax.all_gather(inner, 'rad')  12 us
    all_to_all x1, blocking collectives, shards(): lax.all_to_all(slots.reshape(4, SENT, LATS), 'rad', split_axis=0, concat_...  11.4 us
    all_to_all x1, starting transfers between devices, shards(): lax.all_to_all(late.reshape(32, LATE, LATS), 'lon', split_axis=0, concat_...  10.1 us
    ppermute x1, starting transfers between devices, shards(): high = lax.ppermute(own, 'lon', shift('lon', -1, True))  9.37 us
    ppermute x3, waiting for transfers between devices, shards(): copies = [lax.ppermute(inner, 'sec', [(0, sec)]) for sec in range(1, 4)]  7.98 us
    ppermute x1, waiting for transfers between devices, shards(): below = lax.ppermute(up, 'sec', shift('sec', 1, False))  6.31 us
    all_to_all x1, starting transfers between devices, shards(): lax.all_to_all(early.reshape(32, EARLY, LATS), 'lon', split_axis=0, conca...  6.18 us
  transfers between devices with their start and end apart: 11, of which 5 were waited for; matrix products, arithmetic and copies ran while one was open for 0% of the time, Pallas kernels for 7%

profile of v3, /device:TPU:48, one launch (start us, length us, event | category | flops | bytes accessed | tf_op | source)
XLA Modules:
  0.0 103.3 jit_solution(3667789194649609790)
XLA Ops:
  0.6 0.8 maximum_convert_fusion.speeds
  1.5 0.0 copy-start
  1.5 0.9 copy-done
  2.4 0.0 copy-start.1
  2.4 0.0 copy-start.2
  2.5 4.4 %collective-permute-start = (f32[12,4,16,128]{3,2,1,0:T(8,128)S(1)}, f32[12,4,16,128]{3,2,1,0:T(8,128)S(1)}, u32[]{:S(2)}, u32[]{:S(2)}) collective-permute-start(f32[12,4,16,128]{3,2,1,0:T(8,128)S(1)} %shard_map.94.own), channel_id=1, source_target_pairs={{0,16},{16,32},{32,48},{48,64},{64,80},{80,96},{96,112},{112,128},... | collective-permute-start | bytes 1179656 | tf_op jit(solution)/shard_map/ppermute | solution.py:400
  6.9 9.4 %collective-permute-start.1 = (f32[12,4,16,128]{3,2,1,0:T(8,128)S(1)}, f32[12,4,16,128]{3,2,1,0:T(8,128)S(1)}, u32[]{:S(2)}, u32[]{:S(2)}) collective-permute-start(f32[12,4,16,128]{3,2,1,0:T(8,128)S(1)} %shard_map.94.own), channel_id=1, source_target_pairs={{0,496},{16,0},{32,16},{48,32},{64,48},{80,64},{96,80},{112,96},{1... | collective-permute-start | bytes 1179656 | tf_op jit(solution)/shard_map/ppermute | solution.py:401
  16.3 0.0 copy-start.3
  16.3 0.0 copy-start.4
  16.3 0.0 copy-done.1
  16.3 0.0 copy-done.2
  16.3 0.6 copy-done.3
  16.9 0.0 copy-done.4
  16.9 0.3 shard_map.95
  17.3 11.4 %all_to_all.15 = f32[4,168,128]{2,1,0:T(8,128)S(1)} all-to-all(f32[4,168,128]{2,1,0:T(8,128)S(1)} %bitcast.17), channel_id=1, replica_groups=mesh['lon'=32,'sec'=4,'rad'=4] {'rad'}, dimensions={0} | all-to-all | bytes 688128 | tf_op jit(solution)/shard_map/all_to_all | solution.py:408
  28.6 0.0 collective-permute-done.low
  28.6 0.0 collective-permute-done.1.high
  28.7 1.0 shard_map.97
  29.6 0.3 shard_map.96
  29.9 6.2 %all-to-all-start.1 = ((f32[32,40,128]{2,1,0:T(8,128)}), f32[32,40,128]{2,1,0:T(8,128)S(1)}, u32[]{:S(2)}, u32[]{:S(2)}) async-start(f32[32,40,128]{2,1,0:T(8,128)} %bitcast.7), calls=%async_computation.1 | async-start | bytes 1310720 | tf_op jit(solution)/shard_map/all_to_all | solution.py:416
  36.1 2.7 %collective-permute-start.2 = (f32[12,16,128]{2,1,0:T(8,128)S(1)}, f32[12,16,128]{2,1,0:T(8,128)S(1)}, u32[]{:S(2)}, u32[]{:S(2)}) collective-permute-start(f32[12,16,128]{2,1,0:T(8,128)S(1)} %shard_map.96), channel_id=1, source_target_pairs={{0,1},{1,2},{2,3},{4,5},{5,6},{6,7},{8,9},{9,10},{10,11},{12,13},{... | collective-permute-start | bytes 294920 | tf_op jit(solution)/shard_map/ppermute | solution.py:419
  38.8 1.3 %collective-permute-start.3 = (f32[12,16,128]{2,1,0:T(8,128)S(1)}, f32[12,16,128]{2,1,0:T(8,128)S(1)}, u32[]{:S(2)}, u32[]{:S(2)}) collective-permute-start(f32[12,16,128]{2,1,0:T(8,128)S(1)} %shard_map.96), channel_id=1, source_target_pairs={{1,0},{2,1},{3,2},{5,4},{6,5},{7,6},{9,8},{10,9},{11,10},{13,12},{... | collective-permute-start | bytes 294920 | tf_op jit(solution)/shard_map/ppermute | solution.py:420
  40.1 0.9 collective-permute-done.2.from_low
  41.0 4.3 %collective-permute-done.3.from_high = f32[12,16,128]{2,1,0:T(8,128)S(1)} collective-permute-done((f32[12,16,128]{2,1,0:T(8,128)S(1)}, f32[12,16,128]{2,1,0:T(8,128)S(1)}, u32[]{:S(2)}, u32[]{:S(2)}) %collective-permute-start.3) | collective-permute-done | bytes 98336 | tf_op jit(solution)/shard_map/ppermute | solution.py:420
  45.3 0.5 shard_map.98
  45.9 0.7 collective-permute-start.6
  46.5 0.7 collective-permute-start.4
  47.2 1.3 %collective-permute-start.5 = (f32[8,128]{1,0:T(8,128)S(1)}, f32[8,128]{1,0:T(8,128)S(1)}, u32[]{:S(2)}, u32[]{:S(2)}) collective-permute-start(f32[8,128]{1,0:T(8,128)S(1)} %shard_map.98), channel_id=1, source_target_pairs={{0,8},{1,9},{2,10},{3,11},{16,24},{17,25},{18,26},{19,27},{32,40},... | collective-permute-start | bytes 12296 | tf_op jit(solution)/shard_map/ppermute | solution.py:424
  48.5 0.1 shard_map.100
  48.6 0.0 collective-permute-done.6
  48.6 0.0 collective-permute-done.4
  48.7 8.0 %collective-permute-done.5 = f32[8,128]{1,0:T(8,128)S(1)} collective-permute-done((f32[8,128]{1,0:T(8,128)S(1)}, f32[8,128]{1,0:T(8,128)S(1)}, u32[]{:S(2)}, u32[]{:S(2)}) %collective-permute-start.5) | collective-permute-done | bytes 4128 | tf_op jit(solution)/shard_map/ppermute | solution.py:424
  56.6 12.0 %all-gather.planes = f32[32,128]{1,0:T(8,128)S(1)} all-gather(f32[8,128]{1,0:T(8,128)S(1)} %add_select_fusion), channel_id=2, replica_groups=mesh['lon'=32,'sec'=4,'rad'=4] {'rad'}, dimensions={0}, use_global_device_ids=true | all-gather | bytes 20480 | tf_op jit(solution)/shard_map/all_gather | solution.py:426
  68.6 0.9 shard_map.99
  69.5 0.0 all-to-all-done.1
  69.5 10.1 %all-to-all-start.2 = ((f32[32,24,128]{2,1,0:T(8,128)}), f32[32,24,128]{2,1,0:T(8,128)S(1)}, u32[]{:S(2)}, u32[]{:S(2)}) async-start(f32[32,24,128]{2,1,0:T(8,128)} %bitcast.13), calls=%async_computation.2 | async-start | bytes 786432 | tf_op jit(solution)/shard_map/all_to_all | solution.py:438
  79.6 1.9 %collective-permute-start.7 = (f32[12,32,128]{2,1,0:T(8,128)S(1)}, f32[12,32,128]{2,1,0:T(8,128)S(1)}, u32[]{:S(2)}, u32[]{:S(2)}) collective-permute-start(f32[12,32,128]{2,1,0:T(8,128)S(1)} %get-tuple-element.23), channel_id=1, source_target_pairs={{4,0},{8,4},{12,8},{5,1},{9,5},{13,9},{6,2},{10,6},{14,10},{7,3},{... | collective-permute-start | bytes 589832 | tf_op jit(solution)/shard_map/ppermute | solution.py:437
  81.5 2.4 %collective-permute-start.8 = (f32[12,32,128]{2,1,0:T(8,128)S(1)}, f32[12,32,128]{2,1,0:T(8,128)S(1)}, u32[]{:S(2)}, u32[]{:S(2)}) collective-permute-start(f32[12,32,128]{2,1,0:T(8,128)S(1)} %get-tuple-element.24), channel_id=1, source_target_pairs={{0,4},{4,8},{8,12},{1,5},{5,9},{9,13},{2,6},{6,10},{10,14},{3,7},{... | collective-permute-start | bytes 589832 | tf_op jit(solution)/shard_map/ppermute | solution.py:436
  84.0 0.1 pad_add_fusion.spot
  84.0 3.9 %collective-permute-done.7.above = f32[12,32,128]{2,1,0:T(8,128)S(1)} collective-permute-done((f32[12,32,128]{2,1,0:T(8,128)S(1)}, f32[12,32,128]{2,1,0:T(8,128)S(1)}, u32[]{:S(2)}, u32[]{:S(2)}) %collective-permute-start.7) | collective-permute-done | bytes 196640 | tf_op jit(solution)/shard_map/ppermute | solution.py:437
  87.9 6.3 %collective-permute-done.8.below = f32[12,32,128]{2,1,0:T(8,128)S(1)} collective-permute-done((f32[12,32,128]{2,1,0:T(8,128)S(1)}, f32[12,32,128]{2,1,0:T(8,128)S(1)}, u32[]{:S(2)}, u32[]{:S(2)}) %collective-permute-start.8) | collective-permute-done | bytes 196640 | tf_op jit(solution)/shard_map/ppermute | solution.py:436
  94.2 5.5 %shard_map.101 = f32[8,64,128]{2,1,0:T(8,128)} custom-call(f32[12,4,16,128]{3,2,1,0:T(8,128)S(1)} %collective-permute-done.low, f32[12,4,16,128]{3,2,1,0:T(8,128)S(1)} %shard_map.94.own, f32[12,4,16,128]{3,2,1,0:T(8,128)S(1)} %collective-permute-done.1.high, f32[12,16,128]{2,1,0:T(8,128)S(1)} %collective-permute-done.2.from_low, ...), custom_call_target="tpu_custom_call" | custom-call | flops 1000000 | bytes 1000000 | tf_op jit(solution)/shard_map/pallas_call | solution.py:35
  99.7 0.0 all-to-all-done.2
  99.7 3.6 %shard_map.102 = (f32[4,128]{1,0:T(4,128)}, f32[32,256]{1,0:T(8,128)}) custom-call(s32[3]{0:T(128)S(1)} %pad_add_fusion.spot, f32[1280,128]{1,0:T(8,128)S(1)} %bitcast.15, f32[768,128]{1,0:T(8,128)S(1)} %bitcast.16), custom_call_target="tpu_custom_call" | custom-call | flops 1000000 | bytes 1000000 | tf_op jit(solution)/shard_map/pallas_call | solution.py:35
  (2 shorter events, 0.0 us)
Async XLA Ops:
  1.5 1.0 copy-start
  2.4 13.9 %copy-start.1 = (s32[128,256]{1,0:T(8,128)S(1)}, s32[128,256]{1,0:T(8,128)}, u32[]{:S(2)}) copy-start(s32[128,256]{1,0:T(8,128)} %maps.1) | copy-start | bytes 393220
  2.4 13.8 %copy-start.2 = (f32[4,128]{1,0:T(4,128)S(1)}, f32[4,128]{1,0:T(4,128)}, u32[]{:S(2)}) copy-start(f32[4,128]{1,0:T(4,128)} %conductance.1) | copy-start | bytes 6148
  2.5 26.2 %collective-permute-start = (f32[12,4,16,128]{3,2,1,0:T(8,128)S(1)}, f32[12,4,16,128]{3,2,1,0:T(8,128)S(1)}, u32[]{:S(2)}, u32[]{:S(2)}) collective-permute-start(f32[12,4,16,128]{3,2,1,0:T(8,128)S(1)} %shard_map.94.own), channel_id=1, source_target_pairs={{0,16},{16,32},{32,48},{48,64},{64,80},{80,96},{96,112},{112,128},... | collective-permute-start | bytes 1179656 | tf_op jit(solution)/shard_map/ppermute | solution.py:400
  6.9 21.8 %collective-permute-start.1 = (f32[12,4,16,128]{3,2,1,0:T(8,128)S(1)}, f32[12,4,16,128]{3,2,1,0:T(8,128)S(1)}, u32[]{:S(2)}, u32[]{:S(2)}) collective-permute-start(f32[12,4,16,128]{3,2,1,0:T(8,128)S(1)} %shard_map.94.own), channel_id=1, source_target_pairs={{0,496},{16,0},{32,16},{48,32},{64,48},{80,64},{96,80},{112,96},{1... | collective-permute-start | bytes 1179656 | tf_op jit(solution)/shard_map/ppermute | solution.py:401
  16.3 0.7 copy-start.3
  16.3 0.7 copy-start.4
  29.9 39.5 %all-to-all-start.1 = ((f32[32,40,128]{2,1,0:T(8,128)}), f32[32,40,128]{2,1,0:T(8,128)S(1)}, u32[]{:S(2)}, u32[]{:S(2)}) async-start(f32[32,40,128]{2,1,0:T(8,128)} %bitcast.7), calls=%async_computation.1 | async-start | bytes 1310720 | tf_op jit(solution)/shard_map/all_to_all | solution.py:416
  36.1 4.9 %collective-permute-start.2 = (f32[12,16,128]{2,1,0:T(8,128)S(1)}, f32[12,16,128]{2,1,0:T(8,128)S(1)}, u32[]{:S(2)}, u32[]{:S(2)}) collective-permute-start(f32[12,16,128]{2,1,0:T(8,128)S(1)} %shard_map.96), channel_id=1, source_target_pairs={{0,1},{1,2},{2,3},{4,5},{5,6},{6,7},{8,9},{9,10},{10,11},{12,13},{... | collective-permute-start | bytes 294920 | tf_op jit(solution)/shard_map/ppermute | solution.py:419
  38.8 6.5 %collective-permute-start.3 = (f32[12,16,128]{2,1,0:T(8,128)S(1)}, f32[12,16,128]{2,1,0:T(8,128)S(1)}, u32[]{:S(2)}, u32[]{:S(2)}) collective-permute-start(f32[12,16,128]{2,1,0:T(8,128)S(1)} %shard_map.96), channel_id=1, source_target_pairs={{1,0},{2,1},{3,2},{5,4},{6,5},{7,6},{9,8},{10,9},{11,10},{13,12},{... | collective-permute-start | bytes 294920 | tf_op jit(solution)/shard_map/ppermute | solution.py:420
  45.9 2.8 %collective-permute-start.6 = (f32[8,128]{1,0:T(8,128)S(1)}, f32[8,128]{1,0:T(8,128)S(1)}, u32[]{:S(2)}, u32[]{:S(2)}) collective-permute-start(f32[8,128]{1,0:T(8,128)S(1)} %shard_map.98), channel_id=1, source_target_pairs={{0,12},{1,13},{2,14},{3,15},{16,28},{17,29},{18,30},{19,31},{32,44... | collective-permute-start | bytes 12296 | tf_op jit(solution)/shard_map/ppermute | solution.py:424
  46.5 2.1 %collective-permute-start.4 = (f32[8,128]{1,0:T(8,128)S(1)}, f32[8,128]{1,0:T(8,128)S(1)}, u32[]{:S(2)}, u32[]{:S(2)}) collective-permute-start(f32[8,128]{1,0:T(8,128)S(1)} %shard_map.98), channel_id=1, source_target_pairs={{0,4},{1,5},{2,6},{3,7},{16,20},{17,21},{18,22},{19,23},{32,36},{3... | collective-permute-start | bytes 12296 | tf_op jit(solution)/shard_map/ppermute | solution.py:424
  47.2 9.4 %collective-permute-start.5 = (f32[8,128]{1,0:T(8,128)S(1)}, f32[8,128]{1,0:T(8,128)S(1)}, u32[]{:S(2)}, u32[]{:S(2)}) collective-permute-start(f32[8,128]{1,0:T(8,128)S(1)} %shard_map.98), channel_id=1, source_target_pairs={{0,8},{1,9},{2,10},{3,11},{16,24},{17,25},{18,26},{19,27},{32,40},... | collective-permute-start | bytes 12296 | tf_op jit(solution)/shard_map/ppermute | solution.py:424
  69.5 30.2 %all-to-all-start.2 = ((f32[32,24,128]{2,1,0:T(8,128)}), f32[32,24,128]{2,1,0:T(8,128)S(1)}, u32[]{:S(2)}, u32[]{:S(2)}) async-start(f32[32,24,128]{2,1,0:T(8,128)} %bitcast.13), calls=%async_computation.2 | async-start | bytes 786432 | tf_op jit(solution)/shard_map/all_to_all | solution.py:438
  79.6 8.3 %collective-permute-start.7 = (f32[12,32,128]{2,1,0:T(8,128)S(1)}, f32[12,32,128]{2,1,0:T(8,128)S(1)}, u32[]{:S(2)}, u32[]{:S(2)}) collective-permute-start(f32[12,32,128]{2,1,0:T(8,128)S(1)} %get-tuple-element.23), channel_id=1, source_target_pairs={{4,0},{8,4},{12,8},{5,1},{9,5},{13,9},{6,2},{10,6},{14,10},{7,3},{... | collective-permute-start | bytes 589832 | tf_op jit(solution)/shard_map/ppermute | solution.py:437
  81.5 12.7 %collective-permute-start.8 = (f32[12,32,128]{2,1,0:T(8,128)S(1)}, f32[12,32,128]{2,1,0:T(8,128)S(1)}, u32[]{:S(2)}, u32[]{:S(2)}) collective-permute-start(f32[12,32,128]{2,1,0:T(8,128)S(1)} %get-tuple-element.24), channel_id=1, source_target_pairs={{0,4},{4,8},{8,12},{1,5},{5,9},{9,13},{2,6},{6,10},{10,14},{3,7},{... | collective-permute-start | bytes 589832 | tf_op jit(solution)/shard_map/ppermute | solution.py:436

commit v4 on v3

--- a/solution.py
+++ b/solution.py
@@ -18,8 +18,8 @@
 LONS = 4
 LATS = 128
 WIDE = 3 * LONS
-EARLY = 40
-LATE = 24
+LATE = 64
+RAW = 192
 SENT = 168
 TALL = SHELLS + 2 * PHASES
 F32 = jnp.float32
@@ -101,82 +101,92 @@
     )
 
 
-def inner_body(low, own, high, from_low, from_high, out):
-    lane = lax.broadcasted_iota(jnp.int32, (8, LATS), 1)
-    bottom = lax.broadcasted_iota(jnp.int32, (8, 2 * LATS), 0) == 0
-
-    def plane_of(plane):
-        edges = jnp.where(lane % 8 < 4, from_low[plane, :8, :], from_high[plane, :8, :])
-        made = []
+def raw_chunks():
+    found = []
+    at = 0
+    for plane in (5, 6, 8, 9, 10, 11):
+        reach = PHASES + 1 if plane < FIELDS else PHASES
         for wide in range(WIDE):
-            ref = (low, own, high)[wide // LONS]
-            if 0 < wide < WIDE - 1:
-                tail = halo_lanes(edges, wide)
-            else:
-                tail = jnp.zeros((8, LATS), F32)
-            made.append(jnp.concatenate([ref[plane, wide % LONS, :8, :], tail], axis=1))
-        return made
-
-    speeds = [plane_of(FIELDS + d) for d in range(4)]
+            count = reach - max(LONS - wide, wide - 2 * LONS + 1, 0)
+            if count > 0:
+                found.append((plane, wide, at, count))
+                at += count
+    return found
+
+
+def raw_body(low, own, high, out):
+    for plane, wide, at, count in raw_chunks():
+        ref = (low, own, high)[wide // LONS]
+        out[at : at + count, :] = ref[plane, wide % LONS, :count, :]
+
+
+def inner_body(raw, out, cells):
+    span = 4 * LATS
+    lane = lax.broadcasted_iota(jnp.int32, (8, span), 1)
+    bottom = lax.broadcasted_iota(jnp.int32, (8, span), 0) == 0
+    first, last = lane == 0, lane == span - 1
+    cells[...] = jnp.zeros(cells.shape, F32)
+    order = (5, 6, 8, 9, 10, 11)
+    for plane, wide, at, count in raw_chunks():
+        for rad in range(4):
+            cells[order.index(plane), wide, :count, rad * LATS : (rad + 1) * LATS] = raw[
+                rad * RAW + at : rad * RAW + at + count, :
+            ]
     w = [None] + [
-        weights([speeds[d][wide] for d in range(3)], speeds[3][wide])
+        weights([cells[2 + d, wide] for d in range(3)], cells[5, wide])
         for wide in range(1, WIDE - 1)
     ]
+    made = []
     for part in range(2):
-        cells = plane_of(5 + part)
+        now = [cells[part, wide] for wide in range(WIDE)]
         for phase in range(PHASES):
-            fresh = list(cells)
+            fresh = list(now)
             for wide in range(phase + 1, WIDE - 1 - phase):
-                c = cells[wide]
+                c = now[wide]
                 fresh[wide] = blend(
                     w[wide],
                     c,
                     jnp.where(bottom, 0.0, pltpu.roll(c, 1, axis=0)),
                     pltpu.roll(c, 7, axis=0),
-                    cells[wide - 1],
-                    cells[wide + 1],
-                    pltpu.roll(c, 1, axis=1),
-                    pltpu.roll(c, 2 * LATS - 1, axis=1),
+                    now[wide - 1],
+                    now[wide + 1],
+                    jnp.where(first, 0.0, pltpu.roll(c, 1, axis=1)),
+                    jnp.where(last, 0.0, pltpu.roll(c, span - 1, axis=1)),
                 )
-            cells = fresh
+            now = fresh
+        made.append(now[LONS : 2 * LONS])
+    blon, blat = made
+    for lon in range(LONS):
+        c = blon[lon]
+        source = jnp.where(first, 0.0, pltpu.roll(c, 1, axis=1)) - jnp.where(
+            last, 0.0, pltpu.roll(c, span - 1, axis=1)
+        )
+        if lon < LONS - 1:
+            source = source + blat[lon + 1]
+        if lon > 0:
+            source = source - blat[lon - 1]
+        for rad in range(4):
+            part = slice(rad * LATS, (rad + 1) * LATS)
+            out[rad * 4 + lon : rad * 4 + lon + 1, :] = source[0:1, part]
+            if lon == 0:
+                out[16 + rad : 17 + rad, :] = blat[0][0:1, part]
+            if lon == LONS - 1:
+                out[20 + rad : 21 + rad, :] = blat[LONS - 1][0:1, part]
+
+
+def join_body(spot, own, one, two, three, sent, out):
+    source = jnp.where(spot[0] == 0, own[...], one[...] + two[...] + three[...])
+    for owner in range(32):
+        out[owner * LATE : owner * LATE + 24, :] = source
+    for rad in range(4):
         for lon in range(LONS):
-            row = part * LONS + lon
-            out[row : row + 1, :] = cells[LONS + lon][0:1, :LATS]
-
-
-def early_body(sent, out):
-    for rad in range(4):
+            line = sent[rad * SENT + 160 + lon : rad * SENT + 161 + lon, :]
+            out[pl.ds(24 + rad * 4 + lon, 32, stride=LATE), :] = jnp.broadcast_to(line, (32, LATS))
         for row in range(5):
             at = rad * SENT + row * 32
-            out[pl.ds(rad * 5 + row, 32, stride=EARLY), :] = sent[at : at + 32, :]
-        for lon in range(LONS):
-            line = sent[rad * SENT + 160 + lon : rad * SENT + 161 + lon, :]
-            out[pl.ds(20 + rad * 4 + lon, 32, stride=EARLY), :] = jnp.broadcast_to(line, (32, LATS))
-    for spare in range(36, EARLY):
-        out[pl.ds(spare, 32, stride=EARLY), :] = jnp.zeros((32, LATS), F32)
-
-
-def late_body(planes, out, block):
-    wide = 4 * LATS
-    lane = lax.broadcasted_iota(jnp.int32, (LONS, wide), 1)
-    lon = lax.broadcasted_iota(jnp.int32, (LONS, wide), 0)
-    blon = jnp.concatenate([planes[r * 8 : r * 8 + 4, :] for r in range(4)], axis=1)
-    blat = jnp.concatenate([planes[r * 8 + 4 : r * 8 + 8, :] for r in range(4)], axis=1)
-    upper = jnp.concatenate([blat[1:], blat[:1]], axis=0)
-    lower = jnp.concatenate([blat[3:], blat[:3]], axis=0)
-    north = jnp.where(lane == wide - 1, 0.0, pltpu.roll(blon, wide - 1, axis=1))
-    south = jnp.where(lane == 0, 0.0, pltpu.roll(blon, 1, axis=1))
-    source = (
-        jnp.where(lon == LONS - 1, 0.0, upper) - jnp.where(lon == 0, 0.0, lower) - (north - south)
-    )
-    for rad in range(4):
-        part = slice(rad * LATS, (rad + 1) * LATS)
-        block[rad * 4 : rad * 4 + 4, :] = source[:, part]
-        block[16 + rad : 17 + rad, :] = blat[0:1, part]
-        block[20 + rad : 21 + rad, :] = blat[3:4, part]
-    mine = block[...]
-    for owner in range(32):
-        out[owner * LATE : owner * LATE + LATE, :] = mine
+            out[pl.ds(40 + rad * 5 + row, 32, stride=LATE), :] = sent[at : at + 32, :]
+    for spare in range(60, LATE):
+        out[pl.ds(spare, 32, stride=LATE), :] = jnp.zeros((32, LATS), F32)
 
 
 def chunks():
@@ -290,7 +300,7 @@
         out[at + 4 : at + 8, :] = jnp.zeros((4, LATS), F32)
 
 
-def final_body(spot, early, late, pot, foot, phi, east_w, west_w, north_w, south_w, start, picked, hot):
+def final_body(spot, late, pot, foot, phi, east_w, west_w, north_w, south_w, start, picked, hot):
     devs, rads = 32, 4
     wide = rads * LATS
     lane = lax.broadcasted_iota(jnp.int32, (devs, wide), 1)
@@ -312,7 +322,7 @@
     def lat_down(value):
         return pltpu.roll(value, 1, axis=1)
 
-    cond = [gather(early, 20 + lon, 4, EARLY) for lon in range(LONS)]
+    cond = [gather(late, 24 + lon, 4, LATE) for lon in range(LONS)]
     sources = [gather(late, lon, 4, LATE) for lon in range(LONS)]
     sources[LONS - 1] += pltpu.roll(gather(late, 16, 1, LATE), devs - 1, axis=0)
     sources[0] -= pltpu.roll(gather(late, 20, 1, LATE), 1, axis=0)
@@ -360,13 +370,13 @@
     slot_lane = lax.broadcasted_iota(jnp.int32, (devs, LATS), 1).astype(F32)
     for rad in range(rads):
         table = [phi[done, lon, :, rad * LATS : (rad + 1) * LATS] for lon in range(LONS)]
-        marks = early[pl.ds(rad * 5 + 4, devs, stride=EARLY), :]
+        marks = late[pl.ds(40 + rad * 5 + 4, devs, stride=LATE), :]
         for slot in range(2):
             at = (slot * rads + rad) * devs
             row = marks if slot == 0 else pltpu.roll(marks, 64, axis=1)
             hot[at : at + devs, :] = jnp.where(row == slot_lane, 1.0, 0.0)
             for half in range(2):
-                cell = early[pl.ds(rad * 5 + 2 * slot + half, devs, stride=EARLY), :].astype(jnp.int32)
+                cell = late[pl.ds(40 + rad * 5 + 2 * slot + half, devs, stride=LATE), :].astype(jnp.int32)
                 place, lon_at = cell & 127, cell >> 7
                 value = jnp.zeros((devs, LATS), F32)
                 for lon in range(LONS):
@@ -410,29 +420,28 @@
     )
 
     low, high, sent = lax.optimization_barrier((low, high, sent))
+    raw = call(raw_body, arr(RAW, LATS), (low, own, high))
+    raw = lax.all_gather(raw, "rad")
+    inner = call(
+        inner_body,
+        arr(24, LATS),
+        (raw.reshape(4 * RAW, LATS),),
+        scratch=(pltpu.VMEM((6, WIDE, 8, 4 * LATS), F32),),
+    )
+    copies = [lax.ppermute(inner, "sec", [(0, sec)]) for sec in range(1, 4)]
+    late = call(
+        join_body,
+        arr(32 * LATE, LATS),
+        (spot, inner, *copies, sent.reshape(4 * SENT, LATS)),
+        smem=(0,),
+    )
+    late, low, high = lax.optimization_barrier((late, low, high))
+
     edges = call(edge_body, arr(PLANES, SHELLS, LATS), (low, own, high))
-    early = call(early_body, arr(32 * EARLY, LATS), (sent.reshape(4 * SENT, LATS),))
-    edges, early = lax.optimization_barrier((edges, early))
-    early = lax.all_to_all(
-        early.reshape(32, EARLY, LATS), "lon", split_axis=0, concat_axis=0, tiled=True
-    )
     from_low = lax.ppermute(edges, "rad", shift("rad", 1, False))
     from_high = lax.ppermute(edges, "rad", shift("rad", -1, False))
     blocks = (low, own, high, from_low, from_high)
-
-    inner = call(inner_body, arr(8, LATS), blocks)
-    copies = [lax.ppermute(inner, "sec", [(0, sec)]) for sec in range(1, 4)]
-    inner = jnp.where(lax.axis_index("sec") == 0, inner, copies[0] + copies[1] + copies[2])
-    inner = lax.all_gather(inner, "rad")
     up, down = call(pack_body, (arr(PLANES, 32, LATS), arr(PLANES, 32, LATS)), blocks)
-
-    late = call(
-        late_body,
-        arr(32 * LATE, LATS),
-        (inner.reshape(32, LATS),),
-        scratch=(pltpu.VMEM((LATE, LATS), F32),),
-    )
-    late, early, up, down = lax.optimization_barrier((late, early, up, down))
     below = lax.ppermute(up, "sec", shift("sec", 1, False))
     above = lax.ppermute(down, "sec", shift("sec", -1, False))
     late = lax.all_to_all(
@@ -455,7 +464,7 @@
     potential, foot_table = call(
         final_body,
         (arr(LONS, LATS), arr(ROWS_OWN, 256)),
-        (spot, early.reshape(32 * EARLY, LATS), late.reshape(32 * LATE, LATS)),
+        (spot, late.reshape(32 * LATE, LATS)),
         scratch=(
             pltpu.VMEM((2, LONS, 32, 4 * LATS), F32),
             plane,

time: 104 us -> 103 us (level)
  the two profiles are of different devices: /device:TPU:48 before, /device:TPU:17 now
where the time goes in v4:
time: 103 us; the launch traced here: 102 us
  starting transfers between devices  46.9 us (46%)
  waiting for transfers between devices  27.8 us (27%)
  Pallas kernels  13.9 us (13%)
  blocking collectives  10.6 us (10%)
  local copies, waits for them, and re-layouts  1.59 us (2%)
    ppermute x1, waiting for transfers between devices, shards(): above = lax.ppermute(down, 'sec', shift('sec', -1, False))  14.1 us
    pallas_call x9, Pallas kernels, call(): pl.pallas_call(body, out_shape=out_shape, in_specs=specs, out_specs=[vmem...  13.9 us
    all_gather x1, blocking collectives, shards(): raw = lax.all_gather(raw, 'rad')  10.6 us
    ppermute x1, starting transfers between devices, shards(): above = lax.ppermute(down, 'sec', shift('sec', -1, False))  10.3 us
    ppermute x1, starting transfers between devices, shards(): high = lax.ppermute(own, 'lon', shift('lon', -1, True))  8.47 us
    all_to_all x1, starting transfers between devices, shards(): lax.all_to_all(late.reshape(32, LATE, LATS), 'lon', split_axis=0, concat_...  7.41 us
    ppermute x1, starting transfers between devices, shards(): below = lax.ppermute(up, 'sec', shift('sec', 1, False))  6.79 us
    all_to_all x1, waiting for transfers between devices, shards(): lax.all_to_all(slots.reshape(4, SENT, LATS), 'rad', split_axis=0, concat_...  6.05 us
  transfers between devices with their start and end apart: 11, of which 5 were waited for; matrix products, arithmetic and copies ran while one was open for 0% of the time, Pallas kernels for 7%

profile of v4, /device:TPU:17, one launch (start us, length us, event | category | flops | bytes accessed | tf_op | source)
XLA Modules:
  0.0 102.5 jit_solution(10769300698126324607)
XLA Ops:
  0.6 0.8 maximum_convert_fusion.speeds
  1.5 0.0 copy-start
  1.5 0.9 copy-done
  2.4 0.0 copy-start.1
  2.4 0.0 copy-start.2
  2.5 4.1 %collective-permute-start = (f32[12,4,16,128]{3,2,1,0:T(8,128)S(1)}, f32[12,4,16,128]{3,2,1,0:T(8,128)S(1)}, u32[]{:S(2)}, u32[]{:S(2)}) collective-permute-start(f32[12,4,16,128]{3,2,1,0:T(8,128)S(1)} %shard_map.94.own), channel_id=1, source_target_pairs={{0,16},{16,32},{32,48},{48,64},{64,80},{80,96},{96,112},{112,128},... | collective-permute-start | bytes 1179656 | tf_op jit(solution)/shard_map/ppermute | solution.py:410
  6.6 8.5 %collective-permute-start.1 = (f32[12,4,16,128]{3,2,1,0:T(8,128)S(1)}, f32[12,4,16,128]{3,2,1,0:T(8,128)S(1)}, u32[]{:S(2)}, u32[]{:S(2)}) collective-permute-start(f32[12,4,16,128]{3,2,1,0:T(8,128)S(1)} %shard_map.94.own), channel_id=1, source_target_pairs={{0,496},{16,0},{32,16},{48,32},{64,48},{80,64},{96,80},{112,96},{1... | collective-permute-start | bytes 1179656 | tf_op jit(solution)/shard_map/ppermute | solution.py:411
  15.1 0.0 copy-start.3
  15.1 0.0 copy-start.4
  15.1 0.0 copy-done.1
  15.1 0.0 copy-done.2
  15.1 0.6 copy-done.3
  15.7 0.0 copy-done.4
  15.8 1.1 %shard_map.95 = f32[672,128]{1,0:T(8,128)} custom-call(s32[1,128]{1,0:T(1,128)S(1)} %bitcast.16, s32[1,128]{1,0:T(1,128)S(1)} %bitcast.17, s32[128,256]{1,0:T(8,128)S(1)} %copy-done.1, f32[4,128]{1,0:T(4,128)S(1)} %copy-done.2), custom_call_target="tpu_custom_call" | custom-call | flops 1000000 | bytes 1000000 | tf_op jit(solution)/shard_map/pallas_call | solution.py:35
  16.8 4.0 %all-to-all-start = ((f32[4,168,128]{2,1,0:T(8,128)}), f32[4,168,128]{2,1,0:T(8,128)S(1)}, u32[]{:S(2)}, u32[]{:S(2)}) async-start(f32[4,168,128]{2,1,0:T(8,128)} %bitcast.8), calls=%async_computation | async-start | bytes 688128 | tf_op jit(solution)/shard_map/all_to_all | solution.py:418
  20.9 6.0 %all-to-all-done = f32[4,168,128]{2,1,0:T(8,128)S(1)} async-done(((f32[4,168,128]{2,1,0:T(8,128)}), f32[4,168,128]{2,1,0:T(8,128)S(1)}, u32[]{:S(2)}, u32[]{:S(2)}) %all-to-all-start) | async-done | bytes 344096 | tf_op jit(solution)/shard_map/all_to_all | solution.py:418
  26.9 0.0 collective-permute-done.low
  26.9 0.0 collective-permute-done.1.high
  26.9 10.6 %all-gather.raw = f32[768,128]{1,0:T(8,128)S(1)} all-gather(f32[192,128]{1,0:T(8,128)S(1)} %shard_map.96), channel_id=2, replica_groups=mesh['lon'=32,'sec'=4,'rad'=4] {'rad'}, dimensions={0}, use_global_device_ids=true | all-gather | bytes 491520 | tf_op jit(solution)/shard_map/all_gather | solution.py:424
  37.5 0.8 shard_map.97.own
  38.4 1.3 %collective-permute-start.2 = (f32[24,128]{1,0:T(8,128)S(1)}, f32[24,128]{1,0:T(8,128)S(1)}, u32[]{:S(2)}, u32[]{:S(2)}) collective-permute-start(f32[24,128]{1,0:T(8,128)S(1)} %shard_map.97.own), channel_id=1, source_target_pairs={{0,4},{1,5},{2,6},{3,7},{16,20},{17,21},{18,22},{19,23},{32,36},{3... | collective-permute-start | bytes 36872 | tf_op jit(solution)/shard_map/ppermute | solution.py:431
  39.7 0.7 collective-permute-start.3
  40.3 0.7 collective-permute-start.4
  41.0 0.1 pad_add_fusion.spot
  41.1 3.6 %collective-permute-done.2.one = f32[24,128]{1,0:T(8,128)S(1)} collective-permute-done((f32[24,128]{1,0:T(8,128)S(1)}, f32[24,128]{1,0:T(8,128)S(1)}, u32[]{:S(2)}, u32[]{:S(2)}) %collective-permute-start.2) | collective-permute-done | bytes 12320 | tf_op jit(solution)/shard_map/ppermute | solution.py:431
  44.7 0.0 collective-permute-done.3.two
  44.7 0.0 collective-permute-done.4.three
  44.7 2.2 %shard_map.98 = f32[2048,128]{1,0:T(8,128)} custom-call(s32[3]{0:T(128)S(1)} %pad_add_fusion.spot, f32[24,128]{1,0:T(8,128)S(1)} %shard_map.97.own, f32[24,128]{1,0:T(8,128)S(1)} %collective-permute-done.2.one, f32[24,128]{1,0:T(8,128)S(1)} %collective-permute-done.3.two, f32[24,128]{1,0:T(8,128)S(1)} %collective-permute-done.4.three, f32[672,128]{1,0:T(8,128)S(1)} %bitcast.14), custom_call_target="tpu_custom_call" | custom-call | flops 1000000 | bytes 1000000 | tf_op jit(solution)/shard_map/pallas_call | solution.py:35
  46.9 7.4 %all-to-all-start.1 = ((f32[32,64,128]{2,1,0:T(8,128)}), f32[32,64,128]{2,1,0:T(8,128)S(1)}, u32[]{:S(2)}, u32[]{:S(2)}) async-start(f32[32,64,128]{2,1,0:T(8,128)} %bitcast.11), calls=%async_computation.1 | async-start | bytes 2097152 | tf_op jit(solution)/shard_map/all_to_all | solution.py:447
  54.3 0.3 shard_map.99
  54.6 1.9 %collective-permute-start.5 = (f32[12,16,128]{2,1,0:T(8,128)S(1)}, f32[12,16,128]{2,1,0:T(8,128)S(1)}, u32[]{:S(2)}, u32[]{:S(2)}) collective-permute-start(f32[12,16,128]{2,1,0:T(8,128)S(1)} %shard_map.99), channel_id=1, source_target_pairs={{0,1},{1,2},{2,3},{4,5},{5,6},{6,7},{8,9},{9,10},{10,11},{12,13},{... | collective-permute-start | bytes 294920 | tf_op jit(solution)/shard_map/ppermute | solution.py:441
  56.5 1.3 %collective-permute-start.6 = (f32[12,16,128]{2,1,0:T(8,128)S(1)}, f32[12,16,128]{2,1,0:T(8,128)S(1)}, u32[]{:S(2)}, u32[]{:S(2)}) collective-permute-start(f32[12,16,128]{2,1,0:T(8,128)S(1)} %shard_map.99), channel_id=1, source_target_pairs={{1,0},{2,1},{3,2},{5,4},{6,5},{7,6},{9,8},{10,9},{11,10},{13,12},{... | collective-permute-start | bytes 294920 | tf_op jit(solution)/shard_map/ppermute | solution.py:442
  57.8 0.3 collective-permute-done.5.from_low
  58.1 3.7 %collective-permute-done.6.from_high = f32[12,16,128]{2,1,0:T(8,128)S(1)} collective-permute-done((f32[12,16,128]{2,1,0:T(8,128)S(1)}, f32[12,16,128]{2,1,0:T(8,128)S(1)}, u32[]{:S(2)}, u32[]{:S(2)}) %collective-permute-start.6) | collective-permute-done | bytes 98336 | tf_op jit(solution)/shard_map/ppermute | solution.py:442
  61.9 0.1 shard_map.100
  62.0 10.3 %collective-permute-start.7 = (f32[12,32,128]{2,1,0:T(8,128)S(1)}, f32[12,32,128]{2,1,0:T(8,128)S(1)}, u32[]{:S(2)}, u32[]{:S(2)}) collective-permute-start(f32[12,32,128]{2,1,0:T(8,128)S(1)} %get-tuple-element.18), channel_id=1, source_target_pairs={{4,0},{8,4},{12,8},{5,1},{9,5},{13,9},{6,2},{10,6},{14,10},{7,3},{... | collective-permute-start | bytes 589832 | tf_op jit(solution)/shard_map/ppermute | solution.py:446
  72.3 6.8 %collective-permute-start.8 = (f32[12,32,128]{2,1,0:T(8,128)S(1)}, f32[12,32,128]{2,1,0:T(8,128)S(1)}, u32[]{:S(2)}, u32[]{:S(2)}) collective-permute-start(f32[12,32,128]{2,1,0:T(8,128)S(1)} %get-tuple-element.19), channel_id=1, source_target_pairs={{0,4},{4,8},{8,12},{1,5},{5,9},{9,13},{2,6},{6,10},{10,14},{3,7},{... | collective-permute-start | bytes 589832 | tf_op jit(solution)/shard_map/ppermute | solution.py:445
  79.1 14.1 %collective-permute-done.7.above = f32[12,32,128]{2,1,0:T(8,128)S(1)} collective-permute-done((f32[12,32,128]{2,1,0:T(8,128)S(1)}, f32[12,32,128]{2,1,0:T(8,128)S(1)}, u32[]{:S(2)}, u32[]{:S(2)}) %collective-permute-start.7) | collective-permute-done | bytes 196640 | tf_op jit(solution)/shard_map/ppermute | solution.py:446
  93.2 0.0 collective-permute-done.8.below
  93.2 5.5 %shard_map.101 = f32[8,64,128]{2,1,0:T(8,128)} custom-call(f32[12,4,16,128]{3,2,1,0:T(8,128)S(1)} %collective-permute-done.low, f32[12,4,16,128]{3,2,1,0:T(8,128)S(1)} %shard_map.94.own, f32[12,4,16,128]{3,2,1,0:T(8,128)S(1)} %collective-permute-done.1.high, f32[12,16,128]{2,1,0:T(8,128)S(1)} %collective-permute-done.5.from_low, ...), custom_call_target="tpu_custom_call" | custom-call | flops 1000000 | bytes 1000000 | tf_op jit(solution)/shard_map/pallas_call | solution.py:35
  98.7 0.0 all-to-all-done.1
  98.7 3.8 %shard_map.102 = (f32[4,128]{1,0:T(4,128)}, f32[32,256]{1,0:T(8,128)}) custom-call(s32[3]{0:T(128)S(1)} %pad_add_fusion.spot, f32[2048,128]{1,0:T(8,128)S(1)} %bitcast.13), custom_call_target="tpu_custom_call" | custom-call | flops 1000000 | bytes 1000000 | tf_op jit(solution)/shard_map/pallas_call | solution.py:35
  (2 shorter events, 0.1 us)
Async XLA Ops:
  1.5 1.0 copy-start
  2.4 12.7 %copy-start.1 = (s32[128,256]{1,0:T(8,128)S(1)}, s32[128,256]{1,0:T(8,128)}, u32[]{:S(2)}) copy-start(s32[128,256]{1,0:T(8,128)} %maps.1) | copy-start | bytes 393220
  2.4 12.7 %copy-start.2 = (f32[4,128]{1,0:T(4,128)S(1)}, f32[4,128]{1,0:T(4,128)}, u32[]{:S(2)}) copy-start(f32[4,128]{1,0:T(4,128)} %conductance.1) | copy-start | bytes 6148
  2.5 24.5 %collective-permute-start = (f32[12,4,16,128]{3,2,1,0:T(8,128)S(1)}, f32[12,4,16,128]{3,2,1,0:T(8,128)S(1)}, u32[]{:S(2)}, u32[]{:S(2)}) collective-permute-start(f32[12,4,16,128]{3,2,1,0:T(8,128)S(1)} %shard_map.94.own), channel_id=1, source_target_pairs={{0,16},{16,32},{32,48},{48,64},{64,80},{80,96},{96,112},{112,128},... | collective-permute-start | bytes 1179656 | tf_op jit(solution)/shard_map/ppermute | solution.py:410
  6.6 20.3 %collective-permute-start.1 = (f32[12,4,16,128]{3,2,1,0:T(8,128)S(1)}, f32[12,4,16,128]{3,2,1,0:T(8,128)S(1)}, u32[]{:S(2)}, u32[]{:S(2)}) collective-permute-start(f32[12,4,16,128]{3,2,1,0:T(8,128)S(1)} %shard_map.94.own), channel_id=1, source_target_pairs={{0,496},{16,0},{32,16},{48,32},{64,48},{80,64},{96,80},{112,96},{1... | collective-permute-start | bytes 1179656 | tf_op jit(solution)/shard_map/ppermute | solution.py:411
  15.1 0.7 copy-start.3
  15.1 0.7 copy-start.4
  16.8 10.1 %all-to-all-start = ((f32[4,168,128]{2,1,0:T(8,128)}), f32[4,168,128]{2,1,0:T(8,128)S(1)}, u32[]{:S(2)}, u32[]{:S(2)}) async-start(f32[4,168,128]{2,1,0:T(8,128)} %bitcast.8), calls=%async_computation | async-start | bytes 688128 | tf_op jit(solution)/shard_map/all_to_all | solution.py:418
  38.4 6.3 %collective-permute-start.2 = (f32[24,128]{1,0:T(8,128)S(1)}, f32[24,128]{1,0:T(8,128)S(1)}, u32[]{:S(2)}, u32[]{:S(2)}) collective-permute-start(f32[24,128]{1,0:T(8,128)S(1)} %shard_map.97.own), channel_id=1, source_target_pairs={{0,4},{1,5},{2,6},{3,7},{16,20},{17,21},{18,22},{19,23},{32,36},{3... | collective-permute-start | bytes 36872 | tf_op jit(solution)/shard_map/ppermute | solution.py:431
  39.7 5.0 %collective-permute-start.3 = (f32[24,128]{1,0:T(8,128)S(1)}, f32[24,128]{1,0:T(8,128)S(1)}, u32[]{:S(2)}, u32[]{:S(2)}) collective-permute-start(f32[24,128]{1,0:T(8,128)S(1)} %shard_map.97.own), channel_id=1, source_target_pairs={{0,8},{1,9},{2,10},{3,11},{16,24},{17,25},{18,26},{19,27},{32,40},... | collective-permute-start | bytes 36872 | tf_op jit(solution)/shard_map/ppermute | solution.py:431
  40.3 4.4 %collective-permute-start.4 = (f32[24,128]{1,0:T(8,128)S(1)}, f32[24,128]{1,0:T(8,128)S(1)}, u32[]{:S(2)}, u32[]{:S(2)}) collective-permute-start(f32[24,128]{1,0:T(8,128)S(1)} %shard_map.97.own), channel_id=1, source_target_pairs={{0,12},{1,13},{2,14},{3,15},{16,28},{17,29},{18,30},{19,31},{32,44... | collective-permute-start | bytes 36872 | tf_op jit(solution)/shard_map/ppermute | solution.py:431
  46.9 51.8 %all-to-all-start.1 = ((f32[32,64,128]{2,1,0:T(8,128)}), f32[32,64,128]{2,1,0:T(8,128)S(1)}, u32[]{:S(2)}, u32[]{:S(2)}) async-start(f32[32,64,128]{2,1,0:T(8,128)} %bitcast.11), calls=%async_computation.1 | async-start | bytes 2097152 | tf_op jit(solution)/shard_map/all_to_all | solution.py:447
  54.6 3.5 %collective-permute-start.5 = (f32[12,16,128]{2,1,0:T(8,128)S(1)}, f32[12,16,128]{2,1,0:T(8,128)S(1)}, u32[]{:S(2)}, u32[]{:S(2)}) collective-permute-start(f32[12,16,128]{2,1,0:T(8,128)S(1)} %shard_map.99), channel_id=1, source_target_pairs={{0,1},{1,2},{2,3},{4,5},{5,6},{6,7},{8,9},{9,10},{10,11},{12,13},{... | collective-permute-start | bytes 294920 | tf_op jit(solution)/shard_map/ppermute | solution.py:441
  56.5 5.4 %collective-permute-start.6 = (f32[12,16,128]{2,1,0:T(8,128)S(1)}, f32[12,16,128]{2,1,0:T(8,128)S(1)}, u32[]{:S(2)}, u32[]{:S(2)}) collective-permute-start(f32[12,16,128]{2,1,0:T(8,128)S(1)} %shard_map.99), channel_id=1, source_target_pairs={{1,0},{2,1},{3,2},{5,4},{6,5},{7,6},{9,8},{10,9},{11,10},{13,12},{... | collective-permute-start | bytes 294920 | tf_op jit(solution)/shard_map/ppermute | solution.py:442
  62.0 31.2 %collective-permute-start.7 = (f32[12,32,128]{2,1,0:T(8,128)S(1)}, f32[12,32,128]{2,1,0:T(8,128)S(1)}, u32[]{:S(2)}, u32[]{:S(2)}) collective-permute-start(f32[12,32,128]{2,1,0:T(8,128)S(1)} %get-tuple-element.18), channel_id=1, source_target_pairs={{4,0},{8,4},{12,8},{5,1},{9,5},{13,9},{6,2},{10,6},{14,10},{7,3},{... | collective-permute-start | bytes 589832 | tf_op jit(solution)/shard_map/ppermute | solution.py:446
  72.3 20.9 %collective-permute-start.8 = (f32[12,32,128]{2,1,0:T(8,128)S(1)}, f32[12,32,128]{2,1,0:T(8,128)S(1)}, u32[]{:S(2)}, u32[]{:S(2)}) collective-permute-start(f32[12,32,128]{2,1,0:T(8,128)S(1)} %get-tuple-element.19), channel_id=1, source_target_pairs={{0,4},{4,8},{8,12},{1,5},{5,9},{9,13},{2,6},{6,10},{10,14},{3,7},{... | collective-permute-start | bytes 589832 | tf_op jit(solution)/shard_map/ppermute | solution.py:445

commit v5 on v4

--- a/solution.py
+++ b/solution.py
@@ -38,7 +38,7 @@
         in_specs=specs,
         out_specs=[vmem] * len(out_shape) if many else vmem,
         scratch_shapes=list(scratch),
-        compiler_params=pltpu.CompilerParams(vmem_limit_bytes=40 * 2**20),
+        compiler_params=pltpu.CompilerParams(vmem_limit_bytes=16 * 2**20),
         cost_estimate=pl.CostEstimate(flops=flops, bytes_accessed=traffic, transcendentals=0),
     )(*args)
 
@@ -64,15 +64,23 @@
                 out[plane, lon] = speeds[plane - FIELDS, rows, :]
 
 
-def edge_body(low, own, high, out):
-    group = lax.broadcasted_iota(jnp.int32, (SHELLS, LATS), 1) // 8
+def edge_body(low, own, high, above, below, edges, tall):
+    found, _ = chunks()
+    group = lax.broadcasted_iota(jnp.int32, (TALL, LATS), 1) // 8
     for plane in range(PLANES):
-        packed = jnp.zeros((SHELLS, LATS), F32)
+        for wide in range(WIDE):
+            ref = (low, own, high)[wide // LONS]
+            tall[plane, wide, :SHELLS, :] = ref[plane, wide % LONS]
+            tall[plane, wide, SHELLS:, :] = jnp.zeros((TALL - SHELLS, LATS), F32)
+        for wide, start, count in found:
+            tall[plane, wide, SHELLS : SHELLS + count, :] = above[plane, start : start + count, :]
+            tall[plane, wide, TALL - count :, :] = below[plane, start : start + count, :]
+    for plane in range(PLANES):
+        packed = jnp.zeros((TALL, LATS), F32)
         for wide in range(1, WIDE - 1):
-            ref = (low, own, high)[wide // LONS]
-            turned = pltpu.roll(ref[plane, wide % LONS], 8 * wide + 4, axis=1)
+            turned = pltpu.roll(tall[plane, wide], 8 * wide + 4, axis=1)
             packed = jnp.where(group == wide, turned, packed)
-        out[plane] = packed
+        edges[plane] = packed
 
 
 def halo_lanes(edges, wide):
@@ -174,19 +182,43 @@
                 out[20 + rad : 21 + rad, :] = blat[LONS - 1][0:1, part]
 
 
-def join_body(spot, own, one, two, three, sent, out):
-    source = jnp.where(spot[0] == 0, own[...], one[...] + two[...] + three[...])
-    for owner in range(32):
-        out[owner * LATE : owner * LATE + 24, :] = source
+def base_body(sent, out):
+    step = LATE - 24
     for rad in range(4):
         for lon in range(LONS):
             line = sent[rad * SENT + 160 + lon : rad * SENT + 161 + lon, :]
-            out[pl.ds(24 + rad * 4 + lon, 32, stride=LATE), :] = jnp.broadcast_to(line, (32, LATS))
+            out[pl.ds(rad * 4 + lon, 32, stride=step), :] = jnp.broadcast_to(line, (32, LATS))
         for row in range(5):
             at = rad * SENT + row * 32
-            out[pl.ds(40 + rad * 5 + row, 32, stride=LATE), :] = sent[at : at + 32, :]
-    for spare in range(60, LATE):
-        out[pl.ds(spare, 32, stride=LATE), :] = jnp.zeros((32, LATS), F32)
+            out[pl.ds(16 + rad * 5 + row, 32, stride=step), :] = sent[at : at + 32, :]
+    for spare in range(36, step):
+        out[pl.ds(spare, 32, stride=step), :] = jnp.zeros((32, LATS), F32)
+
+
+def join_body(one, two, base, out, copies, sems):
+    rest = pltpu.make_async_copy(base, out.at[:, pl.ds(24, LATE - 24), :], sems.at[0])
+    rest.start()
+    source = one[...] + two[...]
+    for owner in range(32):
+        copies[owner] = source
+    move = pltpu.make_async_copy(copies, out.at[:, pl.ds(0, 24), :], sems.at[1])
+    move.start()
+    move.wait()
+    rest.wait()
+
+
+def join(one, two, base):
+    vmem = pl.BlockSpec(memory_space=pltpu.VMEM)
+    plain = pl.BlockSpec(memory_space=pl.ANY)
+    return pl.pallas_call(
+        join_body,
+        out_shape=arr(32, LATE, LATS),
+        in_specs=[vmem, vmem, plain],
+        out_specs=plain,
+        scratch_shapes=[pltpu.VMEM((32, 24, LATS), F32), pltpu.SemaphoreType.DMA((2,))],
+        compiler_params=pltpu.CompilerParams(vmem_limit_bytes=4 * 2**20),
+        cost_estimate=pl.CostEstimate(flops=10**5, bytes_accessed=10**6, transcendentals=0),
+    )(one, two, base)
 
 
 def chunks():
@@ -200,33 +232,27 @@
     return found, at
 
 
-def pack_body(low, own, high, from_low, from_high, up, down):
-    found, at = chunks()
-    lane = lax.broadcasted_iota(jnp.int32, (8, LATS), 1)
+def pack_body(low, own, high, up, down):
+    found, rows = chunks()
     for plane in range(PLANES):
         for wide, start, count in found:
             ref = (low, own, high)[wide // LONS]
             up[plane, start : start + count, :] = ref[plane, wide % LONS, SHELLS - count :, :]
             down[plane, start : start + count, :] = ref[plane, wide % LONS, :count, :]
-        first = jnp.where(lane % 8 < 4, from_low[plane, :8, :], from_high[plane, :8, :])
-        last = jnp.where(lane % 8 < 4, from_low[plane, 8:, :], from_high[plane, 8:, :])
-        up[plane, at : at + 4, :] = last[4:]
-        down[plane, at : at + 4, :] = first[:4]
-
-
-def main_body(low, own, high, from_low, from_high, above, below, out, cells, w, speeds, edges):
-    found, at = chunks()
-    lane = lax.broadcasted_iota(jnp.int32, (SHELLS, LATS), 1)
+        up[plane, rows:, :] = jnp.zeros((32 - rows, LATS), F32)
+        down[plane, rows:, :] = jnp.zeros((32 - rows, LATS), F32)
+
+
+def main_body(low, own, high, above, below, from_low, from_high, out, cells, w, speeds):
+    found, _ = chunks()
+    lane = lax.broadcasted_iota(jnp.int32, (TALL, LATS), 1)
 
     def fill(plane, target):
-        edges[:SHELLS, :] = jnp.where(lane % 8 < 4, from_low[plane], from_high[plane])
-        edges[SHELLS : SHELLS + 4, :] = above[plane, at : at + 4, :]
-        edges[SHELLS + 4 :, :] = below[plane, at : at + 4, :]
-        strip = edges[...]
+        strip = jnp.where(lane % 8 < 4, from_low[plane], from_high[plane])
         for wide in range(WIDE):
             ref = (low, own, high)[wide // LONS]
             target[wide, :SHELLS, :LATS] = ref[plane, wide % LONS]
-            target[wide, SHELLS:, :LATS] = jnp.zeros((8, LATS), F32)
+            target[wide, SHELLS:, :LATS] = jnp.zeros((TALL - SHELLS, LATS), F32)
             if 0 < wide < WIDE - 1:
                 target[wide, :, LATS:] = halo_lanes(strip, wide)
             else:
@@ -420,43 +446,46 @@
     )
 
     low, high, sent = lax.optimization_barrier((low, high, sent))
+    up, down = call(pack_body, (arr(PLANES, 32, LATS), arr(PLANES, 32, LATS)), (low, own, high))
+    below = lax.ppermute(up, "sec", shift("sec", 1, False))
+    above = lax.ppermute(down, "sec", shift("sec", -1, False))
     raw = call(raw_body, arr(RAW, LATS), (low, own, high))
     raw = lax.all_gather(raw, "rad")
+    raw, above, below = lax.optimization_barrier((raw, above, below))
     inner = call(
         inner_body,
         arr(24, LATS),
         (raw.reshape(4 * RAW, LATS),),
         scratch=(pltpu.VMEM((6, WIDE, 8, 4 * LATS), F32),),
     )
-    copies = [lax.ppermute(inner, "sec", [(0, sec)]) for sec in range(1, 4)]
-    late = call(
-        join_body,
-        arr(32 * LATE, LATS),
-        (spot, inner, *copies, sent.reshape(4 * SENT, LATS)),
-        smem=(0,),
-    )
+    far = lax.ppermute(inner, "sec", [(0, 3)])
+    far = jnp.where(lax.axis_index("sec") == 0, inner, far)
+    near = lax.ppermute(far, "sec", [(0, 1), (3, 2)])
+    base = call(base_body, arr(32 * (LATE - 24), LATS), (sent.reshape(4 * SENT, LATS),))
+    late = join(far, near, base.reshape(32, LATE - 24, LATS))
     late, low, high = lax.optimization_barrier((late, low, high))
 
-    edges = call(edge_body, arr(PLANES, SHELLS, LATS), (low, own, high))
+    blocks = (low, own, high, above, below)
+    edges = call(
+        edge_body,
+        arr(PLANES, TALL, LATS),
+        blocks,
+        scratch=(pltpu.VMEM((PLANES, WIDE, TALL, LATS), F32),),
+    )
     from_low = lax.ppermute(edges, "rad", shift("rad", 1, False))
     from_high = lax.ppermute(edges, "rad", shift("rad", -1, False))
-    blocks = (low, own, high, from_low, from_high)
-    up, down = call(pack_body, (arr(PLANES, 32, LATS), arr(PLANES, 32, LATS)), blocks)
-    below = lax.ppermute(up, "sec", shift("sec", 1, False))
-    above = lax.ppermute(down, "sec", shift("sec", -1, False))
     late = lax.all_to_all(
-        late.reshape(32, LATE, LATS), "lon", split_axis=0, concat_axis=0, tiled=True
+        late, "lon", split_axis=0, concat_axis=0, tiled=True
     )
 
     advanced = call(
         main_body,
         arr(FIELDS, SHELLS * LONS, LATS),
-        blocks + (above, below),
+        blocks + (from_low, from_high),
         scratch=(
             pltpu.VMEM((2, WIDE, TALL, 2 * LATS), F32),
             pltpu.VMEM((7, WIDE, TALL, 2 * LATS), F32),
             pltpu.VMEM((4, WIDE, TALL, 2 * LATS), F32),
-            pltpu.VMEM((TALL, LATS), F32),
         ),
     ).reshape(FIELDS, SHELLS, LONS, LATS)
 

time: 103 us -> 93.8 us (0.911)
  the two profiles are of different devices: /device:TPU:17 before, /device:TPU:57 now
where the time goes in v5:
time: 93.8 us; the launch traced here: 92.2 us
  starting transfers between devices  32.2 us (34%)
  waiting for transfers between devices  24.4 us (26%)
  blocking collectives  20.1 us (21%)
  Pallas kernels  12.2 us (13%)
  local copies, waits for them, and re-layouts  1.59 us (2%)
    all_to_all x1, waiting for transfers between devices, shards(): late = lax.all_to_all(late, 'lon', split_axis=0, concat_axis=0, tiled=True)  11.3 us
    pallas_call x9, Pallas kernels, call(): pl.pallas_call(body, out_shape=out_shape, in_specs=specs, out_specs=[vmem...  11.2 us
    all_gather x1, blocking collectives, shards(): raw = lax.all_gather(raw, 'rad')  10.2 us
    all_to_all x1, blocking collectives, shards(): lax.all_to_all(slots.reshape(4, SENT, LATS), 'rad', split_axis=0, concat_...  9.86 us
    ppermute x1, starting transfers between devices, shards(): high = lax.ppermute(own, 'lon', shift('lon', -1, True))  9.37 us
    ppermute x1, waiting for transfers between devices, shards(): far = lax.ppermute(inner, 'sec', [(0, 3)])  7.61 us
    all_to_all x1, starting transfers between devices, shards(): late = lax.all_to_all(late, 'lon', split_axis=0, concat_axis=0, tiled=True)  6.45 us
    ppermute x1, starting transfers between devices, shards(): above = lax.ppermute(down, 'sec', shift('sec', -1, False))  4.37 us
  transfers between devices with their start and end apart: 9, of which 5 were waited for; matrix products, arithmetic and copies ran while one was open for 0% of the time, Pallas kernels for 7%

profile of v5, /device:TPU:57, one launch (start us, length us, event | category | flops | bytes accessed | tf_op | source)
XLA Modules:
  0.0 92.2 jit_solution(7682082240558279946)
XLA Ops:
  0.6 0.8 maximum_convert_fusion.speeds
  1.5 0.0 copy-start
  1.5 0.9 %copy-done = f32[8,16,4,128]{3,2,1,0:T(4,128)S(1)} copy-done((f32[8,16,4,128]{3,2,1,0:T(4,128)S(1)}, f32[8,16,4,128]{3,2,1,0:T(4,128)}, u32[]{:S(2)}) %copy-start) | copy-done | bytes 262168
  2.4 0.0 copy-start.1
  2.4 0.0 copy-start.2
  2.5 4.1 %collective-permute-start = (f32[12,4,16,128]{3,2,1,0:T(8,128)S(1)}, f32[12,4,16,128]{3,2,1,0:T(8,128)S(1)}, u32[]{:S(2)}, u32[]{:S(2)}) collective-permute-start(f32[12,4,16,128]{3,2,1,0:T(8,128)S(1)} %shard_map.94.own), channel_id=1, source_target_pairs={{0,16},{16,32},{32,48},{48,64},{64,80},{80,96},{96,112},{112,128},... | collective-permute-start | bytes 1179656 | tf_op jit(solution)/shard_map/ppermute | solution.py:436
  6.6 9.4 %collective-permute-start.1 = (f32[12,4,16,128]{3,2,1,0:T(8,128)S(1)}, f32[12,4,16,128]{3,2,1,0:T(8,128)S(1)}, u32[]{:S(2)}, u32[]{:S(2)}) collective-permute-start(f32[12,4,16,128]{3,2,1,0:T(8,128)S(1)} %shard_map.94.own), channel_id=1, source_target_pairs={{0,496},{16,0},{32,16},{48,32},{64,48},{80,64},{96,80},{112,96},{1... | collective-permute-start | bytes 1179656 | tf_op jit(solution)/shard_map/ppermute | solution.py:437
  16.0 0.0 copy-start.3
  16.0 0.0 copy-start.4
  16.0 0.0 copy-done.1
  16.0 0.0 copy-done.2
  16.0 0.6 copy-done.3
  16.6 0.0 copy-done.4
  16.7 0.3 shard_map.95
  17.0 9.9 %all_to_all.10 = f32[4,168,128]{2,1,0:T(8,128)S(1)} all-to-all(f32[4,168,128]{2,1,0:T(8,128)S(1)} %bitcast.17), channel_id=1, replica_groups=mesh['lon'=32,'sec'=4,'rad'=4] {'rad'}, dimensions={0} | all-to-all | bytes 688128 | tf_op jit(solution)/shard_map/all_to_all | solution.py:444
  26.9 0.0 collective-permute-done.low
  26.9 0.0 collective-permute-done.1.high
  26.9 0.1 shard_map.97
  27.0 4.4 %collective-permute-start.2 = (f32[12,32,128]{2,1,0:T(8,128)S(1)}, f32[12,32,128]{2,1,0:T(8,128)S(1)}, u32[]{:S(2)}, u32[]{:S(2)}) collective-permute-start(f32[12,32,128]{2,1,0:T(8,128)S(1)} %get-tuple-element.18), channel_id=1, source_target_pairs={{4,0},{8,4},{12,8},{5,1},{9,5},{13,9},{6,2},{10,6},{14,10},{7,3},{... | collective-permute-start | bytes 589832 | tf_op jit(solution)/shard_map/ppermute | solution.py:451
  31.3 1.3 %collective-permute-start.3 = (f32[12,32,128]{2,1,0:T(8,128)S(1)}, f32[12,32,128]{2,1,0:T(8,128)S(1)}, u32[]{:S(2)}, u32[]{:S(2)}) collective-permute-start(f32[12,32,128]{2,1,0:T(8,128)S(1)} %get-tuple-element.19), channel_id=1, source_target_pairs={{0,4},{4,8},{8,12},{1,5},{5,9},{9,13},{2,6},{6,10},{10,14},{3,7},{... | collective-permute-start | bytes 589832 | tf_op jit(solution)/shard_map/ppermute | solution.py:450
  32.7 10.2 %all-gather = f32[768,128]{1,0:T(8,128)S(1)} all-gather(f32[192,128]{1,0:T(8,128)S(1)} %shard_map.96), channel_id=2, replica_groups=mesh['lon'=32,'sec'=4,'rad'=4] {'rad'}, dimensions={0}, use_global_device_ids=true | all-gather | bytes 491520 | tf_op jit(solution)/shard_map/all_gather | solution.py:453
  42.9 0.0 collective-permute-done.2.above
  42.9 0.0 collective-permute-done.3.below
  42.9 0.8 shard_map.98
  43.8 1.3 %collective-permute-start.4 = (f32[24,128]{1,0:T(8,128)S(1)}, f32[24,128]{1,0:T(8,128)S(1)}, u32[]{:S(2)}, u32[]{:S(2)}) collective-permute-start(f32[24,128]{1,0:T(8,128)S(1)} %shard_map.98), channel_id=1, source_target_pairs={{0,12},{1,13},{2,14},{3,15},{16,28},{17,29},{18,30},{19,31},{32,44... | collective-permute-start | bytes 36872 | tf_op jit(solution)/shard_map/ppermute | solution.py:461
  45.1 7.6 %collective-permute-done.4 = f32[24,128]{1,0:T(8,128)S(1)} collective-permute-done((f32[24,128]{1,0:T(8,128)S(1)}, f32[24,128]{1,0:T(8,128)S(1)}, u32[]{:S(2)}, u32[]{:S(2)}) %collective-permute-start.4) | collective-permute-done | bytes 12320 | tf_op jit(solution)/shard_map/ppermute | solution.py:461
  52.7 1.3 %collective-permute-start.5 = (f32[24,128]{1,0:T(8,128)S(1)}, f32[24,128]{1,0:T(8,128)S(1)}, u32[]{:S(2)}, u32[]{:S(2)}) collective-permute-start(f32[24,128]{1,0:T(8,128)S(1)} %broadcast_select_fusion.one), channel_id=1, source_target_pairs={{0,4},{12,8},{1,5},{13,9},{2,6},{14,10},{3,7},{15,11},{16,20},{28,... | collective-permute-start | bytes 36872 | tf_op jit(solution)/shard_map/ppermute | solution.py:463
  54.0 0.1 shard_map.99
  54.1 0.7 collective-permute-done.5.two
  54.8 1.0 %shard_map.100 = f32[32,64,128]{2,1,0:T(8,128)} custom-call(f32[24,128]{1,0:T(8,128)S(1)} %broadcast_select_fusion.one, f32[24,128]{1,0:T(8,128)S(1)} %collective-permute-done.5.two, f32[32,40,128]{2,1,0:T(8,128)S(1)} %bitcast.16), custom_call_target="tpu_custom_call" | custom-call | flops 100000 | bytes 1000000 | tf_op jit(solution)/shard_map/pallas_call | solution.py:213
  55.8 6.4 %all-to-all-start.1 = ((f32[32,64,128]{2,1,0:T(8,128)}), f32[32,64,128]{2,1,0:T(8,128)S(1)}, u32[]{:S(2)}, u32[]{:S(2)}) async-start(f32[32,64,128]{2,1,0:T(8,128)} %shard_map.100), calls=%async_computation.1 | async-start | bytes 2097152 | tf_op jit(solution)/shard_map/all_to_all | solution.py:477
  62.3 0.5 shard_map.101
  62.8 2.7 %collective-permute-start.6 = (f32[12,24,128]{2,1,0:T(8,128)S(1)}, f32[12,24,128]{2,1,0:T(8,128)S(1)}, u32[]{:S(2)}, u32[]{:S(2)}) collective-permute-start(f32[12,24,128]{2,1,0:T(8,128)S(1)} %shard_map.101), channel_id=1, source_target_pairs={{0,1},{1,2},{2,3},{4,5},{5,6},{6,7},{8,9},{9,10},{10,11},{12,13},{... | collective-permute-start | bytes 442376 | tf_op jit(solution)/shard_map/ppermute | solution.py:475
  65.5 1.3 %collective-permute-start.7 = (f32[12,24,128]{2,1,0:T(8,128)S(1)}, f32[12,24,128]{2,1,0:T(8,128)S(1)}, u32[]{:S(2)}, u32[]{:S(2)}) collective-permute-start(f32[12,24,128]{2,1,0:T(8,128)S(1)} %shard_map.101), channel_id=1, source_target_pairs={{1,0},{2,1},{3,2},{5,4},{6,5},{7,6},{9,8},{10,9},{11,10},{13,12},{... | collective-permute-start | bytes 442376 | tf_op jit(solution)/shard_map/ppermute | solution.py:476
  66.8 0.1 pad_add_fusion.spot
  66.9 0.7 collective-permute-done.6.from_low
  67.5 4.1 %collective-permute-done.7.from_high = f32[12,24,128]{2,1,0:T(8,128)S(1)} collective-permute-done((f32[12,24,128]{2,1,0:T(8,128)S(1)}, f32[12,24,128]{2,1,0:T(8,128)S(1)}, u32[]{:S(2)}, u32[]{:S(2)}) %collective-permute-start.7) | collective-permute-done | bytes 147488 | tf_op jit(solution)/shard_map/ppermute | solution.py:476
  71.7 5.5 %shard_map.102 = f32[8,64,128]{2,1,0:T(8,128)} custom-call(f32[12,4,16,128]{3,2,1,0:T(8,128)S(1)} %collective-permute-done.low, f32[12,4,16,128]{3,2,1,0:T(8,128)S(1)} %shard_map.94.own, f32[12,4,16,128]{3,2,1,0:T(8,128)S(1)} %collective-permute-done.1.high, f32[12,32,128]{2,1,0:T(8,128)S(1)} %collective-permute-done.2.above, ...), custom_call_target="tpu_custom_call" | custom-call | flops 1000000 | bytes 1000000 | tf_op jit(solution)/shard_map/pallas_call | solution.py:35
  77.1 11.3 %all-to-all-done.1 = f32[32,64,128]{2,1,0:T(8,128)S(1)} async-done(((f32[32,64,128]{2,1,0:T(8,128)}), f32[32,64,128]{2,1,0:T(8,128)S(1)}, u32[]{:S(2)}, u32[]{:S(2)}) %all-to-all-start.1) | async-done | bytes 1048608 | tf_op jit(solution)/shard_map/all_to_all | solution.py:477
  88.4 3.8 %shard_map.103 = (f32[4,128]{1,0:T(4,128)}, f32[32,256]{1,0:T(8,128)}) custom-call(s32[3]{0:T(128)S(1)} %pad_add_fusion.spot, f32[2048,128]{1,0:T(8,128)S(1)} %bitcast.15), custom_call_target="tpu_custom_call" | custom-call | flops 1000000 | bytes 1000000 | tf_op jit(solution)/shard_map/pallas_call | solution.py:35
  (3 shorter events, 0.1 us)
Async XLA Ops:
  1.5 1.0 %copy-start = (f32[8,16,4,128]{3,2,1,0:T(4,128)S(1)}, f32[8,16,4,128]{3,2,1,0:T(4,128)}, u32[]{:S(2)}) copy-start(f32[8,16,4,128]{3,2,1,0:T(4,128)} %param.7) | copy-start | bytes 786436
  2.4 13.6 %copy-start.1 = (s32[128,256]{1,0:T(8,128)S(1)}, s32[128,256]{1,0:T(8,128)}, u32[]{:S(2)}) copy-start(s32[128,256]{1,0:T(8,128)} %maps.1) | copy-start | bytes 393220
  2.4 13.6 %copy-start.2 = (f32[4,128]{1,0:T(4,128)S(1)}, f32[4,128]{1,0:T(4,128)}, u32[]{:S(2)}) copy-start(f32[4,128]{1,0:T(4,128)} %conductance.1) | copy-start | bytes 6148
  2.5 24.4 %collective-permute-start = (f32[12,4,16,128]{3,2,1,0:T(8,128)S(1)}, f32[12,4,16,128]{3,2,1,0:T(8,128)S(1)}, u32[]{:S(2)}, u32[]{:S(2)}) collective-permute-start(f32[12,4,16,128]{3,2,1,0:T(8,128)S(1)} %shard_map.94.own), channel_id=1, source_target_pairs={{0,16},{16,32},{32,48},{48,64},{64,80},{80,96},{96,112},{112,128},... | collective-permute-start | bytes 1179656 | tf_op jit(solution)/shard_map/ppermute | solution.py:436
  6.6 20.3 %collective-permute-start.1 = (f32[12,4,16,128]{3,2,1,0:T(8,128)S(1)}, f32[12,4,16,128]{3,2,1,0:T(8,128)S(1)}, u32[]{:S(2)}, u32[]{:S(2)}) collective-permute-start(f32[12,4,16,128]{3,2,1,0:T(8,128)S(1)} %shard_map.94.own), channel_id=1, source_target_pairs={{0,496},{16,0},{32,16},{48,32},{64,48},{80,64},{96,80},{112,96},{1... | collective-permute-start | bytes 1179656 | tf_op jit(solution)/shard_map/ppermute | solution.py:437
  16.0 0.7 copy-start.3
  16.0 0.7 copy-start.4
  27.0 15.9 %collective-permute-start.2 = (f32[12,32,128]{2,1,0:T(8,128)S(1)}, f32[12,32,128]{2,1,0:T(8,128)S(1)}, u32[]{:S(2)}, u32[]{:S(2)}) collective-permute-start(f32[12,32,128]{2,1,0:T(8,128)S(1)} %get-tuple-element.18), channel_id=1, source_target_pairs={{4,0},{8,4},{12,8},{5,1},{9,5},{13,9},{6,2},{10,6},{14,10},{7,3},{... | collective-permute-start | bytes 589832 | tf_op jit(solution)/shard_map/ppermute | solution.py:451
  31.3 11.6 %collective-permute-start.3 = (f32[12,32,128]{2,1,0:T(8,128)S(1)}, f32[12,32,128]{2,1,0:T(8,128)S(1)}, u32[]{:S(2)}, u32[]{:S(2)}) collective-permute-start(f32[12,32,128]{2,1,0:T(8,128)S(1)} %get-tuple-element.19), channel_id=1, source_target_pairs={{0,4},{4,8},{8,12},{1,5},{5,9},{9,13},{2,6},{6,10},{10,14},{3,7},{... | collective-permute-start | bytes 589832 | tf_op jit(solution)/shard_map/ppermute | solution.py:450
  43.8 8.9 %collective-permute-start.4 = (f32[24,128]{1,0:T(8,128)S(1)}, f32[24,128]{1,0:T(8,128)S(1)}, u32[]{:S(2)}, u32[]{:S(2)}) collective-permute-start(f32[24,128]{1,0:T(8,128)S(1)} %shard_map.98), channel_id=1, source_target_pairs={{0,12},{1,13},{2,14},{3,15},{16,28},{17,29},{18,30},{19,31},{32,44... | collective-permute-start | bytes 36872 | tf_op jit(solution)/shard_map/ppermute | solution.py:461
  52.7 2.1 %collective-permute-start.5 = (f32[24,128]{1,0:T(8,128)S(1)}, f32[24,128]{1,0:T(8,128)S(1)}, u32[]{:S(2)}, u32[]{:S(2)}) collective-permute-start(f32[24,128]{1,0:T(8,128)S(1)} %broadcast_select_fusion.one), channel_id=1, source_target_pairs={{0,4},{12,8},{1,5},{13,9},{2,6},{14,10},{3,7},{15,11},{16,20},{28,... | collective-permute-start | bytes 36872 | tf_op jit(solution)/shard_map/ppermute | solution.py:463
  55.8 32.6 %all-to-all-start.1 = ((f32[32,64,128]{2,1,0:T(8,128)}), f32[32,64,128]{2,1,0:T(8,128)S(1)}, u32[]{:S(2)}, u32[]{:S(2)}) async-start(f32[32,64,128]{2,1,0:T(8,128)} %shard_map.100), calls=%async_computation.1 | async-start | bytes 2097152 | tf_op jit(solution)/shard_map/all_to_all | solution.py:477
  62.8 4.8 %collective-permute-start.6 = (f32[12,24,128]{2,1,0:T(8,128)S(1)}, f32[12,24,128]{2,1,0:T(8,128)S(1)}, u32[]{:S(2)}, u32[]{:S(2)}) collective-permute-start(f32[12,24,128]{2,1,0:T(8,128)S(1)} %shard_map.101), channel_id=1, source_target_pairs={{0,1},{1,2},{2,3},{4,5},{5,6},{6,7},{8,9},{9,10},{10,11},{12,13},{... | collective-permute-start | bytes 442376 | tf_op jit(solution)/shard_map/ppermute | solution.py:475
  65.5 6.2 %collective-permute-start.7 = (f32[12,24,128]{2,1,0:T(8,128)S(1)}, f32[12,24,128]{2,1,0:T(8,128)S(1)}, u32[]{:S(2)}, u32[]{:S(2)}) collective-permute-start(f32[12,24,128]{2,1,0:T(8,128)S(1)} %shard_map.101), channel_id=1, source_target_pairs={{1,0},{2,1},{3,2},{5,4},{6,5},{7,6},{9,8},{10,9},{11,10},{13,12},{... | collective-permute-start | bytes 442376 | tf_op jit(solution)/shard_map/ppermute | solution.py:476

commit v6 on v5

--- a/solution.py
+++ b/solution.py
@@ -18,7 +18,8 @@
 LONS = 4
 LATS = 128
 WIDE = 3 * LONS
-LATE = 64
+LATE = 40
+HALF = 24
 RAW = 192
 SENT = 168
 TALL = SHELLS + 2 * PHASES
@@ -175,50 +176,66 @@
             source = source - blat[lon - 1]
         for rad in range(4):
             part = slice(rad * LATS, (rad + 1) * LATS)
-            out[rad * 4 + lon : rad * 4 + lon + 1, :] = source[0:1, part]
+            at = rad // 2 * 12 + rad % 2 * 4 + lon
+            out[at : at + 1, :] = source[0:1, part]
+            at = rad // 2 * 12 + 8 + rad % 2
             if lon == 0:
-                out[16 + rad : 17 + rad, :] = blat[0][0:1, part]
+                out[at : at + 1, :] = blat[0][0:1, part]
             if lon == LONS - 1:
-                out[20 + rad : 21 + rad, :] = blat[LONS - 1][0:1, part]
-
-
-def base_body(sent, out):
-    step = LATE - 24
+                out[at + 2 : at + 3, :] = blat[LONS - 1][0:1, part]
+
+
+def base_body(spot, sent, out, cond):
+    step = LATE - 16
+    odd = spot[0] % 2 == 1
+    for lon in range(LONS):
+        at = 160 + lon
+        lines = [sent[rad * SENT + at : rad * SENT + at + 1, :] for rad in range(4)]
+        cond[lon : lon + 1, :] = jnp.where(odd, lines[2], lines[0])
+        line = jnp.where(odd, lines[3], lines[1])
+        out[pl.ds(lon, 32, stride=step), :] = jnp.broadcast_to(line, (32, LATS))
     for rad in range(4):
-        for lon in range(LONS):
-            line = sent[rad * SENT + 160 + lon : rad * SENT + 161 + lon, :]
-            out[pl.ds(rad * 4 + lon, 32, stride=step), :] = jnp.broadcast_to(line, (32, LATS))
         for row in range(5):
             at = rad * SENT + row * 32
-            out[pl.ds(16 + rad * 5 + row, 32, stride=step), :] = sent[at : at + 32, :]
-    for spare in range(36, step):
-        out[pl.ds(spare, 32, stride=step), :] = jnp.zeros((32, LATS), F32)
-
-
-def join_body(one, two, base, out, copies, sems):
-    rest = pltpu.make_async_copy(base, out.at[:, pl.ds(24, LATE - 24), :], sems.at[0])
+            out[pl.ds(4 + rad * 5 + row, 32, stride=step), :] = sent[at : at + 32, :]
+
+
+def join_body(spot, one, two, cond, base, out, head, copies, sems):
+    rest = pltpu.make_async_copy(base, out.at[:, pl.ds(16, LATE - 16), :], sems.at[0])
     rest.start()
     source = one[...] + two[...]
+    head[:12, :] = jnp.where(spot[0] % 2 == 1, source[12:], source[:12])
+    head[12:, :] = cond[...]
+    mine = head[...]
     for owner in range(32):
-        copies[owner] = source
-    move = pltpu.make_async_copy(copies, out.at[:, pl.ds(0, 24), :], sems.at[1])
+        copies[owner] = mine
+    move = pltpu.make_async_copy(copies, out.at[:, pl.ds(0, 16), :], sems.at[1])
     move.start()
     move.wait()
     rest.wait()
 
 
-def join(one, two, base):
+def join(spot, one, two, cond, base):
     vmem = pl.BlockSpec(memory_space=pltpu.VMEM)
     plain = pl.BlockSpec(memory_space=pl.ANY)
     return pl.pallas_call(
         join_body,
         out_shape=arr(32, LATE, LATS),
-        in_specs=[vmem, vmem, plain],
+        in_specs=[pl.BlockSpec(memory_space=pltpu.SMEM), vmem, vmem, vmem, plain],
         out_specs=plain,
-        scratch_shapes=[pltpu.VMEM((32, 24, LATS), F32), pltpu.SemaphoreType.DMA((2,))],
+        scratch_shapes=[
+            pltpu.VMEM((16, LATS), F32),
+            pltpu.VMEM((32, 16, LATS), F32),
+            pltpu.SemaphoreType.DMA((2,)),
+        ],
         compiler_params=pltpu.CompilerParams(vmem_limit_bytes=4 * 2**20),
         cost_estimate=pl.CostEstimate(flops=10**5, bytes_accessed=10**6, transcendentals=0),
-    )(one, two, base)
+    )(spot, one, two, cond, base)
+
+
+def half_body(late, out):
+    for owner in range(32):
+        out[owner] = late[owner, :HALF, :]
 
 
 def chunks():
@@ -326,15 +343,21 @@
         out[at + 4 : at + 8, :] = jnp.zeros((4, LATS), F32)
 
 
-def final_body(spot, late, pot, foot, phi, east_w, west_w, north_w, south_w, start, picked, hot):
+def final_body(spot, late, other, pot, foot, phi, east_w, west_w, north_w, south_w, start, picked, hot):
     devs, rads = 32, 4
     wide = rads * LATS
     lane = lax.broadcasted_iota(jnp.int32, (devs, wide), 1)
 
-    def gather(ref, at, step, stride):
-        return jnp.concatenate(
-            [ref[pl.ds(at + rad * step, devs, stride=stride), :] for rad in range(rads)], axis=1
-        )
+    odd = spot[0] % 2
+
+    def gather(at, step):
+        found = []
+        for rad in range(rads):
+            row = at + rad % 2 * step
+            mine = late[pl.ds(row, devs, stride=LATE), :]
+            theirs = other[pl.ds(row, devs, stride=HALF), :]
+            found.append(jnp.where(odd == rad // 2, mine, theirs))
+        return jnp.concatenate(found, axis=1)
 
     def lon_up(values, lon):
         return values[lon + 1] if lon < LONS - 1 else pltpu.roll(values[0], devs - 1, axis=0)
@@ -348,10 +371,10 @@
     def lat_down(value):
         return pltpu.roll(value, 1, axis=1)
 
-    cond = [gather(late, 24 + lon, 4, LATE) for lon in range(LONS)]
-    sources = [gather(late, lon, 4, LATE) for lon in range(LONS)]
-    sources[LONS - 1] += pltpu.roll(gather(late, 16, 1, LATE), devs - 1, axis=0)
-    sources[0] -= pltpu.roll(gather(late, 20, 1, LATE), 1, axis=0)
+    cond = [gather(12 + lon, 4) for lon in range(LONS)]
+    sources = [gather(lon, 4) for lon in range(LONS)]
+    sources[LONS - 1] += pltpu.roll(gather(8, 1), devs - 1, axis=0)
+    sources[0] -= pltpu.roll(gather(10, 1), 1, axis=0)
     last, first = lane == wide - 1, lane == 0
     for lon in range(LONS):
         source = sources[lon]
@@ -396,13 +419,13 @@
     slot_lane = lax.broadcasted_iota(jnp.int32, (devs, LATS), 1).astype(F32)
     for rad in range(rads):
         table = [phi[done, lon, :, rad * LATS : (rad + 1) * LATS] for lon in range(LONS)]
-        marks = late[pl.ds(40 + rad * 5 + 4, devs, stride=LATE), :]
+        marks = late[pl.ds(20 + rad * 5 + 4, devs, stride=LATE), :]
         for slot in range(2):
             at = (slot * rads + rad) * devs
             row = marks if slot == 0 else pltpu.roll(marks, 64, axis=1)
             hot[at : at + devs, :] = jnp.where(row == slot_lane, 1.0, 0.0)
             for half in range(2):
-                cell = late[pl.ds(40 + rad * 5 + 2 * slot + half, devs, stride=LATE), :].astype(jnp.int32)
+                cell = late[pl.ds(20 + rad * 5 + 2 * slot + half, devs, stride=LATE), :].astype(jnp.int32)
                 place, lon_at = cell & 127, cell >> 7
                 value = jnp.zeros((devs, LATS), F32)
                 for lon in range(LONS):
@@ -461,8 +484,13 @@
     far = lax.ppermute(inner, "sec", [(0, 3)])
     far = jnp.where(lax.axis_index("sec") == 0, inner, far)
     near = lax.ppermute(far, "sec", [(0, 1), (3, 2)])
-    base = call(base_body, arr(32 * (LATE - 24), LATS), (sent.reshape(4 * SENT, LATS),))
-    late = join(far, near, base.reshape(32, LATE - 24, LATS))
+    base, cond = call(
+        base_body,
+        (arr(32 * (LATE - 16), LATS), arr(LONS, LATS)),
+        (spot, sent.reshape(4 * SENT, LATS)),
+        smem=(0,),
+    )
+    late = join(spot, far, near, cond, base.reshape(32, LATE - 16, LATS))
     late, low, high = lax.optimization_barrier((late, low, high))
 
     blocks = (low, own, high, above, below)
@@ -489,11 +517,15 @@
         ),
     ).reshape(FIELDS, SHELLS, LONS, LATS)
 
+    late, advanced = lax.optimization_barrier((late, advanced))
+    other = lax.ppermute(
+        call(half_body, arr(32, HALF, LATS), (late,)), "sec", [(0, 1), (1, 0), (2, 3), (3, 2)]
+    )
     plane = pltpu.VMEM((LONS, 32, 4 * LATS), F32)
     potential, foot_table = call(
         final_body,
         (arr(LONS, LATS), arr(ROWS_OWN, 256)),
-        (spot, late.reshape(32 * LATE, LATS)),
+        (spot, late.reshape(32 * LATE, LATS), other.reshape(32 * HALF, LATS)),
         scratch=(
             pltpu.VMEM((2, LONS, 32, 4 * LATS), F32),
             plane,

time: 93.8 us -> 90 us (0.959); the launches traced: 92.2 us -> 89.5 us
  waiting for transfers between devices: 24.4 us -> 18.1 us
  starting transfers between devices: 32.2 us -> 35.1 us
    all_to_all x1, waiting for transfers between devices: 11.3 us -> 4.11 us  [shards(): late = lax.all_to_all(late, 'lon', split_axis=0, concat_axis=0, tiled=True)]
    ppermute x0 -> x1, starting transfers between devices: none -> 2.87 us  [shards(): lax.ppermute(call(half_body, arr(32, HALF, LATS), (late,)), 'sec', [(0, 1...]
    ppermute x0 -> x1, waiting for transfers between devices: none -> 1.33 us  [shards(): lax.ppermute(call(half_body, arr(32, HALF, LATS), (late,)), 'sec', [(0, 1...]
    pallas_call x9 -> x10, Pallas kernels: 11.2 us -> 11.5 us  [call(): pl.pallas_call(body, out_shape=out_shape, in_specs=specs, out_specs=[vmem...]
  transfers between devices with their start and end apart: 9 -> 10, of which waited for: 5 -> 6; matrix products, arithmetic and copies ran while one was open for 0% -> 0% of each run, Pallas kernels for 7% -> 8%
where the time goes in v6:
time: 90 us; the launch traced here: 89.5 us
  starting transfers between devices  35.1 us (39%)
  blocking collectives  20.1 us (22%)
  waiting for transfers between devices  18.1 us (20%)
  Pallas kernels  12.9 us (14%)
  local copies, waits for them, and re-layouts  1.59 us (2%)
  other arithmetic  0.91 us (1%)
    pallas_call x10, Pallas kernels, call(): pl.pallas_call(body, out_shape=out_shape, in_specs=specs, out_specs=[vmem...  11.5 us
    all_gather x1, blocking collectives, shards(): raw = lax.all_gather(raw, 'rad')  10.2 us
    all_to_all x1, blocking collectives, shards(): lax.all_to_all(slots.reshape(4, SENT, LATS), 'rad', split_axis=0, concat_...  9.86 us
    ppermute x1, starting transfers between devices, shards(): high = lax.ppermute(own, 'lon', shift('lon', -1, True))  9.37 us
    ppermute x1, waiting for transfers between devices, shards(): far = lax.ppermute(inner, 'sec', [(0, 3)])  7.61 us
    all_to_all x1, starting transfers between devices, shards(): late = lax.all_to_all(late, 'lon', split_axis=0, concat_axis=0, tiled=True)  6.44 us
    ppermute x1, starting transfers between devices, shards(): above = lax.ppermute(down, 'sec', shift('sec', -1, False))  4.37 us
    ppermute x1, starting transfers between devices, shards(): low = lax.ppermute(own, 'lon', shift('lon', 1, True))  4.13 us
  transfers between devices with their start and end apart: 10, of which 6 were waited for; matrix products, arithmetic and copies ran while one was open for 0% of the time, Pallas kernels for 8%

profile of v6, /device:TPU:57, one launch (start us, length us, event | category | flops | bytes accessed | tf_op | source)
XLA Modules:
  0.0 89.5 jit_solution(6707173143619767580)
XLA Ops:
  0.6 0.8 maximum_convert_fusion.speeds
  1.5 0.0 copy-start
  1.5 0.9 %copy-done = f32[8,16,4,128]{3,2,1,0:T(4,128)S(1)} copy-done((f32[8,16,4,128]{3,2,1,0:T(4,128)S(1)}, f32[8,16,4,128]{3,2,1,0:T(4,128)}, u32[]{:S(2)}) %copy-start) | copy-done | bytes 262168
  2.4 0.0 copy-start.1
  2.4 0.0 copy-start.2
  2.5 4.1 %collective-permute-start = (f32[12,4,16,128]{3,2,1,0:T(8,128)S(1)}, f32[12,4,16,128]{3,2,1,0:T(8,128)S(1)}, u32[]{:S(2)}, u32[]{:S(2)}) collective-permute-start(f32[12,4,16,128]{3,2,1,0:T(8,128)S(1)} %shard_map.94.own), channel_id=1, source_target_pairs={{0,16},{16,32},{32,48},{48,64},{64,80},{80,96},{96,112},{112,128},... | collective-permute-start | bytes 1179656 | tf_op jit(solution)/shard_map/ppermute | solution.py:459
  6.6 9.4 %collective-permute-start.1 = (f32[12,4,16,128]{3,2,1,0:T(8,128)S(1)}, f32[12,4,16,128]{3,2,1,0:T(8,128)S(1)}, u32[]{:S(2)}, u32[]{:S(2)}) collective-permute-start(f32[12,4,16,128]{3,2,1,0:T(8,128)S(1)} %shard_map.94.own), channel_id=1, source_target_pairs={{0,496},{16,0},{32,16},{48,32},{64,48},{80,64},{96,80},{112,96},{1... | collective-permute-start | bytes 1179656 | tf_op jit(solution)/shard_map/ppermute | solution.py:460
  16.0 0.0 copy-start.3
  16.0 0.0 copy-start.4
  16.0 0.0 copy-done.1
  16.0 0.0 copy-done.2
  16.0 0.6 copy-done.3
  16.6 0.0 copy-done.4
  16.7 0.3 shard_map.95
  17.0 9.9 %all_to_all.10 = f32[4,168,128]{2,1,0:T(8,128)S(1)} all-to-all(f32[4,168,128]{2,1,0:T(8,128)S(1)} %bitcast.18), channel_id=1, replica_groups=mesh['lon'=32,'sec'=4,'rad'=4] {'rad'}, dimensions={0} | all-to-all | bytes 688128 | tf_op jit(solution)/shard_map/all_to_all | solution.py:467
  26.9 0.0 collective-permute-done.low
  26.9 0.0 collective-permute-done.1.high
  26.9 0.1 shard_map.97
  27.0 4.4 %collective-permute-start.2 = (f32[12,32,128]{2,1,0:T(8,128)S(1)}, f32[12,32,128]{2,1,0:T(8,128)S(1)}, u32[]{:S(2)}, u32[]{:S(2)}) collective-permute-start(f32[12,32,128]{2,1,0:T(8,128)S(1)} %get-tuple-element.22), channel_id=1, source_target_pairs={{4,0},{8,4},{12,8},{5,1},{9,5},{13,9},{6,2},{10,6},{14,10},{7,3},{... | collective-permute-start | bytes 589832 | tf_op jit(solution)/shard_map/ppermute | solution.py:474
  31.3 1.3 %collective-permute-start.3 = (f32[12,32,128]{2,1,0:T(8,128)S(1)}, f32[12,32,128]{2,1,0:T(8,128)S(1)}, u32[]{:S(2)}, u32[]{:S(2)}) collective-permute-start(f32[12,32,128]{2,1,0:T(8,128)S(1)} %get-tuple-element.23), channel_id=1, source_target_pairs={{0,4},{4,8},{8,12},{1,5},{5,9},{9,13},{2,6},{6,10},{10,14},{3,7},{... | collective-permute-start | bytes 589832 | tf_op jit(solution)/shard_map/ppermute | solution.py:473
  32.7 10.2 %all-gather = f32[768,128]{1,0:T(8,128)S(1)} all-gather(f32[192,128]{1,0:T(8,128)S(1)} %shard_map.96), channel_id=2, replica_groups=mesh['lon'=32,'sec'=4,'rad'=4] {'rad'}, dimensions={0}, use_global_device_ids=true | all-gather | bytes 491520 | tf_op jit(solution)/shard_map/all_gather | solution.py:476
  42.9 0.0 collective-permute-done.2.above
  42.9 0.0 collective-permute-done.3.below
  42.9 0.8 shard_map.98
  43.8 1.3 %collective-permute-start.4 = (f32[24,128]{1,0:T(8,128)S(1)}, f32[24,128]{1,0:T(8,128)S(1)}, u32[]{:S(2)}, u32[]{:S(2)}) collective-permute-start(f32[24,128]{1,0:T(8,128)S(1)} %shard_map.98), channel_id=1, source_target_pairs={{0,12},{1,13},{2,14},{3,15},{16,28},{17,29},{18,30},{19,31},{32,44... | collective-permute-start | bytes 36872 | tf_op jit(solution)/shard_map/ppermute | solution.py:484
  45.1 7.6 %collective-permute-done.4 = f32[24,128]{1,0:T(8,128)S(1)} collective-permute-done((f32[24,128]{1,0:T(8,128)S(1)}, f32[24,128]{1,0:T(8,128)S(1)}, u32[]{:S(2)}, u32[]{:S(2)}) %collective-permute-start.4) | collective-permute-done | bytes 12320 | tf_op jit(solution)/shard_map/ppermute | solution.py:484
  52.7 1.3 %collective-permute-start.5 = (f32[24,128]{1,0:T(8,128)S(1)}, f32[24,128]{1,0:T(8,128)S(1)}, u32[]{:S(2)}, u32[]{:S(2)}) collective-permute-start(f32[24,128]{1,0:T(8,128)S(1)} %broadcast_select_fusion.one), channel_id=1, source_target_pairs={{0,4},{12,8},{1,5},{13,9},{2,6},{14,10},{3,7},{15,11},{16,20},{28,... | collective-permute-start | bytes 36872 | tf_op jit(solution)/shard_map/ppermute | solution.py:486
  54.0 0.1 pad_add_fusion.spot
  54.1 0.6 shard_map.99
  54.7 0.1 collective-permute-done.5.two
  54.8 1.4 %shard_map.100 = f32[32,40,128]{2,1,0:T(8,128)} custom-call(s32[3]{0:T(128)S(1)} %pad_add_fusion.spot, f32[24,128]{1,0:T(8,128)S(1)} %broadcast_select_fusion.one, f32[24,128]{1,0:T(8,128)S(1)} %collective-permute-done.5.two, f32[4,128]{1,0:T(4,128)S(1)} %get-tuple-element.26.cond, f32[32,24,128]{2,1,0:T(8,128)S(1)} %bitcast.19), custom_call_target="tpu_custom_call" | custom-call | flops 100000 | bytes 1000000 | tf_op jit(solution)/shard_map/pallas_call | solution.py:221
  56.2 6.4 %all-to-all-start.1 = ((f32[32,40,128]{2,1,0:T(8,128)}), f32[32,40,128]{2,1,0:T(8,128)S(1)}, u32[]{:S(2)}, u32[]{:S(2)}) async-start(f32[32,40,128]{2,1,0:T(8,128)} %shard_map.100), calls=%async_computation.1 | async-start | bytes 1310720 | tf_op jit(solution)/shard_map/all_to_all | solution.py:505
  62.7 0.5 shard_map.101
  63.2 2.7 %collective-permute-start.6 = (f32[12,24,128]{2,1,0:T(8,128)S(1)}, f32[12,24,128]{2,1,0:T(8,128)S(1)}, u32[]{:S(2)}, u32[]{:S(2)}) collective-permute-start(f32[12,24,128]{2,1,0:T(8,128)S(1)} %shard_map.101), channel_id=1, source_target_pairs={{0,1},{1,2},{2,3},{4,5},{5,6},{6,7},{8,9},{9,10},{10,11},{12,13},{... | collective-permute-start | bytes 442376 | tf_op jit(solution)/shard_map/ppermute | solution.py:503
  65.9 1.3 %collective-permute-start.7 = (f32[12,24,128]{2,1,0:T(8,128)S(1)}, f32[12,24,128]{2,1,0:T(8,128)S(1)}, u32[]{:S(2)}, u32[]{:S(2)}) collective-permute-start(f32[12,24,128]{2,1,0:T(8,128)S(1)} %shard_map.101), channel_id=1, source_target_pairs={{1,0},{2,1},{3,2},{5,4},{6,5},{7,6},{9,8},{10,9},{11,10},{13,12},{... | collective-permute-start | bytes 442376 | tf_op jit(solution)/shard_map/ppermute | solution.py:504
  67.2 0.8 collective-permute-done.6.from_low
  68.0 4.1 %collective-permute-done.7.from_high = f32[12,24,128]{2,1,0:T(8,128)S(1)} collective-permute-done((f32[12,24,128]{2,1,0:T(8,128)S(1)}, f32[12,24,128]{2,1,0:T(8,128)S(1)}, u32[]{:S(2)}, u32[]{:S(2)}) %collective-permute-start.7) | collective-permute-done | bytes 147488 | tf_op jit(solution)/shard_map/ppermute | solution.py:504
  72.1 5.5 %shard_map.102 = f32[8,64,128]{2,1,0:T(8,128)} custom-call(f32[12,4,16,128]{3,2,1,0:T(8,128)S(1)} %collective-permute-done.low, f32[12,4,16,128]{3,2,1,0:T(8,128)S(1)} %shard_map.94.own, f32[12,4,16,128]{3,2,1,0:T(8,128)S(1)} %collective-permute-done.1.high, f32[12,32,128]{2,1,0:T(8,128)S(1)} %collective-permute-done.2.above, ...), custom_call_target="tpu_custom_call" | custom-call | flops 1000000 | bytes 1000000 | tf_op jit(solution)/shard_map/pallas_call | solution.py:36
  77.5 4.1 %all-to-all-done.1.late = f32[32,40,128]{2,1,0:T(8,128)S(1)} async-done(((f32[32,40,128]{2,1,0:T(8,128)}), f32[32,40,128]{2,1,0:T(8,128)S(1)}, u32[]{:S(2)}, u32[]{:S(2)}) %all-to-all-start.1) | async-done | bytes 655392 | tf_op jit(solution)/shard_map/all_to_all | solution.py:505
  81.7 2.9 %collective-permute-start.8 = (f32[32,24,128]{2,1,0:T(8,128)S(1)}, f32[32,24,128]{2,1,0:T(8,128)S(1)}, u32[]{:S(2)}, u32[]{:S(2)}) collective-permute-start(f32[32,24,128]{2,1,0:T(8,128)S(1)} %shard_map.103), channel_id=1, source_target_pairs={{0,4},{4,0},{8,12},{12,8},{1,5},{5,1},{9,13},{13,9},{2,6},{6,2},{1... | collective-permute-start | bytes 1179656 | tf_op jit(solution)/shard_map/ppermute | solution.py:521
  84.5 1.3 %collective-permute-done.8 = f32[32,24,128]{2,1,0:T(8,128)S(1)} collective-permute-done((f32[32,24,128]{2,1,0:T(8,128)S(1)}, f32[32,24,128]{2,1,0:T(8,128)S(1)}, u32[]{:S(2)}, u32[]{:S(2)}) %collective-permute-start.8) | collective-permute-done | bytes 393248 | tf_op jit(solution)/shard_map/ppermute | solution.py:521
  85.9 3.6 %shard_map.104 = (f32[4,128]{1,0:T(4,128)}, f32[32,256]{1,0:T(8,128)}) custom-call(s32[3]{0:T(128)S(1)} %pad_add_fusion.spot, f32[1280,128]{1,0:T(8,128)S(1)} %bitcast.16, f32[768,128]{1,0:T(8,128)S(1)} %bitcast.20), custom_call_target="tpu_custom_call" | custom-call | flops 1000000 | bytes 1000000 | tf_op jit(solution)/shard_map/pallas_call | solution.py:36
  (4 shorter events, 0.1 us)
Async XLA Ops:
  1.5 1.0 %copy-start = (f32[8,16,4,128]{3,2,1,0:T(4,128)S(1)}, f32[8,16,4,128]{3,2,1,0:T(4,128)}, u32[]{:S(2)}) copy-start(f32[8,16,4,128]{3,2,1,0:T(4,128)} %param.7) | copy-start | bytes 786436
  2.4 13.6 %copy-start.1 = (s32[128,256]{1,0:T(8,128)S(1)}, s32[128,256]{1,0:T(8,128)}, u32[]{:S(2)}) copy-start(s32[128,256]{1,0:T(8,128)} %maps.1) | copy-start | bytes 393220
  2.4 13.6 %copy-start.2 = (f32[4,128]{1,0:T(4,128)S(1)}, f32[4,128]{1,0:T(4,128)}, u32[]{:S(2)}) copy-start(f32[4,128]{1,0:T(4,128)} %conductance.1) | copy-start | bytes 6148
  2.5 24.4 %collective-permute-start = (f32[12,4,16,128]{3,2,1,0:T(8,128)S(1)}, f32[12,4,16,128]{3,2,1,0:T(8,128)S(1)}, u32[]{:S(2)}, u32[]{:S(2)}) collective-permute-start(f32[12,4,16,128]{3,2,1,0:T(8,128)S(1)} %shard_map.94.own), channel_id=1, source_target_pairs={{0,16},{16,32},{32,48},{48,64},{64,80},{80,96},{96,112},{112,128},... | collective-permute-start | bytes 1179656 | tf_op jit(solution)/shard_map/ppermute | solution.py:459
  6.6 20.3 %collective-permute-start.1 = (f32[12,4,16,128]{3,2,1,0:T(8,128)S(1)}, f32[12,4,16,128]{3,2,1,0:T(8,128)S(1)}, u32[]{:S(2)}, u32[]{:S(2)}) collective-permute-start(f32[12,4,16,128]{3,2,1,0:T(8,128)S(1)} %shard_map.94.own), channel_id=1, source_target_pairs={{0,496},{16,0},{32,16},{48,32},{64,48},{80,64},{96,80},{112,96},{1... | collective-permute-start | bytes 1179656 | tf_op jit(solution)/shard_map/ppermute | solution.py:460
  16.0 0.7 copy-start.3
  16.0 0.7 copy-start.4
  27.0 15.9 %collective-permute-start.2 = (f32[12,32,128]{2,1,0:T(8,128)S(1)}, f32[12,32,128]{2,1,0:T(8,128)S(1)}, u32[]{:S(2)}, u32[]{:S(2)}) collective-permute-start(f32[12,32,128]{2,1,0:T(8,128)S(1)} %get-tuple-element.22), channel_id=1, source_target_pairs={{4,0},{8,4},{12,8},{5,1},{9,5},{13,9},{6,2},{10,6},{14,10},{7,3},{... | collective-permute-start | bytes 589832 | tf_op jit(solution)/shard_map/ppermute | solution.py:474
  31.3 11.6 %collective-permute-start.3 = (f32[12,32,128]{2,1,0:T(8,128)S(1)}, f32[12,32,128]{2,1,0:T(8,128)S(1)}, u32[]{:S(2)}, u32[]{:S(2)}) collective-permute-start(f32[12,32,128]{2,1,0:T(8,128)S(1)} %get-tuple-element.23), channel_id=1, source_target_pairs={{0,4},{4,8},{8,12},{1,5},{5,9},{9,13},{2,6},{6,10},{10,14},{3,7},{... | collective-permute-start | bytes 589832 | tf_op jit(solution)/shard_map/ppermute | solution.py:473
  43.8 8.9 %collective-permute-start.4 = (f32[24,128]{1,0:T(8,128)S(1)}, f32[24,128]{1,0:T(8,128)S(1)}, u32[]{:S(2)}, u32[]{:S(2)}) collective-permute-start(f32[24,128]{1,0:T(8,128)S(1)} %shard_map.98), channel_id=1, source_target_pairs={{0,12},{1,13},{2,14},{3,15},{16,28},{17,29},{18,30},{19,31},{32,44... | collective-permute-start | bytes 36872 | tf_op jit(solution)/shard_map/ppermute | solution.py:484
  52.7 2.1 %collective-permute-start.5 = (f32[24,128]{1,0:T(8,128)S(1)}, f32[24,128]{1,0:T(8,128)S(1)}, u32[]{:S(2)}, u32[]{:S(2)}) collective-permute-start(f32[24,128]{1,0:T(8,128)S(1)} %broadcast_select_fusion.one), channel_id=1, source_target_pairs={{0,4},{12,8},{1,5},{13,9},{2,6},{14,10},{3,7},{15,11},{16,20},{28,... | collective-permute-start | bytes 36872 | tf_op jit(solution)/shard_map/ppermute | solution.py:486
  56.2 25.4 %all-to-all-start.1 = ((f32[32,40,128]{2,1,0:T(8,128)}), f32[32,40,128]{2,1,0:T(8,128)S(1)}, u32[]{:S(2)}, u32[]{:S(2)}) async-start(f32[32,40,128]{2,1,0:T(8,128)} %shard_map.100), calls=%async_computation.1 | async-start | bytes 1310720 | tf_op jit(solution)/shard_map/all_to_all | solution.py:505
  63.2 4.8 %collective-permute-start.6 = (f32[12,24,128]{2,1,0:T(8,128)S(1)}, f32[12,24,128]{2,1,0:T(8,128)S(1)}, u32[]{:S(2)}, u32[]{:S(2)}) collective-permute-start(f32[12,24,128]{2,1,0:T(8,128)S(1)} %shard_map.101), channel_id=1, source_target_pairs={{0,1},{1,2},{2,3},{4,5},{5,6},{6,7},{8,9},{9,10},{10,11},{12,13},{... | collective-permute-start | bytes 442376 | tf_op jit(solution)/shard_map/ppermute | solution.py:503
  65.9 6.2 %collective-permute-start.7 = (f32[12,24,128]{2,1,0:T(8,128)S(1)}, f32[12,24,128]{2,1,0:T(8,128)S(1)}, u32[]{:S(2)}, u32[]{:S(2)}) collective-permute-start(f32[12,24,128]{2,1,0:T(8,128)S(1)} %shard_map.101), channel_id=1, source_target_pairs={{1,0},{2,1},{3,2},{5,4},{6,5},{7,6},{9,8},{10,9},{11,10},{13,12},{... | collective-permute-start | bytes 442376 | tf_op jit(solution)/shard_map/ppermute | solution.py:504
  81.7 4.2 %collective-permute-start.8 = (f32[32,24,128]{2,1,0:T(8,128)S(1)}, f32[32,24,128]{2,1,0:T(8,128)S(1)}, u32[]{:S(2)}, u32[]{:S(2)}) collective-permute-start(f32[32,24,128]{2,1,0:T(8,128)S(1)} %shard_map.103), channel_id=1, source_target_pairs={{0,4},{4,0},{8,12},{12,8},{1,5},{5,1},{9,13},{13,9},{2,6},{6,2},{1... | collective-permute-start | bytes 1179656 | tf_op jit(solution)/shard_map/ppermute | solution.py:521

commit v7 on v6

--- a/solution.py
+++ b/solution.py
@@ -21,7 +21,7 @@
 LATE = 40
 HALF = 24
 RAW = 192
-SENT = 168
+SENT = 136
 TALL = SHELLS + 2 * PHASES
 F32 = jnp.float32
 
@@ -55,14 +55,47 @@
     ]
 
 
-def stage_body(fields, speeds, out):
+def first_body(*refs):
+    sources, (own, slots, plain), held, sems = refs[:7], refs[7:10], refs[10:17], refs[17]
+    moves = [
+        pltpu.make_async_copy(source, target, sems.at[i])
+        for i, (source, target) in enumerate(zip(sources, held))
+    ]
+    for move in moves:
+        move.start()
+    fields, speeds, resist, owners, rows, maps, conductance = held
+    for move in moves[1:3]:
+        move.wait()
+    for plane in range(4):
+        for shell in range(SHELLS):
+            found = speeds[plane, shell] if plane < 3 else resist[shell]
+            plain[plane, shell * LONS : shell * LONS + LONS, :] = found.astype(F32)
+    moves[0].wait()
     for plane in range(PLANES):
         for lon in range(LONS):
-            rows = pl.ds(lon, SHELLS, stride=LONS)
+            at = pl.ds(lon, SHELLS, stride=LONS)
             if plane < FIELDS:
-                out[plane, lon] = fields[plane, rows, :]
+                own[plane, lon] = fields[plane, at, :]
             else:
-                out[plane, lon] = speeds[plane - FIELDS, rows, :]
+                own[plane, lon] = plain[plane - FIELDS, at, :]
+    for move in moves[3:]:
+        move.wait()
+    slot_body(owners, rows, maps, conductance, slots)
+
+
+def first(*args):
+    vmem = pl.BlockSpec(memory_space=pltpu.VMEM)
+    return pl.pallas_call(
+        first_body,
+        out_shape=(arr(PLANES, LONS, SHELLS, LATS), arr(4 * SENT, LATS)),
+        in_specs=[pl.BlockSpec(memory_space=pltpu.HBM)] * len(args),
+        out_specs=[vmem, vmem],
+        scratch_shapes=[pltpu.VMEM((4, SHELLS * LONS, LATS), F32)]
+        + [pltpu.VMEM(arg.shape, arg.dtype) for arg in args]
+        + [pltpu.SemaphoreType.DMA((len(args),))],
+        compiler_params=pltpu.CompilerParams(vmem_limit_bytes=60 * 2**20),
+        cost_estimate=pl.CostEstimate(flops=10**6, bytes_accessed=10**6, transcendentals=0),
+    )(*args)
 
 
 def edge_body(low, own, high, above, below, edges, tall):
@@ -189,15 +222,25 @@
     step = LATE - 16
     odd = spot[0] % 2 == 1
     for lon in range(LONS):
-        at = 160 + lon
+        at = 130 + lon
         lines = [sent[rad * SENT + at : rad * SENT + at + 1, :] for rad in range(4)]
         cond[lon : lon + 1, :] = jnp.where(odd, lines[2], lines[0])
         line = jnp.where(odd, lines[3], lines[1])
         out[pl.ds(lon, 32, stride=step), :] = jnp.broadcast_to(line, (32, LATS))
+    lane = lax.broadcasted_iota(jnp.int32, (32, LATS), 1)
+    owner = lax.broadcasted_iota(jnp.int32, (32, LATS), 0)
     for rad in range(4):
-        for row in range(5):
+        for row in range(4):
             at = rad * SENT + row * 32
             out[pl.ds(4 + rad * 5 + row, 32, stride=step), :] = sent[at : at + 32, :]
+        marks = []
+        for slot in range(2):
+            at = rad * SENT + 128 + slot
+            line = jnp.broadcast_to(sent[at : at + 1, :], (32, LATS))
+            marks.append(
+                jnp.sum(jnp.where(lane == owner + spot[1] * 32, line, 0.0), axis=1, keepdims=True)
+            )
+        out[pl.ds(8 + rad * 5, 32, stride=step), :] = jnp.where(lane < 64, marks[0], marks[1])
 
 
 def join_body(spot, one, two, cond, base, out, head, copies, sems):
@@ -322,25 +365,27 @@
     cell = maps[...]
     small = (cell & 127).astype(F32).astype(jnp.bfloat16)
     large = (cell >> 7).astype(F32).astype(jnp.bfloat16)
-    row = (rows[...] + 1).astype(F32)
+    row = jnp.broadcast_to((rows[...] + 1).astype(F32), (8, count)).astype(jnp.bfloat16)
     marks = []
     lines = []
     for slot in range(2):
-        chosen = jnp.where(aimed & (earlier == float(slot)), 1.0, 0.0)
-        marks.append(jnp.sum(chosen * row, axis=1, keepdims=True) - 1.0)
-        pick = chosen.astype(jnp.bfloat16)
+        pick = jnp.where(aimed & (earlier == float(slot)), 1.0, 0.0).astype(jnp.bfloat16)
+        marks.append(
+            lax.dot_general(row, pick, (((1,), (1,)), ((), ())), preferred_element_type=F32) - 1.0
+        )
         made = jnp.dot(pick, small, preferred_element_type=F32) + 128.0 * jnp.dot(
             pick, large, preferred_element_type=F32
         )
         lines += [made[:, :128], made[:, 128:]]
-    lines.append(jnp.where(there < 64, marks[0], marks[1]))
     for rad in range(4):
-        for j in range(5):
+        for j in range(4):
             at = rad * SENT + j * 32
             out[at : at + 32, :] = lines[j][rad * 32 : rad * 32 + 32]
-        at = rad * SENT + 160
-        out[at : at + 4, :] = conductance[...]
-        out[at + 4 : at + 8, :] = jnp.zeros((4, LATS), F32)
+        at = rad * SENT + 128
+        out[at : at + 1, :] = marks[0][:1]
+        out[at + 1 : at + 2, :] = marks[1][:1]
+        out[at + 2 : at + 6, :] = conductance[...]
+        out[at + 6 : at + 8, :] = jnp.zeros((2, LATS), F32)
 
 
 def final_body(spot, late, other, pot, foot, phi, east_w, west_w, north_w, south_w, start, picked, hot):
@@ -446,35 +491,29 @@
 
 def shards(plasma_fields, velocity, resistivity, conductance, foot_map, foot_owner, foot_row):
     spot = jnp.stack([lax.axis_index("sec"), lax.axis_index("rad"), lax.axis_index("lon")])
-    speeds = (
-        jnp.concatenate([velocity, resistivity[None]], axis=0)
-        .astype(F32)
-        .reshape(4, SHELLS * LONS, LATS)
-    )
-    own = call(
-        stage_body,
-        arr(PLANES, LONS, SHELLS, LATS),
-        (plasma_fields.reshape(FIELDS, SHELLS * LONS, LATS), speeds),
+    own, slots = first(
+        plasma_fields.reshape(FIELDS, SHELLS * LONS, LATS),
+        velocity,
+        resistivity,
+        foot_owner.reshape(1, -1),
+        foot_row.reshape(1, -1),
+        foot_map,
+        conductance,
     )
     low = lax.ppermute(own, "lon", shift("lon", 1, True))
     high = lax.ppermute(own, "lon", shift("lon", -1, True))
 
-    slots = call(
-        slot_body,
-        arr(4 * SENT, LATS),
-        (foot_owner.reshape(1, -1), foot_row.reshape(1, -1), foot_map, conductance),
-    )
     sent = lax.all_to_all(
         slots.reshape(4, SENT, LATS), "rad", split_axis=0, concat_axis=0, tiled=True
     )
 
     low, high, sent = lax.optimization_barrier((low, high, sent))
     up, down = call(pack_body, (arr(PLANES, 32, LATS), arr(PLANES, 32, LATS)), (low, own, high))
+    above = lax.ppermute(down, "sec", shift("sec", -1, False))
     below = lax.ppermute(up, "sec", shift("sec", 1, False))
-    above = lax.ppermute(down, "sec", shift("sec", -1, False))
     raw = call(raw_body, arr(RAW, LATS), (low, own, high))
     raw = lax.all_gather(raw, "rad")
-    raw, above, below = lax.optimization_barrier((raw, above, below))
+    raw, below, above = lax.optimization_barrier((raw, below, above))
     inner = call(
         inner_body,
         arr(24, LATS),

time: 90 us -> 91.2 us (1.013)
  starting transfers between devices: 35.1 us -> 37.5 us
  Pallas kernels: 12.9 us -> 14.8 us
  local copies, waits for them, and re-layouts: 1.59 us -> 0.01 us
    pallas_call x0 -> x1, Pallas kernels: none -> 2.2 us  [first(): pl.pallas_call(first_body, out_shape=(arr(PLANES, LONS, SHELLS, LATS), ar...]
    unnamed x10 -> x2, local copies, waits for them, and re-layouts: 1.59 us -> 0.01 us
    all_to_all x1, starting transfers between devices: 6.44 us -> 7.62 us  [shards(): late = lax.all_to_all(late, 'lon', split_axis=0, concat_axis=0, tiled=True)]
    pallas_call x10 -> x8, Pallas kernels: 11.5 us -> 11.2 us  [call(): pl.pallas_call(body, out_shape=out_shape, in_specs=specs, out_specs=[vmem...]
  transfers between devices with their start and end apart: 10 -> 10, of which waited for: 6 -> 6; matrix products, arithmetic and copies ran while one was open for 0% -> 0% of each run, Pallas kernels for 8% -> 7%
where the time goes in v7:
time: 91.2 us; the launch traced here: 90.7 us
  starting transfers between devices  37.5 us (41%)
  blocking collectives  19.6 us (21%)
  waiting for transfers between devices  17.9 us (20%)
  Pallas kernels  14.8 us (16%)
    pallas_call x8, Pallas kernels, call(): pl.pallas_call(body, out_shape=out_shape, in_specs=specs, out_specs=[vmem...  11.2 us
    all_gather x1, blocking collectives, shards(): raw = lax.all_gather(raw, 'rad')  9.93 us
    all_to_all x1, blocking collectives, shards(): lax.all_to_all(slots.reshape(4, SENT, LATS), 'rad', split_axis=0, concat_...  9.64 us
    ppermute x1, starting transfers between devices, shards(): high = lax.ppermute(own, 'lon', shift('lon', -1, True))  9.37 us
    ppermute x1, waiting for transfers between devices, shards(): far = lax.ppermute(inner, 'sec', [(0, 3)])  7.62 us
    all_to_all x1, starting transfers between devices, shards(): late = lax.all_to_all(late, 'lon', split_axis=0, concat_axis=0, tiled=True)  7.62 us
    ppermute x1, starting transfers between devices, shards(): above = lax.ppermute(down, 'sec', shift('sec', -1, False))  4.93 us
    ppermute x1, starting transfers between devices, shards(): low = lax.ppermute(own, 'lon', shift('lon', 1, True))  4.13 us
  transfers between devices with their start and end apart: 10, of which 6 were waited for; matrix products, arithmetic and copies ran while one was open for 0% of the time, Pallas kernels for 7%

profile of v7, /device:TPU:57, one launch (start us, length us, event | category | flops | bytes accessed | tf_op | source)
XLA Modules:
  0.0 90.7 jit_solution(16400378379437156934)
XLA Ops:
  0.6 2.2 %shard_map.94 = (f32[12,4,16,128]{3,2,1,0:T(8,128)}, f32[544,128]{1,0:T(8,128)}) custom-call(f32[8,64,128]{2,1,0:T(8,128)} %bitcast.19, bf16[3,16,4,128]{3,2,1,0:T(4,128)(2,1)} %refs_1_.1, bf16[16,4,128]{2,1,0:T(4,128)(2,1)} %refs_2_.1, s32[1,128]{1,0:T(1,128)} %bitcast.21, s32[1,128]{1,0:T(1,128)} %bitcast.22, s32[128,256]{1,0:T(8,128)} %refs_5_.1, ...), custom_call_target="tpu_custom_call" | custom-call | flops 1000000 | bytes 1000000 | tf_op jit(solution)/shard_map/pallas_call | solution.py:88
  2.8 0.0 copy-start
  2.9 4.1 %collective-permute-start = (f32[12,4,16,128]{3,2,1,0:T(8,128)}, f32[12,4,16,128]{3,2,1,0:T(8,128)S(1)}, u32[]{:S(2)}, u32[]{:S(2)}) collective-permute-start(f32[12,4,16,128]{3,2,1,0:T(8,128)} %get-tuple-element.22.own), channel_id=1, source_target_pairs={{0,16},{16,32},{32,48},{48,64},{64,80},{80,96},{96,112},{112,128},... | collective-permute-start | bytes 1179656 | tf_op jit(solution)/shard_map/ppermute | solution.py:503
  7.0 9.4 %collective-permute-start.1 = (f32[12,4,16,128]{3,2,1,0:T(8,128)}, f32[12,4,16,128]{3,2,1,0:T(8,128)S(1)}, u32[]{:S(2)}, u32[]{:S(2)}) collective-permute-start(f32[12,4,16,128]{3,2,1,0:T(8,128)} %get-tuple-element.22.own), channel_id=1, source_target_pairs={{0,496},{16,0},{32,16},{48,32},{64,48},{80,64},{96,80},{112,96},{1... | collective-permute-start | bytes 1179656 | tf_op jit(solution)/shard_map/ppermute | solution.py:504
  16.4 9.6 %all_to_all.10 = f32[4,136,128]{2,1,0:T(8,128)S(1)} all-to-all(f32[4,136,128]{2,1,0:T(8,128)} %bitcast.18), channel_id=1, replica_groups=mesh['lon'=32,'sec'=4,'rad'=4] {'rad'}, dimensions={0} | all-to-all | bytes 557056 | tf_op jit(solution)/shard_map/all_to_all | solution.py:506
  26.0 0.0 collective-permute-done.low
  26.0 0.0 collective-permute-done.1.high
  26.0 0.0 copy-done
  26.0 0.1 shard_map.96
  26.1 1.3 %collective-permute-start.2 = (f32[12,32,128]{2,1,0:T(8,128)S(1)}, f32[12,32,128]{2,1,0:T(8,128)S(1)}, u32[]{:S(2)}, u32[]{:S(2)}) collective-permute-start(f32[12,32,128]{2,1,0:T(8,128)S(1)} %get-tuple-element.26), channel_id=1, source_target_pairs={{0,4},{4,8},{8,12},{1,5},{5,9},{9,13},{2,6},{6,10},{10,14},{3,7},{... | collective-permute-start | bytes 589832 | tf_op jit(solution)/shard_map/ppermute | solution.py:513
  27.4 4.9 %collective-permute-start.3 = (f32[12,32,128]{2,1,0:T(8,128)S(1)}, f32[12,32,128]{2,1,0:T(8,128)S(1)}, u32[]{:S(2)}, u32[]{:S(2)}) collective-permute-start(f32[12,32,128]{2,1,0:T(8,128)S(1)} %get-tuple-element.27), channel_id=1, source_target_pairs={{4,0},{8,4},{12,8},{5,1},{9,5},{13,9},{6,2},{10,6},{14,10},{7,3},{... | collective-permute-start | bytes 589832 | tf_op jit(solution)/shard_map/ppermute | solution.py:512
  32.4 9.9 %all-gather = f32[768,128]{1,0:T(8,128)S(1)} all-gather(f32[192,128]{1,0:T(8,128)S(1)} %shard_map.95), channel_id=2, replica_groups=mesh['lon'=32,'sec'=4,'rad'=4] {'rad'}, dimensions={0}, use_global_device_ids=true | all-gather | bytes 491520 | tf_op jit(solution)/shard_map/all_gather | solution.py:515
  42.3 0.0 collective-permute-done.2.below
  42.3 0.0 collective-permute-done.3.above
  42.3 0.8 shard_map.97
  43.2 1.3 %collective-permute-start.4 = (f32[24,128]{1,0:T(8,128)S(1)}, f32[24,128]{1,0:T(8,128)S(1)}, u32[]{:S(2)}, u32[]{:S(2)}) collective-permute-start(f32[24,128]{1,0:T(8,128)S(1)} %shard_map.97), channel_id=1, source_target_pairs={{0,12},{1,13},{2,14},{3,15},{16,28},{17,29},{18,30},{19,31},{32,44... | collective-permute-start | bytes 36872 | tf_op jit(solution)/shard_map/ppermute | solution.py:523
  44.5 7.6 %collective-permute-done.4 = f32[24,128]{1,0:T(8,128)S(1)} collective-permute-done((f32[24,128]{1,0:T(8,128)S(1)}, f32[24,128]{1,0:T(8,128)S(1)}, u32[]{:S(2)}, u32[]{:S(2)}) %collective-permute-start.4) | collective-permute-done | bytes 12320 | tf_op jit(solution)/shard_map/ppermute | solution.py:523
  52.1 1.9 %collective-permute-start.5 = (f32[24,128]{1,0:T(8,128)S(1)}, f32[24,128]{1,0:T(8,128)S(1)}, u32[]{:S(2)}, u32[]{:S(2)}) collective-permute-start(f32[24,128]{1,0:T(8,128)S(1)} %broadcast_select_fusion.one), channel_id=1, source_target_pairs={{0,4},{12,8},{1,5},{13,9},{2,6},{14,10},{3,7},{15,11},{16,20},{28,... | collective-permute-start | bytes 36872 | tf_op jit(solution)/shard_map/ppermute | solution.py:525
  54.0 0.1 pad_add_fusion.spot
  54.1 0.6 shard_map.98
  54.8 0.1 collective-permute-done.5.two
  54.8 1.4 %shard_map.99 = f32[32,40,128]{2,1,0:T(8,128)} custom-call(s32[3]{0:T(128)S(1)} %pad_add_fusion.spot, f32[24,128]{1,0:T(8,128)S(1)} %broadcast_select_fusion.one, f32[24,128]{1,0:T(8,128)S(1)} %collective-permute-done.5.two, f32[4,128]{1,0:T(4,128)S(1)} %get-tuple-element.30.cond, f32[32,24,128]{2,1,0:T(8,128)S(1)} %bitcast.16), custom_call_target="tpu_custom_call" | custom-call | flops 100000 | bytes 1000000 | tf_op jit(solution)/shard_map/pallas_call | solution.py:264
  56.3 7.6 %all-to-all-start.1 = ((f32[32,40,128]{2,1,0:T(8,128)}), f32[32,40,128]{2,1,0:T(8,128)S(1)}, u32[]{:S(2)}, u32[]{:S(2)}) async-start(f32[32,40,128]{2,1,0:T(8,128)} %shard_map.99), calls=%async_computation.1 | async-start | bytes 1310720 | tf_op jit(solution)/shard_map/all_to_all | solution.py:544
  63.9 0.5 shard_map.100
  64.4 2.8 %collective-permute-start.6 = (f32[12,24,128]{2,1,0:T(8,128)S(1)}, f32[12,24,128]{2,1,0:T(8,128)S(1)}, u32[]{:S(2)}, u32[]{:S(2)}) collective-permute-start(f32[12,24,128]{2,1,0:T(8,128)S(1)} %shard_map.100), channel_id=1, source_target_pairs={{0,1},{1,2},{2,3},{4,5},{5,6},{6,7},{8,9},{9,10},{10,11},{12,13},{... | collective-permute-start | bytes 442376 | tf_op jit(solution)/shard_map/ppermute | solution.py:542
  67.3 1.3 %collective-permute-start.7 = (f32[12,24,128]{2,1,0:T(8,128)S(1)}, f32[12,24,128]{2,1,0:T(8,128)S(1)}, u32[]{:S(2)}, u32[]{:S(2)}) collective-permute-start(f32[12,24,128]{2,1,0:T(8,128)S(1)} %shard_map.100), channel_id=1, source_target_pairs={{1,0},{2,1},{3,2},{5,4},{6,5},{7,6},{9,8},{10,9},{11,10},{13,12},{... | collective-permute-start | bytes 442376 | tf_op jit(solution)/shard_map/ppermute | solution.py:543
  68.6 0.8 collective-permute-done.6.from_low
  69.3 4.1 %collective-permute-done.7.from_high = f32[12,24,128]{2,1,0:T(8,128)S(1)} collective-permute-done((f32[12,24,128]{2,1,0:T(8,128)S(1)}, f32[12,24,128]{2,1,0:T(8,128)S(1)}, u32[]{:S(2)}, u32[]{:S(2)}) %collective-permute-start.7) | collective-permute-done | bytes 147488 | tf_op jit(solution)/shard_map/ppermute | solution.py:543
  73.4 5.5 %shard_map.101 = f32[8,64,128]{2,1,0:T(8,128)} custom-call(f32[12,4,16,128]{3,2,1,0:T(8,128)S(1)} %collective-permute-done.low, f32[12,4,16,128]{3,2,1,0:T(8,128)S(1)} %copy-done, f32[12,4,16,128]{3,2,1,0:T(8,128)S(1)} %collective-permute-done.1.high, f32[12,32,128]{2,1,0:T(8,128)S(1)} %collective-permute-done.3.above, ...), custom_call_target="tpu_custom_call" | custom-call | flops 1000000 | bytes 1000000 | tf_op jit(solution)/shard_map/pallas_call | solution.py:36
  78.9 4.0 %all-to-all-done.1.late = f32[32,40,128]{2,1,0:T(8,128)S(1)} async-done(((f32[32,40,128]{2,1,0:T(8,128)}), f32[32,40,128]{2,1,0:T(8,128)S(1)}, u32[]{:S(2)}, u32[]{:S(2)}) %all-to-all-start.1) | async-done | bytes 655392 | tf_op jit(solution)/shard_map/all_to_all | solution.py:544
  82.9 2.9 %collective-permute-start.8 = (f32[32,24,128]{2,1,0:T(8,128)S(1)}, f32[32,24,128]{2,1,0:T(8,128)S(1)}, u32[]{:S(2)}, u32[]{:S(2)}) collective-permute-start(f32[32,24,128]{2,1,0:T(8,128)S(1)} %shard_map.102), channel_id=1, source_target_pairs={{0,4},{4,0},{8,12},{12,8},{1,5},{5,1},{9,13},{13,9},{2,6},{6,2},{1... | collective-permute-start | bytes 1179656 | tf_op jit(solution)/shard_map/ppermute | solution.py:560
  85.8 1.3 %collective-permute-done.8 = f32[32,24,128]{2,1,0:T(8,128)S(1)} collective-permute-done((f32[32,24,128]{2,1,0:T(8,128)S(1)}, f32[32,24,128]{2,1,0:T(8,128)S(1)}, u32[]{:S(2)}, u32[]{:S(2)}) %collective-permute-start.8) | collective-permute-done | bytes 393248 | tf_op jit(solution)/shard_map/ppermute | solution.py:560
  87.1 3.6 %shard_map.103 = (f32[4,128]{1,0:T(4,128)}, f32[32,256]{1,0:T(8,128)}) custom-call(s32[3]{0:T(128)S(1)} %pad_add_fusion.spot, f32[1280,128]{1,0:T(8,128)S(1)} %bitcast.14, f32[768,128]{1,0:T(8,128)S(1)} %bitcast.17), custom_call_target="tpu_custom_call" | custom-call | flops 1000000 | bytes 1000000 | tf_op jit(solution)/shard_map/pallas_call | solution.py:36
  (3 shorter events, 0.1 us)
Async XLA Ops:
  2.8 23.2 %copy-start = (f32[12,4,16,128]{3,2,1,0:T(8,128)S(1)}, f32[12,4,16,128]{3,2,1,0:T(8,128)}, u32[]{:S(2)}) copy-start(f32[12,4,16,128]{3,2,1,0:T(8,128)} %get-tuple-element.22.own) | copy-start | bytes 1179652
  2.9 23.2 %collective-permute-start = (f32[12,4,16,128]{3,2,1,0:T(8,128)}, f32[12,4,16,128]{3,2,1,0:T(8,128)S(1)}, u32[]{:S(2)}, u32[]{:S(2)}) collective-permute-start(f32[12,4,16,128]{3,2,1,0:T(8,128)} %get-tuple-element.22.own), channel_id=1, source_target_pairs={{0,16},{16,32},{32,48},{48,64},{64,80},{80,96},{96,112},{112,128},... | collective-permute-start | bytes 1179656 | tf_op jit(solution)/shard_map/ppermute | solution.py:503
  7.0 19.0 %collective-permute-start.1 = (f32[12,4,16,128]{3,2,1,0:T(8,128)}, f32[12,4,16,128]{3,2,1,0:T(8,128)S(1)}, u32[]{:S(2)}, u32[]{:S(2)}) collective-permute-start(f32[12,4,16,128]{3,2,1,0:T(8,128)} %get-tuple-element.22.own), channel_id=1, source_target_pairs={{0,496},{16,0},{32,16},{48,32},{64,48},{80,64},{96,80},{112,96},{1... | collective-permute-start | bytes 1179656 | tf_op jit(solution)/shard_map/ppermute | solution.py:504
  26.1 16.2 %collective-permute-start.2 = (f32[12,32,128]{2,1,0:T(8,128)S(1)}, f32[12,32,128]{2,1,0:T(8,128)S(1)}, u32[]{:S(2)}, u32[]{:S(2)}) collective-permute-start(f32[12,32,128]{2,1,0:T(8,128)S(1)} %get-tuple-element.26), channel_id=1, source_target_pairs={{0,4},{4,8},{8,12},{1,5},{5,9},{9,13},{2,6},{6,10},{10,14},{3,7},{... | collective-permute-start | bytes 589832 | tf_op jit(solution)/shard_map/ppermute | solution.py:513
  27.4 14.9 %collective-permute-start.3 = (f32[12,32,128]{2,1,0:T(8,128)S(1)}, f32[12,32,128]{2,1,0:T(8,128)S(1)}, u32[]{:S(2)}, u32[]{:S(2)}) collective-permute-start(f32[12,32,128]{2,1,0:T(8,128)S(1)} %get-tuple-element.27), channel_id=1, source_target_pairs={{4,0},{8,4},{12,8},{5,1},{9,5},{13,9},{6,2},{10,6},{14,10},{7,3},{... | collective-permute-start | bytes 589832 | tf_op jit(solution)/shard_map/ppermute | solution.py:512
  43.2 8.9 %collective-permute-start.4 = (f32[24,128]{1,0:T(8,128)S(1)}, f32[24,128]{1,0:T(8,128)S(1)}, u32[]{:S(2)}, u32[]{:S(2)}) collective-permute-start(f32[24,128]{1,0:T(8,128)S(1)} %shard_map.97), channel_id=1, source_target_pairs={{0,12},{1,13},{2,14},{3,15},{16,28},{17,29},{18,30},{19,31},{32,44... | collective-permute-start | bytes 36872 | tf_op jit(solution)/shard_map/ppermute | solution.py:523
  52.1 2.7 %collective-permute-start.5 = (f32[24,128]{1,0:T(8,128)S(1)}, f32[24,128]{1,0:T(8,128)S(1)}, u32[]{:S(2)}, u32[]{:S(2)}) collective-permute-start(f32[24,128]{1,0:T(8,128)S(1)} %broadcast_select_fusion.one), channel_id=1, source_target_pairs={{0,4},{12,8},{1,5},{13,9},{2,6},{14,10},{3,7},{15,11},{16,20},{28,... | collective-permute-start | bytes 36872 | tf_op jit(solution)/shard_map/ppermute | solution.py:525
  56.3 26.6 %all-to-all-start.1 = ((f32[32,40,128]{2,1,0:T(8,128)}), f32[32,40,128]{2,1,0:T(8,128)S(1)}, u32[]{:S(2)}, u32[]{:S(2)}) async-start(f32[32,40,128]{2,1,0:T(8,128)} %shard_map.99), calls=%async_computation.1 | async-start | bytes 1310720 | tf_op jit(solution)/shard_map/all_to_all | solution.py:544
  64.4 4.9 %collective-permute-start.6 = (f32[12,24,128]{2,1,0:T(8,128)S(1)}, f32[12,24,128]{2,1,0:T(8,128)S(1)}, u32[]{:S(2)}, u32[]{:S(2)}) collective-permute-start(f32[12,24,128]{2,1,0:T(8,128)S(1)} %shard_map.100), channel_id=1, source_target_pairs={{0,1},{1,2},{2,3},{4,5},{5,6},{6,7},{8,9},{9,10},{10,11},{12,13},{... | collective-permute-start | bytes 442376 | tf_op jit(solution)/shard_map/ppermute | solution.py:542
  67.3 6.2 %collective-permute-start.7 = (f32[12,24,128]{2,1,0:T(8,128)S(1)}, f32[12,24,128]{2,1,0:T(8,128)S(1)}, u32[]{:S(2)}, u32[]{:S(2)}) collective-permute-start(f32[12,24,128]{2,1,0:T(8,128)S(1)} %shard_map.100), channel_id=1, source_target_pairs={{1,0},{2,1},{3,2},{5,4},{6,5},{7,6},{9,8},{10,9},{11,10},{13,12},{... | collective-permute-start | bytes 442376 | tf_op jit(solution)/shard_map/ppermute | solution.py:543
  82.9 4.2 %collective-permute-start.8 = (f32[32,24,128]{2,1,0:T(8,128)S(1)}, f32[32,24,128]{2,1,0:T(8,128)S(1)}, u32[]{:S(2)}, u32[]{:S(2)}) collective-permute-start(f32[32,24,128]{2,1,0:T(8,128)S(1)} %shard_map.102), channel_id=1, source_target_pairs={{0,4},{4,0},{8,12},{12,8},{1,5},{5,1},{9,13},{13,9},{2,6},{6,2},{1... | collective-permute-start | bytes 1179656 | tf_op jit(solution)/shard_map/ppermute | solution.py:560

commit v8 on v7

--- a/solution.py
+++ b/solution.py
@@ -512,16 +512,21 @@
     above = lax.ppermute(down, "sec", shift("sec", -1, False))
     below = lax.ppermute(up, "sec", shift("sec", 1, False))
     raw = call(raw_body, arr(RAW, LATS), (low, own, high))
-    raw = lax.all_gather(raw, "rad")
-    raw, below, above = lax.optimization_barrier((raw, below, above))
-    inner = call(
-        inner_body,
-        arr(24, LATS),
-        (raw.reshape(4 * RAW, LATS),),
-        scratch=(pltpu.VMEM((6, WIDE, 8, 4 * LATS), F32),),
-    )
+    owner = lax.axis_index("sec") == 0
+
+    def advance_inner(rows):
+        gathered = lax.all_gather(rows, "rad")
+        return call(
+            inner_body,
+            arr(24, LATS),
+            (gathered.reshape(4 * RAW, LATS),),
+            scratch=(pltpu.VMEM((6, WIDE, 8, 4 * LATS), F32),),
+        )
+
+    inner = lax.cond(owner, advance_inner, lambda rows: jnp.zeros((24, LATS), F32), raw)
+    inner, below, above = lax.optimization_barrier((inner, below, above))
     far = lax.ppermute(inner, "sec", [(0, 3)])
-    far = jnp.where(lax.axis_index("sec") == 0, inner, far)
+    far = inner + far
     near = lax.ppermute(far, "sec", [(0, 1), (3, 2)])
     base, cond = call(
         base_body,

time: 91.2 us -> 88.1 us (0.966)
  blocking collectives: 19.6 us -> 9.64 us
  waiting for transfers between devices: 17.9 us -> 25.3 us
    all_gather x1 -> x0, blocking collectives: 9.93 us -> none  [shards(): raw = lax.all_gather(raw, 'rad')]
    ppermute x1, waiting for transfers between devices: 7.62 us -> 14 us  [shards(): far = lax.ppermute(inner, 'sec', [(0, 3)])]
    ppermute x1, waiting for transfers between devices: 0.01 us -> 0.95 us  [shards(): above = lax.ppermute(down, 'sec', shift('sec', -1, False))]
    pallas_call x8 -> x7, Pallas kernels: 11.2 us -> 10.3 us  [call(): pl.pallas_call(body, out_shape=out_shape, in_specs=specs, out_specs=[vmem...]
  transfers between devices with their start and end apart: 10 -> 10, of which waited for: 6 -> 7; matrix products, arithmetic and copies ran while one was open for 0% -> 0% of each run, Pallas kernels for 7% -> 8%
where the time goes in v8:
time: 88.1 us; the launch traced here: 87.6 us
  starting transfers between devices  37.8 us (43%)
  waiting for transfers between devices  25.3 us (29%)
  Pallas kernels  14 us (16%)
  blocking collectives  9.64 us (11%)
    ppermute x1, waiting for transfers between devices, shards(): far = lax.ppermute(inner, 'sec', [(0, 3)])  14 us
    pallas_call x7, Pallas kernels, call(): pl.pallas_call(body, out_shape=out_shape, in_specs=specs, out_specs=[vmem...  10.3 us
    all_to_all x1, blocking collectives, shards(): lax.all_to_all(slots.reshape(4, SENT, LATS), 'rad', split_axis=0, concat_...  9.64 us
    ppermute x1, starting transfers between devices, shards(): high = lax.ppermute(own, 'lon', shift('lon', -1, True))  9.37 us
    all_to_all x1, starting transfers between devices, shards(): late = lax.all_to_all(late, 'lon', split_axis=0, concat_axis=0, tiled=True)  8.52 us
    ppermute x1, starting transfers between devices, shards(): above = lax.ppermute(down, 'sec', shift('sec', -1, False))  4.93 us
    ppermute x1, starting transfers between devices, shards(): low = lax.ppermute(own, 'lon', shift('lon', 1, True))  4.13 us
    ppermute x1, waiting for transfers between devices, shards(): from_high = lax.ppermute(edges, 'rad', shift('rad', -1, False))  4.11 us
  transfers between devices with their start and end apart: 10, of which 7 were waited for; matrix products, arithmetic and copies ran while one was open for 0% of the time, Pallas kernels for 8%

profile of v8, /device:TPU:57, one launch (start us, length us, event | category | flops | bytes accessed | tf_op | source)
XLA Modules:
  0.0 87.6 jit_solution(3384295917288941641)
XLA Ops:
  0.6 2.2 %shard_map.94 = (f32[12,4,16,128]{3,2,1,0:T(8,128)}, f32[544,128]{1,0:T(8,128)}) custom-call(f32[8,64,128]{2,1,0:T(8,128)} %bitcast.17, bf16[3,16,4,128]{3,2,1,0:T(4,128)(2,1)} %refs_1_.1, bf16[16,4,128]{2,1,0:T(4,128)(2,1)} %refs_2_.1, s32[1,128]{1,0:T(1,128)} %bitcast.19, s32[1,128]{1,0:T(1,128)} %bitcast.20, s32[128,256]{1,0:T(8,128)} %refs_5_.1, ...), custom_call_target="tpu_custom_call" | custom-call | flops 1000000 | bytes 1000000 | tf_op jit(solution)/shard_map/pallas_call | solution.py:88
  2.8 0.0 copy-start
  2.8 4.1 %collective-permute-start = (f32[12,4,16,128]{3,2,1,0:T(8,128)}, f32[12,4,16,128]{3,2,1,0:T(8,128)S(1)}, u32[]{:S(2)}, u32[]{:S(2)}) collective-permute-start(f32[12,4,16,128]{3,2,1,0:T(8,128)} %get-tuple-element.26.own), channel_id=1, source_target_pairs={{0,16},{16,32},{32,48},{48,64},{64,80},{80,96},{96,112},{112,128},... | collective-permute-start | bytes 1179656 | tf_op jit(solution)/shard_map/ppermute | solution.py:503
  7.0 9.4 %collective-permute-start.1 = (f32[12,4,16,128]{3,2,1,0:T(8,128)}, f32[12,4,16,128]{3,2,1,0:T(8,128)S(1)}, u32[]{:S(2)}, u32[]{:S(2)}) collective-permute-start(f32[12,4,16,128]{3,2,1,0:T(8,128)} %get-tuple-element.26.own), channel_id=1, source_target_pairs={{0,496},{16,0},{32,16},{48,32},{64,48},{80,64},{96,80},{112,96},{1... | collective-permute-start | bytes 1179656 | tf_op jit(solution)/shard_map/ppermute | solution.py:504
  16.4 9.6 %all_to_all.10 = f32[4,136,128]{2,1,0:T(8,128)S(1)} all-to-all(f32[4,136,128]{2,1,0:T(8,128)} %bitcast.16), channel_id=1, replica_groups=mesh['lon'=32,'sec'=4,'rad'=4] {'rad'}, dimensions={0} | all-to-all | bytes 557056 | tf_op jit(solution)/shard_map/all_to_all | solution.py:506
  26.0 0.0 collective-permute-done.low
  26.0 0.0 collective-permute-done.1.high
  26.0 0.0 copy-done
  26.0 0.1 shard_map.96
  26.1 1.3 %collective-permute-start.2 = (f32[12,32,128]{2,1,0:T(8,128)S(1)}, f32[12,32,128]{2,1,0:T(8,128)S(1)}, u32[]{:S(2)}, u32[]{:S(2)}) collective-permute-start(f32[12,32,128]{2,1,0:T(8,128)S(1)} %get-tuple-element.30), channel_id=1, source_target_pairs={{0,4},{4,8},{8,12},{1,5},{5,9},{9,13},{2,6},{6,10},{10,14},{3,7},{... | collective-permute-start | bytes 589832 | tf_op jit(solution)/shard_map/ppermute | solution.py:513
  27.4 4.9 %collective-permute-start.3 = (f32[12,32,128]{2,1,0:T(8,128)S(1)}, f32[12,32,128]{2,1,0:T(8,128)S(1)}, u32[]{:S(2)}, u32[]{:S(2)}) collective-permute-start(f32[12,32,128]{2,1,0:T(8,128)S(1)} %get-tuple-element.31), channel_id=1, source_target_pairs={{4,0},{8,4},{12,8},{5,1},{9,5},{13,9},{6,2},{10,6},{14,10},{7,3},{... | collective-permute-start | bytes 589832 | tf_op jit(solution)/shard_map/ppermute | solution.py:512
  32.4 0.0 collective-permute-done.2.below
  32.4 1.0 %collective-permute-done.3.above = f32[12,32,128]{2,1,0:T(8,128)S(1)} collective-permute-done((f32[12,32,128]{2,1,0:T(8,128)S(1)}, f32[12,32,128]{2,1,0:T(8,128)S(1)}, u32[]{:S(2)}, u32[]{:S(2)}) %collective-permute-start.3) | collective-permute-done | bytes 196640 | tf_op jit(solution)/shard_map/ppermute | solution.py:512
  33.4 1.3 %collective-permute-start.4 = (f32[24,128]{1,0:T(8,128)S(1)}, f32[24,128]{1,0:T(8,128)S(1)}, u32[]{:S(2)}, u32[]{:S(2)}) collective-permute-start(f32[24,128]{1,0:T(8,128)S(1)} %get-tuple-element.45), channel_id=1, source_target_pairs={{0,12},{1,13},{2,14},{3,15},{16,28},{17,29},{18,30},{19,31},{32,44... | collective-permute-start | bytes 36872 | tf_op jit(solution)/shard_map/ppermute | solution.py:528
  34.7 14.0 %collective-permute-done.4 = f32[24,128]{1,0:T(8,128)S(1)} collective-permute-done((f32[24,128]{1,0:T(8,128)S(1)}, f32[24,128]{1,0:T(8,128)S(1)}, u32[]{:S(2)}, u32[]{:S(2)}) %collective-permute-start.4) | collective-permute-done | bytes 12320 | tf_op jit(solution)/shard_map/ppermute | solution.py:528
  48.7 1.3 %collective-permute-start.5 = (f32[24,128]{1,0:T(8,128)S(1)}, f32[24,128]{1,0:T(8,128)S(1)}, u32[]{:S(2)}, u32[]{:S(2)}) collective-permute-start(f32[24,128]{1,0:T(8,128)S(1)} %add.3.one), channel_id=1, source_target_pairs={{0,4},{12,8},{1,5},{13,9},{2,6},{14,10},{3,7},{15,11},{16,20},{28,... | collective-permute-start | bytes 36872 | tf_op jit(solution)/shard_map/ppermute | solution.py:530
  50.0 0.1 pad_add_fusion.spot
  50.1 0.6 shard_map.97
  50.8 0.1 collective-permute-done.5.two
  50.8 1.4 %shard_map.98 = f32[32,40,128]{2,1,0:T(8,128)} custom-call(s32[3]{0:T(128)S(1)} %pad_add_fusion.spot, f32[24,128]{1,0:T(8,128)S(1)} %add.3.one, f32[24,128]{1,0:T(8,128)S(1)} %collective-permute-done.5.two, f32[4,128]{1,0:T(4,128)S(1)} %get-tuple-element.34.cond, f32[32,24,128]{2,1,0:T(8,128)S(1)} %bitcast.14), custom_call_target="tpu_custom_call" | custom-call | flops 100000 | bytes 1000000 | tf_op jit(solution)/shard_map/pallas_call | solution.py:264
  52.3 8.5 %all-to-all-start.1 = ((f32[32,40,128]{2,1,0:T(8,128)}), f32[32,40,128]{2,1,0:T(8,128)S(1)}, u32[]{:S(2)}, u32[]{:S(2)}) async-start(f32[32,40,128]{2,1,0:T(8,128)} %shard_map.98), calls=%async_computation.1 | async-start | bytes 1310720 | tf_op jit(solution)/shard_map/all_to_all | solution.py:549
  60.8 0.5 shard_map.99
  61.3 2.8 %collective-permute-start.6 = (f32[12,24,128]{2,1,0:T(8,128)S(1)}, f32[12,24,128]{2,1,0:T(8,128)S(1)}, u32[]{:S(2)}, u32[]{:S(2)}) collective-permute-start(f32[12,24,128]{2,1,0:T(8,128)S(1)} %shard_map.99), channel_id=1, source_target_pairs={{0,1},{1,2},{2,3},{4,5},{5,6},{6,7},{8,9},{9,10},{10,11},{12,13},{... | collective-permute-start | bytes 442376 | tf_op jit(solution)/shard_map/ppermute | solution.py:547
  64.1 1.3 %collective-permute-start.7 = (f32[12,24,128]{2,1,0:T(8,128)S(1)}, f32[12,24,128]{2,1,0:T(8,128)S(1)}, u32[]{:S(2)}, u32[]{:S(2)}) collective-permute-start(f32[12,24,128]{2,1,0:T(8,128)S(1)} %shard_map.99), channel_id=1, source_target_pairs={{1,0},{2,1},{3,2},{5,4},{6,5},{7,6},{9,8},{10,9},{11,10},{13,12},{... | collective-permute-start | bytes 442376 | tf_op jit(solution)/shard_map/ppermute | solution.py:548
  65.4 0.8 collective-permute-done.6.from_low
  66.2 4.1 %collective-permute-done.7.from_high = f32[12,24,128]{2,1,0:T(8,128)S(1)} collective-permute-done((f32[12,24,128]{2,1,0:T(8,128)S(1)}, f32[12,24,128]{2,1,0:T(8,128)S(1)}, u32[]{:S(2)}, u32[]{:S(2)}) %collective-permute-start.7) | collective-permute-done | bytes 147488 | tf_op jit(solution)/shard_map/ppermute | solution.py:548
  70.3 5.5 %shard_map.100 = f32[8,64,128]{2,1,0:T(8,128)} custom-call(f32[12,4,16,128]{3,2,1,0:T(8,128)S(1)} %collective-permute-done.low, f32[12,4,16,128]{3,2,1,0:T(8,128)S(1)} %copy-done, f32[12,4,16,128]{3,2,1,0:T(8,128)S(1)} %collective-permute-done.1.high, f32[12,32,128]{2,1,0:T(8,128)S(1)} %collective-permute-done.3.above, ...), custom_call_target="tpu_custom_call" | custom-call | flops 1000000 | bytes 1000000 | tf_op jit(solution)/shard_map/pallas_call | solution.py:36
  75.8 4.0 %all-to-all-done.1.late = f32[32,40,128]{2,1,0:T(8,128)S(1)} async-done(((f32[32,40,128]{2,1,0:T(8,128)}), f32[32,40,128]{2,1,0:T(8,128)S(1)}, u32[]{:S(2)}, u32[]{:S(2)}) %all-to-all-start.1) | async-done | bytes 655392 | tf_op jit(solution)/shard_map/all_to_all | solution.py:549
  79.8 2.9 %collective-permute-start.8 = (f32[32,24,128]{2,1,0:T(8,128)S(1)}, f32[32,24,128]{2,1,0:T(8,128)S(1)}, u32[]{:S(2)}, u32[]{:S(2)}) collective-permute-start(f32[32,24,128]{2,1,0:T(8,128)S(1)} %shard_map.101), channel_id=1, source_target_pairs={{0,4},{4,0},{8,12},{12,8},{1,5},{5,1},{9,13},{13,9},{2,6},{6,2},{1... | collective-permute-start | bytes 1179656 | tf_op jit(solution)/shard_map/ppermute | solution.py:565
  82.7 1.3 %collective-permute-done.8 = f32[32,24,128]{2,1,0:T(8,128)S(1)} collective-permute-done((f32[32,24,128]{2,1,0:T(8,128)S(1)}, f32[32,24,128]{2,1,0:T(8,128)S(1)}, u32[]{:S(2)}, u32[]{:S(2)}) %collective-permute-start.8) | collective-permute-done | bytes 393248 | tf_op jit(solution)/shard_map/ppermute | solution.py:565
  84.0 3.6 %shard_map.102 = (f32[4,128]{1,0:T(4,128)}, f32[32,256]{1,0:T(8,128)}) custom-call(s32[3]{0:T(128)S(1)} %pad_add_fusion.spot, f32[1280,128]{1,0:T(8,128)S(1)} %bitcast.12, f32[768,128]{1,0:T(8,128)S(1)} %bitcast.15), custom_call_target="tpu_custom_call" | custom-call | flops 1000000 | bytes 1000000 | tf_op jit(solution)/shard_map/pallas_call | solution.py:36
  (5 shorter events, 0.1 us)
Async XLA Ops:
  2.8 23.2 %copy-start = (f32[12,4,16,128]{3,2,1,0:T(8,128)S(1)}, f32[12,4,16,128]{3,2,1,0:T(8,128)}, u32[]{:S(2)}) copy-start(f32[12,4,16,128]{3,2,1,0:T(8,128)} %get-tuple-element.26.own) | copy-start | bytes 1179652
  2.8 23.2 %collective-permute-start = (f32[12,4,16,128]{3,2,1,0:T(8,128)}, f32[12,4,16,128]{3,2,1,0:T(8,128)S(1)}, u32[]{:S(2)}, u32[]{:S(2)}) collective-permute-start(f32[12,4,16,128]{3,2,1,0:T(8,128)} %get-tuple-element.26.own), channel_id=1, source_target_pairs={{0,16},{16,32},{32,48},{48,64},{64,80},{80,96},{96,112},{112,128},... | collective-permute-start | bytes 1179656 | tf_op jit(solution)/shard_map/ppermute | solution.py:503
  7.0 19.0 %collective-permute-start.1 = (f32[12,4,16,128]{3,2,1,0:T(8,128)}, f32[12,4,16,128]{3,2,1,0:T(8,128)S(1)}, u32[]{:S(2)}, u32[]{:S(2)}) collective-permute-start(f32[12,4,16,128]{3,2,1,0:T(8,128)} %get-tuple-element.26.own), channel_id=1, source_target_pairs={{0,496},{16,0},{32,16},{48,32},{64,48},{80,64},{96,80},{112,96},{1... | collective-permute-start | bytes 1179656 | tf_op jit(solution)/shard_map/ppermute | solution.py:504
  26.1 6.3 %collective-permute-start.2 = (f32[12,32,128]{2,1,0:T(8,128)S(1)}, f32[12,32,128]{2,1,0:T(8,128)S(1)}, u32[]{:S(2)}, u32[]{:S(2)}) collective-permute-start(f32[12,32,128]{2,1,0:T(8,128)S(1)} %get-tuple-element.30), channel_id=1, source_target_pairs={{0,4},{4,8},{8,12},{1,5},{5,9},{9,13},{2,6},{6,10},{10,14},{3,7},{... | collective-permute-start | bytes 589832 | tf_op jit(solution)/shard_map/ppermute | solution.py:513
  27.4 6.0 %collective-permute-start.3 = (f32[12,32,128]{2,1,0:T(8,128)S(1)}, f32[12,32,128]{2,1,0:T(8,128)S(1)}, u32[]{:S(2)}, u32[]{:S(2)}) collective-permute-start(f32[12,32,128]{2,1,0:T(8,128)S(1)} %get-tuple-element.31), channel_id=1, source_target_pairs={{4,0},{8,4},{12,8},{5,1},{9,5},{13,9},{6,2},{10,6},{14,10},{7,3},{... | collective-permute-start | bytes 589832 | tf_op jit(solution)/shard_map/ppermute | solution.py:512
  33.4 15.3 %collective-permute-start.4 = (f32[24,128]{1,0:T(8,128)S(1)}, f32[24,128]{1,0:T(8,128)S(1)}, u32[]{:S(2)}, u32[]{:S(2)}) collective-permute-start(f32[24,128]{1,0:T(8,128)S(1)} %get-tuple-element.45), channel_id=1, source_target_pairs={{0,12},{1,13},{2,14},{3,15},{16,28},{17,29},{18,30},{19,31},{32,44... | collective-permute-start | bytes 36872 | tf_op jit(solution)/shard_map/ppermute | solution.py:528
  48.7 2.1 %collective-permute-start.5 = (f32[24,128]{1,0:T(8,128)S(1)}, f32[24,128]{1,0:T(8,128)S(1)}, u32[]{:S(2)}, u32[]{:S(2)}) collective-permute-start(f32[24,128]{1,0:T(8,128)S(1)} %add.3.one), channel_id=1, source_target_pairs={{0,4},{12,8},{1,5},{13,9},{2,6},{14,10},{3,7},{15,11},{16,20},{28,... | collective-permute-start | bytes 36872 | tf_op jit(solution)/shard_map/ppermute | solution.py:530
  52.3 27.5 %all-to-all-start.1 = ((f32[32,40,128]{2,1,0:T(8,128)}), f32[32,40,128]{2,1,0:T(8,128)S(1)}, u32[]{:S(2)}, u32[]{:S(2)}) async-start(f32[32,40,128]{2,1,0:T(8,128)} %shard_map.98), calls=%async_computation.1 | async-start | bytes 1310720 | tf_op jit(solution)/shard_map/all_to_all | solution.py:549
  61.3 4.9 %collective-permute-start.6 = (f32[12,24,128]{2,1,0:T(8,128)S(1)}, f32[12,24,128]{2,1,0:T(8,128)S(1)}, u32[]{:S(2)}, u32[]{:S(2)}) collective-permute-start(f32[12,24,128]{2,1,0:T(8,128)S(1)} %shard_map.99), channel_id=1, source_target_pairs={{0,1},{1,2},{2,3},{4,5},{5,6},{6,7},{8,9},{9,10},{10,11},{12,13},{... | collective-permute-start | bytes 442376 | tf_op jit(solution)/shard_map/ppermute | solution.py:547
  64.1 6.2 %collective-permute-start.7 = (f32[12,24,128]{2,1,0:T(8,128)S(1)}, f32[12,24,128]{2,1,0:T(8,128)S(1)}, u32[]{:S(2)}, u32[]{:S(2)}) collective-permute-start(f32[12,24,128]{2,1,0:T(8,128)S(1)} %shard_map.99), channel_id=1, source_target_pairs={{1,0},{2,1},{3,2},{5,4},{6,5},{7,6},{9,8},{10,9},{11,10},{13,12},{... | collective-permute-start | bytes 442376 | tf_op jit(solution)/shard_map/ppermute | solution.py:548
  79.8 4.2 %collective-permute-start.8 = (f32[32,24,128]{2,1,0:T(8,128)S(1)}, f32[32,24,128]{2,1,0:T(8,128)S(1)}, u32[]{:S(2)}, u32[]{:S(2)}) collective-permute-start(f32[32,24,128]{2,1,0:T(8,128)S(1)} %shard_map.101), channel_id=1, source_target_pairs={{0,4},{4,0},{8,12},{12,8},{1,5},{5,1},{9,13},{13,9},{2,6},{6,2},{1... | collective-permute-start | bytes 1179656 | tf_op jit(solution)/shard_map/ppermute | solution.py:565

commit v9 on v8

--- a/solution.py
+++ b/solution.py
@@ -19,7 +19,7 @@
 LATS = 128
 WIDE = 3 * LONS
 LATE = 40
-HALF = 24
+HALF = 20
 RAW = 192
 SENT = 136
 TALL = SHELLS + 2 * PHASES
@@ -277,8 +277,22 @@
 
 
 def half_body(late, out):
-    for owner in range(32):
-        out[owner] = late[owner, :HALF, :]
+    for row in range(HALF):
+        out[row] = late[pl.ds(row, 32, stride=LATE), :]
+
+
+def mark_body(late, cells, hot):
+    lane = lax.broadcasted_iota(jnp.int32, (32, LATS), 1).astype(F32)
+    for rad in range(4):
+        marks = late[pl.ds(HALF + rad * 5 + 4, 32, stride=LATE), :]
+        for slot in range(2):
+            row = marks if slot == 0 else pltpu.roll(marks, 64, axis=1)
+            at = (slot * 4 + rad) * 32
+            hot[at : at + 32, :] = jnp.where(row == lane, 1.0, 0.0)
+            for half in range(2):
+                cells[(rad * 2 + slot) * 2 + half] = late[
+                    pl.ds(HALF + rad * 5 + 2 * slot + half, 32, stride=LATE), :
+                ].astype(jnp.int32)
 
 
 def chunks():
@@ -388,7 +402,9 @@
         out[at + 6 : at + 8, :] = jnp.zeros((2, LATS), F32)
 
 
-def final_body(spot, late, other, pot, foot, phi, east_w, west_w, north_w, south_w, start, picked, hot):
+def final_body(
+    spot, mine, other, cells, hot, pot, foot, phi, east_w, west_w, north_w, south_w, start, picked
+):
     devs, rads = 32, 4
     wide = rads * LATS
     lane = lax.broadcasted_iota(jnp.int32, (devs, wide), 1)
@@ -399,9 +415,7 @@
         found = []
         for rad in range(rads):
             row = at + rad % 2 * step
-            mine = late[pl.ds(row, devs, stride=LATE), :]
-            theirs = other[pl.ds(row, devs, stride=HALF), :]
-            found.append(jnp.where(odd == rad // 2, mine, theirs))
+            found.append(jnp.where(odd == rad // 2, mine[row], other[row]))
         return jnp.concatenate(found, axis=1)
 
     def lon_up(values, lon):
@@ -461,16 +475,12 @@
                     jnp.where(at_lon, block, 0.0), axis=0, keepdims=True
                 )
 
-    slot_lane = lax.broadcasted_iota(jnp.int32, (devs, LATS), 1).astype(F32)
     for rad in range(rads):
         table = [phi[done, lon, :, rad * LATS : (rad + 1) * LATS] for lon in range(LONS)]
-        marks = late[pl.ds(20 + rad * 5 + 4, devs, stride=LATE), :]
         for slot in range(2):
             at = (slot * rads + rad) * devs
-            row = marks if slot == 0 else pltpu.roll(marks, 64, axis=1)
-            hot[at : at + devs, :] = jnp.where(row == slot_lane, 1.0, 0.0)
             for half in range(2):
-                cell = late[pl.ds(20 + rad * 5 + 2 * slot + half, devs, stride=LATE), :].astype(jnp.int32)
+                cell = cells[(rad * 2 + slot) * 2 + half]
                 place, lon_at = cell & 127, cell >> 7
                 value = jnp.zeros((devs, LATS), F32)
                 for lon in range(LONS):
@@ -479,13 +489,15 @@
                     )
                     value = jnp.where(lon_at == lon, found, value)
                 picked[at : at + devs, 128 * half : 128 * half + 128] = value
-    summed = lax.dot_general(
-        hot[...],
-        picked[...],
-        (((0,), (0,)), ((), ())),
-        precision=lax.Precision.HIGHEST,
-        preferred_element_type=F32,
-    )
+    rest = picked[...]
+    rows = hot[...].astype(jnp.bfloat16)
+    summed = jnp.zeros((LATS, 2 * LATS), F32)
+    for part in range(3):
+        piece = rest.astype(jnp.bfloat16)
+        rest = rest - piece.astype(F32)
+        summed = summed + lax.dot_general(
+            rows, piece, (((0,), (0,)), ((), ())), preferred_element_type=F32
+        )
     foot[...] = summed[:ROWS_OWN]
 
 
@@ -562,14 +574,19 @@
     ).reshape(FIELDS, SHELLS, LONS, LATS)
 
     late, advanced = lax.optimization_barrier((late, advanced))
-    other = lax.ppermute(
-        call(half_body, arr(32, HALF, LATS), (late,)), "sec", [(0, 1), (1, 0), (2, 3), (3, 2)]
+    late = late.reshape(32 * LATE, LATS)
+    mine = call(half_body, arr(HALF, 32, LATS), (late,))
+    other = lax.ppermute(mine, "sec", [(0, 1), (1, 0), (2, 3), (3, 2)])
+    cells, hot = call(
+        mark_body,
+        (jax.ShapeDtypeStruct((16, 32, LATS), jnp.int32), arr(256, LATS)),
+        (late,),
     )
     plane = pltpu.VMEM((LONS, 32, 4 * LATS), F32)
     potential, foot_table = call(
         final_body,
         (arr(LONS, LATS), arr(ROWS_OWN, 256)),
-        (spot, late.reshape(32 * LATE, LATS), other.reshape(32 * HALF, LATS)),
+        (spot, mine, other, cells, hot),
         scratch=(
             pltpu.VMEM((2, LONS, 32, 4 * LATS), F32),
             plane,
@@ -578,7 +595,6 @@
             plane,
             plane,
             pltpu.VMEM((256, 256), F32),
-            pltpu.VMEM((256, 128), F32),
         ),
         smem=(0,),
     )

time: 88.1 us -> 88 us (level)
    pallas_call x7 -> x8, Pallas kernels: 10.3 us -> 10.4 us  [call(): pl.pallas_call(body, out_shape=out_shape, in_specs=specs, out_specs=[vmem...]
where the time goes in v9:
time: 88 us; the launch traced here: 87.5 us
  starting transfers between devices  37.8 us (43%)
  waiting for transfers between devices  25.1 us (29%)
  Pallas kernels  14 us (16%)
  blocking collectives  9.64 us (11%)
    ppermute x1, waiting for transfers between devices, shards(): far = lax.ppermute(inner, 'sec', [(0, 3)])  14 us
    pallas_call x8, Pallas kernels, call(): pl.pallas_call(body, out_shape=out_shape, in_specs=specs, out_specs=[vmem...  10.4 us
    all_to_all x1, blocking collectives, shards(): lax.all_to_all(slots.reshape(4, SENT, LATS), 'rad', split_axis=0, concat_...  9.64 us
    ppermute x1, starting transfers between devices, shards(): high = lax.ppermute(own, 'lon', shift('lon', -1, True))  9.37 us
    all_to_all x1, starting transfers between devices, shards(): late = lax.all_to_all(late, 'lon', split_axis=0, concat_axis=0, tiled=True)  8.52 us
    ppermute x1, starting transfers between devices, shards(): above = lax.ppermute(down, 'sec', shift('sec', -1, False))  4.93 us
    ppermute x1, starting transfers between devices, shards(): low = lax.ppermute(own, 'lon', shift('lon', 1, True))  4.13 us
    ppermute x1, waiting for transfers between devices, shards(): from_high = lax.ppermute(edges, 'rad', shift('rad', -1, False))  4.11 us
  transfers between devices with their start and end apart: 10, of which 7 were waited for; matrix products, arithmetic and copies ran while one was open for 0% of the time, Pallas kernels for 8%

profile of v9, /device:TPU:57, one launch (start us, length us, event | category | flops | bytes accessed | tf_op | source)
XLA Modules:
  0.0 87.5 jit_solution(2646286259146822359)
XLA Ops:
  0.6 2.2 %shard_map.94 = (f32[12,4,16,128]{3,2,1,0:T(8,128)}, f32[544,128]{1,0:T(8,128)}) custom-call(f32[8,64,128]{2,1,0:T(8,128)} %bitcast.16, bf16[3,16,4,128]{3,2,1,0:T(4,128)(2,1)} %refs_1_.1, bf16[16,4,128]{2,1,0:T(4,128)(2,1)} %refs_2_.1, s32[1,128]{1,0:T(1,128)} %bitcast.18, s32[1,128]{1,0:T(1,128)} %bitcast.19, s32[128,256]{1,0:T(8,128)} %refs_5_.1, ...), custom_call_target="tpu_custom_call" | custom-call | flops 1000000 | bytes 1000000 | tf_op jit(solution)/shard_map/pallas_call | solution.py:88
  2.8 0.0 copy-start
  2.8 4.1 %collective-permute-start = (f32[12,4,16,128]{3,2,1,0:T(8,128)}, f32[12,4,16,128]{3,2,1,0:T(8,128)S(1)}, u32[]{:S(2)}, u32[]{:S(2)}) collective-permute-start(f32[12,4,16,128]{3,2,1,0:T(8,128)} %get-tuple-element.28.own), channel_id=1, source_target_pairs={{0,16},{16,32},{32,48},{48,64},{64,80},{80,96},{96,112},{112,128},... | collective-permute-start | bytes 1179656 | tf_op jit(solution)/shard_map/ppermute | solution.py:515
  7.0 9.4 %collective-permute-start.1 = (f32[12,4,16,128]{3,2,1,0:T(8,128)}, f32[12,4,16,128]{3,2,1,0:T(8,128)S(1)}, u32[]{:S(2)}, u32[]{:S(2)}) collective-permute-start(f32[12,4,16,128]{3,2,1,0:T(8,128)} %get-tuple-element.28.own), channel_id=1, source_target_pairs={{0,496},{16,0},{32,16},{48,32},{64,48},{80,64},{96,80},{112,96},{1... | collective-permute-start | bytes 1179656 | tf_op jit(solution)/shard_map/ppermute | solution.py:516
  16.4 9.6 %all_to_all.10 = f32[4,136,128]{2,1,0:T(8,128)S(1)} all-to-all(f32[4,136,128]{2,1,0:T(8,128)} %bitcast.15), channel_id=1, replica_groups=mesh['lon'=32,'sec'=4,'rad'=4] {'rad'}, dimensions={0} | all-to-all | bytes 557056 | tf_op jit(solution)/shard_map/all_to_all | solution.py:518
  26.0 0.0 collective-permute-done.low
  26.0 0.0 collective-permute-done.1.high
  26.0 0.0 copy-done
  26.0 0.1 shard_map.96
  26.1 1.3 %collective-permute-start.2 = (f32[12,32,128]{2,1,0:T(8,128)S(1)}, f32[12,32,128]{2,1,0:T(8,128)S(1)}, u32[]{:S(2)}, u32[]{:S(2)}) collective-permute-start(f32[12,32,128]{2,1,0:T(8,128)S(1)} %get-tuple-element.32), channel_id=1, source_target_pairs={{0,4},{4,8},{8,12},{1,5},{5,9},{9,13},{2,6},{6,10},{10,14},{3,7},{... | collective-permute-start | bytes 589832 | tf_op jit(solution)/shard_map/ppermute | solution.py:525
  27.4 4.9 %collective-permute-start.3 = (f32[12,32,128]{2,1,0:T(8,128)S(1)}, f32[12,32,128]{2,1,0:T(8,128)S(1)}, u32[]{:S(2)}, u32[]{:S(2)}) collective-permute-start(f32[12,32,128]{2,1,0:T(8,128)S(1)} %get-tuple-element.33), channel_id=1, source_target_pairs={{4,0},{8,4},{12,8},{5,1},{9,5},{13,9},{6,2},{10,6},{14,10},{7,3},{... | collective-permute-start | bytes 589832 | tf_op jit(solution)/shard_map/ppermute | solution.py:524
  32.4 0.0 collective-permute-done.2.below
  32.4 1.0 %collective-permute-done.3.above = f32[12,32,128]{2,1,0:T(8,128)S(1)} collective-permute-done((f32[12,32,128]{2,1,0:T(8,128)S(1)}, f32[12,32,128]{2,1,0:T(8,128)S(1)}, u32[]{:S(2)}, u32[]{:S(2)}) %collective-permute-start.3) | collective-permute-done | bytes 196640 | tf_op jit(solution)/shard_map/ppermute | solution.py:524
  33.4 1.3 %collective-permute-start.4 = (f32[24,128]{1,0:T(8,128)S(1)}, f32[24,128]{1,0:T(8,128)S(1)}, u32[]{:S(2)}, u32[]{:S(2)}) collective-permute-start(f32[24,128]{1,0:T(8,128)S(1)} %get-tuple-element.49), channel_id=1, source_target_pairs={{0,12},{1,13},{2,14},{3,15},{16,28},{17,29},{18,30},{19,31},{32,44... | collective-permute-start | bytes 36872 | tf_op jit(solution)/shard_map/ppermute | solution.py:540
  34.7 14.0 %collective-permute-done.4 = f32[24,128]{1,0:T(8,128)S(1)} collective-permute-done((f32[24,128]{1,0:T(8,128)S(1)}, f32[24,128]{1,0:T(8,128)S(1)}, u32[]{:S(2)}, u32[]{:S(2)}) %collective-permute-start.4) | collective-permute-done | bytes 12320 | tf_op jit(solution)/shard_map/ppermute | solution.py:540
  48.7 1.3 %collective-permute-start.5 = (f32[24,128]{1,0:T(8,128)S(1)}, f32[24,128]{1,0:T(8,128)S(1)}, u32[]{:S(2)}, u32[]{:S(2)}) collective-permute-start(f32[24,128]{1,0:T(8,128)S(1)} %add.3.one), channel_id=1, source_target_pairs={{0,4},{12,8},{1,5},{13,9},{2,6},{14,10},{3,7},{15,11},{16,20},{28,... | collective-permute-start | bytes 36872 | tf_op jit(solution)/shard_map/ppermute | solution.py:542
  50.0 0.1 pad_add_fusion.spot
  50.1 0.6 shard_map.97
  50.8 0.1 collective-permute-done.5.two
  50.8 1.4 %shard_map.98 = f32[32,40,128]{2,1,0:T(8,128)} custom-call(s32[3]{0:T(128)S(1)} %pad_add_fusion.spot, f32[24,128]{1,0:T(8,128)S(1)} %add.3.one, f32[24,128]{1,0:T(8,128)S(1)} %collective-permute-done.5.two, f32[4,128]{1,0:T(4,128)S(1)} %get-tuple-element.36.cond, f32[32,24,128]{2,1,0:T(8,128)S(1)} %bitcast.14), custom_call_target="tpu_custom_call" | custom-call | flops 100000 | bytes 1000000 | tf_op jit(solution)/shard_map/pallas_call | solution.py:264
  52.3 8.5 %all-to-all-start.1 = ((f32[32,40,128]{2,1,0:T(8,128)}), f32[32,40,128]{2,1,0:T(8,128)S(1)}, u32[]{:S(2)}, u32[]{:S(2)}) async-start(f32[32,40,128]{2,1,0:T(8,128)} %shard_map.98), calls=%async_computation.1 | async-start | bytes 1310720 | tf_op jit(solution)/shard_map/all_to_all | solution.py:561
  60.8 0.5 shard_map.99
  61.3 2.8 %collective-permute-start.6 = (f32[12,24,128]{2,1,0:T(8,128)S(1)}, f32[12,24,128]{2,1,0:T(8,128)S(1)}, u32[]{:S(2)}, u32[]{:S(2)}) collective-permute-start(f32[12,24,128]{2,1,0:T(8,128)S(1)} %shard_map.99), channel_id=1, source_target_pairs={{0,1},{1,2},{2,3},{4,5},{5,6},{6,7},{8,9},{9,10},{10,11},{12,13},{... | collective-permute-start | bytes 442376 | tf_op jit(solution)/shard_map/ppermute | solution.py:559
  64.1 1.3 %collective-permute-start.7 = (f32[12,24,128]{2,1,0:T(8,128)S(1)}, f32[12,24,128]{2,1,0:T(8,128)S(1)}, u32[]{:S(2)}, u32[]{:S(2)}) collective-permute-start(f32[12,24,128]{2,1,0:T(8,128)S(1)} %shard_map.99), channel_id=1, source_target_pairs={{1,0},{2,1},{3,2},{5,4},{6,5},{7,6},{9,8},{10,9},{11,10},{13,12},{... | collective-permute-start | bytes 442376 | tf_op jit(solution)/shard_map/ppermute | solution.py:560
  65.4 0.8 collective-permute-done.6.from_low
  66.2 4.1 %collective-permute-done.7.from_high = f32[12,24,128]{2,1,0:T(8,128)S(1)} collective-permute-done((f32[12,24,128]{2,1,0:T(8,128)S(1)}, f32[12,24,128]{2,1,0:T(8,128)S(1)}, u32[]{:S(2)}, u32[]{:S(2)}) %collective-permute-start.7) | collective-permute-done | bytes 147488 | tf_op jit(solution)/shard_map/ppermute | solution.py:560
  70.3 5.5 %shard_map.100 = f32[8,64,128]{2,1,0:T(8,128)} custom-call(f32[12,4,16,128]{3,2,1,0:T(8,128)S(1)} %collective-permute-done.low, f32[12,4,16,128]{3,2,1,0:T(8,128)S(1)} %copy-done, f32[12,4,16,128]{3,2,1,0:T(8,128)S(1)} %collective-permute-done.1.high, f32[12,32,128]{2,1,0:T(8,128)S(1)} %collective-permute-done.3.above, ...), custom_call_target="tpu_custom_call" | custom-call | flops 1000000 | bytes 1000000 | tf_op jit(solution)/shard_map/pallas_call | solution.py:36
  75.8 4.0 %all-to-all-done.1 = f32[32,40,128]{2,1,0:T(8,128)S(1)} async-done(((f32[32,40,128]{2,1,0:T(8,128)}), f32[32,40,128]{2,1,0:T(8,128)S(1)}, u32[]{:S(2)}, u32[]{:S(2)}) %all-to-all-start.1) | async-done | bytes 655392 | tf_op jit(solution)/shard_map/all_to_all | solution.py:561
  79.8 0.1 shard_map.101.mine
  79.8 2.9 %collective-permute-start.8 = (f32[20,32,128]{2,1,0:T(8,128)S(1)}, f32[20,32,128]{2,1,0:T(8,128)S(1)}, u32[]{:S(2)}, u32[]{:S(2)}) collective-permute-start(f32[20,32,128]{2,1,0:T(8,128)S(1)} %shard_map.101.mine), channel_id=1, source_target_pairs={{0,4},{4,0},{8,12},{12,8},{1,5},{5,1},{9,13},{13,9},{2,6},{6,2},{1... | collective-permute-start | bytes 983048 | tf_op jit(solution)/shard_map/ppermute | solution.py:579
  82.7 0.1 shard_map.102
  82.8 1.1 %collective-permute-done.8.other = f32[20,32,128]{2,1,0:T(8,128)S(1)} collective-permute-done((f32[20,32,128]{2,1,0:T(8,128)S(1)}, f32[20,32,128]{2,1,0:T(8,128)S(1)}, u32[]{:S(2)}, u32[]{:S(2)}) %collective-permute-start.8) | collective-permute-done | bytes 327712 | tf_op jit(solution)/shard_map/ppermute | solution.py:579
  83.9 3.5 %shard_map.103 = (f32[4,128]{1,0:T(4,128)}, f32[32,256]{1,0:T(8,128)}) custom-call(s32[3]{0:T(128)S(1)} %pad_add_fusion.spot, f32[20,32,128]{2,1,0:T(8,128)S(1)} %shard_map.101.mine, f32[20,32,128]{2,1,0:T(8,128)S(1)} %collective-permute-done.8.other, s32[16,32,128]{2,1,0:T(8,128)S(1)} %get-tuple-element.45.cells, f32[256,128]{1,0:T(8,128)S(1)} %get-tuple-element.46.hot), custom_call_target="tpu_custom_call" | custom-call | flops 1000000 | bytes 1000000 | tf_op jit(solution)/shard_map/pallas_call | solution.py:36
  (4 shorter events, 0.1 us)
Async XLA Ops:
  2.8 23.2 %copy-start = (f32[12,4,16,128]{3,2,1,0:T(8,128)S(1)}, f32[12,4,16,128]{3,2,1,0:T(8,128)}, u32[]{:S(2)}) copy-start(f32[12,4,16,128]{3,2,1,0:T(8,128)} %get-tuple-element.28.own) | copy-start | bytes 1179652
  2.8 23.2 %collective-permute-start = (f32[12,4,16,128]{3,2,1,0:T(8,128)}, f32[12,4,16,128]{3,2,1,0:T(8,128)S(1)}, u32[]{:S(2)}, u32[]{:S(2)}) collective-permute-start(f32[12,4,16,128]{3,2,1,0:T(8,128)} %get-tuple-element.28.own), channel_id=1, source_target_pairs={{0,16},{16,32},{32,48},{48,64},{64,80},{80,96},{96,112},{112,128},... | collective-permute-start | bytes 1179656 | tf_op jit(solution)/shard_map/ppermute | solution.py:515
  7.0 19.0 %collective-permute-start.1 = (f32[12,4,16,128]{3,2,1,0:T(8,128)}, f32[12,4,16,128]{3,2,1,0:T(8,128)S(1)}, u32[]{:S(2)}, u32[]{:S(2)}) collective-permute-start(f32[12,4,16,128]{3,2,1,0:T(8,128)} %get-tuple-element.28.own), channel_id=1, source_target_pairs={{0,496},{16,0},{32,16},{48,32},{64,48},{80,64},{96,80},{112,96},{1... | collective-permute-start | bytes 1179656 | tf_op jit(solution)/shard_map/ppermute | solution.py:516
  26.1 6.3 %collective-permute-start.2 = (f32[12,32,128]{2,1,0:T(8,128)S(1)}, f32[12,32,128]{2,1,0:T(8,128)S(1)}, u32[]{:S(2)}, u32[]{:S(2)}) collective-permute-start(f32[12,32,128]{2,1,0:T(8,128)S(1)} %get-tuple-element.32), channel_id=1, source_target_pairs={{0,4},{4,8},{8,12},{1,5},{5,9},{9,13},{2,6},{6,10},{10,14},{3,7},{... | collective-permute-start | bytes 589832 | tf_op jit(solution)/shard_map/ppermute | solution.py:525
  27.4 6.0 %collective-permute-start.3 = (f32[12,32,128]{2,1,0:T(8,128)S(1)}, f32[12,32,128]{2,1,0:T(8,128)S(1)}, u32[]{:S(2)}, u32[]{:S(2)}) collective-permute-start(f32[12,32,128]{2,1,0:T(8,128)S(1)} %get-tuple-element.33), channel_id=1, source_target_pairs={{4,0},{8,4},{12,8},{5,1},{9,5},{13,9},{6,2},{10,6},{14,10},{7,3},{... | collective-permute-start | bytes 589832 | tf_op jit(solution)/shard_map/ppermute | solution.py:524
  33.4 15.3 %collective-permute-start.4 = (f32[24,128]{1,0:T(8,128)S(1)}, f32[24,128]{1,0:T(8,128)S(1)}, u32[]{:S(2)}, u32[]{:S(2)}) collective-permute-start(f32[24,128]{1,0:T(8,128)S(1)} %get-tuple-element.49), channel_id=1, source_target_pairs={{0,12},{1,13},{2,14},{3,15},{16,28},{17,29},{18,30},{19,31},{32,44... | collective-permute-start | bytes 36872 | tf_op jit(solution)/shard_map/ppermute | solution.py:540
  48.7 2.1 %collective-permute-start.5 = (f32[24,128]{1,0:T(8,128)S(1)}, f32[24,128]{1,0:T(8,128)S(1)}, u32[]{:S(2)}, u32[]{:S(2)}) collective-permute-start(f32[24,128]{1,0:T(8,128)S(1)} %add.3.one), channel_id=1, source_target_pairs={{0,4},{12,8},{1,5},{13,9},{2,6},{14,10},{3,7},{15,11},{16,20},{28,... | collective-permute-start | bytes 36872 | tf_op jit(solution)/shard_map/ppermute | solution.py:542
  52.3 27.5 %all-to-all-start.1 = ((f32[32,40,128]{2,1,0:T(8,128)}), f32[32,40,128]{2,1,0:T(8,128)S(1)}, u32[]{:S(2)}, u32[]{:S(2)}) async-start(f32[32,40,128]{2,1,0:T(8,128)} %shard_map.98), calls=%async_computation.1 | async-start | bytes 1310720 | tf_op jit(solution)/shard_map/all_to_all | solution.py:561
  61.3 4.9 %collective-permute-start.6 = (f32[12,24,128]{2,1,0:T(8,128)S(1)}, f32[12,24,128]{2,1,0:T(8,128)S(1)}, u32[]{:S(2)}, u32[]{:S(2)}) collective-permute-start(f32[12,24,128]{2,1,0:T(8,128)S(1)} %shard_map.99), channel_id=1, source_target_pairs={{0,1},{1,2},{2,3},{4,5},{5,6},{6,7},{8,9},{9,10},{10,11},{12,13},{... | collective-permute-start | bytes 442376 | tf_op jit(solution)/shard_map/ppermute | solution.py:559
  64.1 6.2 %collective-permute-start.7 = (f32[12,24,128]{2,1,0:T(8,128)S(1)}, f32[12,24,128]{2,1,0:T(8,128)S(1)}, u32[]{:S(2)}, u32[]{:S(2)}) collective-permute-start(f32[12,24,128]{2,1,0:T(8,128)S(1)} %shard_map.99), channel_id=1, source_target_pairs={{1,0},{2,1},{3,2},{5,4},{6,5},{7,6},{9,8},{10,9},{11,10},{13,12},{... | collective-permute-start | bytes 442376 | tf_op jit(solution)/shard_map/ppermute | solution.py:560
  79.8 4.1 %collective-permute-start.8 = (f32[20,32,128]{2,1,0:T(8,128)S(1)}, f32[20,32,128]{2,1,0:T(8,128)S(1)}, u32[]{:S(2)}, u32[]{:S(2)}) collective-permute-start(f32[20,32,128]{2,1,0:T(8,128)S(1)} %shard_map.101.mine), channel_id=1, source_target_pairs={{0,4},{4,0},{8,12},{12,8},{1,5},{5,1},{9,13},{13,9},{2,6},{6,2},{1... | collective-permute-start | bytes 983048 | tf_op jit(solution)/shard_map/ppermute | solution.py:579

commit v10 on v9

--- a/solution.py
+++ b/solution.py
@@ -56,7 +56,7 @@
 
 
 def first_body(*refs):
-    sources, (own, slots, plain), held, sems = refs[:7], refs[7:10], refs[10:17], refs[17]
+    sources, (staged, slots, plain, own), held, sems = refs[:7], refs[7:11], refs[11:18], refs[18]
     moves = [
         pltpu.make_async_copy(source, target, sems.at[i])
         for i, (source, target) in enumerate(zip(sources, held))
@@ -78,9 +78,12 @@
                 own[plane, lon] = fields[plane, at, :]
             else:
                 own[plane, lon] = plain[plane - FIELDS, at, :]
+    leave = pltpu.make_async_copy(own, staged, sems.at[7])
+    leave.start()
     for move in moves[3:]:
         move.wait()
     slot_body(owners, rows, maps, conductance, slots)
+    leave.wait()
 
 
 def first(*args):
@@ -89,10 +92,13 @@
         first_body,
         out_shape=(arr(PLANES, LONS, SHELLS, LATS), arr(4 * SENT, LATS)),
         in_specs=[pl.BlockSpec(memory_space=pltpu.HBM)] * len(args),
-        out_specs=[vmem, vmem],
-        scratch_shapes=[pltpu.VMEM((4, SHELLS * LONS, LATS), F32)]
+        out_specs=[pl.BlockSpec(memory_space=pl.ANY), vmem],
+        scratch_shapes=[
+            pltpu.VMEM((4, SHELLS * LONS, LATS), F32),
+            pltpu.VMEM((PLANES, LONS, SHELLS, LATS), F32),
+        ]
         + [pltpu.VMEM(arg.shape, arg.dtype) for arg in args]
-        + [pltpu.SemaphoreType.DMA((len(args),))],
+        + [pltpu.SemaphoreType.DMA((len(args) + 1,))],
         compiler_params=pltpu.CompilerParams(vmem_limit_bytes=60 * 2**20),
         cost_estimate=pl.CostEstimate(flops=10**6, bytes_accessed=10**6, transcendentals=0),
     )(*args)
@@ -219,20 +225,21 @@
 
 
 def base_body(spot, sent, out, cond):
-    step = LATE - 16
     odd = spot[0] % 2 == 1
+    for row in range(16):
+        out[pl.ds(row, 32, stride=LATE), :] = jnp.zeros((32, LATS), F32)
     for lon in range(LONS):
         at = 130 + lon
         lines = [sent[rad * SENT + at : rad * SENT + at + 1, :] for rad in range(4)]
         cond[lon : lon + 1, :] = jnp.where(odd, lines[2], lines[0])
         line = jnp.where(odd, lines[3], lines[1])
-        out[pl.ds(lon, 32, stride=step), :] = jnp.broadcast_to(line, (32, LATS))
+        out[pl.ds(16 + lon, 32, stride=LATE), :] = jnp.broadcast_to(line, (32, LATS))
     lane = lax.broadcasted_iota(jnp.int32, (32, LATS), 1)
     owner = lax.broadcasted_iota(jnp.int32, (32, LATS), 0)
     for rad in range(4):
         for row in range(4):
             at = rad * SENT + row * 32
-            out[pl.ds(4 + rad * 5 + row, 32, stride=step), :] = sent[at : at + 32, :]
+            out[pl.ds(20 + rad * 5 + row, 32, stride=LATE), :] = sent[at : at + 32, :]
         marks = []
         for slot in range(2):
             at = rad * SENT + 128 + slot
@@ -240,22 +247,19 @@
             marks.append(
                 jnp.sum(jnp.where(lane == owner + spot[1] * 32, line, 0.0), axis=1, keepdims=True)
             )
-        out[pl.ds(8 + rad * 5, 32, stride=step), :] = jnp.where(lane < 64, marks[0], marks[1])
-
-
-def join_body(spot, one, two, cond, base, out, head, copies, sems):
-    rest = pltpu.make_async_copy(base, out.at[:, pl.ds(16, LATE - 16), :], sems.at[0])
-    rest.start()
+        out[pl.ds(24 + rad * 5, 32, stride=LATE), :] = jnp.where(lane < 64, marks[0], marks[1])
+
+
+def join_body(spot, one, two, cond, base, out, head, copies, sem):
     source = one[...] + two[...]
     head[:12, :] = jnp.where(spot[0] % 2 == 1, source[12:], source[:12])
     head[12:, :] = cond[...]
     mine = head[...]
     for owner in range(32):
         copies[owner] = mine
-    move = pltpu.make_async_copy(copies, out.at[:, pl.ds(0, 16), :], sems.at[1])
+    move = pltpu.make_async_copy(copies, out.at[:, pl.ds(0, 16), :], sem)
     move.start()
     move.wait()
-    rest.wait()
 
 
 def join(spot, one, two, cond, base):
@@ -269,8 +273,9 @@
         scratch_shapes=[
             pltpu.VMEM((16, LATS), F32),
             pltpu.VMEM((32, 16, LATS), F32),
-            pltpu.SemaphoreType.DMA((2,)),
+            pltpu.SemaphoreType.DMA,
         ],
+        input_output_aliases={4: 0},
         compiler_params=pltpu.CompilerParams(vmem_limit_bytes=4 * 2**20),
         cost_estimate=pl.CostEstimate(flops=10**5, bytes_accessed=10**6, transcendentals=0),
     )(spot, one, two, cond, base)
@@ -281,18 +286,19 @@
         out[row] = late[pl.ds(row, 32, stride=LATE), :]
 
 
-def mark_body(late, cells, hot):
+def mark_body(late, cells, hot, tall):
     lane = lax.broadcasted_iota(jnp.int32, (32, LATS), 1).astype(F32)
     for rad in range(4):
         marks = late[pl.ds(HALF + rad * 5 + 4, 32, stride=LATE), :]
         for slot in range(2):
             row = marks if slot == 0 else pltpu.roll(marks, 64, axis=1)
-            at = (slot * 4 + rad) * 32
-            hot[at : at + 32, :] = jnp.where(row == lane, 1.0, 0.0)
+            tall[slot, rad * 32 : rad * 32 + 32, :] = jnp.where(row == lane, 1.0, 0.0)
             for half in range(2):
                 cells[(rad * 2 + slot) * 2 + half] = late[
                     pl.ds(HALF + rad * 5 + 2 * slot + half, 32, stride=LATE), :
                 ].astype(jnp.int32)
+    for slot in range(2):
+        hot[:, slot * LATS : (slot + 1) * LATS] = jnp.transpose(tall[slot])[:ROWS_OWN]
 
 
 def chunks():
@@ -489,16 +495,13 @@
                     )
                     value = jnp.where(lon_at == lon, found, value)
                 picked[at : at + devs, 128 * half : 128 * half + 128] = value
-    rest = picked[...]
+    records = picked[...]
     rows = hot[...].astype(jnp.bfloat16)
-    summed = jnp.zeros((LATS, 2 * LATS), F32)
-    for part in range(3):
-        piece = rest.astype(jnp.bfloat16)
-        rest = rest - piece.astype(F32)
-        summed = summed + lax.dot_general(
-            rows, piece, (((0,), (0,)), ((), ())), preferred_element_type=F32
-        )
-    foot[...] = summed[:ROWS_OWN]
+    large = records.astype(jnp.bfloat16)
+    small = (records - large.astype(F32)).astype(jnp.bfloat16)
+    foot[...] = jnp.dot(rows, large, preferred_element_type=F32) + jnp.dot(
+        rows, small, preferred_element_type=F32
+    )
 
 
 def shards(plasma_fields, velocity, resistivity, conductance, foot_map, foot_owner, foot_row):
@@ -542,11 +545,11 @@
     near = lax.ppermute(far, "sec", [(0, 1), (3, 2)])
     base, cond = call(
         base_body,
-        (arr(32 * (LATE - 16), LATS), arr(LONS, LATS)),
+        (arr(32 * LATE, LATS), arr(LONS, LATS)),
         (spot, sent.reshape(4 * SENT, LATS)),
         smem=(0,),
     )
-    late = join(spot, far, near, cond, base.reshape(32, LATE - 16, LATS))
+    late = join(spot, far, near, cond, base.reshape(32, LATE, LATS))
     late, low, high = lax.optimization_barrier((late, low, high))
 
     blocks = (low, own, high, above, below)
@@ -579,8 +582,9 @@
     other = lax.ppermute(mine, "sec", [(0, 1), (1, 0), (2, 3), (3, 2)])
     cells, hot = call(
         mark_body,
-        (jax.ShapeDtypeStruct((16, 32, LATS), jnp.int32), arr(256, LATS)),
+        (jax.ShapeDtypeStruct((16, 32, LATS), jnp.int32), arr(ROWS_OWN, 2 * LATS)),
         (late,),
+        scratch=(pltpu.VMEM((2, LATS, LATS), F32),),
     )
     plane = pltpu.VMEM((LONS, 32, 4 * LATS), F32)
     potential, foot_table = call(

time: 88 us -> 90.9 us (1.033)
  waiting for transfers between devices: 25.1 us -> 26.6 us
  Pallas kernels: 14 us -> 15 us
    ppermute x1, starting transfers between devices: 4.13 us -> 1.92 us  [shards(): low = lax.ppermute(own, 'lon', shift('lon', 1, True))]
    ppermute x1, starting transfers between devices: 9.37 us -> 11.6 us  [shards(): high = lax.ppermute(own, 'lon', shift('lon', -1, True))]
    ppermute x1, waiting for transfers between devices: 0.01 us -> 2.01 us  [shards(): low = lax.ppermute(own, 'lon', shift('lon', 1, True))]
    ppermute x1, waiting for transfers between devices: 4.11 us -> 2.14 us  [shards(): from_high = lax.ppermute(edges, 'rad', shift('rad', -1, False))]
    ppermute x1, starting transfers between devices: 2.83 us -> 3.99 us  [shards(): from_low = lax.ppermute(edges, 'rad', shift('rad', 1, False))]
    all_to_all x1, waiting for transfers between devices: 3.99 us -> 5.05 us  [shards(): late = lax.all_to_all(late, 'lon', split_axis=0, concat_axis=0, tiled=True)]
where the time goes in v10:
time: 90.9 us; the launch traced here: 90.5 us
  starting transfers between devices  38 us (42%)
  waiting for transfers between devices  26.6 us (29%)
  Pallas kernels  15 us (17%)
  blocking collectives  9.94 us (11%)
    ppermute x1, waiting for transfers between devices, shards(): far = lax.ppermute(inner, 'sec', [(0, 3)])  14.4 us
    ppermute x1, starting transfers between devices, shards(): high = lax.ppermute(own, 'lon', shift('lon', -1, True))  11.6 us
    pallas_call x8, Pallas kernels, call(): pl.pallas_call(body, out_shape=out_shape, in_specs=specs, out_specs=[vmem...  11.2 us
    all_to_all x1, blocking collectives, shards(): lax.all_to_all(slots.reshape(4, SENT, LATS), 'rad', split_axis=0, concat_...  9.94 us
    all_to_all x1, starting transfers between devices, shards(): late = lax.all_to_all(late, 'lon', split_axis=0, concat_axis=0, tiled=True)  8.61 us
    all_to_all x1, waiting for transfers between devices, shards(): late = lax.all_to_all(late, 'lon', split_axis=0, concat_axis=0, tiled=True)  5.05 us
    ppermute x1, starting transfers between devices, shards(): above = lax.ppermute(down, 'sec', shift('sec', -1, False))  4.41 us
    ppermute x1, starting transfers between devices, shards(): from_low = lax.ppermute(edges, 'rad', shift('rad', 1, False))  3.99 us
  transfers between devices with their start and end apart: 10, of which 7 were waited for; matrix products, arithmetic and copies ran while one was open for 0% of the time, Pallas kernels for 8%

profile of v10, /device:TPU:57, one launch (start us, length us, event | category | flops | bytes accessed | tf_op | source)
XLA Modules:
  0.0 90.5 jit_solution(3911475116668905336)
XLA Ops:
  0.6 2.5 %shard_map.94 = (f32[12,4,16,128]{3,2,1,0:T(8,128)}, f32[544,128]{1,0:T(8,128)}) custom-call(f32[8,64,128]{2,1,0:T(8,128)} %bitcast.15, bf16[3,16,4,128]{3,2,1,0:T(4,128)(2,1)} %refs_1_.1, bf16[16,4,128]{2,1,0:T(4,128)(2,1)} %refs_2_.1, s32[1,128]{1,0:T(1,128)} %bitcast.17, s32[1,128]{1,0:T(1,128)} %bitcast.18, s32[128,256]{1,0:T(8,128)} %refs_5_.1, ...), custom_call_target="tpu_custom_call" | custom-call | flops 1000000 | bytes 1000000 | tf_op jit(solution)/shard_map/pallas_call | solution.py:91
  3.1 0.0 copy-start
  3.2 11.6 %collective-permute-start.1 = (f32[12,4,16,128]{3,2,1,0:T(8,128)}, f32[12,4,16,128]{3,2,1,0:T(8,128)S(1)}, u32[]{:S(2)}, u32[]{:S(2)}) collective-permute-start(f32[12,4,16,128]{3,2,1,0:T(8,128)} %get-tuple-element.28.own), channel_id=1, source_target_pairs={{0,496},{16,0},{32,16},{48,32},{64,48},{80,64},{96,80},{112,96},{1... | collective-permute-start | bytes 1179656 | tf_op jit(solution)/shard_map/ppermute | solution.py:519
  14.7 1.9 %collective-permute-start = (f32[12,4,16,128]{3,2,1,0:T(8,128)}, f32[12,4,16,128]{3,2,1,0:T(8,128)S(1)}, u32[]{:S(2)}, u32[]{:S(2)}) collective-permute-start(f32[12,4,16,128]{3,2,1,0:T(8,128)} %get-tuple-element.28.own), channel_id=1, source_target_pairs={{0,16},{16,32},{32,48},{48,64},{64,80},{80,96},{96,112},{112,128},... | collective-permute-start | bytes 1179656 | tf_op jit(solution)/shard_map/ppermute | solution.py:518
  16.7 9.9 %all_to_all.10 = f32[4,136,128]{2,1,0:T(8,128)S(1)} all-to-all(f32[4,136,128]{2,1,0:T(8,128)} %bitcast.14), channel_id=1, replica_groups=mesh['lon'=32,'sec'=4,'rad'=4] {'rad'}, dimensions={0} | all-to-all | bytes 557056 | tf_op jit(solution)/shard_map/all_to_all | solution.py:521
  26.6 0.0 collective-permute-done.1.high
  26.6 2.0 %collective-permute-done.low = f32[12,4,16,128]{3,2,1,0:T(8,128)S(1)} collective-permute-done((f32[12,4,16,128]{3,2,1,0:T(8,128)}, f32[12,4,16,128]{3,2,1,0:T(8,128)S(1)}, u32[]{:S(2)}, u32[]{:S(2)}) %collective-permute-start) | collective-permute-done | bytes 393248 | tf_op jit(solution)/shard_map/ppermute | solution.py:518
  28.6 0.0 copy-done
  28.6 0.1 shard_map.96
  28.7 1.3 %collective-permute-start.2 = (f32[12,32,128]{2,1,0:T(8,128)S(1)}, f32[12,32,128]{2,1,0:T(8,128)S(1)}, u32[]{:S(2)}, u32[]{:S(2)}) collective-permute-start(f32[12,32,128]{2,1,0:T(8,128)S(1)} %get-tuple-element.32), channel_id=1, source_target_pairs={{0,4},{4,8},{8,12},{1,5},{5,9},{9,13},{2,6},{6,10},{10,14},{3,7},{... | collective-permute-start | bytes 589832 | tf_op jit(solution)/shard_map/ppermute | solution.py:528
  30.0 4.4 %collective-permute-start.3 = (f32[12,32,128]{2,1,0:T(8,128)S(1)}, f32[12,32,128]{2,1,0:T(8,128)S(1)}, u32[]{:S(2)}, u32[]{:S(2)}) collective-permute-start(f32[12,32,128]{2,1,0:T(8,128)S(1)} %get-tuple-element.33), channel_id=1, source_target_pairs={{4,0},{8,4},{12,8},{5,1},{9,5},{13,9},{6,2},{10,6},{14,10},{7,3},{... | collective-permute-start | bytes 589832 | tf_op jit(solution)/shard_map/ppermute | solution.py:527
  34.5 0.0 collective-permute-done.2.below
  34.5 1.0 %collective-permute-done.3.above = f32[12,32,128]{2,1,0:T(8,128)S(1)} collective-permute-done((f32[12,32,128]{2,1,0:T(8,128)S(1)}, f32[12,32,128]{2,1,0:T(8,128)S(1)}, u32[]{:S(2)}, u32[]{:S(2)}) %collective-permute-start.3) | collective-permute-done | bytes 196640 | tf_op jit(solution)/shard_map/ppermute | solution.py:527
  35.5 1.3 %collective-permute-start.4 = (f32[24,128]{1,0:T(8,128)S(1)}, f32[24,128]{1,0:T(8,128)S(1)}, u32[]{:S(2)}, u32[]{:S(2)}) collective-permute-start(f32[24,128]{1,0:T(8,128)S(1)} %get-tuple-element.49), channel_id=1, source_target_pairs={{0,12},{1,13},{2,14},{3,15},{16,28},{17,29},{18,30},{19,31},{32,44... | collective-permute-start | bytes 36872 | tf_op jit(solution)/shard_map/ppermute | solution.py:543
  36.8 14.4 %collective-permute-done.4 = f32[24,128]{1,0:T(8,128)S(1)} collective-permute-done((f32[24,128]{1,0:T(8,128)S(1)}, f32[24,128]{1,0:T(8,128)S(1)}, u32[]{:S(2)}, u32[]{:S(2)}) %collective-permute-start.4) | collective-permute-done | bytes 12320 | tf_op jit(solution)/shard_map/ppermute | solution.py:543
  51.2 1.3 %collective-permute-start.5 = (f32[24,128]{1,0:T(8,128)S(1)}, f32[24,128]{1,0:T(8,128)S(1)}, u32[]{:S(2)}, u32[]{:S(2)}) collective-permute-start(f32[24,128]{1,0:T(8,128)S(1)} %add.3.one), channel_id=1, source_target_pairs={{0,4},{12,8},{1,5},{13,9},{2,6},{14,10},{3,7},{15,11},{16,20},{28,... | collective-permute-start | bytes 36872 | tf_op jit(solution)/shard_map/ppermute | solution.py:545
  52.5 0.1 pad_add_fusion.spot
  52.5 1.5 %shard_map.97 = (f32[1280,128]{1,0:T(8,128)}, f32[4,128]{1,0:T(4,128)S(1)}) custom-call(s32[3]{0:T(128)S(1)} %pad_add_fusion.spot, f32[544,128]{1,0:T(8,128)S(1)} %bitcast.13), custom_call_target="tpu_custom_call" | custom-call | flops 1000000 | bytes 1000000 | tf_op jit(solution)/shard_map/pallas_call | solution.py:36
  54.0 0.0 collective-permute-done.5.two
  54.0 1.3 %shard_map.98 = f32[32,40,128]{2,1,0:T(8,128)} custom-call(s32[3]{0:T(128)S(1)} %pad_add_fusion.spot, f32[24,128]{1,0:T(8,128)S(1)} %add.3.one, f32[24,128]{1,0:T(8,128)S(1)} %collective-permute-done.5.two, f32[4,128]{1,0:T(4,128)S(1)} %get-tuple-element.36.cond, f32[32,40,128]{2,1,0:T(8,128)} %bitcast.8.base), custom_call_target="tpu_custom_call", output_to_operand_aliasing={{}: (4, {})} | custom-call | flops 100000 | bytes 1000000 | tf_op jit(solution)/shard_map/pallas_call | solution.py:268
  55.3 8.6 %all-to-all-start.1 = ((f32[32,40,128]{2,1,0:T(8,128)}), f32[32,40,128]{2,1,0:T(8,128)S(1)}, u32[]{:S(2)}, u32[]{:S(2)}) async-start(f32[32,40,128]{2,1,0:T(8,128)} %shard_map.98), calls=%async_computation.1 | async-start | bytes 1310720 | tf_op jit(solution)/shard_map/all_to_all | solution.py:564
  64.0 0.5 shard_map.99
  64.5 1.3 %collective-permute-start.7 = (f32[12,24,128]{2,1,0:T(8,128)S(1)}, f32[12,24,128]{2,1,0:T(8,128)S(1)}, u32[]{:S(2)}, u32[]{:S(2)}) collective-permute-start(f32[12,24,128]{2,1,0:T(8,128)S(1)} %shard_map.99), channel_id=1, source_target_pairs={{1,0},{2,1},{3,2},{5,4},{6,5},{7,6},{9,8},{10,9},{11,10},{13,12},{... | collective-permute-start | bytes 442376 | tf_op jit(solution)/shard_map/ppermute | solution.py:563
  65.8 4.0 %collective-permute-start.6 = (f32[12,24,128]{2,1,0:T(8,128)S(1)}, f32[12,24,128]{2,1,0:T(8,128)S(1)}, u32[]{:S(2)}, u32[]{:S(2)}) collective-permute-start(f32[12,24,128]{2,1,0:T(8,128)S(1)} %shard_map.99), channel_id=1, source_target_pairs={{0,1},{1,2},{2,3},{4,5},{5,6},{6,7},{8,9},{9,10},{10,11},{12,13},{... | collective-permute-start | bytes 442376 | tf_op jit(solution)/shard_map/ppermute | solution.py:562
  69.8 2.1 %collective-permute-done.7.from_high = f32[12,24,128]{2,1,0:T(8,128)S(1)} collective-permute-done((f32[12,24,128]{2,1,0:T(8,128)S(1)}, f32[12,24,128]{2,1,0:T(8,128)S(1)}, u32[]{:S(2)}, u32[]{:S(2)}) %collective-permute-start.7) | collective-permute-done | bytes 147488 | tf_op jit(solution)/shard_map/ppermute | solution.py:563
  71.9 0.9 %collective-permute-done.6.from_low = f32[12,24,128]{2,1,0:T(8,128)S(1)} collective-permute-done((f32[12,24,128]{2,1,0:T(8,128)S(1)}, f32[12,24,128]{2,1,0:T(8,128)S(1)}, u32[]{:S(2)}, u32[]{:S(2)}) %collective-permute-start.6) | collective-permute-done | bytes 147488 | tf_op jit(solution)/shard_map/ppermute | solution.py:562
  72.8 5.5 %shard_map.100 = f32[8,64,128]{2,1,0:T(8,128)} custom-call(f32[12,4,16,128]{3,2,1,0:T(8,128)S(1)} %collective-permute-done.low, f32[12,4,16,128]{3,2,1,0:T(8,128)S(1)} %copy-done, f32[12,4,16,128]{3,2,1,0:T(8,128)S(1)} %collective-permute-done.1.high, f32[12,32,128]{2,1,0:T(8,128)S(1)} %collective-permute-done.3.above, ...), custom_call_target="tpu_custom_call" | custom-call | flops 1000000 | bytes 1000000 | tf_op jit(solution)/shard_map/pallas_call | solution.py:36
  78.3 5.0 %all-to-all-done.1 = f32[32,40,128]{2,1,0:T(8,128)S(1)} async-done(((f32[32,40,128]{2,1,0:T(8,128)}), f32[32,40,128]{2,1,0:T(8,128)S(1)}, u32[]{:S(2)}, u32[]{:S(2)}) %all-to-all-start.1) | async-done | bytes 655392 | tf_op jit(solution)/shard_map/all_to_all | solution.py:564
  83.3 0.1 shard_map.101.mine
  83.4 2.3 %collective-permute-start.8 = (f32[20,32,128]{2,1,0:T(8,128)S(1)}, f32[20,32,128]{2,1,0:T(8,128)S(1)}, u32[]{:S(2)}, u32[]{:S(2)}) collective-permute-start(f32[20,32,128]{2,1,0:T(8,128)S(1)} %shard_map.101.mine), channel_id=1, source_target_pairs={{0,4},{4,0},{8,12},{12,8},{1,5},{5,1},{9,13},{13,9},{2,6},{6,2},{1... | collective-permute-start | bytes 983048 | tf_op jit(solution)/shard_map/ppermute | solution.py:582
  85.8 0.1 shard_map.102
  85.9 1.1 %collective-permute-done.8.other = f32[20,32,128]{2,1,0:T(8,128)S(1)} collective-permute-done((f32[20,32,128]{2,1,0:T(8,128)S(1)}, f32[20,32,128]{2,1,0:T(8,128)S(1)}, u32[]{:S(2)}, u32[]{:S(2)}) %collective-permute-start.8) | collective-permute-done | bytes 327712 | tf_op jit(solution)/shard_map/ppermute | solution.py:582
  87.0 3.5 %shard_map.103 = (f32[4,128]{1,0:T(4,128)}, f32[32,256]{1,0:T(8,128)}) custom-call(s32[3]{0:T(128)S(1)} %pad_add_fusion.spot, f32[20,32,128]{2,1,0:T(8,128)S(1)} %shard_map.101.mine, f32[20,32,128]{2,1,0:T(8,128)S(1)} %collective-permute-done.8.other, s32[16,32,128]{2,1,0:T(8,128)S(1)} %get-tuple-element.45.cells, f32[32,256]{1,0:T(8,128)S(1)} %get-tuple-element.46.hot), custom_call_target="tpu_custom_call" | custom-call | flops 1000000 | bytes 1000000 | tf_op jit(solution)/shard_map/pallas_call | solution.py:36
  (4 shorter events, 0.1 us)
Async XLA Ops:
  3.1 25.5 %copy-start = (f32[12,4,16,128]{3,2,1,0:T(8,128)S(1)}, f32[12,4,16,128]{3,2,1,0:T(8,128)}, u32[]{:S(2)}) copy-start(f32[12,4,16,128]{3,2,1,0:T(8,128)} %get-tuple-element.28.own) | copy-start | bytes 1179652
  3.2 23.5 %collective-permute-start.1 = (f32[12,4,16,128]{3,2,1,0:T(8,128)}, f32[12,4,16,128]{3,2,1,0:T(8,128)S(1)}, u32[]{:S(2)}, u32[]{:S(2)}) collective-permute-start(f32[12,4,16,128]{3,2,1,0:T(8,128)} %get-tuple-element.28.own), channel_id=1, source_target_pairs={{0,496},{16,0},{32,16},{48,32},{64,48},{80,64},{96,80},{112,96},{1... | collective-permute-start | bytes 1179656 | tf_op jit(solution)/shard_map/ppermute | solution.py:519
  14.7 13.9 %collective-permute-start = (f32[12,4,16,128]{3,2,1,0:T(8,128)}, f32[12,4,16,128]{3,2,1,0:T(8,128)S(1)}, u32[]{:S(2)}, u32[]{:S(2)}) collective-permute-start(f32[12,4,16,128]{3,2,1,0:T(8,128)} %get-tuple-element.28.own), channel_id=1, source_target_pairs={{0,16},{16,32},{32,48},{48,64},{64,80},{80,96},{96,112},{112,128},... | collective-permute-start | bytes 1179656 | tf_op jit(solution)/shard_map/ppermute | solution.py:518
  28.7 5.8 %collective-permute-start.2 = (f32[12,32,128]{2,1,0:T(8,128)S(1)}, f32[12,32,128]{2,1,0:T(8,128)S(1)}, u32[]{:S(2)}, u32[]{:S(2)}) collective-permute-start(f32[12,32,128]{2,1,0:T(8,128)S(1)} %get-tuple-element.32), channel_id=1, source_target_pairs={{0,4},{4,8},{8,12},{1,5},{5,9},{9,13},{2,6},{6,10},{10,14},{3,7},{... | collective-permute-start | bytes 589832 | tf_op jit(solution)/shard_map/ppermute | solution.py:528
  30.0 5.5 %collective-permute-start.3 = (f32[12,32,128]{2,1,0:T(8,128)S(1)}, f32[12,32,128]{2,1,0:T(8,128)S(1)}, u32[]{:S(2)}, u32[]{:S(2)}) collective-permute-start(f32[12,32,128]{2,1,0:T(8,128)S(1)} %get-tuple-element.33), channel_id=1, source_target_pairs={{4,0},{8,4},{12,8},{5,1},{9,5},{13,9},{6,2},{10,6},{14,10},{7,3},{... | collective-permute-start | bytes 589832 | tf_op jit(solution)/shard_map/ppermute | solution.py:527
  35.5 15.7 %collective-permute-start.4 = (f32[24,128]{1,0:T(8,128)S(1)}, f32[24,128]{1,0:T(8,128)S(1)}, u32[]{:S(2)}, u32[]{:S(2)}) collective-permute-start(f32[24,128]{1,0:T(8,128)S(1)} %get-tuple-element.49), channel_id=1, source_target_pairs={{0,12},{1,13},{2,14},{3,15},{16,28},{17,29},{18,30},{19,31},{32,44... | collective-permute-start | bytes 36872 | tf_op jit(solution)/shard_map/ppermute | solution.py:543
  51.2 2.9 %collective-permute-start.5 = (f32[24,128]{1,0:T(8,128)S(1)}, f32[24,128]{1,0:T(8,128)S(1)}, u32[]{:S(2)}, u32[]{:S(2)}) collective-permute-start(f32[24,128]{1,0:T(8,128)S(1)} %add.3.one), channel_id=1, source_target_pairs={{0,4},{12,8},{1,5},{13,9},{2,6},{14,10},{3,7},{15,11},{16,20},{28,... | collective-permute-start | bytes 36872 | tf_op jit(solution)/shard_map/ppermute | solution.py:545
  55.3 28.0 %all-to-all-start.1 = ((f32[32,40,128]{2,1,0:T(8,128)}), f32[32,40,128]{2,1,0:T(8,128)S(1)}, u32[]{:S(2)}, u32[]{:S(2)}) async-start(f32[32,40,128]{2,1,0:T(8,128)} %shard_map.98), calls=%async_computation.1 | async-start | bytes 1310720 | tf_op jit(solution)/shard_map/all_to_all | solution.py:564
  64.5 7.4 %collective-permute-start.7 = (f32[12,24,128]{2,1,0:T(8,128)S(1)}, f32[12,24,128]{2,1,0:T(8,128)S(1)}, u32[]{:S(2)}, u32[]{:S(2)}) collective-permute-start(f32[12,24,128]{2,1,0:T(8,128)S(1)} %shard_map.99), channel_id=1, source_target_pairs={{1,0},{2,1},{3,2},{5,4},{6,5},{7,6},{9,8},{10,9},{11,10},{13,12},{... | collective-permute-start | bytes 442376 | tf_op jit(solution)/shard_map/ppermute | solution.py:563
  65.8 7.1 %collective-permute-start.6 = (f32[12,24,128]{2,1,0:T(8,128)S(1)}, f32[12,24,128]{2,1,0:T(8,128)S(1)}, u32[]{:S(2)}, u32[]{:S(2)}) collective-permute-start(f32[12,24,128]{2,1,0:T(8,128)S(1)} %shard_map.99), channel_id=1, source_target_pairs={{0,1},{1,2},{2,3},{4,5},{5,6},{6,7},{8,9},{9,10},{10,11},{12,13},{... | collective-permute-start | bytes 442376 | tf_op jit(solution)/shard_map/ppermute | solution.py:562
  83.4 3.6 %collective-permute-start.8 = (f32[20,32,128]{2,1,0:T(8,128)S(1)}, f32[20,32,128]{2,1,0:T(8,128)S(1)}, u32[]{:S(2)}, u32[]{:S(2)}) collective-permute-start(f32[20,32,128]{2,1,0:T(8,128)S(1)} %shard_map.101.mine), channel_id=1, source_target_pairs={{0,4},{4,0},{8,12},{12,8},{1,5},{5,1},{9,13},{13,9},{2,6},{6,2},{1... | collective-permute-start | bytes 983048 | tf_op jit(solution)/shard_map/ppermute | solution.py:582

commit v11 on v9

--- a/solution.py
+++ b/solution.py
@@ -159,7 +159,9 @@
 def raw_body(low, own, high, out):
     for plane, wide, at, count in raw_chunks():
         ref = (low, own, high)[wide // LONS]
-        out[at : at + count, :] = ref[plane, wide % LONS, :count, :]
+        for block in range(4):
+            row = block * RAW + at
+            out[row : row + count, :] = ref[plane, wide % LONS, :count, :]
 
 
 def inner_body(raw, out, cells):
@@ -281,18 +283,19 @@
         out[row] = late[pl.ds(row, 32, stride=LATE), :]
 
 
-def mark_body(late, cells, hot):
+def mark_body(late, cells, hot, tall):
     lane = lax.broadcasted_iota(jnp.int32, (32, LATS), 1).astype(F32)
     for rad in range(4):
         marks = late[pl.ds(HALF + rad * 5 + 4, 32, stride=LATE), :]
         for slot in range(2):
             row = marks if slot == 0 else pltpu.roll(marks, 64, axis=1)
-            at = (slot * 4 + rad) * 32
-            hot[at : at + 32, :] = jnp.where(row == lane, 1.0, 0.0)
+            tall[slot, rad * 32 : rad * 32 + 32, :] = jnp.where(row == lane, 1.0, 0.0)
             for half in range(2):
                 cells[(rad * 2 + slot) * 2 + half] = late[
                     pl.ds(HALF + rad * 5 + 2 * slot + half, 32, stride=LATE), :
                 ].astype(jnp.int32)
+    for slot in range(2):
+        hot[:, slot * LATS : (slot + 1) * LATS] = jnp.transpose(tall[slot])[:ROWS_OWN]
 
 
 def chunks():
@@ -489,16 +492,13 @@
                     )
                     value = jnp.where(lon_at == lon, found, value)
                 picked[at : at + devs, 128 * half : 128 * half + 128] = value
-    rest = picked[...]
+    records = picked[...]
     rows = hot[...].astype(jnp.bfloat16)
-    summed = jnp.zeros((LATS, 2 * LATS), F32)
-    for part in range(3):
-        piece = rest.astype(jnp.bfloat16)
-        rest = rest - piece.astype(F32)
-        summed = summed + lax.dot_general(
-            rows, piece, (((0,), (0,)), ((), ())), preferred_element_type=F32
-        )
-    foot[...] = summed[:ROWS_OWN]
+    large = records.astype(jnp.bfloat16)
+    small = (records - large.astype(F32)).astype(jnp.bfloat16)
+    foot[...] = jnp.dot(rows, large, preferred_element_type=F32) + jnp.dot(
+        rows, small, preferred_element_type=F32
+    )
 
 
 def shards(plasma_fields, velocity, resistivity, conductance, foot_map, foot_owner, foot_row):
@@ -523,11 +523,13 @@
     up, down = call(pack_body, (arr(PLANES, 32, LATS), arr(PLANES, 32, LATS)), (low, own, high))
     above = lax.ppermute(down, "sec", shift("sec", -1, False))
     below = lax.ppermute(up, "sec", shift("sec", 1, False))
-    raw = call(raw_body, arr(RAW, LATS), (low, own, high))
+    raw = call(raw_body, arr(4 * RAW, LATS), (low, own, high))
     owner = lax.axis_index("sec") == 0
 
     def advance_inner(rows):
-        gathered = lax.all_gather(rows, "rad")
+        gathered = lax.all_to_all(
+            rows.reshape(4, RAW, LATS), "rad", split_axis=0, concat_axis=0, tiled=True
+        )
         return call(
             inner_body,
             arr(24, LATS),
@@ -579,8 +581,9 @@
     other = lax.ppermute(mine, "sec", [(0, 1), (1, 0), (2, 3), (3, 2)])
     cells, hot = call(
         mark_body,
-        (jax.ShapeDtypeStruct((16, 32, LATS), jnp.int32), arr(256, LATS)),
+        (jax.ShapeDtypeStruct((16, 32, LATS), jnp.int32), arr(ROWS_OWN, 2 * LATS)),
         (late,),
+        scratch=(pltpu.VMEM((2, LATS, LATS), F32),),
     )
     plane = pltpu.VMEM((LONS, 32, 4 * LATS), F32)
     potential, foot_table = call(

time: 88 us -> 86.6 us (0.984)
  waiting for transfers between devices: 25.1 us -> 22.9 us
    ppermute x1, waiting for transfers between devices: 14 us -> 11.3 us  [shards(): far = lax.ppermute(inner, 'sec', [(0, 3)])]
    all_to_all x1, starting transfers between devices: 8.52 us -> 9.87 us  [shards(): late = lax.all_to_all(late, 'lon', split_axis=0, concat_axis=0, tiled=True)]
where the time goes in v11:
time: 86.6 us; the launch traced here: 86 us
  starting transfers between devices  38.5 us (44%)
  waiting for transfers between devices  22.9 us (26%)
  Pallas kernels  14 us (16%)
  blocking collectives  9.64 us (11%)
    ppermute x1, waiting for transfers between devices, shards(): far = lax.ppermute(inner, 'sec', [(0, 3)])  11.3 us
    pallas_call x8, Pallas kernels, call(): pl.pallas_call(body, out_shape=out_shape, in_specs=specs, out_specs=[vmem...  10.4 us
    all_to_all x1, starting transfers between devices, shards(): late = lax.all_to_all(late, 'lon', split_axis=0, concat_axis=0, tiled=True)  9.87 us
    all_to_all x1, blocking collectives, shards(): lax.all_to_all(slots.reshape(4, SENT, LATS), 'rad', split_axis=0, concat_...  9.64 us
    ppermute x1, starting transfers between devices, shards(): high = lax.ppermute(own, 'lon', shift('lon', -1, True))  9.37 us
    ppermute x1, starting transfers between devices, shards(): above = lax.ppermute(down, 'sec', shift('sec', -1, False))  4.93 us
    all_to_all x1, waiting for transfers between devices, shards(): late = lax.all_to_all(late, 'lon', split_axis=0, concat_axis=0, tiled=True)  4.62 us
    ppermute x1, starting transfers between devices, shards(): low = lax.ppermute(own, 'lon', shift('lon', 1, True))  4.13 us
  transfers between devices with their start and end apart: 10, of which 7 were waited for; matrix products, arithmetic and copies ran while one was open for 0% of the time, Pallas kernels for 8%

profile of v11, /device:TPU:57, one launch (start us, length us, event | category | flops | bytes accessed | tf_op | source)
XLA Modules:
  0.0 86.0 jit_solution(16087458965176100515)
XLA Ops:
  0.6 2.2 %shard_map.94 = (f32[12,4,16,128]{3,2,1,0:T(8,128)}, f32[544,128]{1,0:T(8,128)}) custom-call(f32[8,64,128]{2,1,0:T(8,128)} %bitcast.20, bf16[3,16,4,128]{3,2,1,0:T(4,128)(2,1)} %refs_1_.1, bf16[16,4,128]{2,1,0:T(4,128)(2,1)} %refs_2_.1, s32[1,128]{1,0:T(1,128)} %bitcast.22, s32[1,128]{1,0:T(1,128)} %bitcast.23, s32[128,256]{1,0:T(8,128)} %refs_5_.1, ...), custom_call_target="tpu_custom_call" | custom-call | flops 1000000 | bytes 1000000 | tf_op jit(solution)/shard_map/pallas_call | solution.py:88
  2.8 0.0 copy-start
  2.8 4.1 %collective-permute-start = (f32[12,4,16,128]{3,2,1,0:T(8,128)}, f32[12,4,16,128]{3,2,1,0:T(8,128)S(1)}, u32[]{:S(2)}, u32[]{:S(2)}) collective-permute-start(f32[12,4,16,128]{3,2,1,0:T(8,128)} %get-tuple-element.28.own), channel_id=1, source_target_pairs={{0,16},{16,32},{32,48},{48,64},{64,80},{80,96},{96,112},{112,128},... | collective-permute-start | bytes 1179656 | tf_op jit(solution)/shard_map/ppermute | solution.py:515
  7.0 9.4 %collective-permute-start.1 = (f32[12,4,16,128]{3,2,1,0:T(8,128)}, f32[12,4,16,128]{3,2,1,0:T(8,128)S(1)}, u32[]{:S(2)}, u32[]{:S(2)}) collective-permute-start(f32[12,4,16,128]{3,2,1,0:T(8,128)} %get-tuple-element.28.own), channel_id=1, source_target_pairs={{0,496},{16,0},{32,16},{48,32},{64,48},{80,64},{96,80},{112,96},{1... | collective-permute-start | bytes 1179656 | tf_op jit(solution)/shard_map/ppermute | solution.py:516
  16.4 9.6 %all_to_all.15 = f32[4,136,128]{2,1,0:T(8,128)S(1)} all-to-all(f32[4,136,128]{2,1,0:T(8,128)} %bitcast.19), channel_id=1, replica_groups=mesh['lon'=32,'sec'=4,'rad'=4] {'rad'}, dimensions={0} | all-to-all | bytes 557056 | tf_op jit(solution)/shard_map/all_to_all | solution.py:518
  26.0 0.0 collective-permute-done.low
  26.0 0.0 collective-permute-done.1.high
  26.0 0.0 copy-done
  26.0 0.1 shard_map.96
  26.1 1.3 %collective-permute-start.2 = (f32[12,32,128]{2,1,0:T(8,128)S(1)}, f32[12,32,128]{2,1,0:T(8,128)S(1)}, u32[]{:S(2)}, u32[]{:S(2)}) collective-permute-start(f32[12,32,128]{2,1,0:T(8,128)S(1)} %get-tuple-element.32), channel_id=1, source_target_pairs={{0,4},{4,8},{8,12},{1,5},{5,9},{9,13},{2,6},{6,10},{10,14},{3,7},{... | collective-permute-start | bytes 589832 | tf_op jit(solution)/shard_map/ppermute | solution.py:525
  27.4 4.9 %collective-permute-start.3 = (f32[12,32,128]{2,1,0:T(8,128)S(1)}, f32[12,32,128]{2,1,0:T(8,128)S(1)}, u32[]{:S(2)}, u32[]{:S(2)}) collective-permute-start(f32[12,32,128]{2,1,0:T(8,128)S(1)} %get-tuple-element.33), channel_id=1, source_target_pairs={{4,0},{8,4},{12,8},{5,1},{9,5},{13,9},{6,2},{10,6},{14,10},{7,3},{... | collective-permute-start | bytes 589832 | tf_op jit(solution)/shard_map/ppermute | solution.py:524
  32.4 0.1 shard_map.95
  32.5 0.0 collective-permute-done.2.below
  32.5 0.9 %collective-permute-done.3.above = f32[12,32,128]{2,1,0:T(8,128)S(1)} collective-permute-done((f32[12,32,128]{2,1,0:T(8,128)S(1)}, f32[12,32,128]{2,1,0:T(8,128)S(1)}, u32[]{:S(2)}, u32[]{:S(2)}) %collective-permute-start.3) | collective-permute-done | bytes 196640 | tf_op jit(solution)/shard_map/ppermute | solution.py:524
  33.4 1.3 %collective-permute-start.4 = (f32[24,128]{1,0:T(8,128)S(1)}, f32[24,128]{1,0:T(8,128)S(1)}, u32[]{:S(2)}, u32[]{:S(2)}) collective-permute-start(f32[24,128]{1,0:T(8,128)S(1)} %get-tuple-element.49), channel_id=1, source_target_pairs={{0,12},{1,13},{2,14},{3,15},{16,28},{17,29},{18,30},{19,31},{32,44... | collective-permute-start | bytes 36872 | tf_op jit(solution)/shard_map/ppermute | solution.py:542
  34.7 11.3 %collective-permute-done.4 = f32[24,128]{1,0:T(8,128)S(1)} collective-permute-done((f32[24,128]{1,0:T(8,128)S(1)}, f32[24,128]{1,0:T(8,128)S(1)}, u32[]{:S(2)}, u32[]{:S(2)}) %collective-permute-start.4) | collective-permute-done | bytes 12320 | tf_op jit(solution)/shard_map/ppermute | solution.py:542
  46.0 1.3 %collective-permute-start.5 = (f32[24,128]{1,0:T(8,128)S(1)}, f32[24,128]{1,0:T(8,128)S(1)}, u32[]{:S(2)}, u32[]{:S(2)}) collective-permute-start(f32[24,128]{1,0:T(8,128)S(1)} %add.3.one), channel_id=1, source_target_pairs={{0,4},{12,8},{1,5},{13,9},{2,6},{14,10},{3,7},{15,11},{16,20},{28,... | collective-permute-start | bytes 36872 | tf_op jit(solution)/shard_map/ppermute | solution.py:544
  47.3 0.1 pad_add_fusion.spot
  47.4 0.6 shard_map.97
  48.1 0.1 collective-permute-done.5.two
  48.1 1.4 %shard_map.98 = f32[32,40,128]{2,1,0:T(8,128)} custom-call(s32[3]{0:T(128)S(1)} %pad_add_fusion.spot, f32[24,128]{1,0:T(8,128)S(1)} %add.3.one, f32[24,128]{1,0:T(8,128)S(1)} %collective-permute-done.5.two, f32[4,128]{1,0:T(4,128)S(1)} %get-tuple-element.36.cond, f32[32,24,128]{2,1,0:T(8,128)S(1)} %bitcast.17), custom_call_target="tpu_custom_call" | custom-call | flops 100000 | bytes 1000000 | tf_op jit(solution)/shard_map/pallas_call | solution.py:266
  49.6 9.9 %all-to-all-start.2 = ((f32[32,40,128]{2,1,0:T(8,128)}), f32[32,40,128]{2,1,0:T(8,128)S(1)}, u32[]{:S(2)}, u32[]{:S(2)}) async-start(f32[32,40,128]{2,1,0:T(8,128)} %shard_map.98), calls=%async_computation.2 | async-start | bytes 1310720 | tf_op jit(solution)/shard_map/all_to_all | solution.py:563
  59.4 0.5 shard_map.99
  59.9 2.2 %collective-permute-start.6 = (f32[12,24,128]{2,1,0:T(8,128)S(1)}, f32[12,24,128]{2,1,0:T(8,128)S(1)}, u32[]{:S(2)}, u32[]{:S(2)}) collective-permute-start(f32[12,24,128]{2,1,0:T(8,128)S(1)} %shard_map.99), channel_id=1, source_target_pairs={{0,1},{1,2},{2,3},{4,5},{5,6},{6,7},{8,9},{9,10},{10,11},{12,13},{... | collective-permute-start | bytes 442376 | tf_op jit(solution)/shard_map/ppermute | solution.py:561
  62.1 1.3 %collective-permute-start.7 = (f32[12,24,128]{2,1,0:T(8,128)S(1)}, f32[12,24,128]{2,1,0:T(8,128)S(1)}, u32[]{:S(2)}, u32[]{:S(2)}) collective-permute-start(f32[12,24,128]{2,1,0:T(8,128)S(1)} %shard_map.99), channel_id=1, source_target_pairs={{1,0},{2,1},{3,2},{5,4},{6,5},{7,6},{9,8},{10,9},{11,10},{13,12},{... | collective-permute-start | bytes 442376 | tf_op jit(solution)/shard_map/ppermute | solution.py:562
  63.4 0.8 collective-permute-done.6.from_low
  64.2 4.1 %collective-permute-done.7.from_high = f32[12,24,128]{2,1,0:T(8,128)S(1)} collective-permute-done((f32[12,24,128]{2,1,0:T(8,128)S(1)}, f32[12,24,128]{2,1,0:T(8,128)S(1)}, u32[]{:S(2)}, u32[]{:S(2)}) %collective-permute-start.7) | collective-permute-done | bytes 147488 | tf_op jit(solution)/shard_map/ppermute | solution.py:562
  68.3 5.5 %shard_map.100 = f32[8,64,128]{2,1,0:T(8,128)} custom-call(f32[12,4,16,128]{3,2,1,0:T(8,128)S(1)} %collective-permute-done.low, f32[12,4,16,128]{3,2,1,0:T(8,128)S(1)} %copy-done, f32[12,4,16,128]{3,2,1,0:T(8,128)S(1)} %collective-permute-done.1.high, f32[12,32,128]{2,1,0:T(8,128)S(1)} %collective-permute-done.3.above, ...), custom_call_target="tpu_custom_call" | custom-call | flops 1000000 | bytes 1000000 | tf_op jit(solution)/shard_map/pallas_call | solution.py:36
  73.8 4.6 %all-to-all-done.2 = f32[32,40,128]{2,1,0:T(8,128)S(1)} async-done(((f32[32,40,128]{2,1,0:T(8,128)}), f32[32,40,128]{2,1,0:T(8,128)S(1)}, u32[]{:S(2)}, u32[]{:S(2)}) %all-to-all-start.2) | async-done | bytes 655392 | tf_op jit(solution)/shard_map/all_to_all | solution.py:563
  78.4 0.1 shard_map.101.mine
  78.5 2.9 %collective-permute-start.8 = (f32[20,32,128]{2,1,0:T(8,128)S(1)}, f32[20,32,128]{2,1,0:T(8,128)S(1)}, u32[]{:S(2)}, u32[]{:S(2)}) collective-permute-start(f32[20,32,128]{2,1,0:T(8,128)S(1)} %shard_map.101.mine), channel_id=1, source_target_pairs={{0,4},{4,0},{8,12},{12,8},{1,5},{5,1},{9,13},{13,9},{2,6},{6,2},{1... | collective-permute-start | bytes 983048 | tf_op jit(solution)/shard_map/ppermute | solution.py:581
  81.3 0.1 shard_map.102
  81.5 1.1 %collective-permute-done.8.other = f32[20,32,128]{2,1,0:T(8,128)S(1)} collective-permute-done((f32[20,32,128]{2,1,0:T(8,128)S(1)}, f32[20,32,128]{2,1,0:T(8,128)S(1)}, u32[]{:S(2)}, u32[]{:S(2)}) %collective-permute-start.8) | collective-permute-done | bytes 327712 | tf_op jit(solution)/shard_map/ppermute | solution.py:581
  82.6 3.5 %shard_map.103 = (f32[4,128]{1,0:T(4,128)}, f32[32,256]{1,0:T(8,128)}) custom-call(s32[3]{0:T(128)S(1)} %pad_add_fusion.spot, f32[20,32,128]{2,1,0:T(8,128)S(1)} %shard_map.101.mine, f32[20,32,128]{2,1,0:T(8,128)S(1)} %collective-permute-done.8.other, s32[16,32,128]{2,1,0:T(8,128)S(1)} %get-tuple-element.45.cells, f32[32,256]{1,0:T(8,128)S(1)} %get-tuple-element.46.hot), custom_call_target="tpu_custom_call" | custom-call | flops 1000000 | bytes 1000000 | tf_op jit(solution)/shard_map/pallas_call | solution.py:36
  (3 shorter events, 0.0 us)
Async XLA Ops:
  2.8 23.2 %copy-start = (f32[12,4,16,128]{3,2,1,0:T(8,128)S(1)}, f32[12,4,16,128]{3,2,1,0:T(8,128)}, u32[]{:S(2)}) copy-start(f32[12,4,16,128]{3,2,1,0:T(8,128)} %get-tuple-element.28.own) | copy-start | bytes 1179652
  2.8 23.2 %collective-permute-start = (f32[12,4,16,128]{3,2,1,0:T(8,128)}, f32[12,4,16,128]{3,2,1,0:T(8,128)S(1)}, u32[]{:S(2)}, u32[]{:S(2)}) collective-permute-start(f32[12,4,16,128]{3,2,1,0:T(8,128)} %get-tuple-element.28.own), channel_id=1, source_target_pairs={{0,16},{16,32},{32,48},{48,64},{64,80},{80,96},{96,112},{112,128},... | collective-permute-start | bytes 1179656 | tf_op jit(solution)/shard_map/ppermute | solution.py:515
  7.0 19.0 %collective-permute-start.1 = (f32[12,4,16,128]{3,2,1,0:T(8,128)}, f32[12,4,16,128]{3,2,1,0:T(8,128)S(1)}, u32[]{:S(2)}, u32[]{:S(2)}) collective-permute-start(f32[12,4,16,128]{3,2,1,0:T(8,128)} %get-tuple-element.28.own), channel_id=1, source_target_pairs={{0,496},{16,0},{32,16},{48,32},{64,48},{80,64},{96,80},{112,96},{1... | collective-permute-start | bytes 1179656 | tf_op jit(solution)/shard_map/ppermute | solution.py:516
  26.1 6.4 %collective-permute-start.2 = (f32[12,32,128]{2,1,0:T(8,128)S(1)}, f32[12,32,128]{2,1,0:T(8,128)S(1)}, u32[]{:S(2)}, u32[]{:S(2)}) collective-permute-start(f32[12,32,128]{2,1,0:T(8,128)S(1)} %get-tuple-element.32), channel_id=1, source_target_pairs={{0,4},{4,8},{8,12},{1,5},{5,9},{9,13},{2,6},{6,10},{10,14},{3,7},{... | collective-permute-start | bytes 589832 | tf_op jit(solution)/shard_map/ppermute | solution.py:525
  27.4 6.0 %collective-permute-start.3 = (f32[12,32,128]{2,1,0:T(8,128)S(1)}, f32[12,32,128]{2,1,0:T(8,128)S(1)}, u32[]{:S(2)}, u32[]{:S(2)}) collective-permute-start(f32[12,32,128]{2,1,0:T(8,128)S(1)} %get-tuple-element.33), channel_id=1, source_target_pairs={{4,0},{8,4},{12,8},{5,1},{9,5},{13,9},{6,2},{10,6},{14,10},{7,3},{... | collective-permute-start | bytes 589832 | tf_op jit(solution)/shard_map/ppermute | solution.py:524
  33.4 12.6 %collective-permute-start.4 = (f32[24,128]{1,0:T(8,128)S(1)}, f32[24,128]{1,0:T(8,128)S(1)}, u32[]{:S(2)}, u32[]{:S(2)}) collective-permute-start(f32[24,128]{1,0:T(8,128)S(1)} %get-tuple-element.49), channel_id=1, source_target_pairs={{0,12},{1,13},{2,14},{3,15},{16,28},{17,29},{18,30},{19,31},{32,44... | collective-permute-start | bytes 36872 | tf_op jit(solution)/shard_map/ppermute | solution.py:542
  46.0 2.1 %collective-permute-start.5 = (f32[24,128]{1,0:T(8,128)S(1)}, f32[24,128]{1,0:T(8,128)S(1)}, u32[]{:S(2)}, u32[]{:S(2)}) collective-permute-start(f32[24,128]{1,0:T(8,128)S(1)} %add.3.one), channel_id=1, source_target_pairs={{0,4},{12,8},{1,5},{13,9},{2,6},{14,10},{3,7},{15,11},{16,20},{28,... | collective-permute-start | bytes 36872 | tf_op jit(solution)/shard_map/ppermute | solution.py:544
  49.6 28.8 %all-to-all-start.2 = ((f32[32,40,128]{2,1,0:T(8,128)}), f32[32,40,128]{2,1,0:T(8,128)S(1)}, u32[]{:S(2)}, u32[]{:S(2)}) async-start(f32[32,40,128]{2,1,0:T(8,128)} %shard_map.98), calls=%async_computation.2 | async-start | bytes 1310720 | tf_op jit(solution)/shard_map/all_to_all | solution.py:563
  59.9 4.3 %collective-permute-start.6 = (f32[12,24,128]{2,1,0:T(8,128)S(1)}, f32[12,24,128]{2,1,0:T(8,128)S(1)}, u32[]{:S(2)}, u32[]{:S(2)}) collective-permute-start(f32[12,24,128]{2,1,0:T(8,128)S(1)} %shard_map.99), channel_id=1, source_target_pairs={{0,1},{1,2},{2,3},{4,5},{5,6},{6,7},{8,9},{9,10},{10,11},{12,13},{... | collective-permute-start | bytes 442376 | tf_op jit(solution)/shard_map/ppermute | solution.py:561
  62.1 6.2 %collective-permute-start.7 = (f32[12,24,128]{2,1,0:T(8,128)S(1)}, f32[12,24,128]{2,1,0:T(8,128)S(1)}, u32[]{:S(2)}, u32[]{:S(2)}) collective-permute-start(f32[12,24,128]{2,1,0:T(8,128)S(1)} %shard_map.99), channel_id=1, source_target_pairs={{1,0},{2,1},{3,2},{5,4},{6,5},{7,6},{9,8},{10,9},{11,10},{13,12},{... | collective-permute-start | bytes 442376 | tf_op jit(solution)/shard_map/ppermute | solution.py:562
  78.5 4.1 %collective-permute-start.8 = (f32[20,32,128]{2,1,0:T(8,128)S(1)}, f32[20,32,128]{2,1,0:T(8,128)S(1)}, u32[]{:S(2)}, u32[]{:S(2)}) collective-permute-start(f32[20,32,128]{2,1,0:T(8,128)S(1)} %shard_map.101.mine), channel_id=1, source_target_pairs={{0,4},{4,0},{8,12},{12,8},{1,5},{5,1},{9,13},{13,9},{2,6},{6,2},{1... | collective-permute-start | bytes 983048 | tf_op jit(solution)/shard_map/ppermute | solution.py:581

commit v12 on v11

--- a/solution.py
+++ b/solution.py
@@ -512,14 +512,19 @@
         foot_map,
         conductance,
     )
-    low = lax.ppermute(own, "lon", shift("lon", 1, True))
-    high = lax.ppermute(own, "lon", shift("lon", -1, True))
+    count = lax.axis_size("lon")
+    wrap = [(i, (i + (1 if i % 2 else -1)) % count) for i in range(count)]
+    first_swap = lax.ppermute(own, "lon", wrap)
+    second_swap = lax.ppermute(own, "lon", [(i, i ^ 1) for i in range(count)])
 
     sent = lax.all_to_all(
         slots.reshape(4, SENT, LATS), "rad", split_axis=0, concat_axis=0, tiled=True
     )
 
-    low, high, sent = lax.optimization_barrier((low, high, sent))
+    first_swap, second_swap, sent = lax.optimization_barrier((first_swap, second_swap, sent))
+    odd = lax.axis_index("lon") % 2 == 1
+    low = jnp.where(odd, second_swap, first_swap)
+    high = jnp.where(odd, first_swap, second_swap)
     up, down = call(pack_body, (arr(PLANES, 32, LATS), arr(PLANES, 32, LATS)), (low, own, high))
     above = lax.ppermute(down, "sec", shift("sec", -1, False))
     below = lax.ppermute(up, "sec", shift("sec", 1, False))

time: 86.6 us -> 85.9 us (level); the launches traced: 86 us -> 84.3 us
  blocking collectives: 9.64 us -> 0 us
  waiting for transfers between devices: 22.9 us -> 29.6 us
  starting transfers between devices: 38.5 us -> 39.7 us
    all_to_all x1 -> x0, blocking collectives: 9.64 us -> none  [shards(): lax.all_to_all(slots.reshape(4, SENT, LATS), 'rad', split_axis=0, concat_...]
    all_to_all x0 -> x1, waiting for transfers between devices: none -> 5.62 us  [shards(): lax.all_to_all(slots.reshape(4, SENT, LATS), 'rad', split_axis=0, concat_...]
    all_to_all x0 -> x1, starting transfers between devices: none -> 4.02 us  [shards(): lax.all_to_all(slots.reshape(4, SENT, LATS), 'rad', split_axis=0, concat_...]
    all_to_all x1, starting transfers between devices: 9.87 us -> 6.81 us  [shards(): late = lax.all_to_all(late, 'lon', split_axis=0, concat_axis=0, tiled=True)]
    ppermute x1, waiting for transfers between devices: 11.3 us -> 12.7 us  [shards(): far = lax.ppermute(inner, 'sec', [(0, 3)])]
  transfers between devices with their start and end apart: 10 -> 11, of which waited for: 7 -> 9; matrix products, arithmetic and copies ran while one was open for 0% -> 0% of each run, Pallas kernels for 8% -> 8%
where the time goes in v12:
time: 85.9 us; the launch traced here: 84.3 us
  starting transfers between devices  39.7 us (46%)
  waiting for transfers between devices  29.6 us (34%)
  Pallas kernels  14.1 us (16%)
    ppermute x1, waiting for transfers between devices, shards(): far = lax.ppermute(inner, 'sec', [(0, 3)])  12.7 us
    ppermute x1, starting transfers between devices, shards(): first_swap = lax.ppermute(own, 'lon', wrap)  11.5 us
    pallas_call x8, Pallas kernels, call(): pl.pallas_call(body, out_shape=out_shape, in_specs=specs, out_specs=[vmem...  10.4 us
    all_to_all x1, starting transfers between devices, shards(): late = lax.all_to_all(late, 'lon', split_axis=0, concat_axis=0, tiled=True)  6.81 us
    all_to_all x1, waiting for transfers between devices, shards(): lax.all_to_all(slots.reshape(4, SENT, LATS), 'rad', split_axis=0, concat_...  5.62 us
    ppermute x1, starting transfers between devices, shards(): above = lax.ppermute(down, 'sec', shift('sec', -1, False))  4.74 us
    all_to_all x1, starting transfers between devices, shards(): lax.all_to_all(slots.reshape(4, SENT, LATS), 'rad', split_axis=0, concat_...  4.02 us
    all_to_all x1, waiting for transfers between devices, shards(): late = lax.all_to_all(late, 'lon', split_axis=0, concat_axis=0, tiled=True)  3.95 us
  transfers between devices with their start and end apart: 11, of which 9 were waited for; matrix products, arithmetic and copies ran while one was open for 0% of the time, Pallas kernels for 8%

profile of v12, /device:TPU:57, one launch (start us, length us, event | category | flops | bytes accessed | tf_op | source)
XLA Modules:
  0.0 84.3 jit_solution(14400226641954838314)
XLA Ops:
  0.6 2.2 %shard_map.94 = (f32[12,4,16,128]{3,2,1,0:T(8,128)}, f32[544,128]{1,0:T(8,128)}) custom-call(f32[8,64,128]{2,1,0:T(8,128)} %bitcast.20, bf16[3,16,4,128]{3,2,1,0:T(4,128)(2,1)} %refs_1_.1, bf16[16,4,128]{2,1,0:T(4,128)(2,1)} %refs_2_.1, s32[1,128]{1,0:T(1,128)} %bitcast.22, s32[1,128]{1,0:T(1,128)} %bitcast.23, s32[128,256]{1,0:T(8,128)} %refs_5_.1, ...), custom_call_target="tpu_custom_call" | custom-call | flops 1000000 | bytes 1000000 | tf_op jit(solution)/shard_map/pallas_call | solution.py:88
  2.8 11.5 %collective-permute-start = (f32[12,4,16,128]{3,2,1,0:T(8,128)}, f32[12,4,16,128]{3,2,1,0:T(8,128)S(1)}, u32[]{:S(2)}, u32[]{:S(2)}) collective-permute-start(f32[12,4,16,128]{3,2,1,0:T(8,128)} %get-tuple-element.28.own), channel_id=1, source_target_pairs={{0,496},{16,32},{32,16},{48,64},{64,48},{80,96},{96,80},{112,128},... | collective-permute-start | bytes 1179656 | tf_op jit(solution)/shard_map/ppermute | solution.py:517
  14.3 1.9 %collective-permute-start.1 = (f32[12,4,16,128]{3,2,1,0:T(8,128)}, f32[12,4,16,128]{3,2,1,0:T(8,128)S(1)}, u32[]{:S(2)}, u32[]{:S(2)}) collective-permute-start(f32[12,4,16,128]{3,2,1,0:T(8,128)} %get-tuple-element.28.own), channel_id=1, source_target_pairs={{0,16},{16,0},{32,48},{48,32},{64,80},{80,64},{96,112},{112,96},{1... | collective-permute-start | bytes 1179656 | tf_op jit(solution)/shard_map/ppermute | solution.py:518
  16.2 4.0 %all-to-all-start.1 = ((f32[4,136,128]{2,1,0:T(8,128)}), f32[4,136,128]{2,1,0:T(8,128)S(1)}, u32[]{:S(2)}, u32[]{:S(2)}) async-start(f32[4,136,128]{2,1,0:T(8,128)} %bitcast.19), calls=%async_computation.1 | async-start | bytes 557056 | tf_op jit(solution)/shard_map/all_to_all | solution.py:520
  20.3 0.0 copy-start
  20.3 5.6 %all-to-all-done.1 = f32[4,136,128]{2,1,0:T(8,128)S(1)} async-done(((f32[4,136,128]{2,1,0:T(8,128)}), f32[4,136,128]{2,1,0:T(8,128)S(1)}, u32[]{:S(2)}, u32[]{:S(2)}) %all-to-all-start.1) | async-done | bytes 278560 | tf_op jit(solution)/shard_map/all_to_all | solution.py:520
  25.9 0.0 collective-permute-done
  25.9 0.2 collective-permute-done.1
  26.1 0.1 broadcast_select_fusion
  26.1 0.0 copy-done
  26.2 0.1 shard_map.96
  26.3 1.3 %collective-permute-start.2 = (f32[12,32,128]{2,1,0:T(8,128)S(1)}, f32[12,32,128]{2,1,0:T(8,128)S(1)}, u32[]{:S(2)}, u32[]{:S(2)}) collective-permute-start(f32[12,32,128]{2,1,0:T(8,128)S(1)} %get-tuple-element.32), channel_id=1, source_target_pairs={{0,4},{4,8},{8,12},{1,5},{5,9},{9,13},{2,6},{6,10},{10,14},{3,7},{... | collective-permute-start | bytes 589832 | tf_op jit(solution)/shard_map/ppermute | solution.py:530
  27.6 4.7 %collective-permute-start.3 = (f32[12,32,128]{2,1,0:T(8,128)S(1)}, f32[12,32,128]{2,1,0:T(8,128)S(1)}, u32[]{:S(2)}, u32[]{:S(2)}) collective-permute-start(f32[12,32,128]{2,1,0:T(8,128)S(1)} %get-tuple-element.33), channel_id=1, source_target_pairs={{4,0},{8,4},{12,8},{5,1},{9,5},{13,9},{6,2},{10,6},{14,10},{7,3},{... | collective-permute-start | bytes 589832 | tf_op jit(solution)/shard_map/ppermute | solution.py:529
  32.3 0.1 shard_map.95
  32.4 0.0 collective-permute-done.2.below
  32.4 0.9 %collective-permute-done.3.above = f32[12,32,128]{2,1,0:T(8,128)S(1)} collective-permute-done((f32[12,32,128]{2,1,0:T(8,128)S(1)}, f32[12,32,128]{2,1,0:T(8,128)S(1)}, u32[]{:S(2)}, u32[]{:S(2)}) %collective-permute-start.3) | collective-permute-done | bytes 196640 | tf_op jit(solution)/shard_map/ppermute | solution.py:529
  33.3 1.3 %collective-permute-start.4 = (f32[24,128]{1,0:T(8,128)S(1)}, f32[24,128]{1,0:T(8,128)S(1)}, u32[]{:S(2)}, u32[]{:S(2)}) collective-permute-start(f32[24,128]{1,0:T(8,128)S(1)} %get-tuple-element.51), channel_id=1, source_target_pairs={{0,12},{1,13},{2,14},{3,15},{16,28},{17,29},{18,30},{19,31},{32,44... | collective-permute-start | bytes 36872 | tf_op jit(solution)/shard_map/ppermute | solution.py:547
  34.6 12.7 %collective-permute-done.4 = f32[24,128]{1,0:T(8,128)S(1)} collective-permute-done((f32[24,128]{1,0:T(8,128)S(1)}, f32[24,128]{1,0:T(8,128)S(1)}, u32[]{:S(2)}, u32[]{:S(2)}) %collective-permute-start.4) | collective-permute-done | bytes 12320 | tf_op jit(solution)/shard_map/ppermute | solution.py:547
  47.3 1.3 %collective-permute-start.5 = (f32[24,128]{1,0:T(8,128)S(1)}, f32[24,128]{1,0:T(8,128)S(1)}, u32[]{:S(2)}, u32[]{:S(2)}) collective-permute-start(f32[24,128]{1,0:T(8,128)S(1)} %add.8.one), channel_id=1, source_target_pairs={{0,4},{12,8},{1,5},{13,9},{2,6},{14,10},{3,7},{15,11},{16,20},{28,... | collective-permute-start | bytes 36872 | tf_op jit(solution)/shard_map/ppermute | solution.py:549
  48.6 0.1 pad_add_fusion.spot
  48.7 0.6 shard_map.97
  49.4 0.1 collective-permute-done.5.two
  49.4 1.5 %shard_map.98 = f32[32,40,128]{2,1,0:T(8,128)} custom-call(s32[3]{0:T(128)S(1)} %pad_add_fusion.spot, f32[24,128]{1,0:T(8,128)S(1)} %add.8.one, f32[24,128]{1,0:T(8,128)S(1)} %collective-permute-done.5.two, f32[4,128]{1,0:T(4,128)S(1)} %get-tuple-element.36.cond, f32[32,24,128]{2,1,0:T(8,128)S(1)} %bitcast.17), custom_call_target="tpu_custom_call" | custom-call | flops 100000 | bytes 1000000 | tf_op jit(solution)/shard_map/pallas_call | solution.py:266
  50.9 6.8 %all-to-all-start.2 = ((f32[32,40,128]{2,1,0:T(8,128)}), f32[32,40,128]{2,1,0:T(8,128)S(1)}, u32[]{:S(2)}, u32[]{:S(2)}) async-start(f32[32,40,128]{2,1,0:T(8,128)} %shard_map.98), calls=%async_computation.2 | async-start | bytes 1310720 | tf_op jit(solution)/shard_map/all_to_all | solution.py:568
  57.7 0.5 shard_map.99
  58.2 2.2 %collective-permute-start.6 = (f32[12,24,128]{2,1,0:T(8,128)S(1)}, f32[12,24,128]{2,1,0:T(8,128)S(1)}, u32[]{:S(2)}, u32[]{:S(2)}) collective-permute-start(f32[12,24,128]{2,1,0:T(8,128)S(1)} %shard_map.99), channel_id=1, source_target_pairs={{0,1},{1,2},{2,3},{4,5},{5,6},{6,7},{8,9},{9,10},{10,11},{12,13},{... | collective-permute-start | bytes 442376 | tf_op jit(solution)/shard_map/ppermute | solution.py:566
  60.4 1.3 %collective-permute-start.7 = (f32[12,24,128]{2,1,0:T(8,128)S(1)}, f32[12,24,128]{2,1,0:T(8,128)S(1)}, u32[]{:S(2)}, u32[]{:S(2)}) collective-permute-start(f32[12,24,128]{2,1,0:T(8,128)S(1)} %shard_map.99), channel_id=1, source_target_pairs={{1,0},{2,1},{3,2},{5,4},{6,5},{7,6},{9,8},{10,9},{11,10},{13,12},{... | collective-permute-start | bytes 442376 | tf_op jit(solution)/shard_map/ppermute | solution.py:567
  61.7 1.2 %collective-permute-done.6.from_low = f32[12,24,128]{2,1,0:T(8,128)S(1)} collective-permute-done((f32[12,24,128]{2,1,0:T(8,128)S(1)}, f32[12,24,128]{2,1,0:T(8,128)S(1)}, u32[]{:S(2)}, u32[]{:S(2)}) %collective-permute-start.6) | collective-permute-done | bytes 147488 | tf_op jit(solution)/shard_map/ppermute | solution.py:566
  62.9 3.8 %collective-permute-done.7.from_high = f32[12,24,128]{2,1,0:T(8,128)S(1)} collective-permute-done((f32[12,24,128]{2,1,0:T(8,128)S(1)}, f32[12,24,128]{2,1,0:T(8,128)S(1)}, u32[]{:S(2)}, u32[]{:S(2)}) %collective-permute-start.7) | collective-permute-done | bytes 147488 | tf_op jit(solution)/shard_map/ppermute | solution.py:567
  66.7 5.5 %shard_map.100 = f32[8,64,128]{2,1,0:T(8,128)} custom-call(f32[12,4,16,128]{3,2,1,0:T(8,128)S(1)} %get-tuple-element.39.low, f32[12,4,16,128]{3,2,1,0:T(8,128)S(1)} %copy-done, f32[12,4,16,128]{3,2,1,0:T(8,128)S(1)} %get-tuple-element.40.high, f32[12,32,128]{2,1,0:T(8,128)S(1)} %collective-permute-done.3.above, ...), custom_call_target="tpu_custom_call" | custom-call | flops 1000000 | bytes 1000000 | tf_op jit(solution)/shard_map/pallas_call | solution.py:36
  72.2 3.9 %all-to-all-done.2 = f32[32,40,128]{2,1,0:T(8,128)S(1)} async-done(((f32[32,40,128]{2,1,0:T(8,128)}), f32[32,40,128]{2,1,0:T(8,128)S(1)}, u32[]{:S(2)}, u32[]{:S(2)}) %all-to-all-start.2) | async-done | bytes 655392 | tf_op jit(solution)/shard_map/all_to_all | solution.py:568
  76.1 0.1 shard_map.101.mine
  76.2 3.4 %collective-permute-start.8 = (f32[20,32,128]{2,1,0:T(8,128)S(1)}, f32[20,32,128]{2,1,0:T(8,128)S(1)}, u32[]{:S(2)}, u32[]{:S(2)}) collective-permute-start(f32[20,32,128]{2,1,0:T(8,128)S(1)} %shard_map.101.mine), channel_id=1, source_target_pairs={{0,4},{4,0},{8,12},{12,8},{1,5},{5,1},{9,13},{13,9},{2,6},{6,2},{1... | collective-permute-start | bytes 983048 | tf_op jit(solution)/shard_map/ppermute | solution.py:586
  79.6 0.1 shard_map.102
  79.8 1.1 %collective-permute-done.8.other = f32[20,32,128]{2,1,0:T(8,128)S(1)} collective-permute-done((f32[20,32,128]{2,1,0:T(8,128)S(1)}, f32[20,32,128]{2,1,0:T(8,128)S(1)}, u32[]{:S(2)}, u32[]{:S(2)}) %collective-permute-start.8) | collective-permute-done | bytes 327712 | tf_op jit(solution)/shard_map/ppermute | solution.py:586
  80.8 3.5 %shard_map.103 = (f32[4,128]{1,0:T(4,128)}, f32[32,256]{1,0:T(8,128)}) custom-call(s32[3]{0:T(128)S(1)} %pad_add_fusion.spot, f32[20,32,128]{2,1,0:T(8,128)S(1)} %shard_map.101.mine, f32[20,32,128]{2,1,0:T(8,128)S(1)} %collective-permute-done.8.other, s32[16,32,128]{2,1,0:T(8,128)S(1)} %get-tuple-element.45.cells, f32[32,256]{1,0:T(8,128)S(1)} %get-tuple-element.46.hot), custom_call_target="tpu_custom_call" | custom-call | flops 1000000 | bytes 1000000 | tf_op jit(solution)/shard_map/pallas_call | solution.py:36
  (3 shorter events, 0.0 us)
Async XLA Ops:
  2.8 23.0 %collective-permute-start = (f32[12,4,16,128]{3,2,1,0:T(8,128)}, f32[12,4,16,128]{3,2,1,0:T(8,128)S(1)}, u32[]{:S(2)}, u32[]{:S(2)}) collective-permute-start(f32[12,4,16,128]{3,2,1,0:T(8,128)} %get-tuple-element.28.own), channel_id=1, source_target_pairs={{0,496},{16,32},{32,16},{48,64},{64,48},{80,96},{96,80},{112,128},... | collective-permute-start | bytes 1179656 | tf_op jit(solution)/shard_map/ppermute | solution.py:517
  14.3 11.8 %collective-permute-start.1 = (f32[12,4,16,128]{3,2,1,0:T(8,128)}, f32[12,4,16,128]{3,2,1,0:T(8,128)S(1)}, u32[]{:S(2)}, u32[]{:S(2)}) collective-permute-start(f32[12,4,16,128]{3,2,1,0:T(8,128)} %get-tuple-element.28.own), channel_id=1, source_target_pairs={{0,16},{16,0},{32,48},{48,32},{64,80},{80,64},{96,112},{112,96},{1... | collective-permute-start | bytes 1179656 | tf_op jit(solution)/shard_map/ppermute | solution.py:518
  16.2 9.6 %all-to-all-start.1 = ((f32[4,136,128]{2,1,0:T(8,128)}), f32[4,136,128]{2,1,0:T(8,128)S(1)}, u32[]{:S(2)}, u32[]{:S(2)}) async-start(f32[4,136,128]{2,1,0:T(8,128)} %bitcast.19), calls=%async_computation.1 | async-start | bytes 557056 | tf_op jit(solution)/shard_map/all_to_all | solution.py:520
  20.3 5.9 %copy-start = (f32[12,4,16,128]{3,2,1,0:T(8,128)S(1)}, f32[12,4,16,128]{3,2,1,0:T(8,128)}, u32[]{:S(2)}) copy-start(f32[12,4,16,128]{3,2,1,0:T(8,128)} %get-tuple-element.28.own) | copy-start | bytes 1179652
  26.3 6.2 %collective-permute-start.2 = (f32[12,32,128]{2,1,0:T(8,128)S(1)}, f32[12,32,128]{2,1,0:T(8,128)S(1)}, u32[]{:S(2)}, u32[]{:S(2)}) collective-permute-start(f32[12,32,128]{2,1,0:T(8,128)S(1)} %get-tuple-element.32), channel_id=1, source_target_pairs={{0,4},{4,8},{8,12},{1,5},{5,9},{9,13},{2,6},{6,10},{10,14},{3,7},{... | collective-permute-start | bytes 589832 | tf_op jit(solution)/shard_map/ppermute | solution.py:530
  27.6 5.8 %collective-permute-start.3 = (f32[12,32,128]{2,1,0:T(8,128)S(1)}, f32[12,32,128]{2,1,0:T(8,128)S(1)}, u32[]{:S(2)}, u32[]{:S(2)}) collective-permute-start(f32[12,32,128]{2,1,0:T(8,128)S(1)} %get-tuple-element.33), channel_id=1, source_target_pairs={{4,0},{8,4},{12,8},{5,1},{9,5},{13,9},{6,2},{10,6},{14,10},{7,3},{... | collective-permute-start | bytes 589832 | tf_op jit(solution)/shard_map/ppermute | solution.py:529
  33.3 14.0 %collective-permute-start.4 = (f32[24,128]{1,0:T(8,128)S(1)}, f32[24,128]{1,0:T(8,128)S(1)}, u32[]{:S(2)}, u32[]{:S(2)}) collective-permute-start(f32[24,128]{1,0:T(8,128)S(1)} %get-tuple-element.51), channel_id=1, source_target_pairs={{0,12},{1,13},{2,14},{3,15},{16,28},{17,29},{18,30},{19,31},{32,44... | collective-permute-start | bytes 36872 | tf_op jit(solution)/shard_map/ppermute | solution.py:547
  47.3 2.1 %collective-permute-start.5 = (f32[24,128]{1,0:T(8,128)S(1)}, f32[24,128]{1,0:T(8,128)S(1)}, u32[]{:S(2)}, u32[]{:S(2)}) collective-permute-start(f32[24,128]{1,0:T(8,128)S(1)} %add.8.one), channel_id=1, source_target_pairs={{0,4},{12,8},{1,5},{13,9},{2,6},{14,10},{3,7},{15,11},{16,20},{28,... | collective-permute-start | bytes 36872 | tf_op jit(solution)/shard_map/ppermute | solution.py:549
  50.9 25.2 %all-to-all-start.2 = ((f32[32,40,128]{2,1,0:T(8,128)}), f32[32,40,128]{2,1,0:T(8,128)S(1)}, u32[]{:S(2)}, u32[]{:S(2)}) async-start(f32[32,40,128]{2,1,0:T(8,128)} %shard_map.98), calls=%async_computation.2 | async-start | bytes 1310720 | tf_op jit(solution)/shard_map/all_to_all | solution.py:568
  58.2 4.7 %collective-permute-start.6 = (f32[12,24,128]{2,1,0:T(8,128)S(1)}, f32[12,24,128]{2,1,0:T(8,128)S(1)}, u32[]{:S(2)}, u32[]{:S(2)}) collective-permute-start(f32[12,24,128]{2,1,0:T(8,128)S(1)} %shard_map.99), channel_id=1, source_target_pairs={{0,1},{1,2},{2,3},{4,5},{5,6},{6,7},{8,9},{9,10},{10,11},{12,13},{... | collective-permute-start | bytes 442376 | tf_op jit(solution)/shard_map/ppermute | solution.py:566
  60.4 6.3 %collective-permute-start.7 = (f32[12,24,128]{2,1,0:T(8,128)S(1)}, f32[12,24,128]{2,1,0:T(8,128)S(1)}, u32[]{:S(2)}, u32[]{:S(2)}) collective-permute-start(f32[12,24,128]{2,1,0:T(8,128)S(1)} %shard_map.99), channel_id=1, source_target_pairs={{1,0},{2,1},{3,2},{5,4},{6,5},{7,6},{9,8},{10,9},{11,10},{13,12},{... | collective-permute-start | bytes 442376 | tf_op jit(solution)/shard_map/ppermute | solution.py:567
  76.2 4.6 %collective-permute-start.8 = (f32[20,32,128]{2,1,0:T(8,128)S(1)}, f32[20,32,128]{2,1,0:T(8,128)S(1)}, u32[]{:S(2)}, u32[]{:S(2)}) collective-permute-start(f32[20,32,128]{2,1,0:T(8,128)S(1)} %shard_map.101.mine), channel_id=1, source_target_pairs={{0,4},{4,0},{8,12},{12,8},{1,5},{5,1},{9,13},{13,9},{2,6},{6,2},{1... | collective-permute-start | bytes 983048 | tf_op jit(solution)/shard_map/ppermute | solution.py:586

commit v13 on v12

--- a/solution.py
+++ b/solution.py
@@ -309,15 +309,18 @@
     return found, at
 
 
-def pack_body(low, own, high, up, down):
+def pack_body(spot, low, own, high, near, away):
     found, rows = chunks()
+    odd = spot[0] % 2 == 1
     for plane in range(PLANES):
         for wide, start, count in found:
             ref = (low, own, high)[wide // LONS]
-            up[plane, start : start + count, :] = ref[plane, wide % LONS, SHELLS - count :, :]
-            down[plane, start : start + count, :] = ref[plane, wide % LONS, :count, :]
-        up[plane, rows:, :] = jnp.zeros((32 - rows, LATS), F32)
-        down[plane, rows:, :] = jnp.zeros((32 - rows, LATS), F32)
+            up = ref[plane, wide % LONS, SHELLS - count :, :]
+            down = ref[plane, wide % LONS, :count, :]
+            near[plane, start : start + count, :] = jnp.where(odd, down, up)
+            away[plane, start : start + count, :] = jnp.where(odd, up, down)
+        near[plane, rows:, :] = jnp.zeros((32 - rows, LATS), F32)
+        away[plane, rows:, :] = jnp.zeros((32 - rows, LATS), F32)
 
 
 def main_body(low, own, high, above, below, from_low, from_high, out, cells, w, speeds):
@@ -525,9 +528,13 @@
     odd = lax.axis_index("lon") % 2 == 1
     low = jnp.where(odd, second_swap, first_swap)
     high = jnp.where(odd, first_swap, second_swap)
-    up, down = call(pack_body, (arr(PLANES, 32, LATS), arr(PLANES, 32, LATS)), (low, own, high))
-    above = lax.ppermute(down, "sec", shift("sec", -1, False))
-    below = lax.ppermute(up, "sec", shift("sec", 1, False))
+    near_rows, away_rows = call(
+        pack_body,
+        (arr(PLANES, 32, LATS), arr(PLANES, 32, LATS)),
+        (spot, low, own, high),
+        smem=(0,),
+    )
+    away_rows = lax.ppermute(away_rows, "sec", [(1, 2), (2, 1)])
     raw = call(raw_body, arr(4 * RAW, LATS), (low, own, high))
     owner = lax.axis_index("sec") == 0
 
@@ -543,7 +550,7 @@
         )
 
     inner = lax.cond(owner, advance_inner, lambda rows: jnp.zeros((24, LATS), F32), raw)
-    inner, below, above = lax.optimization_barrier((inner, below, above))
+    away_rows, inner = lax.optimization_barrier((away_rows, inner))
     far = lax.ppermute(inner, "sec", [(0, 3)])
     far = inner + far
     near = lax.ppermute(far, "sec", [(0, 1), (3, 2)])
@@ -554,8 +561,12 @@
         smem=(0,),
     )
     late = join(spot, far, near, cond, base.reshape(32, LATE - 16, LATS))
-    late, low, high = lax.optimization_barrier((late, low, high))
-
+    late, low, high, near_rows = lax.optimization_barrier((late, low, high, near_rows))
+    near_rows = lax.ppermute(near_rows, "sec", [(0, 1), (1, 0), (2, 3), (3, 2)])
+
+    odd = lax.axis_index("sec") % 2 == 1
+    above = jnp.where(odd, away_rows, near_rows)
+    below = jnp.where(odd, near_rows, away_rows)
     blocks = (low, own, high, above, below)
     edges = call(
         edge_body,

time: 85.9 us -> 83.5 us (0.972); the launches traced: 84.3 us -> 83 us
  starting transfers between devices: 39.7 us -> 37 us
    ppermute x1, waiting for transfers between devices: 12.7 us -> 17 us  [shards(): far = lax.ppermute(inner, 'sec', [(0, 3)])]
    all_to_all x1, waiting for transfers between devices: 3.95 us -> 0.01 us  [shards(): late = lax.all_to_all(late, 'lon', split_axis=0, concat_axis=0, tiled=True)]
    ppermute x2, starting transfers between devices: 6.03 us -> 3.25 us  [the longest x1 2.58 us: shards(): near_rows = lax.ppermute(near_rows, 'sec', [(0, 1), (1, 0), (2, 3), (3, 2)])]
  transfers between devices with their start and end apart: 11 -> 11, of which waited for: 9 -> 8; matrix products, arithmetic and copies ran while one was open for 0% -> 0% of each run, Pallas kernels for 8% -> 8%
where the time goes in v13:
time: 83.5 us; the launch traced here: 83 us
  starting transfers between devices  37 us (44%)
  waiting for transfers between devices  30.4 us (36%)
  Pallas kernels  14.6 us (17%)
    ppermute x1, waiting for transfers between devices, shards(): far = lax.ppermute(inner, 'sec', [(0, 3)])  17 us
    ppermute x1, starting transfers between devices, shards(): first_swap = lax.ppermute(own, 'lon', wrap)  11.5 us
    pallas_call x8, Pallas kernels, call(): pl.pallas_call(body, out_shape=out_shape, in_specs=specs, out_specs=[vmem...  11 us
    all_to_all x1, starting transfers between devices, shards(): late = lax.all_to_all(late, 'lon', split_axis=0, concat_axis=0, tiled=True)  6.82 us
    all_to_all x1, waiting for transfers between devices, shards(): lax.all_to_all(slots.reshape(4, SENT, LATS), 'rad', split_axis=0, concat_...  5.54 us
    all_to_all x1, starting transfers between devices, shards(): lax.all_to_all(slots.reshape(4, SENT, LATS), 'rad', split_axis=0, concat_...  4.02 us
    ppermute x1, waiting for transfers between devices, shards(): from_high = lax.ppermute(edges, 'rad', shift('rad', -1, False))  3.8 us
    ppermute x1, starting transfers between devices, shards(): other = lax.ppermute(mine, 'sec', [(0, 1), (1, 0), (2, 3), (3, 2)])  3.43 us
  transfers between devices with their start and end apart: 11, of which 8 were waited for; matrix products, arithmetic and copies ran while one was open for 0% of the time, Pallas kernels for 8%

profile of v13, /device:TPU:57, one launch (start us, length us, event | category | flops | bytes accessed | tf_op | source)
XLA Modules:
  0.0 83.0 jit_solution(8373245467109748124)
XLA Ops:
  0.6 2.2 %shard_map.94 = (f32[12,4,16,128]{3,2,1,0:T(8,128)}, f32[544,128]{1,0:T(8,128)}) custom-call(f32[8,64,128]{2,1,0:T(8,128)} %bitcast.20, bf16[3,16,4,128]{3,2,1,0:T(4,128)(2,1)} %refs_1_.1, bf16[16,4,128]{2,1,0:T(4,128)(2,1)} %refs_2_.1, s32[1,128]{1,0:T(1,128)} %bitcast.22, s32[1,128]{1,0:T(1,128)} %bitcast.23, s32[128,256]{1,0:T(8,128)} %refs_5_.1, ...), custom_call_target="tpu_custom_call" | custom-call | flops 1000000 | bytes 1000000 | tf_op jit(solution)/shard_map/pallas_call | solution.py:88
  2.9 11.5 %collective-permute-start = (f32[12,4,16,128]{3,2,1,0:T(8,128)}, f32[12,4,16,128]{3,2,1,0:T(8,128)S(1)}, u32[]{:S(2)}, u32[]{:S(2)}) collective-permute-start(f32[12,4,16,128]{3,2,1,0:T(8,128)} %get-tuple-element.28.own), channel_id=1, source_target_pairs={{0,496},{16,32},{32,16},{48,64},{64,48},{80,96},{96,80},{112,128},... | collective-permute-start | bytes 1179656 | tf_op jit(solution)/shard_map/ppermute | solution.py:520
  14.3 1.9 %collective-permute-start.1 = (f32[12,4,16,128]{3,2,1,0:T(8,128)}, f32[12,4,16,128]{3,2,1,0:T(8,128)S(1)}, u32[]{:S(2)}, u32[]{:S(2)}) collective-permute-start(f32[12,4,16,128]{3,2,1,0:T(8,128)} %get-tuple-element.28.own), channel_id=1, source_target_pairs={{0,16},{16,0},{32,48},{48,32},{64,80},{80,64},{96,112},{112,96},{1... | collective-permute-start | bytes 1179656 | tf_op jit(solution)/shard_map/ppermute | solution.py:521
  16.2 4.0 %all-to-all-start.1 = ((f32[4,136,128]{2,1,0:T(8,128)}), f32[4,136,128]{2,1,0:T(8,128)S(1)}, u32[]{:S(2)}, u32[]{:S(2)}) async-start(f32[4,136,128]{2,1,0:T(8,128)} %bitcast.19), calls=%async_computation.1 | async-start | bytes 557056 | tf_op jit(solution)/shard_map/all_to_all | solution.py:523
  20.3 0.1 pad_add_fusion.spot
  20.3 0.0 copy-start
  20.3 5.5 %all-to-all-done.1 = f32[4,136,128]{2,1,0:T(8,128)S(1)} async-done(((f32[4,136,128]{2,1,0:T(8,128)}), f32[4,136,128]{2,1,0:T(8,128)S(1)}, u32[]{:S(2)}, u32[]{:S(2)}) %all-to-all-start.1) | async-done | bytes 278560 | tf_op jit(solution)/shard_map/all_to_all | solution.py:523
  25.9 0.0 collective-permute-done
  25.9 0.2 collective-permute-done.1
  26.1 0.1 broadcast_select_fusion
  26.2 0.0 copy-done
  26.2 0.6 shard_map.95
  26.8 0.7 collective-permute-start.2
  27.5 0.1 shard_map.96
  27.6 0.0 collective-permute-done.2
  27.6 1.3 %collective-permute-start.3 = (f32[24,128]{1,0:T(8,128)S(1)}, f32[24,128]{1,0:T(8,128)S(1)}, u32[]{:S(2)}, u32[]{:S(2)}) collective-permute-start(f32[24,128]{1,0:T(8,128)S(1)} %get-tuple-element.53), channel_id=1, source_target_pairs={{0,12},{1,13},{2,14},{3,15},{16,28},{17,29},{18,30},{19,31},{32,44... | collective-permute-start | bytes 36872 | tf_op jit(solution)/shard_map/ppermute | solution.py:554
  28.9 17.0 %collective-permute-done.3 = f32[24,128]{1,0:T(8,128)S(1)} collective-permute-done((f32[24,128]{1,0:T(8,128)S(1)}, f32[24,128]{1,0:T(8,128)S(1)}, u32[]{:S(2)}, u32[]{:S(2)}) %collective-permute-start.3) | collective-permute-done | bytes 12320 | tf_op jit(solution)/shard_map/ppermute | solution.py:554
  46.0 1.3 %collective-permute-start.4 = (f32[24,128]{1,0:T(8,128)S(1)}, f32[24,128]{1,0:T(8,128)S(1)}, u32[]{:S(2)}, u32[]{:S(2)}) collective-permute-start(f32[24,128]{1,0:T(8,128)S(1)} %add.11.one), channel_id=1, source_target_pairs={{0,4},{12,8},{1,5},{13,9},{2,6},{14,10},{3,7},{15,11},{16,20},{28,... | collective-permute-start | bytes 36872 | tf_op jit(solution)/shard_map/ppermute | solution.py:556
  47.2 0.6 shard_map.97
  47.9 0.2 collective-permute-done.4.two
  48.1 1.4 %shard_map.98 = f32[32,40,128]{2,1,0:T(8,128)} custom-call(s32[3]{0:T(128)S(1)} %pad_add_fusion.spot, f32[24,128]{1,0:T(8,128)S(1)} %add.11.one, f32[24,128]{1,0:T(8,128)S(1)} %collective-permute-done.4.two, f32[4,128]{1,0:T(4,128)S(1)} %get-tuple-element.35.cond, f32[32,24,128]{2,1,0:T(8,128)S(1)} %bitcast.17), custom_call_target="tpu_custom_call" | custom-call | flops 100000 | bytes 1000000 | tf_op jit(solution)/shard_map/pallas_call | solution.py:266
  49.5 6.8 %all-to-all-start.2 = ((f32[32,40,128]{2,1,0:T(8,128)}), f32[32,40,128]{2,1,0:T(8,128)S(1)}, u32[]{:S(2)}, u32[]{:S(2)}) async-start(f32[32,40,128]{2,1,0:T(8,128)} %shard_map.98), calls=%async_computation.2 | async-start | bytes 1310720 | tf_op jit(solution)/shard_map/all_to_all | solution.py:579
  56.3 2.6 %collective-permute-start.5 = (f32[12,32,128]{2,1,0:T(8,128)S(1)}, f32[12,32,128]{2,1,0:T(8,128)S(1)}, u32[]{:S(2)}, u32[]{:S(2)}) collective-permute-start(f32[12,32,128]{2,1,0:T(8,128)S(1)} %get-tuple-element.42), channel_id=1, source_target_pairs={{0,4},{4,0},{8,12},{12,8},{1,5},{5,1},{9,13},{13,9},{2,6},{6,2},{1... | collective-permute-start | bytes 589832 | tf_op jit(solution)/shard_map/ppermute | solution.py:565
  58.9 1.0 %collective-permute-done.5 = f32[12,32,128]{2,1,0:T(8,128)S(1)} collective-permute-done((f32[12,32,128]{2,1,0:T(8,128)S(1)}, f32[12,32,128]{2,1,0:T(8,128)S(1)}, u32[]{:S(2)}, u32[]{:S(2)}) %collective-permute-start.5) | collective-permute-done | bytes 196640 | tf_op jit(solution)/shard_map/ppermute | solution.py:565
  60.0 0.5 shard_map.99
  60.5 2.2 %collective-permute-start.6 = (f32[12,24,128]{2,1,0:T(8,128)S(1)}, f32[12,24,128]{2,1,0:T(8,128)S(1)}, u32[]{:S(2)}, u32[]{:S(2)}) collective-permute-start(f32[12,24,128]{2,1,0:T(8,128)S(1)} %shard_map.99), channel_id=1, source_target_pairs={{0,1},{1,2},{2,3},{4,5},{5,6},{6,7},{8,9},{9,10},{10,11},{12,13},{... | collective-permute-start | bytes 442376 | tf_op jit(solution)/shard_map/ppermute | solution.py:577
  62.7 1.3 %collective-permute-start.7 = (f32[12,24,128]{2,1,0:T(8,128)S(1)}, f32[12,24,128]{2,1,0:T(8,128)S(1)}, u32[]{:S(2)}, u32[]{:S(2)}) collective-permute-start(f32[12,24,128]{2,1,0:T(8,128)S(1)} %shard_map.99), channel_id=1, source_target_pairs={{1,0},{2,1},{3,2},{5,4},{6,5},{7,6},{9,8},{10,9},{11,10},{13,12},{... | collective-permute-start | bytes 442376 | tf_op jit(solution)/shard_map/ppermute | solution.py:578
  64.0 1.5 %collective-permute-done.6.from_low = f32[12,24,128]{2,1,0:T(8,128)S(1)} collective-permute-done((f32[12,24,128]{2,1,0:T(8,128)S(1)}, f32[12,24,128]{2,1,0:T(8,128)S(1)}, u32[]{:S(2)}, u32[]{:S(2)}) %collective-permute-start.6) | collective-permute-done | bytes 147488 | tf_op jit(solution)/shard_map/ppermute | solution.py:577
  65.5 3.8 %collective-permute-done.7.from_high = f32[12,24,128]{2,1,0:T(8,128)S(1)} collective-permute-done((f32[12,24,128]{2,1,0:T(8,128)S(1)}, f32[12,24,128]{2,1,0:T(8,128)S(1)}, u32[]{:S(2)}, u32[]{:S(2)}) %collective-permute-start.7) | collective-permute-done | bytes 147488 | tf_op jit(solution)/shard_map/ppermute | solution.py:578
  69.3 5.5 %shard_map.100 = f32[8,64,128]{2,1,0:T(8,128)} custom-call(f32[12,4,16,128]{3,2,1,0:T(8,128)S(1)} %get-tuple-element.39.low, f32[12,4,16,128]{3,2,1,0:T(8,128)S(1)} %copy-done, f32[12,4,16,128]{3,2,1,0:T(8,128)S(1)} %get-tuple-element.40.high, f32[12,32,128]{2,1,0:T(8,128)S(1)} %get-tuple-element.52.above, f32[12,32,128]{2,1,0:T(8,128)S(1)} %get-tuple-element.51.below, ...), custom_call_target="tpu_custom_call" | custom-call | flops 1000000 | bytes 1000000 | tf_op jit(solution)/shard_map/pallas_call | solution.py:36
  74.8 0.0 all-to-all-done.2
  74.8 0.1 shard_map.101.mine
  74.9 3.4 %collective-permute-start.8 = (f32[20,32,128]{2,1,0:T(8,128)S(1)}, f32[20,32,128]{2,1,0:T(8,128)S(1)}, u32[]{:S(2)}, u32[]{:S(2)}) collective-permute-start(f32[20,32,128]{2,1,0:T(8,128)S(1)} %shard_map.101.mine), channel_id=1, source_target_pairs={{0,4},{4,0},{8,12},{12,8},{1,5},{5,1},{9,13},{13,9},{2,6},{6,2},{1... | collective-permute-start | bytes 983048 | tf_op jit(solution)/shard_map/ppermute | solution.py:597
  78.3 0.1 shard_map.102
  78.5 1.1 %collective-permute-done.8.other = f32[20,32,128]{2,1,0:T(8,128)S(1)} collective-permute-done((f32[20,32,128]{2,1,0:T(8,128)S(1)}, f32[20,32,128]{2,1,0:T(8,128)S(1)}, u32[]{:S(2)}, u32[]{:S(2)}) %collective-permute-start.8) | collective-permute-done | bytes 327712 | tf_op jit(solution)/shard_map/ppermute | solution.py:597
  79.5 3.5 %shard_map.103 = (f32[4,128]{1,0:T(4,128)}, f32[32,256]{1,0:T(8,128)}) custom-call(s32[3]{0:T(128)S(1)} %pad_add_fusion.spot, f32[20,32,128]{2,1,0:T(8,128)S(1)} %shard_map.101.mine, f32[20,32,128]{2,1,0:T(8,128)S(1)} %collective-permute-done.8.other, s32[16,32,128]{2,1,0:T(8,128)S(1)} %get-tuple-element.45.cells, f32[32,256]{1,0:T(8,128)S(1)} %get-tuple-element.46.hot), custom_call_target="tpu_custom_call" | custom-call | flops 1000000 | bytes 1000000 | tf_op jit(solution)/shard_map/pallas_call | solution.py:36
  (4 shorter events, 0.1 us)
Async XLA Ops:
  2.9 23.0 %collective-permute-start = (f32[12,4,16,128]{3,2,1,0:T(8,128)}, f32[12,4,16,128]{3,2,1,0:T(8,128)S(1)}, u32[]{:S(2)}, u32[]{:S(2)}) collective-permute-start(f32[12,4,16,128]{3,2,1,0:T(8,128)} %get-tuple-element.28.own), channel_id=1, source_target_pairs={{0,496},{16,32},{32,16},{48,64},{64,48},{80,96},{96,80},{112,128},... | collective-permute-start | bytes 1179656 | tf_op jit(solution)/shard_map/ppermute | solution.py:520
  14.3 11.8 %collective-permute-start.1 = (f32[12,4,16,128]{3,2,1,0:T(8,128)}, f32[12,4,16,128]{3,2,1,0:T(8,128)S(1)}, u32[]{:S(2)}, u32[]{:S(2)}) collective-permute-start(f32[12,4,16,128]{3,2,1,0:T(8,128)} %get-tuple-element.28.own), channel_id=1, source_target_pairs={{0,16},{16,0},{32,48},{48,32},{64,80},{80,64},{96,112},{112,96},{1... | collective-permute-start | bytes 1179656 | tf_op jit(solution)/shard_map/ppermute | solution.py:521
  16.2 9.6 %all-to-all-start.1 = ((f32[4,136,128]{2,1,0:T(8,128)}), f32[4,136,128]{2,1,0:T(8,128)S(1)}, u32[]{:S(2)}, u32[]{:S(2)}) async-start(f32[4,136,128]{2,1,0:T(8,128)} %bitcast.19), calls=%async_computation.1 | async-start | bytes 557056 | tf_op jit(solution)/shard_map/all_to_all | solution.py:523
  20.3 5.8 %copy-start = (f32[12,4,16,128]{3,2,1,0:T(8,128)S(1)}, f32[12,4,16,128]{3,2,1,0:T(8,128)}, u32[]{:S(2)}) copy-start(f32[12,4,16,128]{3,2,1,0:T(8,128)} %get-tuple-element.28.own) | copy-start | bytes 1179652
  26.8 0.8 collective-permute-start.2
  27.6 18.3 %collective-permute-start.3 = (f32[24,128]{1,0:T(8,128)S(1)}, f32[24,128]{1,0:T(8,128)S(1)}, u32[]{:S(2)}, u32[]{:S(2)}) collective-permute-start(f32[24,128]{1,0:T(8,128)S(1)} %get-tuple-element.53), channel_id=1, source_target_pairs={{0,12},{1,13},{2,14},{3,15},{16,28},{17,29},{18,30},{19,31},{32,44... | collective-permute-start | bytes 36872 | tf_op jit(solution)/shard_map/ppermute | solution.py:554
  46.0 2.1 %collective-permute-start.4 = (f32[24,128]{1,0:T(8,128)S(1)}, f32[24,128]{1,0:T(8,128)S(1)}, u32[]{:S(2)}, u32[]{:S(2)}) collective-permute-start(f32[24,128]{1,0:T(8,128)S(1)} %add.11.one), channel_id=1, source_target_pairs={{0,4},{12,8},{1,5},{13,9},{2,6},{14,10},{3,7},{15,11},{16,20},{28,... | collective-permute-start | bytes 36872 | tf_op jit(solution)/shard_map/ppermute | solution.py:556
  49.5 25.3 %all-to-all-start.2 = ((f32[32,40,128]{2,1,0:T(8,128)}), f32[32,40,128]{2,1,0:T(8,128)S(1)}, u32[]{:S(2)}, u32[]{:S(2)}) async-start(f32[32,40,128]{2,1,0:T(8,128)} %shard_map.98), calls=%async_computation.2 | async-start | bytes 1310720 | tf_op jit(solution)/shard_map/all_to_all | solution.py:579
  56.3 3.6 %collective-permute-start.5 = (f32[12,32,128]{2,1,0:T(8,128)S(1)}, f32[12,32,128]{2,1,0:T(8,128)S(1)}, u32[]{:S(2)}, u32[]{:S(2)}) collective-permute-start(f32[12,32,128]{2,1,0:T(8,128)S(1)} %get-tuple-element.42), channel_id=1, source_target_pairs={{0,4},{4,0},{8,12},{12,8},{1,5},{5,1},{9,13},{13,9},{2,6},{6,2},{1... | collective-permute-start | bytes 589832 | tf_op jit(solution)/shard_map/ppermute | solution.py:565
  60.5 5.0 %collective-permute-start.6 = (f32[12,24,128]{2,1,0:T(8,128)S(1)}, f32[12,24,128]{2,1,0:T(8,128)S(1)}, u32[]{:S(2)}, u32[]{:S(2)}) collective-permute-start(f32[12,24,128]{2,1,0:T(8,128)S(1)} %shard_map.99), channel_id=1, source_target_pairs={{0,1},{1,2},{2,3},{4,5},{5,6},{6,7},{8,9},{9,10},{10,11},{12,13},{... | collective-permute-start | bytes 442376 | tf_op jit(solution)/shard_map/ppermute | solution.py:577
  62.7 6.6 %collective-permute-start.7 = (f32[12,24,128]{2,1,0:T(8,128)S(1)}, f32[12,24,128]{2,1,0:T(8,128)S(1)}, u32[]{:S(2)}, u32[]{:S(2)}) collective-permute-start(f32[12,24,128]{2,1,0:T(8,128)S(1)} %shard_map.99), channel_id=1, source_target_pairs={{1,0},{2,1},{3,2},{5,4},{6,5},{7,6},{9,8},{10,9},{11,10},{13,12},{... | collective-permute-start | bytes 442376 | tf_op jit(solution)/shard_map/ppermute | solution.py:578
  74.9 4.7 %collective-permute-start.8 = (f32[20,32,128]{2,1,0:T(8,128)S(1)}, f32[20,32,128]{2,1,0:T(8,128)S(1)}, u32[]{:S(2)}, u32[]{:S(2)}) collective-permute-start(f32[20,32,128]{2,1,0:T(8,128)S(1)} %shard_map.101.mine), channel_id=1, source_target_pairs={{0,4},{4,0},{8,12},{12,8},{1,5},{5,1},{9,13},{13,9},{2,6},{6,2},{1... | collective-permute-start | bytes 983048 | tf_op jit(solution)/shard_map/ppermute | solution.py:597

commit v14 on v13

--- a/solution.py
+++ b/solution.py
@@ -311,16 +311,23 @@
 
 def pack_body(spot, low, own, high, near, away):
     found, rows = chunks()
-    odd = spot[0] % 2 == 1
-    for plane in range(PLANES):
-        for wide, start, count in found:
-            ref = (low, own, high)[wide // LONS]
-            up = ref[plane, wide % LONS, SHELLS - count :, :]
-            down = ref[plane, wide % LONS, :count, :]
-            near[plane, start : start + count, :] = jnp.where(odd, down, up)
-            away[plane, start : start + count, :] = jnp.where(odd, up, down)
-        near[plane, rows:, :] = jnp.zeros((32 - rows, LATS), F32)
-        away[plane, rows:, :] = jnp.zeros((32 - rows, LATS), F32)
+
+    def pack(up, down):
+        for plane in range(PLANES):
+            for wide, start, count in found:
+                ref = (low, own, high)[wide // LONS]
+                up[plane, start : start + count, :] = ref[plane, wide % LONS, SHELLS - count :, :]
+                down[plane, start : start + count, :] = ref[plane, wide % LONS, :count, :]
+            up[plane, rows:, :] = jnp.zeros((32 - rows, LATS), F32)
+            down[plane, rows:, :] = jnp.zeros((32 - rows, LATS), F32)
+
+    @pl.when(spot[0] % 2 == 0)
+    def _():
+        pack(near, away)
+
+    @pl.when(spot[0] % 2 == 1)
+    def _():
+        pack(away, near)
 
 
 def main_body(low, own, high, above, below, from_low, from_high, out, cells, w, speeds):
@@ -355,8 +362,7 @@
             new = cells.at[(phase + 1) % 2]
             for wide in range(phase + 1, WIDE - 1 - phase):
                 c = old[wide]
-                made = blend(
-                    [w[i, wide] for i in range(7)],
+                sides = [
                     c,
                     pltpu.roll(c, 1, axis=0),
                     pltpu.roll(c, TALL - 1, axis=0),
@@ -364,11 +370,15 @@
                     old[wide + 1],
                     pltpu.roll(c, 1, axis=1),
                     pltpu.roll(c, 2 * LATS - 1, axis=1),
-                )
+                ]
                 if phase == PHASES - 1:
-                    out[field, pl.ds(wide - LONS, SHELLS, stride=LONS), :] = made[:SHELLS, :LATS]
+                    made = blend(
+                        [w[i, wide, :SHELLS, :LATS] for i in range(7)],
+                        *[side[:SHELLS, :LATS] for side in sides],
+                    )
+                    out[field, pl.ds(wide - LONS, SHELLS, stride=LONS), :] = made
                 else:
-                    new[wide] = made
+                    new[wide] = blend([w[i, wide] for i in range(7)], *sides)
         return carry
 
     lax.fori_loop(0, FIELDS, one, 0)

time: 83.5 us -> 83.5 us (level)
  no operation moved by 1% of the time
where the time goes in v14:
time: 83.5 us; the launch traced here: 83 us
  starting transfers between devices  37 us (44%)
  waiting for transfers between devices  30.4 us (36%)
  Pallas kernels  14.6 us (17%)
    ppermute x1, waiting for transfers between devices, shards(): far = lax.ppermute(inner, 'sec', [(0, 3)])  17 us
    ppermute x1, starting transfers between devices, shards(): first_swap = lax.ppermute(own, 'lon', wrap)  11.5 us
    pallas_call x8, Pallas kernels, call(): pl.pallas_call(body, out_shape=out_shape, in_specs=specs, out_specs=[vmem...  11 us
    all_to_all x1, starting transfers between devices, shards(): late = lax.all_to_all(late, 'lon', split_axis=0, concat_axis=0, tiled=True)  6.82 us
    all_to_all x1, waiting for transfers between devices, shards(): lax.all_to_all(slots.reshape(4, SENT, LATS), 'rad', split_axis=0, concat_...  5.54 us
    all_to_all x1, starting transfers between devices, shards(): lax.all_to_all(slots.reshape(4, SENT, LATS), 'rad', split_axis=0, concat_...  4.02 us
    ppermute x1, waiting for transfers between devices, shards(): from_high = lax.ppermute(edges, 'rad', shift('rad', -1, False))  3.8 us
    ppermute x1, starting transfers between devices, shards(): other = lax.ppermute(mine, 'sec', [(0, 1), (1, 0), (2, 3), (3, 2)])  3.43 us
  transfers between devices with their start and end apart: 11, of which 8 were waited for; matrix products, arithmetic and copies ran while one was open for 0% of the time, Pallas kernels for 8%

profile of v14, /device:TPU:57, one launch (start us, length us, event | category | flops | bytes accessed | tf_op | source)
XLA Modules:
  0.0 83.0 jit_solution(10273778535505101613)
XLA Ops:
  0.6 2.2 %shard_map.94 = (f32[12,4,16,128]{3,2,1,0:T(8,128)}, f32[544,128]{1,0:T(8,128)}) custom-call(f32[8,64,128]{2,1,0:T(8,128)} %bitcast.20, bf16[3,16,4,128]{3,2,1,0:T(4,128)(2,1)} %refs_1_.1, bf16[16,4,128]{2,1,0:T(4,128)(2,1)} %refs_2_.1, s32[1,128]{1,0:T(1,128)} %bitcast.22, s32[1,128]{1,0:T(1,128)} %bitcast.23, s32[128,256]{1,0:T(8,128)} %refs_5_.1, ...), custom_call_target="tpu_custom_call" | custom-call | flops 1000000 | bytes 1000000 | tf_op jit(solution)/shard_map/pallas_call | solution.py:88
  2.9 11.5 %collective-permute-start = (f32[12,4,16,128]{3,2,1,0:T(8,128)}, f32[12,4,16,128]{3,2,1,0:T(8,128)S(1)}, u32[]{:S(2)}, u32[]{:S(2)}) collective-permute-start(f32[12,4,16,128]{3,2,1,0:T(8,128)} %get-tuple-element.28.own), channel_id=1, source_target_pairs={{0,496},{16,32},{32,16},{48,64},{64,48},{80,96},{96,80},{112,128},... | collective-permute-start | bytes 1179656 | tf_op jit(solution)/shard_map/ppermute | solution.py:530
  14.3 1.9 %collective-permute-start.1 = (f32[12,4,16,128]{3,2,1,0:T(8,128)}, f32[12,4,16,128]{3,2,1,0:T(8,128)S(1)}, u32[]{:S(2)}, u32[]{:S(2)}) collective-permute-start(f32[12,4,16,128]{3,2,1,0:T(8,128)} %get-tuple-element.28.own), channel_id=1, source_target_pairs={{0,16},{16,0},{32,48},{48,32},{64,80},{80,64},{96,112},{112,96},{1... | collective-permute-start | bytes 1179656 | tf_op jit(solution)/shard_map/ppermute | solution.py:531
  16.2 4.0 %all-to-all-start.1 = ((f32[4,136,128]{2,1,0:T(8,128)}), f32[4,136,128]{2,1,0:T(8,128)S(1)}, u32[]{:S(2)}, u32[]{:S(2)}) async-start(f32[4,136,128]{2,1,0:T(8,128)} %bitcast.19), calls=%async_computation.1 | async-start | bytes 557056 | tf_op jit(solution)/shard_map/all_to_all | solution.py:533
  20.3 0.1 pad_add_fusion.spot
  20.3 0.0 copy-start
  20.3 5.5 %all-to-all-done.1 = f32[4,136,128]{2,1,0:T(8,128)S(1)} async-done(((f32[4,136,128]{2,1,0:T(8,128)}), f32[4,136,128]{2,1,0:T(8,128)S(1)}, u32[]{:S(2)}, u32[]{:S(2)}) %all-to-all-start.1) | async-done | bytes 278560 | tf_op jit(solution)/shard_map/all_to_all | solution.py:533
  25.9 0.0 collective-permute-done
  25.9 0.2 collective-permute-done.1
  26.1 0.1 broadcast_select_fusion
  26.2 0.0 copy-done
  26.2 0.7 shard_map.95
  26.8 0.7 collective-permute-start.2
  27.5 0.1 shard_map.96
  27.6 0.0 collective-permute-done.2
  27.6 1.3 %collective-permute-start.3 = (f32[24,128]{1,0:T(8,128)S(1)}, f32[24,128]{1,0:T(8,128)S(1)}, u32[]{:S(2)}, u32[]{:S(2)}) collective-permute-start(f32[24,128]{1,0:T(8,128)S(1)} %get-tuple-element.53), channel_id=1, source_target_pairs={{0,12},{1,13},{2,14},{3,15},{16,28},{17,29},{18,30},{19,31},{32,44... | collective-permute-start | bytes 36872 | tf_op jit(solution)/shard_map/ppermute | solution.py:564
  28.9 17.0 %collective-permute-done.3 = f32[24,128]{1,0:T(8,128)S(1)} collective-permute-done((f32[24,128]{1,0:T(8,128)S(1)}, f32[24,128]{1,0:T(8,128)S(1)}, u32[]{:S(2)}, u32[]{:S(2)}) %collective-permute-start.3) | collective-permute-done | bytes 12320 | tf_op jit(solution)/shard_map/ppermute | solution.py:564
  46.0 1.3 %collective-permute-start.4 = (f32[24,128]{1,0:T(8,128)S(1)}, f32[24,128]{1,0:T(8,128)S(1)}, u32[]{:S(2)}, u32[]{:S(2)}) collective-permute-start(f32[24,128]{1,0:T(8,128)S(1)} %add.11.one), channel_id=1, source_target_pairs={{0,4},{12,8},{1,5},{13,9},{2,6},{14,10},{3,7},{15,11},{16,20},{28,... | collective-permute-start | bytes 36872 | tf_op jit(solution)/shard_map/ppermute | solution.py:566
  47.3 0.6 shard_map.97
  47.9 0.2 collective-permute-done.4.two
  48.1 1.4 %shard_map.98 = f32[32,40,128]{2,1,0:T(8,128)} custom-call(s32[3]{0:T(128)S(1)} %pad_add_fusion.spot, f32[24,128]{1,0:T(8,128)S(1)} %add.11.one, f32[24,128]{1,0:T(8,128)S(1)} %collective-permute-done.4.two, f32[4,128]{1,0:T(4,128)S(1)} %get-tuple-element.35.cond, f32[32,24,128]{2,1,0:T(8,128)S(1)} %bitcast.17), custom_call_target="tpu_custom_call" | custom-call | flops 100000 | bytes 1000000 | tf_op jit(solution)/shard_map/pallas_call | solution.py:266
  49.5 6.8 %all-to-all-start.2 = ((f32[32,40,128]{2,1,0:T(8,128)}), f32[32,40,128]{2,1,0:T(8,128)S(1)}, u32[]{:S(2)}, u32[]{:S(2)}) async-start(f32[32,40,128]{2,1,0:T(8,128)} %shard_map.98), calls=%async_computation.2 | async-start | bytes 1310720 | tf_op jit(solution)/shard_map/all_to_all | solution.py:589
  56.3 2.6 %collective-permute-start.5 = (f32[12,32,128]{2,1,0:T(8,128)S(1)}, f32[12,32,128]{2,1,0:T(8,128)S(1)}, u32[]{:S(2)}, u32[]{:S(2)}) collective-permute-start(f32[12,32,128]{2,1,0:T(8,128)S(1)} %get-tuple-element.42), channel_id=1, source_target_pairs={{0,4},{4,0},{8,12},{12,8},{1,5},{5,1},{9,13},{13,9},{2,6},{6,2},{1... | collective-permute-start | bytes 589832 | tf_op jit(solution)/shard_map/ppermute | solution.py:575
  58.9 1.0 %collective-permute-done.5 = f32[12,32,128]{2,1,0:T(8,128)S(1)} collective-permute-done((f32[12,32,128]{2,1,0:T(8,128)S(1)}, f32[12,32,128]{2,1,0:T(8,128)S(1)}, u32[]{:S(2)}, u32[]{:S(2)}) %collective-permute-start.5) | collective-permute-done | bytes 196640 | tf_op jit(solution)/shard_map/ppermute | solution.py:575
  60.0 0.5 shard_map.99
  60.5 2.2 %collective-permute-start.6 = (f32[12,24,128]{2,1,0:T(8,128)S(1)}, f32[12,24,128]{2,1,0:T(8,128)S(1)}, u32[]{:S(2)}, u32[]{:S(2)}) collective-permute-start(f32[12,24,128]{2,1,0:T(8,128)S(1)} %shard_map.99), channel_id=1, source_target_pairs={{0,1},{1,2},{2,3},{4,5},{5,6},{6,7},{8,9},{9,10},{10,11},{12,13},{... | collective-permute-start | bytes 442376 | tf_op jit(solution)/shard_map/ppermute | solution.py:587
  62.7 1.3 %collective-permute-start.7 = (f32[12,24,128]{2,1,0:T(8,128)S(1)}, f32[12,24,128]{2,1,0:T(8,128)S(1)}, u32[]{:S(2)}, u32[]{:S(2)}) collective-permute-start(f32[12,24,128]{2,1,0:T(8,128)S(1)} %shard_map.99), channel_id=1, source_target_pairs={{1,0},{2,1},{3,2},{5,4},{6,5},{7,6},{9,8},{10,9},{11,10},{13,12},{... | collective-permute-start | bytes 442376 | tf_op jit(solution)/shard_map/ppermute | solution.py:588
  64.0 1.5 %collective-permute-done.6.from_low = f32[12,24,128]{2,1,0:T(8,128)S(1)} collective-permute-done((f32[12,24,128]{2,1,0:T(8,128)S(1)}, f32[12,24,128]{2,1,0:T(8,128)S(1)}, u32[]{:S(2)}, u32[]{:S(2)}) %collective-permute-start.6) | collective-permute-done | bytes 147488 | tf_op jit(solution)/shard_map/ppermute | solution.py:587
  65.5 3.8 %collective-permute-done.7.from_high = f32[12,24,128]{2,1,0:T(8,128)S(1)} collective-permute-done((f32[12,24,128]{2,1,0:T(8,128)S(1)}, f32[12,24,128]{2,1,0:T(8,128)S(1)}, u32[]{:S(2)}, u32[]{:S(2)}) %collective-permute-start.7) | collective-permute-done | bytes 147488 | tf_op jit(solution)/shard_map/ppermute | solution.py:588
  69.3 5.4 %shard_map.100 = f32[8,64,128]{2,1,0:T(8,128)} custom-call(f32[12,4,16,128]{3,2,1,0:T(8,128)S(1)} %get-tuple-element.39.low, f32[12,4,16,128]{3,2,1,0:T(8,128)S(1)} %copy-done, f32[12,4,16,128]{3,2,1,0:T(8,128)S(1)} %get-tuple-element.40.high, f32[12,32,128]{2,1,0:T(8,128)S(1)} %get-tuple-element.52.above, f32[12,32,128]{2,1,0:T(8,128)S(1)} %get-tuple-element.51.below, ...), custom_call_target="tpu_custom_call" | custom-call | flops 1000000 | bytes 1000000 | tf_op jit(solution)/shard_map/pallas_call | solution.py:36
  74.8 0.0 all-to-all-done.2
  74.8 0.1 shard_map.101.mine
  74.9 3.4 %collective-permute-start.8 = (f32[20,32,128]{2,1,0:T(8,128)S(1)}, f32[20,32,128]{2,1,0:T(8,128)S(1)}, u32[]{:S(2)}, u32[]{:S(2)}) collective-permute-start(f32[20,32,128]{2,1,0:T(8,128)S(1)} %shard_map.101.mine), channel_id=1, source_target_pairs={{0,4},{4,0},{8,12},{12,8},{1,5},{5,1},{9,13},{13,9},{2,6},{6,2},{1... | collective-permute-start | bytes 983048 | tf_op jit(solution)/shard_map/ppermute | solution.py:607
  78.3 0.1 shard_map.102
  78.4 1.1 %collective-permute-done.8.other = f32[20,32,128]{2,1,0:T(8,128)S(1)} collective-permute-done((f32[20,32,128]{2,1,0:T(8,128)S(1)}, f32[20,32,128]{2,1,0:T(8,128)S(1)}, u32[]{:S(2)}, u32[]{:S(2)}) %collective-permute-start.8) | collective-permute-done | bytes 327712 | tf_op jit(solution)/shard_map/ppermute | solution.py:607
  79.5 3.5 %shard_map.103 = (f32[4,128]{1,0:T(4,128)}, f32[32,256]{1,0:T(8,128)}) custom-call(s32[3]{0:T(128)S(1)} %pad_add_fusion.spot, f32[20,32,128]{2,1,0:T(8,128)S(1)} %shard_map.101.mine, f32[20,32,128]{2,1,0:T(8,128)S(1)} %collective-permute-done.8.other, s32[16,32,128]{2,1,0:T(8,128)S(1)} %get-tuple-element.45.cells, f32[32,256]{1,0:T(8,128)S(1)} %get-tuple-element.46.hot), custom_call_target="tpu_custom_call" | custom-call | flops 1000000 | bytes 1000000 | tf_op jit(solution)/shard_map/pallas_call | solution.py:36
  (4 shorter events, 0.1 us)
Async XLA Ops:
  2.9 23.0 %collective-permute-start = (f32[12,4,16,128]{3,2,1,0:T(8,128)}, f32[12,4,16,128]{3,2,1,0:T(8,128)S(1)}, u32[]{:S(2)}, u32[]{:S(2)}) collective-permute-start(f32[12,4,16,128]{3,2,1,0:T(8,128)} %get-tuple-element.28.own), channel_id=1, source_target_pairs={{0,496},{16,32},{32,16},{48,64},{64,48},{80,96},{96,80},{112,128},... | collective-permute-start | bytes 1179656 | tf_op jit(solution)/shard_map/ppermute | solution.py:530
  14.3 11.8 %collective-permute-start.1 = (f32[12,4,16,128]{3,2,1,0:T(8,128)}, f32[12,4,16,128]{3,2,1,0:T(8,128)S(1)}, u32[]{:S(2)}, u32[]{:S(2)}) collective-permute-start(f32[12,4,16,128]{3,2,1,0:T(8,128)} %get-tuple-element.28.own), channel_id=1, source_target_pairs={{0,16},{16,0},{32,48},{48,32},{64,80},{80,64},{96,112},{112,96},{1... | collective-permute-start | bytes 1179656 | tf_op jit(solution)/shard_map/ppermute | solution.py:531
  16.2 9.6 %all-to-all-start.1 = ((f32[4,136,128]{2,1,0:T(8,128)}), f32[4,136,128]{2,1,0:T(8,128)S(1)}, u32[]{:S(2)}, u32[]{:S(2)}) async-start(f32[4,136,128]{2,1,0:T(8,128)} %bitcast.19), calls=%async_computation.1 | async-start | bytes 557056 | tf_op jit(solution)/shard_map/all_to_all | solution.py:533
  20.3 5.8 %copy-start = (f32[12,4,16,128]{3,2,1,0:T(8,128)S(1)}, f32[12,4,16,128]{3,2,1,0:T(8,128)}, u32[]{:S(2)}) copy-start(f32[12,4,16,128]{3,2,1,0:T(8,128)} %get-tuple-element.28.own) | copy-start | bytes 1179652
  26.8 0.8 collective-permute-start.2
  27.6 18.3 %collective-permute-start.3 = (f32[24,128]{1,0:T(8,128)S(1)}, f32[24,128]{1,0:T(8,128)S(1)}, u32[]{:S(2)}, u32[]{:S(2)}) collective-permute-start(f32[24,128]{1,0:T(8,128)S(1)} %get-tuple-element.53), channel_id=1, source_target_pairs={{0,12},{1,13},{2,14},{3,15},{16,28},{17,29},{18,30},{19,31},{32,44... | collective-permute-start | bytes 36872 | tf_op jit(solution)/shard_map/ppermute | solution.py:564
  46.0 2.1 %collective-permute-start.4 = (f32[24,128]{1,0:T(8,128)S(1)}, f32[24,128]{1,0:T(8,128)S(1)}, u32[]{:S(2)}, u32[]{:S(2)}) collective-permute-start(f32[24,128]{1,0:T(8,128)S(1)} %add.11.one), channel_id=1, source_target_pairs={{0,4},{12,8},{1,5},{13,9},{2,6},{14,10},{3,7},{15,11},{16,20},{28,... | collective-permute-start | bytes 36872 | tf_op jit(solution)/shard_map/ppermute | solution.py:566
  49.5 25.3 %all-to-all-start.2 = ((f32[32,40,128]{2,1,0:T(8,128)}), f32[32,40,128]{2,1,0:T(8,128)S(1)}, u32[]{:S(2)}, u32[]{:S(2)}) async-start(f32[32,40,128]{2,1,0:T(8,128)} %shard_map.98), calls=%async_computation.2 | async-start | bytes 1310720 | tf_op jit(solution)/shard_map/all_to_all | solution.py:589
  56.3 3.6 %collective-permute-start.5 = (f32[12,32,128]{2,1,0:T(8,128)S(1)}, f32[12,32,128]{2,1,0:T(8,128)S(1)}, u32[]{:S(2)}, u32[]{:S(2)}) collective-permute-start(f32[12,32,128]{2,1,0:T(8,128)S(1)} %get-tuple-element.42), channel_id=1, source_target_pairs={{0,4},{4,0},{8,12},{12,8},{1,5},{5,1},{9,13},{13,9},{2,6},{6,2},{1... | collective-permute-start | bytes 589832 | tf_op jit(solution)/shard_map/ppermute | solution.py:575
  60.5 5.0 %collective-permute-start.6 = (f32[12,24,128]{2,1,0:T(8,128)S(1)}, f32[12,24,128]{2,1,0:T(8,128)S(1)}, u32[]{:S(2)}, u32[]{:S(2)}) collective-permute-start(f32[12,24,128]{2,1,0:T(8,128)S(1)} %shard_map.99), channel_id=1, source_target_pairs={{0,1},{1,2},{2,3},{4,5},{5,6},{6,7},{8,9},{9,10},{10,11},{12,13},{... | collective-permute-start | bytes 442376 | tf_op jit(solution)/shard_map/ppermute | solution.py:587
  62.7 6.6 %collective-permute-start.7 = (f32[12,24,128]{2,1,0:T(8,128)S(1)}, f32[12,24,128]{2,1,0:T(8,128)S(1)}, u32[]{:S(2)}, u32[]{:S(2)}) collective-permute-start(f32[12,24,128]{2,1,0:T(8,128)S(1)} %shard_map.99), channel_id=1, source_target_pairs={{1,0},{2,1},{3,2},{5,4},{6,5},{7,6},{9,8},{10,9},{11,10},{13,12},{... | collective-permute-start | bytes 442376 | tf_op jit(solution)/shard_map/ppermute | solution.py:588
  74.9 4.7 %collective-permute-start.8 = (f32[20,32,128]{2,1,0:T(8,128)S(1)}, f32[20,32,128]{2,1,0:T(8,128)S(1)}, u32[]{:S(2)}, u32[]{:S(2)}) collective-permute-start(f32[20,32,128]{2,1,0:T(8,128)S(1)} %shard_map.101.mine), channel_id=1, source_target_pairs={{0,4},{4,0},{8,12},{12,8},{1,5},{5,1},{9,13},{13,9},{2,6},{6,2},{1... | collective-permute-start | bytes 983048 | tf_op jit(solution)/shard_map/ppermute | solution.py:607

commit v15 on v14

--- a/solution.py
+++ b/solution.py
@@ -46,6 +46,10 @@
 
 def arr(*shape):
     return jax.ShapeDtypeStruct(shape, F32)
+
+
+def where():
+    return [lax.axis_index(axis) for axis in ("sec", "rad", "lon")]
 
 
 def shift(axis, step, closed):
@@ -220,7 +224,8 @@
                 out[at + 2 : at + 3, :] = blat[LONS - 1][0:1, part]
 
 
-def base_body(spot, sent, out, cond):
+def base_body(sent, out, cond):
+    spot = where()
     step = LATE - 16
     odd = spot[0] % 2 == 1
     for lon in range(LONS):
@@ -245,10 +250,11 @@
         out[pl.ds(8 + rad * 5, 32, stride=step), :] = jnp.where(lane < 64, marks[0], marks[1])
 
 
-def join_body(spot, one, two, cond, base, out, head, copies, sems):
+def join_body(one, two, cond, base, out, head, copies, sems):
     rest = pltpu.make_async_copy(base, out.at[:, pl.ds(16, LATE - 16), :], sems.at[0])
     rest.start()
     source = one[...] + two[...]
+    spot = where()
     head[:12, :] = jnp.where(spot[0] % 2 == 1, source[12:], source[:12])
     head[12:, :] = cond[...]
     mine = head[...]
@@ -260,13 +266,13 @@
     rest.wait()
 
 
-def join(spot, one, two, cond, base):
+def join(one, two, cond, base):
     vmem = pl.BlockSpec(memory_space=pltpu.VMEM)
     plain = pl.BlockSpec(memory_space=pl.ANY)
     return pl.pallas_call(
         join_body,
         out_shape=arr(32, LATE, LATS),
-        in_specs=[pl.BlockSpec(memory_space=pltpu.SMEM), vmem, vmem, vmem, plain],
+        in_specs=[vmem, vmem, vmem, plain],
         out_specs=plain,
         scratch_shapes=[
             pltpu.VMEM((16, LATS), F32),
@@ -275,7 +281,7 @@
         ],
         compiler_params=pltpu.CompilerParams(vmem_limit_bytes=4 * 2**20),
         cost_estimate=pl.CostEstimate(flops=10**5, bytes_accessed=10**6, transcendentals=0),
-    )(spot, one, two, cond, base)
+    )(one, two, cond, base)
 
 
 def half_body(late, out):
@@ -309,8 +315,9 @@
     return found, at
 
 
-def pack_body(spot, low, own, high, near, away):
+def pack_body(low, own, high, near, away):
     found, rows = chunks()
+    spot = where()
 
     def pack(up, down):
         for plane in range(PLANES):
@@ -419,9 +426,10 @@
 
 
 def final_body(
-    spot, mine, other, cells, hot, pot, foot, phi, east_w, west_w, north_w, south_w, start, picked
+    mine, other, cells, hot, pot, foot, phi, east_w, west_w, north_w, south_w, start, picked
 ):
     devs, rads = 32, 4
+    spot = where()
     wide = rads * LATS
     lane = lax.broadcasted_iota(jnp.int32, (devs, wide), 1)
 
@@ -515,7 +523,6 @@
 
 
 def shards(plasma_fields, velocity, resistivity, conductance, foot_map, foot_owner, foot_row):
-    spot = jnp.stack([lax.axis_index("sec"), lax.axis_index("rad"), lax.axis_index("lon")])
     own, slots = first(
         plasma_fields.reshape(FIELDS, SHELLS * LONS, LATS),
         velocity,
@@ -541,8 +548,7 @@
     near_rows, away_rows = call(
         pack_body,
         (arr(PLANES, 32, LATS), arr(PLANES, 32, LATS)),
-        (spot, low, own, high),
-        smem=(0,),
+        (low, own, high),
     )
     away_rows = lax.ppermute(away_rows, "sec", [(1, 2), (2, 1)])
     raw = call(raw_body, arr(4 * RAW, LATS), (low, own, high))
@@ -567,10 +573,9 @@
     base, cond = call(
         base_body,
         (arr(32 * (LATE - 16), LATS), arr(LONS, LATS)),
-        (spot, sent.reshape(4 * SENT, LATS)),
-        smem=(0,),
-    )
-    late = join(spot, far, near, cond, base.reshape(32, LATE - 16, LATS))
+        (sent.reshape(4 * SENT, LATS),),
+    )
+    late = join(far, near, cond, base.reshape(32, LATE - 16, LATS))
     late, low, high, near_rows = lax.optimization_barrier((late, low, high, near_rows))
     near_rows = lax.ppermute(near_rows, "sec", [(0, 1), (1, 0), (2, 3), (3, 2)])
 
@@ -615,7 +620,7 @@
     potential, foot_table = call(
         final_body,
         (arr(LONS, LATS), arr(ROWS_OWN, 256)),
-        (spot, mine, other, cells, hot),
+        (mine, other, cells, hot),
         scratch=(
             pltpu.VMEM((2, LONS, 32, 4 * LATS), F32),
             plane,
@@ -625,7 +630,6 @@
             plane,
             pltpu.VMEM((256, 256), F32),
         ),
-        smem=(0,),
     )
     return (advanced, potential, foot_table)
 

time: 83.5 us -> 81.9 us (0.981)
  Pallas kernels: 14.6 us -> 12.5 us
    pallas_call x8, Pallas kernels: 11 us -> 9.36 us  [call(): pl.pallas_call(body, out_shape=out_shape, in_specs=specs, out_specs=[vmem...]
where the time goes in v15:
time: 81.9 us; the launch traced here: 81.3 us
  starting transfers between devices  37 us (45%)
  waiting for transfers between devices  31 us (38%)
  Pallas kernels  12.5 us (15%)
  between operations  0.83 us (1%)
    ppermute x1, waiting for transfers between devices, shards(): far = lax.ppermute(inner, 'sec', [(0, 3)])  17 us
    ppermute x1, starting transfers between devices, shards(): first_swap = lax.ppermute(own, 'lon', wrap)  11.5 us
    pallas_call x8, Pallas kernels, call(): pl.pallas_call(body, out_shape=out_shape, in_specs=specs, out_specs=[vmem...  9.36 us
    all_to_all x1, starting transfers between devices, shards(): late = lax.all_to_all(late, 'lon', split_axis=0, concat_axis=0, tiled=True)  6.82 us
    all_to_all x1, waiting for transfers between devices, shards(): lax.all_to_all(slots.reshape(4, SENT, LATS), 'rad', split_axis=0, concat_...  5.62 us
    all_to_all x1, starting transfers between devices, shards(): lax.all_to_all(slots.reshape(4, SENT, LATS), 'rad', split_axis=0, concat_...  4.02 us
    ppermute x1, waiting for transfers between devices, shards(): from_high = lax.ppermute(edges, 'rad', shift('rad', -1, False))  3.8 us
    ppermute x1, starting transfers between devices, shards(): other = lax.ppermute(mine, 'sec', [(0, 1), (1, 0), (2, 3), (3, 2)])  3.43 us
  transfers between devices with their start and end apart: 11, of which 8 were waited for; matrix products, arithmetic and copies ran while one was open for 0% of the time, Pallas kernels for 8%

profile of v15, /device:TPU:57, one launch (start us, length us, event | category | flops | bytes accessed | tf_op | source)
XLA Modules:
  0.0 81.3 jit_solution(11937146025510380571)
XLA Ops:
  0.6 2.2 %shard_map.94 = (f32[12,4,16,128]{3,2,1,0:T(8,128)}, f32[544,128]{1,0:T(8,128)}) custom-call(f32[8,64,128]{2,1,0:T(8,128)} %bitcast.17, bf16[3,16,4,128]{3,2,1,0:T(4,128)(2,1)} %refs_1_.1, bf16[16,4,128]{2,1,0:T(4,128)(2,1)} %refs_2_.1, s32[1,128]{1,0:T(1,128)} %bitcast.19, s32[1,128]{1,0:T(1,128)} %bitcast.20, s32[128,256]{1,0:T(8,128)} %refs_5_.1, ...), custom_call_target="tpu_custom_call" | custom-call | flops 1000000 | bytes 1000000 | tf_op jit(solution)/shard_map/pallas_call | solution.py:92
  2.9 11.5 %collective-permute-start = (f32[12,4,16,128]{3,2,1,0:T(8,128)}, f32[12,4,16,128]{3,2,1,0:T(8,128)S(1)}, u32[]{:S(2)}, u32[]{:S(2)}) collective-permute-start(f32[12,4,16,128]{3,2,1,0:T(8,128)} %get-tuple-element.28.own), channel_id=1, source_target_pairs={{0,496},{16,32},{32,16},{48,64},{64,48},{80,96},{96,80},{112,128},... | collective-permute-start | bytes 1179656 | tf_op jit(solution)/shard_map/ppermute | solution.py:537
  14.3 1.9 %collective-permute-start.1 = (f32[12,4,16,128]{3,2,1,0:T(8,128)}, f32[12,4,16,128]{3,2,1,0:T(8,128)S(1)}, u32[]{:S(2)}, u32[]{:S(2)}) collective-permute-start(f32[12,4,16,128]{3,2,1,0:T(8,128)} %get-tuple-element.28.own), channel_id=1, source_target_pairs={{0,16},{16,0},{32,48},{48,32},{64,80},{80,64},{96,112},{112,96},{1... | collective-permute-start | bytes 1179656 | tf_op jit(solution)/shard_map/ppermute | solution.py:538
  16.2 4.0 %all-to-all-start.1 = ((f32[4,136,128]{2,1,0:T(8,128)}), f32[4,136,128]{2,1,0:T(8,128)S(1)}, u32[]{:S(2)}, u32[]{:S(2)}) async-start(f32[4,136,128]{2,1,0:T(8,128)} %bitcast.16), calls=%async_computation.1 | async-start | bytes 557056 | tf_op jit(solution)/shard_map/all_to_all | solution.py:540
  20.3 0.0 copy-start
  20.3 5.6 %all-to-all-done.1 = f32[4,136,128]{2,1,0:T(8,128)S(1)} async-done(((f32[4,136,128]{2,1,0:T(8,128)}), f32[4,136,128]{2,1,0:T(8,128)S(1)}, u32[]{:S(2)}, u32[]{:S(2)}) %all-to-all-start.1) | async-done | bytes 278560 | tf_op jit(solution)/shard_map/all_to_all | solution.py:540
  25.9 0.0 collective-permute-done
  25.9 0.2 collective-permute-done.1
  26.1 0.1 broadcast_select_fusion
  26.2 0.0 copy-done
  26.2 0.1 shard_map.95
  26.3 0.7 collective-permute-start.2
  27.0 0.1 shard_map.96
  27.1 0.0 collective-permute-done.2
  27.1 1.3 %collective-permute-start.3 = (f32[24,128]{1,0:T(8,128)S(1)}, f32[24,128]{1,0:T(8,128)S(1)}, u32[]{:S(2)}, u32[]{:S(2)}) collective-permute-start(f32[24,128]{1,0:T(8,128)S(1)} %get-tuple-element.53), channel_id=1, source_target_pairs={{0,12},{1,13},{2,14},{3,15},{16,28},{17,29},{18,30},{19,31},{32,44... | collective-permute-start | bytes 36872 | tf_op jit(solution)/shard_map/ppermute | solution.py:570
  28.4 17.0 %collective-permute-done.3 = f32[24,128]{1,0:T(8,128)S(1)} collective-permute-done((f32[24,128]{1,0:T(8,128)S(1)}, f32[24,128]{1,0:T(8,128)S(1)}, u32[]{:S(2)}, u32[]{:S(2)}) %collective-permute-start.3) | collective-permute-done | bytes 12320 | tf_op jit(solution)/shard_map/ppermute | solution.py:570
  45.4 1.3 %collective-permute-start.4 = (f32[24,128]{1,0:T(8,128)S(1)}, f32[24,128]{1,0:T(8,128)S(1)}, u32[]{:S(2)}, u32[]{:S(2)}) collective-permute-start(f32[24,128]{1,0:T(8,128)S(1)} %add.11.one), channel_id=1, source_target_pairs={{0,4},{12,8},{1,5},{13,9},{2,6},{14,10},{3,7},{15,11},{16,20},{28,... | collective-permute-start | bytes 36872 | tf_op jit(solution)/shard_map/ppermute | solution.py:572
  46.7 0.2 shard_map.97
  46.9 0.7 collective-permute-done.4.two
  47.6 0.9 %shard_map.98 = f32[32,40,128]{2,1,0:T(8,128)} custom-call(f32[24,128]{1,0:T(8,128)S(1)} %add.11.one, f32[24,128]{1,0:T(8,128)S(1)} %collective-permute-done.4.two, f32[4,128]{1,0:T(4,128)S(1)} %get-tuple-element.35.cond, f32[32,24,128]{2,1,0:T(8,128)S(1)} %bitcast.14), custom_call_target="tpu_custom_call" | custom-call | flops 100000 | bytes 1000000 | tf_op jit(solution)/shard_map/pallas_call | solution.py:272
  48.5 6.8 %all-to-all-start.2 = ((f32[32,40,128]{2,1,0:T(8,128)}), f32[32,40,128]{2,1,0:T(8,128)S(1)}, u32[]{:S(2)}, u32[]{:S(2)}) async-start(f32[32,40,128]{2,1,0:T(8,128)} %shard_map.98), calls=%async_computation.2 | async-start | bytes 1310720 | tf_op jit(solution)/shard_map/all_to_all | solution.py:594
  55.3 2.6 %collective-permute-start.5 = (f32[12,32,128]{2,1,0:T(8,128)S(1)}, f32[12,32,128]{2,1,0:T(8,128)S(1)}, u32[]{:S(2)}, u32[]{:S(2)}) collective-permute-start(f32[12,32,128]{2,1,0:T(8,128)S(1)} %get-tuple-element.42), channel_id=1, source_target_pairs={{0,4},{4,0},{8,12},{12,8},{1,5},{5,1},{9,13},{13,9},{2,6},{6,2},{1... | collective-permute-start | bytes 589832 | tf_op jit(solution)/shard_map/ppermute | solution.py:580
  57.9 1.0 %collective-permute-done.5 = f32[12,32,128]{2,1,0:T(8,128)S(1)} collective-permute-done((f32[12,32,128]{2,1,0:T(8,128)S(1)}, f32[12,32,128]{2,1,0:T(8,128)S(1)}, u32[]{:S(2)}, u32[]{:S(2)}) %collective-permute-start.5) | collective-permute-done | bytes 196640 | tf_op jit(solution)/shard_map/ppermute | solution.py:580
  58.9 0.5 shard_map.99
  59.4 2.2 %collective-permute-start.6 = (f32[12,24,128]{2,1,0:T(8,128)S(1)}, f32[12,24,128]{2,1,0:T(8,128)S(1)}, u32[]{:S(2)}, u32[]{:S(2)}) collective-permute-start(f32[12,24,128]{2,1,0:T(8,128)S(1)} %shard_map.99), channel_id=1, source_target_pairs={{0,1},{1,2},{2,3},{4,5},{5,6},{6,7},{8,9},{9,10},{10,11},{12,13},{... | collective-permute-start | bytes 442376 | tf_op jit(solution)/shard_map/ppermute | solution.py:592
  61.6 1.3 %collective-permute-start.7 = (f32[12,24,128]{2,1,0:T(8,128)S(1)}, f32[12,24,128]{2,1,0:T(8,128)S(1)}, u32[]{:S(2)}, u32[]{:S(2)}) collective-permute-start(f32[12,24,128]{2,1,0:T(8,128)S(1)} %shard_map.99), channel_id=1, source_target_pairs={{1,0},{2,1},{3,2},{5,4},{6,5},{7,6},{9,8},{10,9},{11,10},{13,12},{... | collective-permute-start | bytes 442376 | tf_op jit(solution)/shard_map/ppermute | solution.py:593
  62.9 1.5 %collective-permute-done.6.from_low = f32[12,24,128]{2,1,0:T(8,128)S(1)} collective-permute-done((f32[12,24,128]{2,1,0:T(8,128)S(1)}, f32[12,24,128]{2,1,0:T(8,128)S(1)}, u32[]{:S(2)}, u32[]{:S(2)}) %collective-permute-start.6) | collective-permute-done | bytes 147488 | tf_op jit(solution)/shard_map/ppermute | solution.py:592
  64.5 3.8 %collective-permute-done.7.from_high = f32[12,24,128]{2,1,0:T(8,128)S(1)} collective-permute-done((f32[12,24,128]{2,1,0:T(8,128)S(1)}, f32[12,24,128]{2,1,0:T(8,128)S(1)}, u32[]{:S(2)}, u32[]{:S(2)}) %collective-permute-start.7) | collective-permute-done | bytes 147488 | tf_op jit(solution)/shard_map/ppermute | solution.py:593
  68.3 5.4 %shard_map.100 = f32[8,64,128]{2,1,0:T(8,128)} custom-call(f32[12,4,16,128]{3,2,1,0:T(8,128)S(1)} %get-tuple-element.39.low, f32[12,4,16,128]{3,2,1,0:T(8,128)S(1)} %copy-done, f32[12,4,16,128]{3,2,1,0:T(8,128)S(1)} %get-tuple-element.40.high, f32[12,32,128]{2,1,0:T(8,128)S(1)} %get-tuple-element.52.above, f32[12,32,128]{2,1,0:T(8,128)S(1)} %get-tuple-element.51.below, ...), custom_call_target="tpu_custom_call" | custom-call | flops 1000000 | bytes 1000000 | tf_op jit(solution)/shard_map/pallas_call | solution.py:36
  73.7 0.0 all-to-all-done.2
  73.7 0.1 shard_map.101.mine
  73.8 3.4 %collective-permute-start.8 = (f32[20,32,128]{2,1,0:T(8,128)S(1)}, f32[20,32,128]{2,1,0:T(8,128)S(1)}, u32[]{:S(2)}, u32[]{:S(2)}) collective-permute-start(f32[20,32,128]{2,1,0:T(8,128)S(1)} %shard_map.101.mine), channel_id=1, source_target_pairs={{0,4},{4,0},{8,12},{12,8},{1,5},{5,1},{9,13},{13,9},{2,6},{6,2},{1... | collective-permute-start | bytes 983048 | tf_op jit(solution)/shard_map/ppermute | solution.py:612
  77.2 0.1 shard_map.102
  77.3 1.1 %collective-permute-done.8.other = f32[20,32,128]{2,1,0:T(8,128)S(1)} collective-permute-done((f32[20,32,128]{2,1,0:T(8,128)S(1)}, f32[20,32,128]{2,1,0:T(8,128)S(1)}, u32[]{:S(2)}, u32[]{:S(2)}) %collective-permute-start.8) | collective-permute-done | bytes 327712 | tf_op jit(solution)/shard_map/ppermute | solution.py:612
  78.4 2.9 %shard_map.103 = (f32[4,128]{1,0:T(4,128)}, f32[32,256]{1,0:T(8,128)}) custom-call(f32[20,32,128]{2,1,0:T(8,128)S(1)} %shard_map.101.mine, f32[20,32,128]{2,1,0:T(8,128)S(1)} %collective-permute-done.8.other, s32[16,32,128]{2,1,0:T(8,128)S(1)} %get-tuple-element.45.cells, f32[32,256]{1,0:T(8,128)S(1)} %get-tuple-element.46.hot), custom_call_target="tpu_custom_call" | custom-call | flops 1000000 | bytes 1000000 | tf_op jit(solution)/shard_map/pallas_call | solution.py:36
  (4 shorter events, 0.1 us)
Async XLA Ops:
  2.9 23.0 %collective-permute-start = (f32[12,4,16,128]{3,2,1,0:T(8,128)}, f32[12,4,16,128]{3,2,1,0:T(8,128)S(1)}, u32[]{:S(2)}, u32[]{:S(2)}) collective-permute-start(f32[12,4,16,128]{3,2,1,0:T(8,128)} %get-tuple-element.28.own), channel_id=1, source_target_pairs={{0,496},{16,32},{32,16},{48,64},{64,48},{80,96},{96,80},{112,128},... | collective-permute-start | bytes 1179656 | tf_op jit(solution)/shard_map/ppermute | solution.py:537
  14.3 11.8 %collective-permute-start.1 = (f32[12,4,16,128]{3,2,1,0:T(8,128)}, f32[12,4,16,128]{3,2,1,0:T(8,128)S(1)}, u32[]{:S(2)}, u32[]{:S(2)}) collective-permute-start(f32[12,4,16,128]{3,2,1,0:T(8,128)} %get-tuple-element.28.own), channel_id=1, source_target_pairs={{0,16},{16,0},{32,48},{48,32},{64,80},{80,64},{96,112},{112,96},{1... | collective-permute-start | bytes 1179656 | tf_op jit(solution)/shard_map/ppermute | solution.py:538
  16.2 9.6 %all-to-all-start.1 = ((f32[4,136,128]{2,1,0:T(8,128)}), f32[4,136,128]{2,1,0:T(8,128)S(1)}, u32[]{:S(2)}, u32[]{:S(2)}) async-start(f32[4,136,128]{2,1,0:T(8,128)} %bitcast.16), calls=%async_computation.1 | async-start | bytes 557056 | tf_op jit(solution)/shard_map/all_to_all | solution.py:540
  20.3 5.9 %copy-start = (f32[12,4,16,128]{3,2,1,0:T(8,128)S(1)}, f32[12,4,16,128]{3,2,1,0:T(8,128)}, u32[]{:S(2)}) copy-start(f32[12,4,16,128]{3,2,1,0:T(8,128)} %get-tuple-element.28.own) | copy-start | bytes 1179652
  26.3 0.8 collective-permute-start.2
  27.1 18.3 %collective-permute-start.3 = (f32[24,128]{1,0:T(8,128)S(1)}, f32[24,128]{1,0:T(8,128)S(1)}, u32[]{:S(2)}, u32[]{:S(2)}) collective-permute-start(f32[24,128]{1,0:T(8,128)S(1)} %get-tuple-element.53), channel_id=1, source_target_pairs={{0,12},{1,13},{2,14},{3,15},{16,28},{17,29},{18,30},{19,31},{32,44... | collective-permute-start | bytes 36872 | tf_op jit(solution)/shard_map/ppermute | solution.py:570
  45.4 2.1 %collective-permute-start.4 = (f32[24,128]{1,0:T(8,128)S(1)}, f32[24,128]{1,0:T(8,128)S(1)}, u32[]{:S(2)}, u32[]{:S(2)}) collective-permute-start(f32[24,128]{1,0:T(8,128)S(1)} %add.11.one), channel_id=1, source_target_pairs={{0,4},{12,8},{1,5},{13,9},{2,6},{14,10},{3,7},{15,11},{16,20},{28,... | collective-permute-start | bytes 36872 | tf_op jit(solution)/shard_map/ppermute | solution.py:572
  48.5 25.2 %all-to-all-start.2 = ((f32[32,40,128]{2,1,0:T(8,128)}), f32[32,40,128]{2,1,0:T(8,128)S(1)}, u32[]{:S(2)}, u32[]{:S(2)}) async-start(f32[32,40,128]{2,1,0:T(8,128)} %shard_map.98), calls=%async_computation.2 | async-start | bytes 1310720 | tf_op jit(solution)/shard_map/all_to_all | solution.py:594
  55.3 3.6 %collective-permute-start.5 = (f32[12,32,128]{2,1,0:T(8,128)S(1)}, f32[12,32,128]{2,1,0:T(8,128)S(1)}, u32[]{:S(2)}, u32[]{:S(2)}) collective-permute-start(f32[12,32,128]{2,1,0:T(8,128)S(1)} %get-tuple-element.42), channel_id=1, source_target_pairs={{0,4},{4,0},{8,12},{12,8},{1,5},{5,1},{9,13},{13,9},{2,6},{6,2},{1... | collective-permute-start | bytes 589832 | tf_op jit(solution)/shard_map/ppermute | solution.py:580
  59.4 5.0 %collective-permute-start.6 = (f32[12,24,128]{2,1,0:T(8,128)S(1)}, f32[12,24,128]{2,1,0:T(8,128)S(1)}, u32[]{:S(2)}, u32[]{:S(2)}) collective-permute-start(f32[12,24,128]{2,1,0:T(8,128)S(1)} %shard_map.99), channel_id=1, source_target_pairs={{0,1},{1,2},{2,3},{4,5},{5,6},{6,7},{8,9},{9,10},{10,11},{12,13},{... | collective-permute-start | bytes 442376 | tf_op jit(solution)/shard_map/ppermute | solution.py:592
  61.6 6.6 %collective-permute-start.7 = (f32[12,24,128]{2,1,0:T(8,128)S(1)}, f32[12,24,128]{2,1,0:T(8,128)S(1)}, u32[]{:S(2)}, u32[]{:S(2)}) collective-permute-start(f32[12,24,128]{2,1,0:T(8,128)S(1)} %shard_map.99), channel_id=1, source_target_pairs={{1,0},{2,1},{3,2},{5,4},{6,5},{7,6},{9,8},{10,9},{11,10},{13,12},{... | collective-permute-start | bytes 442376 | tf_op jit(solution)/shard_map/ppermute | solution.py:593
  73.8 4.7 %collective-permute-start.8 = (f32[20,32,128]{2,1,0:T(8,128)S(1)}, f32[20,32,128]{2,1,0:T(8,128)S(1)}, u32[]{:S(2)}, u32[]{:S(2)}) collective-permute-start(f32[20,32,128]{2,1,0:T(8,128)S(1)} %shard_map.101.mine), channel_id=1, source_target_pairs={{0,4},{4,0},{8,12},{12,8},{1,5},{5,1},{9,13},{13,9},{2,6},{6,2},{1... | collective-permute-start | bytes 983048 | tf_op jit(solution)/shard_map/ppermute | solution.py:612
